TPU v7x, 32 devices: a whole 2x2x4 slice. The times are simulated.
32 devices in a mesh: dp: 8 (over y, x, core), tensor: 4 (over z).
Axes of the slice: x: 2, y: 2, z: 4, core: 2. Of those that a mesh axis runs over, the one named last changes fastest.
Arguments:
- content_stream: bfloat16 [16, 512, 768], P('dp', 'tensor'), may hold values from -6 to 6
- query_stream: bfloat16 [16, 512, 768], P('dp', 'tensor'), may hold values from -6 to 6
- memory: bfloat16 [16, 512, 768], P('dp', 'tensor'), may hold values from -6 to 6
- content_tangent: bfloat16 [16, 512, 768], P('dp', 'tensor'), may hold values from -6 to 6
- query_tangent: bfloat16 [16, 512, 768], P('dp', 'tensor'), may hold values from -6 to 6
- seq_lengths: int32 [16], P('dp'), may hold values from 128 to 512, as said below
- factor_order: int32 [16, 512], P('dp'), may hold values from 0 to 511, each once within a row
- memory_lengths: int32 [16], P('dp'), may hold values from 64 to 512, as said below
- slot_sequence: int32 [16], replicated, may hold values from 0 to 15, each once
- query_weight: bfloat16 [768, 768], P('dp', 'tensor'), may hold values from -0.21875 to 0.21875
- key_weight: bfloat16 [768, 768], P('dp', 'tensor'), may hold values from -0.21875 to 0.21875
- value_weight: bfloat16 [768, 768], P('dp', 'tensor'), may hold values from -0.21875 to 0.21875
- pos_weight: bfloat16 [768, 768], P('dp', 'tensor'), may hold values from -0.21875 to 0.21875
- out_weight: bfloat16 [768, 768], P('dp', 'tensor'), may hold values from -2 to 2
- up_weight: bfloat16 [768, 3072], P('dp', 'tensor'), may hold values from -0.21875 to 0.21875
- up_bias: float32 [3072], replicated, may hold values from -3 to 3
- down_weight: bfloat16 [768, 3072], P('dp', 'tensor'), may hold values from -0.109375 to 0.109375
- down_bias: float32 [768], replicated, may hold values from -2 to 2
- word_bias: float32 [12, 64], replicated, may hold values from -3 to 3
- pos_bias: float32 [12, 64], replicated, may hold values from -3 to 3
- first_gain: float32 [768], replicated, may hold values from 0.5 to 1.5
- first_shift: float32 [768], replicated, may hold values from -2 to 2
- second_gain: float32 [768], replicated, may hold values from 0.5 to 1.5
- second_shift: float32 [768], replicated, may hold values from -2 to 2
Outputs:
- content_out: bfloat16 [16, 512, 768], P('dp', 'tensor')
- query_out: bfloat16 [16, 512, 768], P('dp', 'tensor')
- content_grad: bfloat16 [16, 512, 768], P('dp', 'tensor')
- query_grad: bfloat16 [16, 512, 768], P('dp', 'tensor')
- grad_query: float32 [768, 768], P('dp', 'tensor')
- grad_key: float32 [768, 768], P('dp', 'tensor')
- grad_value: float32 [768, 768], P('dp', 'tensor')
- grad_pos: float32 [768, 768], P('dp', 'tensor')
- grad_out: float32 [768, 768], P('dp', 'tensor')
- grad_up: float32 [768, 3072], P('dp', 'tensor')
- grad_up_bias: float32 [3072], replicated
- grad_down: float32 [768, 3072], P('dp', 'tensor')
- grad_down_bias: float32 [768], replicated
- grad_word: float32 [12, 64], replicated
- grad_pos_bias: float32 [12, 64], replicated
- grad_first_gain: float32 [768], replicated
- grad_first_shift: float32 [768], replicated
- grad_second_gain: float32 [768], replicated
- grad_second_shift: float32 [768], replicated
Inputs may be any that keep to these rules, and one draw needn't show every extreme that they name: Each row of factor_order holds every number from 0 to 511 once. slot_sequence holds every sequence number once. Positions at or past seq_lengths[s] are padding and never visible as keys. The valid memory rows of a slot are its last memory_lengths rows.
All inputs are finite; a program needn't handle non-finite values.
Results may differ from a plain program's by a relative error of at most 0.017.
Values may be sent and summed in bfloat16 or wider, within the bound.
A program may use at most 256 MiB of HBM per device.

v0:
```python
import jax
import jax.numpy as jnp
from jax import lax
from jax.sharding import PartitionSpec as P

HEADS = 12
DH = 64
FF = 3072


EPS = 1e-06


def positions(count, first, width):
    dist = jnp.arange(count, dtype=jnp.float32) + first
    half = width // 2
    freq = 1.0 / 10000.0 ** (jnp.arange(half, dtype=jnp.float32) * (2.0 / width))
    angle = dist[:, None] * freq[None, :]
    return jnp.concatenate([jnp.sin(angle), jnp.cos(angle)], axis=1)


def norm_apply(value, gain, shift):
    center = value - jnp.mean(value, axis=-1, keepdims=True)
    spread = jnp.mean(center * center, axis=-1, keepdims=True)
    return center * lax.rsqrt(spread + EPS) * gain + shift


def gelu_apply(value):
    return jax.nn.gelu(value, approximate=True)


def matmul(left, right):
    return jnp.dot(left, right, preferred_element_type=jnp.float32)


def outer_sum(left, right):
    return lax.dot_general(
        left, right, (((0,), (0,)), ((), ())), preferred_element_type=jnp.float32
    )


def times_rows(left, right):
    return lax.dot_general(
        left, right, (((1,), (1,)), ((), ())), preferred_element_type=jnp.float32
    )


def widen(first, second):
    return (
        lax.all_gather(first, "tensor", axis=0, tiled=True),
        lax.all_gather(second, "tensor", axis=0, tiled=True),
    )


def narrow(first, second):
    return (
        lax.psum_scatter(first, "tensor", scatter_dimension=0, tiled=True),
        lax.psum_scatter(second, "tensor", scatter_dimension=0, tiled=True),
    )


def skewed_rows(raw, key_count):
    head_count, row_count, span_len = raw.shape
    flattened = raw.reshape(head_count, row_count * span_len)
    flattened = flattened[:, row_count - 1 : row_count - 1 + row_count * (span_len - 1)]
    return flattened.reshape(head_count, row_count, span_len - 1)[:, :, :key_count]


def unskew_rows(grad, span_len):
    head_count, row_count, key_count = grad.shape
    padded = jnp.pad(grad, ((0, 0), (0, 0), (0, span_len - 1 - key_count)))
    flattened = jnp.pad(
        padded.reshape(head_count, row_count * (span_len - 1)), ((0, 0), (row_count - 1, 1))
    )
    return flattened.reshape(head_count, row_count, span_len)


def visibility(rank_blk, key_rank, mem_ok, content_ok, strict):
    if strict:
        earlier = key_rank[None, :] < rank_blk[:, None]
    else:
        earlier = key_rank[None, :] <= rank_blk[:, None]
    return mem_ok[None, :] | content_ok[None, :] & earlier


def block_probs(q_word, q_pos, keys3, rel_rev, visible):
    content = jnp.einsum("ihd,jhd->hij", q_word, keys3, preferred_element_type=jnp.float32)
    raw = jnp.einsum("ihd,rhd->hir", q_pos, rel_rev, preferred_element_type=jnp.float32)
    score = 0.125 * (content + skewed_rows(raw, keys3.shape[0]))
    masked = jnp.where(visible[None], score, -1e30)
    top = jnp.max(masked, axis=2, keepdims=True)
    expo = jnp.exp(masked - top)
    return expo / jnp.sum(expo, axis=2, keepdims=True)


def attend_forward(
    q_word, q_pos, keys3, values3, rel3, rank, key_rank, mem_ok, content_ok, strict, block
):
    seq_len, heads_here, head = q_word.shape
    klen = keys3.shape[0]
    span = klen + block - 1
    visible = visibility(rank, key_rank, mem_ok, content_ok, strict)
    rel_rev = rel3[0:span][::-1]
    prob = block_probs(q_word, q_pos, keys3, rel_rev, visible)
    pieces = jnp.einsum(
        "hij,jhd->ihd", prob.astype(jnp.bfloat16), values3, preferred_element_type=jnp.float32
    )
    return pieces.reshape(seq_len, heads_here * head).astype(jnp.bfloat16)


def attend_backward(
    q_word,
    q_pos,
    keys3,
    values3,
    rel3,
    rank,
    key_rank,
    mem_ok,
    content_ok,
    strict,
    block,
    d_vec,
    d_keys,
    d_values,
    d_rel,
):
    klen = keys3.shape[0]
    span = klen + block - 1
    rel_rev = rel3[0:span][::-1]
    visible = visibility(rank, key_rank, mem_ok, content_ok, strict)
    prob = block_probs(q_word, q_pos, keys3, rel_rev, visible)
    d_prob = jnp.einsum("ihd,jhd->hij", d_vec, values3, preferred_element_type=jnp.float32)
    d_values = d_values + jnp.einsum(
        "hij,ihd->jhd", prob.astype(jnp.bfloat16), d_vec, preferred_element_type=jnp.float32
    )
    d_score = prob * (d_prob - jnp.sum(prob * d_prob, axis=2, keepdims=True))
    d_sum = (0.125 * d_score).astype(jnp.bfloat16)
    word_parts = jnp.einsum("hij,jhd->ihd", d_sum, keys3, preferred_element_type=jnp.float32)
    d_keys = d_keys + jnp.einsum("hij,ihd->jhd", d_sum, q_word, preferred_element_type=jnp.float32)
    d_raw = unskew_rows(d_sum, span)
    pos_parts = jnp.einsum("hir,rhd->ihd", d_raw, rel_rev, preferred_element_type=jnp.float32)
    d_rel = d_rel.at[0:span].add(
        jnp.einsum("hir,ihd->rhd", d_raw, q_pos, preferred_element_type=jnp.float32)[::-1]
    )
    return (word_parts, pos_parts, d_keys, d_values, d_rel)


def body(
    content_stream,
    query_stream,
    memory,
    content_tangent,
    query_tangent,
    seq_lengths,
    factor_order,
    memory_lengths,
    slot_sequence,
    query_weight,
    key_weight,
    value_weight,
    pos_weight,
    out_weight,
    up_weight,
    up_bias,
    down_weight,
    down_bias,
    word_bias,
    pos_bias,
    first_gain,
    first_shift,
    second_gain,
    second_shift,
):
    groups = lax.axis_size("dp")
    tensors = lax.axis_size("tensor")
    micro, part_len, width = content_stream.shape
    mem_part = memory.shape[1]
    seq_len = part_len * tensors
    mem_total = mem_part * tensors
    klen = mem_total + seq_len
    count = micro * groups
    piece = part_len // groups
    cols = query_weight.shape[1]
    inner = up_weight.shape[1]
    heads_here = cols // DH
    block = min(512, seq_len)
    here = lax.axis_index("dp")
    lane = lax.axis_index("tensor")
    all_lengths, all_orders = (
        lax.all_gather(seq_lengths, "dp", axis=0, tiled=True),
        lax.all_gather(factor_order, "dp", axis=0, tiled=True),
    )

    def to_slots(arr):
        flat = arr.transpose(1, 0, 2, 3).reshape(count, piece, width)
        return jnp.take(flat, slot_sequence, axis=0).reshape(groups, micro, piece, width)

    def from_slots(arr):
        flat = (
            jnp.zeros((count, piece, width), arr.dtype)
            .at[slot_sequence]
            .set(arr.reshape(count, piece, width))
        )
        return flat.reshape(groups, micro, piece, width).transpose(1, 0, 2, 3)

    def join_pieces(arr):
        return arr.transpose(1, 0, 2, 3).reshape(micro, part_len, width)

    def to_pieces(arr):
        return arr.reshape(micro, groups, piece, width).transpose(1, 0, 2, 3)

    split = (
        lax.all_to_all(
            content_stream.reshape(micro, groups, piece, width),
            "dp",
            split_axis=1,
            concat_axis=1,
            tiled=True,
        ),
        lax.all_to_all(
            query_stream.reshape(micro, groups, piece, width),
            "dp",
            split_axis=1,
            concat_axis=1,
            tiled=True,
        ),
        lax.all_to_all(
            content_tangent.reshape(micro, groups, piece, width),
            "dp",
            split_axis=1,
            concat_axis=1,
            tiled=True,
        ),
        lax.all_to_all(
            query_tangent.reshape(micro, groups, piece, width),
            "dp",
            split_axis=1,
            concat_axis=1,
            tiled=True,
        ),
    )
    routed = (
        lax.all_to_all(to_slots(split[0]), "dp", split_axis=0, concat_axis=0, tiled=True),
        lax.all_to_all(to_slots(split[1]), "dp", split_axis=0, concat_axis=0, tiled=True),
        lax.all_to_all(to_slots(split[2]), "dp", split_axis=0, concat_axis=0, tiled=True),
        lax.all_to_all(to_slots(split[3]), "dp", split_axis=0, concat_axis=0, tiled=True),
    )
    content_here = join_pieces(routed[0])
    query_here = join_pieces(routed[1])
    content_back = join_pieces(routed[2])
    query_back = join_pieces(routed[3])

    def fetch_weights():
        return (
            lax.all_gather(query_weight, "dp", axis=0, tiled=True),
            lax.all_gather(key_weight, "dp", axis=0, tiled=True),
            lax.all_gather(value_weight, "dp", axis=0, tiled=True),
            lax.all_gather(pos_weight, "dp", axis=0, tiled=True),
            lax.all_gather(out_weight, "dp", axis=0, tiled=True),
            lax.all_gather(up_weight, "dp", axis=0, tiled=True),
            lax.all_gather(down_weight, "dp", axis=0, tiled=True),
        )

    word_here = lax.dynamic_slice_in_dim(word_bias.reshape(-1), lane * cols, cols)
    pos_here = lax.dynamic_slice_in_dim(pos_bias.reshape(-1), lane * cols, cols)
    up_here = lax.dynamic_slice_in_dim(up_bias, lane * inner, inner)
    table = positions(mem_total + 2 * seq_len, 1 - seq_len, width).astype(jnp.bfloat16)
    key_pos = jnp.arange(klen, dtype=jnp.int32)
    mat_grads = [jnp.zeros((width, cols), jnp.float32) for weight in range(5)] + [
        jnp.zeros((width, inner), jnp.float32) for weight in range(2)
    ]
    grad_word = jnp.zeros((cols,), jnp.float32)
    grad_posb = jnp.zeros((cols,), jnp.float32)
    grad_upb = jnp.zeros((inner,), jnp.float32)
    grad_downb = jnp.zeros((width,), jnp.float32)
    gain_one = jnp.zeros((width,), jnp.float32)
    shift_one = jnp.zeros((width,), jnp.float32)
    gain_two = jnp.zeros((width,), jnp.float32)
    shift_two = jnp.zeros((width,), jnp.float32)
    content_outs, query_outs, content_grads, query_grads = ([], [], [], [])
    for slot in range(micro):
        seq_id = slot_sequence[here * micro + slot]
        length = all_lengths[seq_id]
        rank = all_orders[seq_id]
        mem_valid = memory_lengths[slot]
        mem_ok = (key_pos < mem_total) & (key_pos >= mem_total - mem_valid)
        content_ok = (key_pos >= mem_total) & (key_pos - mem_total < length)
        key_rank = jnp.concatenate([jnp.zeros((mem_total,), jnp.int32), rank])
        weights = fetch_weights()
        query_mat, key_mat, value_mat, pos_mat, out_mat, up_mat, down_mat = weights
        joined, query_full = widen(
            jnp.concatenate([memory[slot], content_here[slot]], 0), query_here[slot]
        )
        joined = joined.reshape(tensors, mem_part + part_len, width)
        content_full = joined[:, mem_part:].reshape(seq_len, width)
        context = jnp.concatenate([joined[:, :mem_part].reshape(mem_total, width), content_full], 0)
        keys = matmul(context, key_mat).astype(jnp.bfloat16)
        values = matmul(context, value_mat).astype(jnp.bfloat16)
        relative = matmul(table, pos_mat).astype(jnp.bfloat16)
        keys3 = keys.reshape(klen, heads_here, DH)
        values3 = values.reshape(klen, heads_here, DH)
        rel3 = relative.reshape(relative.shape[0], heads_here, DH)
        fulls = (content_full, query_full)
        stricts = (False, True)
        saved = []
        for stream, strict in zip(fulls, stricts):
            proj = matmul(stream, query_mat)
            q_word = (proj + word_here).astype(jnp.bfloat16).reshape(seq_len, heads_here, DH)
            q_pos = (proj + pos_here).astype(jnp.bfloat16).reshape(seq_len, heads_here, DH)
            vec = attend_forward(
                q_word,
                q_pos,
                keys3,
                values3,
                rel3,
                rank,
                key_rank,
                mem_ok,
                content_ok,
                strict,
                block,
            )
            saved.append((q_word, q_pos, vec))
        part_mix_c = times_rows(saved[0][2], out_mat)
        part_mix_q = times_rows(saved[1][2], out_mat)
        mixed_c, mixed_q = narrow(part_mix_c, part_mix_q)
        first_c, pull_first_c = jax.vjp(
            norm_apply, mixed_c + content_here[slot].astype(jnp.float32), first_gain, first_shift
        )
        first_q, pull_first_q = jax.vjp(
            norm_apply, mixed_q + query_here[slot].astype(jnp.float32), first_gain, first_shift
        )
        wide_c, wide_q = widen(first_c.astype(jnp.bfloat16), first_q.astype(jnp.bfloat16))
        upper_c = matmul(wide_c, up_mat) + up_here
        upper_q = matmul(wide_q, up_mat) + up_here
        act_c, pull_gelu_c = jax.vjp(gelu_apply, upper_c)
        act_q, pull_gelu_q = jax.vjp(gelu_apply, upper_q)
        act_c = act_c.astype(jnp.bfloat16)
        act_q = act_q.astype(jnp.bfloat16)
        down_c, down_q = narrow(times_rows(act_c, down_mat), times_rows(act_q, down_mat))
        out_c, pull_second_c = jax.vjp(
            norm_apply, down_c + down_bias + first_c, second_gain, second_shift
        )
        out_q, pull_second_q = jax.vjp(
            norm_apply, down_q + down_bias + first_q, second_gain, second_shift
        )
        content_outs.append(out_c.astype(jnp.bfloat16))
        query_outs.append(out_q.astype(jnp.bfloat16))
        dsec_c, dgain_c, dshift_c = pull_second_c(content_back[slot].astype(jnp.float32))
        dsec_q, dgain_q, dshift_q = pull_second_q(query_back[slot].astype(jnp.float32))
        gain_two = gain_two + dgain_c + dgain_q
        shift_two = shift_two + dshift_c + dshift_q
        grad_downb = grad_downb + jnp.sum(dsec_c, axis=0) + jnp.sum(dsec_q, axis=0)
        weights = fetch_weights()
        query_mat, key_mat, value_mat, pos_mat, out_mat, up_mat, down_mat = weights
        gdown_c, gdown_q = widen(dsec_c.astype(jnp.bfloat16), dsec_q.astype(jnp.bfloat16))
        back_parts = []
        for gdown, act, pull_gelu, wide in (
            (gdown_c, act_c, pull_gelu_c, wide_c),
            (gdown_q, act_q, pull_gelu_q, wide_q),
        ):
            d_act = matmul(gdown, down_mat)
            mat_grads[6] = mat_grads[6] + outer_sum(gdown, act)
            d_upper = pull_gelu(d_act)[0]
            grad_upb = grad_upb + jnp.sum(d_upper, axis=0)
            g_upper = d_upper.astype(jnp.bfloat16)
            mat_grads[5] = mat_grads[5] + outer_sum(wide, g_upper)
            back_parts.append(times_rows(g_upper, up_mat))
        back_c, back_q = narrow(back_parts[0], back_parts[1])
        dmix_c, dgone_c, dsone_c = pull_first_c(dsec_c + back_c)
        dmix_q, dgone_q, dsone_q = pull_first_q(dsec_q + back_q)
        gain_one = gain_one + dgone_c + dgone_q
        shift_one = shift_one + dsone_c + dsone_q
        gmix_c, gmix_q = widen(dmix_c.astype(jnp.bfloat16), dmix_q.astype(jnp.bfloat16))
        d_keys = jnp.zeros((klen, heads_here, DH), jnp.float32)
        d_values = jnp.zeros((klen, heads_here, DH), jnp.float32)
        d_rel = jnp.zeros(rel3.shape, jnp.float32)
        proj_grads = []
        for gmix, kept_fwd, strict in ((gmix_c, saved[0], False), (gmix_q, saved[1], True)):
            q_word, q_pos, vec = kept_fwd
            mat_grads[4] = mat_grads[4] + outer_sum(gmix, vec)
            d_vec = matmul(gmix, out_mat).astype(jnp.bfloat16).reshape(seq_len, heads_here, DH)
            d_qword, d_qpos, d_keys, d_values, d_rel = attend_backward(
                q_word,
                q_pos,
                keys3,
                values3,
                rel3,
                rank,
                key_rank,
                mem_ok,
                content_ok,
                strict,
                block,
                d_vec,
                d_keys,
                d_values,
                d_rel,
            )
            grad_word = grad_word + jnp.sum(d_qword, axis=0).reshape(cols)
            grad_posb = grad_posb + jnp.sum(d_qpos, axis=0).reshape(cols)
            proj_grads.append((d_qword + d_qpos).reshape(seq_len, cols).astype(jnp.bfloat16))
        mat_grads[0] = (
            mat_grads[0]
            + outer_sum(content_full, proj_grads[0])
            + outer_sum(query_full, proj_grads[1])
        )
        g_keys = d_keys.reshape(klen, cols).astype(jnp.bfloat16)
        g_values = d_values.reshape(klen, cols).astype(jnp.bfloat16)
        g_rel = d_rel.reshape(rel3.shape[0], cols).astype(jnp.bfloat16)
        mat_grads[1] = mat_grads[1] + outer_sum(context, g_keys)
        mat_grads[2] = mat_grads[2] + outer_sum(context, g_values)
        mat_grads[3] = mat_grads[3] + outer_sum(table, g_rel)
        d_context = times_rows(g_keys[mem_total:], key_mat) + times_rows(
            g_values[mem_total:], value_mat
        )
        part_c = d_context + times_rows(proj_grads[0], query_mat)
        part_q = times_rows(proj_grads[1], query_mat)
        input_c, input_q = narrow(part_c, part_q)
        content_grads.append((dmix_c + input_c).astype(jnp.bfloat16))
        query_grads.append((dmix_q + input_q).astype(jnp.bfloat16))
    mat_shards = (
        lax.psum_scatter(mat_grads[0], "dp", scatter_dimension=0, tiled=True),
        lax.psum_scatter(mat_grads[1], "dp", scatter_dimension=0, tiled=True),
        lax.psum_scatter(mat_grads[2], "dp", scatter_dimension=0, tiled=True),
        lax.psum_scatter(mat_grads[3], "dp", scatter_dimension=0, tiled=True),
        lax.psum_scatter(mat_grads[4], "dp", scatter_dimension=0, tiled=True),
        lax.psum_scatter(mat_grads[5], "dp", scatter_dimension=0, tiled=True),
        lax.psum_scatter(mat_grads[6], "dp", scatter_dimension=0, tiled=True),
    )
    word_full = lax.dynamic_update_slice_in_dim(
        jnp.zeros((HEADS * DH,), jnp.float32), grad_word, lane * cols, 0
    )
    posb_full = lax.dynamic_update_slice_in_dim(
        jnp.zeros((HEADS * DH,), jnp.float32), grad_posb, lane * cols, 0
    )
    upb_full = lax.dynamic_update_slice_in_dim(
        jnp.zeros((FF,), jnp.float32), grad_upb, lane * inner, 0
    )
    small = lax.psum(
        (word_full, posb_full, upb_full, grad_downb, gain_one, shift_one, gain_two, shift_two),
        ("dp", "tensor"),
    )
    leaving = (
        jnp.stack(content_outs),
        jnp.stack(query_outs),
        jnp.stack(content_grads),
        jnp.stack(query_grads),
    )
    back = (
        lax.all_to_all(to_pieces(leaving[0]), "dp", split_axis=0, concat_axis=0, tiled=True),
        lax.all_to_all(to_pieces(leaving[1]), "dp", split_axis=0, concat_axis=0, tiled=True),
        lax.all_to_all(to_pieces(leaving[2]), "dp", split_axis=0, concat_axis=0, tiled=True),
        lax.all_to_all(to_pieces(leaving[3]), "dp", split_axis=0, concat_axis=0, tiled=True),
    )
    home = (
        lax.all_to_all(from_slots(back[0]), "dp", split_axis=1, concat_axis=1, tiled=True),
        lax.all_to_all(from_slots(back[1]), "dp", split_axis=1, concat_axis=1, tiled=True),
        lax.all_to_all(from_slots(back[2]), "dp", split_axis=1, concat_axis=1, tiled=True),
        lax.all_to_all(from_slots(back[3]), "dp", split_axis=1, concat_axis=1, tiled=True),
    )
    finals = [arr.reshape(micro, part_len, width) for arr in home]
    return (
        finals[0],
        finals[1],
        finals[2],
        finals[3],
        mat_shards[0],
        mat_shards[1],
        mat_shards[2],
        mat_shards[3],
        mat_shards[4],
        mat_shards[5],
        small[2],
        mat_shards[6],
        small[3],
        small[0].reshape(HEADS, DH),
        small[1].reshape(HEADS, DH),
        small[4],
        small[5],
        small[6],
        small[7],
    )


def solution(mesh):
    placed = (
        P("dp", "tensor", None),
        P("dp", "tensor", None),
        P("dp", "tensor", None),
        P("dp", "tensor", None),
        P("dp", "tensor", None),
        P("dp"),
        P("dp", None),
        P("dp"),
        P(),
        P("dp", "tensor"),
        P("dp", "tensor"),
        P("dp", "tensor"),
        P("dp", "tensor"),
        P("dp", "tensor"),
        P("dp", "tensor"),
        P(),
        P("dp", "tensor"),
        P(),
        P(),
        P(),
        P(),
        P(),
        P(),
        P(),
    )
    return jax.shard_map(
        body,
        mesh=mesh,
        in_specs=placed,
        out_specs=(
            P("dp", "tensor", None),
            P("dp", "tensor", None),
            P("dp", "tensor", None),
            P("dp", "tensor", None),
            P("dp", "tensor"),
            P("dp", "tensor"),
            P("dp", "tensor"),
            P("dp", "tensor"),
            P("dp", "tensor"),
            P("dp", "tensor"),
            P(),
            P("dp", "tensor"),
            P(),
            P(),
            P(),
            P(),
            P(),
            P(),
            P(),
        ),
        check_vma=False,
    )
```

profile of v0, /device:TPU:0, one launch (start us, length us, event | category | flops | bytes accessed | tf_op | source)
XLA Modules:
  0.0 1798.8 jit_solution(1355125088662010386)
XLA Ops:
  166.0 21.1 %all_gather.109 = bf16[512,768]{1,0:T(8,128)(2,1)S(1)} all-gather(bf16[128,768]{1,0:T(8,128)(2,1)S(1)} %bitcast.492), channel_id=1, replica_groups=mesh['dp'=8,'tensor'=4] {'tensor'}, dimensions={0}, use_global_device_ids=true | all-gather | bytes 983040 | tf_op jit(solution)/shard_map/all_gather | solution.py:51
  188.3 18.1 %all_gather.107 = bf16[512,768]{1,0:T(8,128)(2,1)S(1)} all-gather(bf16[128,768]{1,0:T(8,128)(2,1)S(1)} %bitcast.493), channel_id=1, replica_groups=mesh['dp'=8,'tensor'=4] {'tensor'}, dimensions={0}, use_global_device_ids=true | all-gather | bytes 983040 | tf_op jit(solution)/shard_map/all_gather | solution.py:51
  222.3 15.1 reshape.1150
  250.6 13.8 slice.266
  315.3 15.3 reshape.1162
  343.9 13.8 slice.269
  409.6 15.3 reshape.1154
  438.2 13.8 slice.261
  502.3 15.4 reshape.1158
  517.6 13.4 reshape.1028
  531.0 13.6 slice.272
  592.0 28.1 %all_gather.108 = bf16[512,768]{1,0:T(8,128)(2,1)S(1)} all-gather(bf16[128,768]{1,0:T(8,128)(2,1)S(1)} %get-tuple-element.209), channel_id=1, replica_groups=mesh['dp'=8,'tensor'=4] {'tensor'}, dimensions={0}, use_global_device_ids=true | all-gather | bytes 983040 | tf_op jit(solution)/shard_map/all_gather | solution.py:51
  627.6 19.4 %all_gather.106 = bf16[512,768]{1,0:T(8,128)(2,1)S(1)} all-gather(bf16[128,768]{1,0:T(8,128)(2,1)S(1)} %get-tuple-element.210), channel_id=1, replica_groups=mesh['dp'=8,'tensor'=4] {'tensor'}, dimensions={0}, use_global_device_ids=true | all-gather | bytes 983040 | tf_op jit(solution)/shard_map/all_gather | solution.py:50
  653.0 28.7 %all_gather.102 = bf16[512,768]{1,0:T(8,128)(2,1)S(1)} all-gather(bf16[128,768]{1,0:T(8,128)(2,1)S(1)} %get-tuple-element.211), channel_id=1, replica_groups=mesh['dp'=8,'tensor'=4] {'tensor'}, dimensions={0}, use_global_device_ids=true | all-gather | bytes 983040 | tf_op jit(solution)/shard_map/all_gather | solution.py:50
  689.1 34.4 %reduce-scatter.30.cloned.1.call-done = f32[128,768]{1,0:T(8,128)} async-done(((f32[512,768]{1,0:T(8,128)}), f32[128,768]{1,0:T(8,128)}) %reduce-scatter.30.cloned.1.call-update) | async-done | bytes 393232 | tf_op jit(solution)/shard_map/reduce_scatter | solution.py:57
  723.5 36.6 %reduce-scatter.26.cloned.1.call-done = f32[128,768]{1,0:T(8,128)} async-done(((f32[512,768]{1,0:T(8,128)}), f32[128,768]{1,0:T(8,128)}) %reduce-scatter.26.cloned.1.call-update) | async-done | bytes 393232 | tf_op jit(solution)/shard_map/reduce_scatter | solution.py:57
  761.9 17.9 all_gather.110
  792.8 28.6 %reduce-scatter.38.cloned.1.call-done = f32[128,768]{1,0:T(8,128)} async-done(((f32[512,768]{1,0:T(8,128)}), f32[128,768]{1,0:T(8,128)}) %reduce-scatter.38.cloned.1.call-update) | async-done | bytes 393232 | tf_op jit(solution)/shard_map/reduce_scatter | solution.py:58
  842.2 17.5 all_gather.117
  868.5 27.5 %all_gather.111 = bf16[512,768]{1,0:T(8,128)(2,1)S(1)} all-gather(bf16[128,768]{1,0:T(8,128)(2,1)S(1)} %get-tuple-element.169), channel_id=1, replica_groups=mesh['dp'=8,'tensor'=4] {'tensor'}, dimensions={0}, use_global_device_ids=true | all-gather | bytes 983040 | tf_op jit(solution)/shard_map/all_gather | solution.py:50
  901.9 21.0 %all_gather.115 = bf16[512,768]{1,0:T(8,128)(2,1)S(1)} all-gather(bf16[128,768]{1,0:T(8,128)(2,1)S(1)} %get-tuple-element.171), channel_id=1, replica_groups=mesh['dp'=8,'tensor'=4] {'tensor'}, dimensions={0}, use_global_device_ids=true | all-gather | bytes 983040 | tf_op jit(solution)/shard_map/all_gather | solution.py:50
  930.8 28.3 %all_gather.113 = bf16[512,768]{1,0:T(8,128)(2,1)S(1)} all-gather(bf16[128,768]{1,0:T(8,128)(2,1)S(1)} %get-tuple-element.167), channel_id=1, replica_groups=mesh['dp'=8,'tensor'=4] {'tensor'}, dimensions={0}, use_global_device_ids=true | all-gather | bytes 983040 | tf_op jit(solution)/shard_map/all_gather | solution.py:51
  970.1 30.8 %reduce-scatter.46.cloned.1.call-done = f32[128,768]{1,0:T(8,128)} async-done(((f32[512,768]{1,0:T(8,128)}), f32[128,768]{1,0:T(8,128)}) %reduce-scatter.46.cloned.1.call-update) | async-done | bytes 393232 | tf_op jit(solution)/shard_map/reduce_scatter | solution.py:57
  1000.9 36.5 %reduce-scatter.42.cloned.1.call-done = f32[128,768]{1,0:T(8,128)} async-done(((f32[512,768]{1,0:T(8,128)}), f32[128,768]{1,0:T(8,128)}) %reduce-scatter.42.cloned.1.call-update) | async-done | bytes 393232 | tf_op jit(solution)/shard_map/reduce_scatter | solution.py:58
  1042.6 18.3 %all_gather.112 = bf16[512,768]{1,0:T(8,128)(2,1)S(1)} all-gather(bf16[128,768]{1,0:T(8,128)(2,1)S(1)} %add_convert_fusion.23), channel_id=1, replica_groups=mesh['dp'=8,'tensor'=4] {'tensor'}, dimensions={0}, use_global_device_ids=true | all-gather | bytes 983040 | tf_op jit(solution)/shard_map/all_gather | solution.py:50
  1091.5 17.8 all_gather.114
  1138.9 17.7 all_gather.116
  1157.8 16.3 all_gather.118
  1648.4 42.0 %all-reduce.13 = (f32[3072]{0:T(1024)}, f32[768]{0:T(1024)}, f32[12,64]{1,0:T(8,128)}, f32[12,64]{1,0:T(8,128)}, f32[768]{0:T(1024)}, /*index=5*/f32[768]{0:T(1024)}, f32[768]{0:T(1024)}, f32[768]{0:T(1024)}) all-reduce(f32[3072]{0:T(1024)S(1)} %add_dynamic-update-slice_fusion, ...), channel_id=1, replica_groups=mesh['dp'=8,'tensor'=4] {'dp','tensor'}, use_global_device_ids=true, to_apply=%region_74.76 | all-reduce | flops 8448 | bytes 67584 | tf_op jit(solution)/shard_map/psum | solution.py:441
  1691.9 22.3 %reduce-scatter.60.cloned.1.call-done = f32[96,192]{1,0:T(8,128)} async-done(((f32[768,192]{1,0:T(8,128)}), f32[96,192]{1,0:T(8,128)}) %reduce-scatter.60.cloned.1.call-update) | async-done | bytes 73744 | tf_op jit(solution)/shard_map/reduce_scatter | solution.py:426
  1714.2 38.6 %reduce-scatter.56.cloned.1.call-done = f32[96,192]{1,0:T(8,128)} async-done(((f32[768,192]{1,0:T(8,128)}), f32[96,192]{1,0:T(8,128)}) %reduce-scatter.56.cloned.1.call-update) | async-done | bytes 73744 | tf_op jit(solution)/shard_map/reduce_scatter | solution.py:424
  1752.7 38.7 %reduce-scatter.62.cloned.1.call-done = f32[96,192]{1,0:T(8,128)} async-done(((f32[768,192]{1,0:T(8,128)}), f32[96,192]{1,0:T(8,128)}) %reduce-scatter.62.cloned.1.call-update) | async-done | bytes 73744 | tf_op jit(solution)/shard_map/reduce_scatter | solution.py:427
  (951 shorter events, 1038.5 us)
Async XLA Ops:
  64.0 143.6 %all-gather.6.cloned.1.call-start = ((), (), s32[]{:S(2)}) async-start(), calls=%async_computation.39 | async-start | bytes 1966080 | tf_op jit(solution)/shard_map/all_gather | solution.py:50
  73.8 137.4 %all-gather.12.cloned.1.call-start = ((), (), s32[]{:S(2)}) async-start(), calls=%async_computation.44 | async-start | bytes 1966080 | tf_op jit(solution)/shard_map/all_gather | solution.py:50
  146.0 20.0 %all-to-all-start.5 = ((bf16[8,2,16,768]{3,2,1,0:T(8,128)(2,1)}), bf16[8,2,16,768]{3,2,1,0:T(8,128)(2,1)S(1)}, u32[]{:S(2)}, u32[]{:S(2)}) async-start(bf16[8,2,16,768]{3,2,1,0:T(8,128)(2,1)} %bitcast.50), calls=%async_computation.9 | async-start | bytes 786432 | tf_op jit(solution)/shard_map/all_to_all | solution.py:245
  149.4 438.1 %reduce-scatter.28.cloned.1.call-start = ((), (), s32[]{:S(2)}) async-start(), calls=%async_computation.45 | async-start | bytes 1966080 | tf_op jit(solution)/shard_map/reduce_scatter | solution.py:57
  306.9 282.0 %reduce-scatter.32.cloned.1.call-start = ((), (), s32[]{:S(2)}) async-start(), calls=%async_computation.47 | async-start | bytes 1966080 | tf_op jit(solution)/shard_map/reduce_scatter | solution.py:58
  404.4 185.9 %reduce-scatter.24.cloned.1.call-start = ((), (), s32[]{:S(2)}) async-start(), calls=%async_computation.40 | async-start | bytes 1966080 | tf_op jit(solution)/shard_map/reduce_scatter | solution.py:57
  495.1 125.0 %all-gather.8.cloned.1.call-start = ((), (), s32[]{:S(2)}) async-start(), calls=%async_computation.41 | async-start | bytes 1327104 | tf_op jit(solution)/shard_map/all_gather | solution.py:261
  495.6 127.9 %all-gather.10.cloned.1.call-start = ((), (), s32[]{:S(2)}) async-start(), calls=%async_computation.42 | async-start | bytes 1327104 | tf_op jit(solution)/shard_map/all_gather | solution.py:262
  496.2 191.5 %reduce-scatter.36.cloned.1.call-start = ((), (), s32[]{:S(2)}) async-start(), calls=%async_computation.49 | async-start | bytes 1966080 | tf_op jit(solution)/shard_map/reduce_scatter | solution.py:58
  587.5 101.7 %reduce-scatter.34.cloned.1.call-start = ((), (), s32[]{:S(2)}) async-start(), calls=%async_computation.48 | async-start | bytes 1966080 | tf_op jit(solution)/shard_map/reduce_scatter | solution.py:58
  627.6 95.9 %reduce-scatter.30.cloned.1.call-start = ((), (), s32[]{:S(2)}) async-start(), calls=%async_computation.46 | async-start | bytes 1966080 | tf_op jit(solution)/shard_map/reduce_scatter | solution.py:57
  653.0 107.2 %reduce-scatter.26.cloned.1.call-start = ((), (), s32[]{:S(2)}) async-start(), calls=%async_computation.43 | async-start | bytes 1966080 | tf_op jit(solution)/shard_map/reduce_scatter | solution.py:57
  687.5 133.9 %reduce-scatter.38.cloned.1.call-start = ((), (), s32[]{:S(2)}) async-start(), calls=%async_computation.50 | async-start | bytes 1966080 | tf_op jit(solution)/shard_map/reduce_scatter | solution.py:58
  786.4 36.2 %all-to-all-start.11 = ((bf16[8,2,16,768]{3,2,1,0:T(8,128)(2,1)}), bf16[8,2,16,768]{3,2,1,0:T(8,128)(2,1)}, u32[]{:S(2)}, u32[]{:S(2)}) async-start(bf16[8,2,16,768]{3,2,1,0:T(8,128)(2,1)} %bitcast.81), calls=%async_computation.20 | async-start | bytes 786432 | tf_op jit(solution)/shard_map/all_to_all | solution.py:247
  826.8 139.6 %reduce-scatter.48.cloned.1.call-start = ((), (), s32[]{:S(2)}) async-start(), calls=%async_computation.55 | async-start | bytes 1966080 | tf_op jit(solution)/shard_map/reduce_scatter | solution.py:58
  864.8 101.6 %reduce-scatter.40.cloned.1.call-start = ((), (), s32[]{:S(2)}) async-start(), calls=%async_computation.51 | async-start | bytes 1966080 | tf_op jit(solution)/shard_map/reduce_scatter | solution.py:57
  901.1 99.8 %reduce-scatter.46.cloned.1.call-start = ((), (), s32[]{:S(2)}) async-start(), calls=%async_computation.54 | async-start | bytes 1966080 | tf_op jit(solution)/shard_map/reduce_scatter | solution.py:57
  930.0 107.4 %reduce-scatter.42.cloned.1.call-start = ((), (), s32[]{:S(2)}) async-start(), calls=%async_computation.52 | async-start | bytes 1966080 | tf_op jit(solution)/shard_map/reduce_scatter | solution.py:58
  966.3 632.2 %reduce-scatter.44.cloned.1.call-start = ((), (), s32[]{:S(2)}) async-start(), calls=%async_computation.53 | async-start | bytes 1966080 | tf_op jit(solution)/shard_map/reduce_scatter | solution.py:57
  1252.8 346.9 %reduce-scatter.50.cloned.1.call-start = ((), (), s32[]{:S(2)}) async-start(), calls=%async_computation.56 | async-start | bytes 1966080 | tf_op jit(solution)/shard_map/reduce_scatter | solution.py:57
  1347.4 257.9 %reduce-scatter.52.cloned.1.call-start = ((), (), s32[]{:S(2)}) async-start(), calls=%async_computation.57 | async-start | bytes 1966080 | tf_op jit(solution)/shard_map/reduce_scatter | solution.py:58
  1406.1 200.3 %reduce-scatter.54.cloned.1.call-start = ((), (), s32[]{:S(2)}) async-start(), calls=%async_computation.58 | async-start | bytes 1966080 | tf_op jit(solution)/shard_map/reduce_scatter | solution.py:58
  1465.8 226.1 %reduce-scatter.68.cloned.1.call-start = ((), (), s32[]{:S(2)}) async-start(), calls=%async_computation.65 | async-start | bytes 2654208 | tf_op jit(solution)/shard_map/reduce_scatter | solution.py:430
  1474.7 217.2 %reduce-scatter.66.cloned.1.call-start = ((), (), s32[]{:S(2)}) async-start(), calls=%async_computation.64 | async-start | bytes 2654208 | tf_op jit(solution)/shard_map/reduce_scatter | solution.py:429
  1519.5 14.7 all-to-all-start.3
  1523.0 168.9 %reduce-scatter.64.cloned.1.call-start = ((), (), s32[]{:S(2)}) async-start(), calls=%async_computation.63 | async-start | bytes 884736 | tf_op jit(solution)/shard_map/reduce_scatter | solution.py:428
  1544.5 147.4 %reduce-scatter.58.cloned.1.call-start = ((), (), s32[]{:S(2)}) async-start(), calls=%async_computation.60 | async-start | bytes 884736 | tf_op jit(solution)/shard_map/reduce_scatter | solution.py:425
  1555.6 158.6 %reduce-scatter.60.cloned.1.call-start = ((), (), s32[]{:S(2)}) async-start(), calls=%async_computation.61 | async-start | bytes 884736 | tf_op jit(solution)/shard_map/reduce_scatter | solution.py:426
  1574.7 178.0 %reduce-scatter.56.cloned.1.call-start = ((), (), s32[]{:S(2)}) async-start(), calls=%async_computation.59 | async-start | bytes 884736 | tf_op jit(solution)/shard_map/reduce_scatter | solution.py:424
  1613.5 18.9 %all-to-all-start.14 = ((bf16[8,2,16,768]{3,2,1,0:T(8,128)(2,1)}), bf16[8,2,16,768]{3,2,1,0:T(8,128)(2,1)S(1)}, u32[]{:S(2)}, u32[]{:S(2)}) async-start(bf16[8,2,16,768]{3,2,1,0:T(8,128)(2,1)} %maximum_bitcast_fusion.3), calls=%async_computation.30 | async-start | bytes 786432 | tf_op jit(solution)/shard_map/all_to_all | solution.py:455
  1617.0 174.5 %reduce-scatter.62.cloned.1.call-start = ((), (), s32[]{:S(2)}) async-start(), calls=%async_computation.62 | async-start | bytes 884736 | tf_op jit(solution)/shard_map/reduce_scatter | solution.py:427
  1644.8 46.3 %all-to-all-start.15 = ((bf16[2,8,16,768]{3,2,0,1:T(8,128)(2,1)}), bf16[2,8,16,768]{3,2,0,1:T(8,128)(2,1)S(1)}, u32[]{:S(2)}, u32[]{:S(2)}) async-start(bf16[2,8,16,768]{3,2,0,1:T(8,128)(2,1)} %bitcast.125), calls=%async_computation.31 | async-start | bytes 786432 | tf_op jit(solution)/shard_map/all_to_all | solution.py:461
  (283 other events, 5392.1 us)
Sparse Core Ops, SparseCore 0:
  73.9 36.4 all-gather.5
  137.2 40.0 all-gather.11
  307.0 34.8 reduce-scatter.27
  404.5 34.9 reduce-scatter.31
  495.2 35.1 reduce-scatter.23
  587.6 48.7 reduce-scatter.35
  638.7 47.6 reduce-scatter.33
  688.7 34.7 reduce-scatter.29
  725.8 34.2 reduce-scatter.25
  786.5 34.8 reduce-scatter.37
  865.0 49.1 reduce-scatter.47
  916.3 47.9 reduce-scatter.39
  966.6 34.2 reduce-scatter.45
  1003.1 34.2 reduce-scatter.41
  1253.0 35.9 reduce-scatter.43
  1347.5 35.8 reduce-scatter.49
  1406.2 35.8 reduce-scatter.51
  1466.0 35.8 reduce-scatter.53
  1505.8 43.4 reduce-scatter.67
  1553.0 42.4 reduce-scatter.65
  1599.2 37.4 reduce-scatter.63
  1640.4 35.0 reduce-scatter.57
  1679.2 34.9 reduce-scatter.59
  1717.8 34.9 reduce-scatter.55
  1756.5 34.9 reduce-scatter.61
Sparse Core Ops, SparseCore 1:
  497.4 23.5 all-gather.7
  522.8 23.8 all-gather.9
where the time goes:
time: 1810 us; the launch traced here: 1800 us
  local copies, waits for them, and re-layouts  551 us (30%)
  blocking collectives  404 us (22%)
  waiting for transfers between devices  344 us (19%)
  matrix products  330 us (18%)
  other arithmetic  83.1 us (5%)
  starting transfers between devices  61.3 us (3%)
  between operations  24.8 us (1%)
    unnamed x568, local copies, waits for them, and re-layouts  229 us
    all_gather x8, blocking collectives, widen(): lax.all_gather(second, 'tensor', axis=0, tiled=True)  165 us
    all_gather x6, blocking collectives, widen(): lax.all_gather(first, 'tensor', axis=0, tiled=True)  133 us
    reduce_scatter x8, waiting for transfers between devices, narrow(): lax.psum_scatter(first, 'tensor', scatter_dimension=0, tiled=True)  102 us
    reduce_scatter x8, waiting for transfers between devices, narrow(): lax.psum_scatter(second, 'tensor', scatter_dimension=0, tiled=True)  65.2 us
    slice x4, local copies, waits for them, and re-layouts, skewed_rows(): flattened[:, row_count - 1:row_count - 1 + row_count * (span_len - 1)]  55 us
    reshape x4, local copies, waits for them, and re-layouts, skewed_rows(): flattened = raw.reshape(head_count, row_count * span_len)  53.1 us
    reshape x4, local copies, waits for them, and re-layouts, skewed_rows(): flattened.reshape(head_count, row_count, span_len - 1)[:, :, :key_count]  44.8 us
  transfers between devices with their start and end apart: 43, of which 20 were waited for; matrix products, arithmetic and copies ran while one was open for 38% of the time, Pallas kernels for 0%

commit v1 on v0

v1 whole, which is shorter than its diff:
```python
import functools

import jax
import jax.numpy as jnp
from jax import lax
from jax.experimental import pallas as pl
from jax.experimental.pallas import tpu as pltpu
from jax.sharding import PartitionSpec as P

HEADS = 12
DH = 64
PAIR = 2 * DH
EPS = 1e-06
BF = jnp.bfloat16
F32 = jnp.float32
LIMIT = 60 * 1024 * 1024


def nn(left, right):
    return jnp.dot(left, right, preferred_element_type=F32)


def nt(left, right):
    return lax.dot_general(left, right, (((1,), (1,)), ((), ())), preferred_element_type=F32)


def tn(left, right):
    return lax.dot_general(left, right, (((0,), (0,)), ((), ())), preferred_element_type=F32)


def tt(left, right):
    return lax.dot_general(left, right, (((0,), (1,)), ((), ())), preferred_element_type=F32)


def reversed_table(count, first, width):
    dist = first - jnp.arange(count, dtype=F32)
    half = width // 2
    freq = 1.0 / 10000.0 ** (jnp.arange(half, dtype=F32) * (2.0 / width))
    angle = dist[:, None] * freq[None, :]
    return jnp.concatenate([jnp.sin(angle), jnp.cos(angle)], axis=1).astype(BF)


def head_lanes(array, head):
    lane = lax.broadcasted_iota(jnp.int32, array.shape, 1)
    return jnp.where((lane >= DH) == (head == 1), array, jnp.zeros_like(array))


def attend_forward_kernel(
    block, qw_ref, qp_ref, k_ref, v_ref, rel_ref, thr_ref, kr_ref, vec_ref, prob_ref
):
    rows, klen = qw_ref.shape[0], k_ref.shape[0]
    width = klen + block
    keys, values = k_ref[...], v_ref[...]
    for part in range(rows // block):
        at = slice(part * block, (part + 1) * block)
        first = rows - (part + 1) * block
        qw, qp = qw_ref[at, :], qp_ref[at, :]
        rel = rel_ref[first : first + width, :]
        seen = kr_ref[...] < thr_ref[at, :]
        vecs = []
        for head in range(2):
            raw = nt(head_lanes(qp, head), rel)
            moved = pltpu.roll(raw, 0, 1, stride=1, stride_axis=0)[:, block:]
            score = nt(head_lanes(qw, head), keys) + moved
            score = jnp.where(seen, score, -1e30)
            expo = jnp.exp(score - jnp.max(score, axis=1, keepdims=True))
            prob = (expo * (1.0 / jnp.sum(expo, axis=1, keepdims=True))).astype(BF)
            prob_ref[head, at, :] = prob
            vecs.append(nn(prob, values))
        lane = lax.broadcasted_iota(jnp.int32, vecs[0].shape, 1)
        vec_ref[at, :] = jnp.where(lane < DH, vecs[0], vecs[1]).astype(BF)


def attend_forward(qw, qp, keys, values, rel, thr, key_rank, block):
    rows, width = qw.shape
    klen, span = keys.shape[0], rel.shape[0]
    col = lambda count: pl.BlockSpec((count, PAIR), lambda p: (0, p))
    return pl.pallas_call(
        functools.partial(attend_forward_kernel, block),
        grid=(width // PAIR,),
        in_specs=[
            col(rows),
            col(rows),
            col(klen),
            col(klen),
            col(span),
            pl.BlockSpec((rows, 1), lambda p: (0, 0)),
            pl.BlockSpec((1, klen), lambda p: (0, 0)),
        ],
        out_specs=[col(rows), pl.BlockSpec((2, rows, klen), lambda p: (p, 0, 0))],
        out_shape=[
            jax.ShapeDtypeStruct((rows, width), BF),
            jax.ShapeDtypeStruct((width // DH, rows, klen), BF),
        ],
        compiler_params=pltpu.CompilerParams(vmem_limit_bytes=LIMIT),
        cost_estimate=pl.CostEstimate(
            flops=8 * rows * klen * width, bytes_accessed=16 << 20, transcendentals=12 * rows * klen
        ),
        name="attend_forward",
    )(qw, qp, keys, values, rel, thr, key_rank)


def attend_backward_kernel(
    block,
    prob_ref,
    gvec_ref,
    qw_ref,
    qp_ref,
    k_ref,
    v_ref,
    rel_ref,
    dproj_ref,
    dk_ref,
    dv_ref,
    drel_ref,
    bias_ref,
    rel_acc,
):
    rows, klen = qw_ref.shape[0], k_ref.shape[0]
    width = klen + block
    keys, values = k_ref[...], v_ref[...]
    row = lax.broadcasted_iota(jnp.int32, (block, block), 0)
    col = lax.broadcasted_iota(jnp.int32, (block, block), 1)
    mirror = (row + col == block - 1).astype(BF)
    rel_acc[...] = jnp.zeros_like(rel_acc)
    d_keys, d_values = [None, None], [None, None]
    word_sum = jnp.zeros((1, PAIR), F32)
    pos_sum = jnp.zeros((1, PAIR), F32)
    for part in range(rows // block):
        at = slice(part * block, (part + 1) * block)
        first = rows - (part + 1) * block
        gvec, qw = gvec_ref[at, :], qw_ref[at, :]
        gvec_t = jnp.transpose(gvec.astype(F32)).astype(BF)
        qw_t = jnp.transpose(qw.astype(F32)).astype(BF)
        qp_t = jnp.transpose(nn(mirror, qp_ref[at, :])).astype(BF)
        rel = rel_ref[first : first + width, :]
        word_parts, pos_parts = [], []
        for head in range(2):
            own = slice(head * DH, (head + 1) * DH)
            prob = prob_ref[head, at, :]
            d_prob = nt(head_lanes(gvec, head), values)
            weight = prob.astype(F32)
            inner = jnp.sum(weight * d_prob, axis=1, keepdims=True)
            g_sum = (weight * (d_prob - inner) * 0.125).astype(BF)
            dv = nn(gvec_t[own, :], prob)
            dk = nn(qw_t[own, :], g_sum)
            d_values[head] = dv if part == 0 else d_values[head] + dv
            d_keys[head] = dk if part == 0 else d_keys[head] + dk
            turned = nn(mirror, g_sum)
            padded = jnp.concatenate([jnp.zeros((block, block), F32), turned], axis=1)
            moved = pltpu.roll(padded, width - block + 1, 1, stride=1, stride_axis=0).astype(BF)
            word_parts.append(nn(turned.astype(BF), keys))
            pos_parts.append(nn(moved, rel))
            rel_acc[own, first : first + width] += nn(qp_t[own, :], moved)
        lane = lax.broadcasted_iota(jnp.int32, word_parts[0].shape, 1)
        word = jnp.where(lane < DH, word_parts[0], word_parts[1])
        pos = jnp.where(lane < DH, pos_parts[0], pos_parts[1])
        word_sum = word_sum + jnp.sum(word, axis=0, keepdims=True)
        pos_sum = pos_sum + jnp.sum(pos, axis=0, keepdims=True)
        dproj_ref[at, :] = nn(mirror, (word + pos).astype(BF)).astype(BF)
    for head in range(2):
        own = slice(head * DH, (head + 1) * DH)
        dv_ref[own, :] = d_values[head].astype(BF)
        dk_ref[own, :] = (8.0 * d_keys[head]).astype(BF)
    drel_ref[...] = (8.0 * rel_acc[...]).astype(BF)
    bias_ref[0:1, :] = word_sum
    bias_ref[1:2, :] = pos_sum


def attend_backward(prob, gvec, qw, qp, keys, values, rel, block):
    rows, width = qw.shape
    klen, span = keys.shape[0], rel.shape[0]
    col = lambda count: pl.BlockSpec((count, PAIR), lambda p: (0, p))
    rowb = lambda count: pl.BlockSpec((PAIR, count), lambda p: (p, 0))
    return pl.pallas_call(
        functools.partial(attend_backward_kernel, block),
        grid=(width // PAIR,),
        in_specs=[
            pl.BlockSpec((2, rows, klen), lambda p: (p, 0, 0)),
            col(rows),
            col(rows),
            col(rows),
            col(klen),
            col(klen),
            col(span),
        ],
        out_specs=[col(rows), rowb(klen), rowb(klen), rowb(span), col(2)],
        out_shape=[
            jax.ShapeDtypeStruct((rows, width), BF),
            jax.ShapeDtypeStruct((width, klen), BF),
            jax.ShapeDtypeStruct((width, klen), BF),
            jax.ShapeDtypeStruct((width, span), BF),
            jax.ShapeDtypeStruct((2, width), F32),
        ],
        scratch_shapes=[pltpu.VMEM((PAIR, span), F32)],
        compiler_params=pltpu.CompilerParams(vmem_limit_bytes=LIMIT),
        cost_estimate=pl.CostEstimate(
            flops=16 * rows * klen * width, bytes_accessed=20 << 20, transcendentals=0
        ),
        name="attend_backward",
    )(prob, gvec, qw, qp, keys, values, rel)


def norm_parts(value):
    center = value - jnp.mean(value, axis=1, keepdims=True)
    scale = lax.rsqrt(jnp.mean(center * center, axis=1, keepdims=True) + EPS)
    return center * scale, scale


def norm_pull(normed, scale, err):
    inner = jnp.mean(err * normed, axis=1, keepdims=True)
    return (err - jnp.mean(err, axis=1, keepdims=True) - normed * inner) * scale


def sum_rows(value):
    return jnp.sum(value, axis=0, keepdims=True)


def feed_kernel(
    steps,
    vec_ref,
    x_ref,
    tan_ref,
    wo_ref,
    up_ref,
    dn_ref,
    upb_ref,
    dnb_ref,
    g1_ref,
    s1_ref,
    g2_ref,
    s2_ref,
    out_ref,
    dmix_ref,
    gvec_ref,
    go_ref,
    gup_ref,
    gdn_ref,
    gupb_ref,
    small_ref,
    n1_ref,
    r1_ref,
    fb_ref,
    fbt_ref,
    acc_ref,
    act_ref,
    slope_ref,
    gd_ref,
    gdt_ref,
):
    step = pl.program_id(0)

    @pl.when(step == 0)
    def _():
        normed, scale = norm_parts(nt(vec_ref[...], wo_ref[...]) + x_ref[...].astype(F32))
        n1_ref[...] = normed
        r1_ref[...] = scale
        first = normed * g1_ref[...] + s1_ref[...]
        fb_ref[...] = first.astype(BF)
        fbt_ref[...] = jnp.transpose(first).astype(BF)
        acc_ref[...] = first + dnb_ref[...]

    @pl.when(step < steps)
    def _():
        upper = nn(fb_ref[...], up_ref[...]) + upb_ref[...]
        square = upper * upper
        root = 0.7978845608028654
        bend = jnp.tanh(root * (upper + 0.044715 * (square * upper)))
        half = 0.5 * (1.0 + bend)
        act = (upper * half).astype(BF)
        act_ref[step] = act
        slope_ref[step] = half + 0.5 * upper * (1.0 - bend * bend) * (
            root + (3 * 0.044715 * root) * square
        )
        acc_ref[...] += nt(act, dn_ref[...])

    @pl.when(step == steps - 1)
    def _():
        normed, scale = norm_parts(acc_ref[...])
        out_ref[...] = (normed * g2_ref[...] + s2_ref[...]).astype(BF)
        tan = tan_ref[...].astype(F32)
        d_down = norm_pull(normed, scale, tan * g2_ref[...])
        small_ref[0:1, :] = sum_rows(d_down)
        small_ref[3:4, :] = sum_rows(tan * normed)
        small_ref[4:5, :] = sum_rows(tan)
        gd_ref[...] = d_down.astype(BF)
        gdt_ref[...] = jnp.transpose(d_down).astype(BF)
        acc_ref[...] = d_down

    @pl.when(step >= steps)
    def _():
        at = step - steps
        d_up = nn(gd_ref[...], dn_ref[...]) * slope_ref[at]
        gupb_ref[...] = sum_rows(d_up)
        g_up = d_up.astype(BF)
        gdn_ref[...] = nn(gdt_ref[...], act_ref[at]).astype(BF)
        gup_ref[...] = nn(fbt_ref[...], g_up).astype(BF)
        acc_ref[...] += nt(g_up, up_ref[...])

    @pl.when(step == 2 * steps - 1)
    def _():
        d_first, normed = acc_ref[...], n1_ref[...]
        small_ref[1:2, :] = sum_rows(d_first * normed)
        small_ref[2:3, :] = sum_rows(d_first)
        d_mixed = norm_pull(normed, r1_ref[...], d_first * g1_ref[...])
        dmix_ref[...] = d_mixed
        g_mixed = d_mixed.astype(BF)
        go_ref[...] = nn(jnp.transpose(d_mixed).astype(BF), vec_ref[...]).astype(BF)
        gvec_ref[...] = nn(g_mixed, wo_ref[...]).astype(BF)


def feed(vec, x, tan, wo, up, dn, upb, dnb, g1, s1, g2, s2):
    rows, width = vec.shape
    inner = up.shape[1]
    chunk = 512
    steps = inner // chunk
    whole = lambda a, b: pl.BlockSpec((a, b), lambda i: (0, 0))
    cols = lambda a: pl.BlockSpec((a, chunk), lambda i: (0, lax.rem(i, steps)))
    late = lambda a: pl.BlockSpec((a, chunk), lambda i: (0, jnp.maximum(i - steps, 0)))
    return pl.pallas_call(
        functools.partial(feed_kernel, steps),
        grid=(2 * steps,),
        in_specs=[
            whole(rows, width),
            whole(rows, width),
            whole(rows, width),
            whole(width, width),
            cols(width),
            cols(width),
            cols(1),
        ]
        + [whole(1, width)] * 5,
        out_specs=[
            whole(rows, width),
            whole(rows, width),
            whole(rows, width),
            whole(width, width),
            late(width),
            late(width),
            late(1),
            whole(8, width),
        ],
        out_shape=[
            jax.ShapeDtypeStruct((rows, width), BF),
            jax.ShapeDtypeStruct((rows, width), F32),
            jax.ShapeDtypeStruct((rows, width), BF),
            jax.ShapeDtypeStruct((width, width), BF),
            jax.ShapeDtypeStruct((width, inner), BF),
            jax.ShapeDtypeStruct((width, inner), BF),
            jax.ShapeDtypeStruct((1, inner), F32),
            jax.ShapeDtypeStruct((8, width), F32),
        ],
        scratch_shapes=[
            pltpu.VMEM((rows, width), F32),
            pltpu.VMEM((rows, 1), F32),
            pltpu.VMEM((rows, width), BF),
            pltpu.VMEM((width, rows), BF),
            pltpu.VMEM((rows, width), F32),
            pltpu.VMEM((steps, rows, chunk), BF),
            pltpu.VMEM((steps, rows, chunk), F32),
            pltpu.VMEM((rows, width), BF),
            pltpu.VMEM((width, rows), BF),
        ],
        compiler_params=pltpu.CompilerParams(vmem_limit_bytes=LIMIT),
        cost_estimate=pl.CostEstimate(
            flops=12 * rows * width * inner, bytes_accessed=36 << 20, transcendentals=rows * inner
        ),
        name="feed",
    )(vec, x, tan, wo, up, dn, upb, dnb, g1, s1, g2, s2)


def gather_weights(shards):
    rows, cols = shards[0].shape
    groups, tensors = lax.axis_size("dp"), lax.axis_size("tensor")
    stack = jnp.stack(shards)
    both = lax.all_gather(stack, ("dp", "tensor"), axis=0, tiled=False)
    both = both.reshape(groups, tensors, len(shards), rows, cols)
    both = both.transpose(2, 0, 3, 1, 4).reshape(len(shards), groups * rows, tensors * cols)
    return [both[i] for i in range(len(shards))]


def scatter_grads(grads):
    groups, tensors = lax.axis_size("dp"), lax.axis_size("tensor")
    rows, cols = grads[0].shape[0] // groups, grads[0].shape[1] // tensors
    stack = jnp.stack(grads).reshape(len(grads), groups, rows, tensors, cols)
    stack = stack.transpose(1, 3, 0, 2, 4).reshape(groups * tensors, len(grads), rows, cols)
    mine = lax.psum_scatter(stack, ("dp", "tensor"), scatter_dimension=0, tiled=True)
    mine = mine.reshape(len(grads), rows, cols).astype(F32)
    return [mine[i] for i in range(len(grads))]


def body(
    content_stream,
    query_stream,
    memory,
    content_tangent,
    query_tangent,
    seq_lengths,
    factor_order,
    memory_lengths,
    slot_sequence,
    query_weight,
    key_weight,
    value_weight,
    pos_weight,
    out_weight,
    up_weight,
    up_bias,
    down_weight,
    down_bias,
    word_bias,
    pos_bias,
    first_gain,
    first_shift,
    second_gain,
    second_shift,
):
    groups, tensors = lax.axis_size("dp"), lax.axis_size("tensor")
    micro, part_len, width = content_stream.shape
    mem_part = memory.shape[1]
    seq_len, mem_total = part_len * tensors, mem_part * tensors
    klen, span = mem_total + seq_len, mem_total + 2 * seq_len
    count = micro * groups
    here, lane = lax.axis_index("dp"), lax.axis_index("tensor")
    core = here % 2
    lead = core == 0
    block = 256
    assert 2 * micro == tensors
    pairs = [(i, i ^ 1) for i in range(groups)]

    def swap(arr):
        return lax.ppermute(arr, "dp", pairs)

    def to_unit(first, second):
        got = swap(jnp.where(lead, second, first))
        low = jnp.where(lead, first, got)
        high = jnp.where(lead, got, second)
        both = jnp.concatenate([low, high], 0)
        both = lax.all_to_all(both, "tensor", split_axis=0, concat_axis=0, tiled=True)
        return both.reshape(seq_len, width)

    def from_unit(arr):
        both = arr.reshape(tensors, part_len, width)
        both = lax.all_to_all(both, "tensor", split_axis=0, concat_axis=0, tiled=True)
        low, high = both[:micro], both[micro:]
        got = swap(jnp.where(lead, high, low))
        return jnp.where(lead, low, got), jnp.where(lead, got, high)

    seq_id = (here // 2) * tensors + lane
    ids = jnp.arange(count, dtype=jnp.int32)
    slot_of = jnp.sum(jnp.where(slot_sequence[None, :] == ids[:, None], ids[None, :], 0), axis=1)
    lengths = lax.all_gather(
        jnp.concatenate([seq_lengths, memory_lengths]), "dp", axis=0, tiled=False
    )
    length = lengths[:, :micro].reshape(count)[seq_id]
    mem_valid = lengths[:, micro:].reshape(count)[slot_of[seq_id]]
    other = swap(factor_order)
    orders = jnp.concatenate(
        [jnp.where(lead, factor_order, other), jnp.where(lead, other, factor_order)], 0
    )
    rank = lax.dynamic_index_in_dim(orders, lane, 0, keepdims=False)
    key_pos = jnp.arange(klen, dtype=jnp.int32)
    hidden = jnp.int32(1 << 20)
    mem_rank = jnp.where(key_pos[:mem_total] >= mem_total - mem_valid, -1, hidden)
    own_rank = jnp.where(key_pos[:seq_len] < length, rank, hidden)
    key_rank = jnp.concatenate([mem_rank, own_rank])[None, :]
    thr = (rank + jnp.where(lead, 1, 0))[:, None]

    stream = to_unit(content_stream, query_stream)
    content = jnp.where(lead, stream, swap(stream))

    piece = mem_part // groups
    spread = lax.all_to_all(
        memory.reshape(micro, groups, piece, width), "dp", split_axis=1, concat_axis=1, tiled=True
    )
    spread = spread.transpose(1, 0, 2, 3).reshape(count, piece, width)
    spread = jnp.take(spread, slot_of, axis=0)
    spread = spread.reshape(groups // 2, tensors, 2, piece // 2, width).transpose(0, 2, 1, 3, 4)
    spread = lax.all_to_all(
        spread.reshape(groups, tensors, piece // 2, width),
        "dp",
        split_axis=0,
        concat_axis=0,
        tiled=True,
    )
    spread = lax.all_to_all(spread, "tensor", split_axis=1, concat_axis=1, tiled=True)
    got = swap(spread)
    mem_rows = jnp.stack([jnp.where(lead, spread, got), jnp.where(lead, got, spread)])
    mem_rows = mem_rows.transpose(2, 1, 0, 3, 4).reshape(mem_total, width)

    tangent = to_unit(content_tangent, query_tangent)

    key_mat, value_mat, query_mat, pos_mat, out_mat = gather_weights(
        [key_weight, value_weight, query_weight, pos_weight, out_weight]
    )
    up_mat, down_mat = gather_weights([up_weight, down_weight])

    context = jnp.concatenate([mem_rows, content], 0)
    table = reversed_table(span, klen, width)
    keys = nn(context, key_mat).astype(BF)
    values = nn(context, value_mat).astype(BF)
    rel = nn(table, pos_mat).astype(BF)
    proj = nn(stream, query_mat)
    scale = jnp.asarray(0.125, BF)
    q_word = (proj + word_bias.reshape(1, width)).astype(BF) * scale
    q_pos = (proj + pos_bias.reshape(1, width)).astype(BF) * scale

    vec, prob = attend_forward(q_word, q_pos, keys, values, rel, thr, key_rank, block)
    row = lambda v: v.reshape(1, -1)
    out, d_mixed, g_vec, g_out, g_up, g_down, g_upb, small = feed(
        vec,
        stream,
        tangent,
        out_mat,
        up_mat,
        down_mat,
        row(up_bias),
        row(down_bias),
        row(first_gain),
        row(first_shift),
        row(second_gain),
        row(second_shift),
    )
    content_out, query_out = from_unit(out)
    grad_up, grad_down = scatter_grads([g_up, g_down])
    early = lax.psum(
        jnp.concatenate([g_upb.reshape(-1), small[:5].reshape(-1)]), ("dp", "tensor")
    )

    d_proj, dk_t, dv_t, drel_t, biases = attend_backward(
        prob, g_vec, q_word, q_pos, keys, values, rel, block
    )
    late = lax.psum(biases, ("dp", "tensor"))
    d_context = tt(dk_t[:, mem_total:], key_mat) + tt(dv_t[:, mem_total:], value_mat)
    partner = swap(d_context.astype(BF))
    d_stream = d_mixed + nt(d_proj, query_mat)
    d_stream = d_stream + jnp.where(lead, d_context + partner.astype(F32), 0.0)
    content_grad, query_grad = from_unit(d_stream.astype(BF))
    grad_query, grad_key, grad_value, grad_pos, grad_out = scatter_grads(
        [
            tn(stream, d_proj).astype(BF),
            tt(context, dk_t).astype(BF),
            tt(context, dv_t).astype(BF),
            tt(table, drel_t).astype(BF),
            g_out,
        ]
    )
    inner = up_bias.shape[0]
    rest = early[inner:].reshape(5, width)
    return (
        content_out,
        query_out,
        content_grad,
        query_grad,
        grad_query,
        grad_key,
        grad_value,
        grad_pos,
        grad_out,
        grad_up,
        early[:inner],
        grad_down,
        rest[0],
        late[0].reshape(HEADS, DH),
        late[1].reshape(HEADS, DH),
        rest[1],
        rest[2],
        rest[3],
        rest[4],
    )


def solution(mesh):
    rows = P("dp", "tensor", None)
    mat = P("dp", "tensor")
    return jax.shard_map(
        body,
        mesh=mesh,
        in_specs=(rows,) * 5
        + (P("dp"), P("dp", None), P("dp"), P())
        + (mat,) * 6
        + (P(), mat)
        + (P(),) * 7,
        out_specs=(rows,) * 4 + (mat,) * 6 + (P(), mat) + (P(),) * 7,
        check_vma=False,
    )
```

time: 1810 us -> 633 us (0.35)
  local copies, waits for them, and re-layouts: 551 us -> 149 us
  blocking collectives: 404 us -> 56.1 us
  matrix products: 330 us -> 30.5 us
  waiting for transfers between devices: 344 us -> 218 us
  Pallas kernels: 0 us -> 91.3 us
  other arithmetic: 83.1 us -> 33.2 us
  starting transfers between devices: 61.3 us -> 31.2 us
    all_gather x20 -> x0, blocking collectives: 356 us -> none  [the longest x8 165 us: widen(): lax.all_gather(second, 'tensor', axis=0, tiled=True)]
    dot_general x95 -> x11, matrix products: 292 us -> 30.5 us  [the longest x5 12.9 us: tt(): lax.dot_general(left, right, (((0,), (1,)), ((), ())), preferred_element_...]
    unnamed x568 -> x108, local copies, waits for them, and re-layouts: 229 us -> 22 us
    reshape x24 -> x11, local copies, waits for them, and re-layouts: 176 us -> 30.1 us  [the longest x2 26.2 us: gather_weights(): both = both.reshape(groups, tensors, len(shards), rows, cols)]
    reduce_scatter x23 -> x2, waiting for transfers between devices: 267 us -> 132 us  [scatter_grads(): lax.psum_scatter(stack, ('dp', 'tensor'), scatter_dimension=0, tiled=True)]
    pallas_call x0 -> x3, Pallas kernels: none -> 91.3 us  [the longest x1 33.1 us: attend_backward(): pl.pallas_call(functools.partial(attend_backward_kernel, block), grid=(wi...]
    pad x8 -> x0, local copies, waits for them, and re-layouts: 50 us -> none  [the longest x4 34.1 us: unskew_rows(): jnp.pad(padded.reshape(head_count, row_count * (span_len - 1)), ((0, 0),...]
    slice x13 -> x6, local copies, waits for them, and re-layouts: 61.1 us -> 18.4 us  [the longest x2 17.1 us: gather_weights(): return [both[i] for i in range(len(shards))]]
  transfers between devices with their start and end apart: 43 -> 19, of which waited for: 20 -> 7; matrix products, arithmetic and copies ran while one was open for 38% -> 26% of each run, Pallas kernels for 0% -> 4%
where the time goes in v1:
time: 633 us; the launch traced here: 627 us
  waiting for transfers between devices  218 us (34%)
  local copies, waits for them, and re-layouts  149 us (24%)
  Pallas kernels  91.3 us (14%)
  blocking collectives  56.1 us (9%)
  other arithmetic  33.2 us (5%)
  starting transfers between devices  31.2 us (5%)
  matrix products  30.5 us (5%)
  between operations  18 us (3%)
    reduce_scatter x2, waiting for transfers between devices, scatter_grads(): lax.psum_scatter(stack, ('dp', 'tensor'), scatter_dimension=0, tiled=True)  132 us
    psum x1, blocking collectives, body(): lax.psum(jnp.concatenate([g_upb.reshape(-1), small[:5].reshape(-1)]), ('d...  47.8 us
    another operation x8, local copies, waits for them, and re-layouts, scatter_grads(): stack = jnp.stack(grads).reshape(len(grads), groups, rows, tensors, cols)  37.9 us
    all_to_all x2, waiting for transfers between devices, from_unit(): lax.all_to_all(both, 'tensor', split_axis=0, concat_axis=0, tiled=True)  35.7 us
    pallas_call x1, Pallas kernels, attend_backward(): pl.pallas_call(functools.partial(attend_backward_kernel, block), grid=(wi...  33.1 us
    pallas_call x1, Pallas kernels, feed(): pl.pallas_call(functools.partial(feed_kernel, steps), grid=(2 * steps,),...  31.5 us
    pallas_call x1, Pallas kernels, attend_forward(): pl.pallas_call(functools.partial(attend_forward_kernel, block), grid=(wid...  26.6 us
    reshape x2, local copies, waits for them, and re-layouts, gather_weights(): both = both.reshape(groups, tensors, len(shards), rows, cols)  26.2 us
  transfers between devices with their start and end apart: 19, of which 7 were waited for; matrix products, arithmetic and copies ran while one was open for 26% of the time, Pallas kernels for 4%

profile of v1, /device:TPU:0, one launch (start us, length us, event | category | flops | bytes accessed | tf_op | source)
XLA Modules:
  0.0 626.9 jit_solution(701601231731929859)
XLA Ops:
  15.2 4.8 all-to-all-start.1
  20.9 9.2 %all-to-all-done.1 = bf16[2,8,16,768]{3,2,0,1:T(8,128)(2,1)S(1)} async-done(((bf16[2,8,16,768]{3,2,0,1:T(8,128)(2,1)}), bf16[2,8,16,768]{3,2,0,1:T(8,128)(2,1)S(1)}, u32[]{:S(2)}, u32[]{:S(2)}) %all-to-all-start.1) | async-done | bytes 393248 | tf_op jit(solution)/shard_map/all_to_all | solution.py:473
  37.7 8.3 %all-reduce = s32[32]{0:T(128)S(1)} all-reduce(s32[32]{0:T(128)S(1)} %add_dynamic-update-slice_fusion), channel_id=3, replica_groups=mesh['dp'=8,'tensor'=4] {'dp'}, use_global_device_ids=true, to_apply=%add | all-reduce | flops 32 | bytes 256
  46.9 4.9 all-to-all-start.3
  52.9 13.7 %all-to-all-done.3 = bf16[8,4,8,768]{3,2,0,1:T(8,128)(2,1)S(1)} async-done(((bf16[8,4,8,768]{3,2,0,1:T(8,128)(2,1)}), bf16[8,4,8,768]{3,2,0,1:T(8,128)(2,1)S(1)}, u32[]{:S(2)}, u32[]{:S(2)}) %all-to-all-start.3) | async-done | bytes 393248 | tf_op jit(solution)/shard_map/all_to_all | solution.py:486
  70.3 10.2 %fusion = (bf16[1536,384]{1,0:T(8,128)(2,1)}, bf16[1536,384]{1,0:T(8,128)(2,1)}) fusion(f32[384]{0:T(512)S(1)} %negate_power_fusion, f32[1536]{0:T(1024)S(1)} %iota_subtract_fusion), kind=kLoop, calls=%fused_computation.7 | loop fusion | flops 1769472 | bytes 2366976 | tf_op jit(solution)/shard_map/convert
  91.0 17.8 %all-to-all-done = bf16[4,128,768]{2,1,0:T(8,128)(2,1)S(1)} async-done(((bf16[4,128,768]{2,1,0:T(8,128)(2,1)}), bf16[4,128,768]{2,1,0:T(8,128)(2,1)S(1)}, u32[]{:S(2)}, u32[]{:S(2)}) %all-to-all-start) | async-done | bytes 786464 | tf_op jit(solution)/shard_map/all_to_all | solution.py:439
  110.0 4.2 all-to-all-start.4
  117.9 13.8 %copy.86 = bf16[8,4,5,96,192]{4,1,3,0,2:T(4,128)(2,1)} copy(bf16[8,4,5,96,192]{4,3,2,1,0:T(8,128)(2,1)} %bitcast.104) | data formatting | bytes 11796480 | tf_op jit(solution)/shard_map/reshape | solution.py:377
  131.8 6.3 %fusion.13 = (bf16[1,8,96,4,192]{4,3,2,1,0:T(4,128)(2,1)}, bf16[1,8,96,4,192]{4,3,2,1,0:T(4,128)(2,1)S(1)}, bf16[1,8,96,4,192]{4,3,2,1,0:T(4,128)(2,1)}, bf16[1,...) fusion(bf16[5,8,96,4,192]{4,3,2,1,0:T(4,128)(2,1)} %bitcast.97), kind=kLoop, calls=%fused_computation.88 | loop fusion | bytes 11796480 | tf_op jit(solution)/shard_map/slice | solution.py:379
  138.0 4.0 squeeze.65.wo_ref
  142.1 4.0 squeeze.60
  146.1 4.0 squeeze.59
  165.2 26.6 %attend_forward.1 = (bf16[512,768]{1,0:T(8,128)(2,1)}, bf16[12,512,1024]{2,1,0:T(8,128)(2,1)}) custom-call(bf16[512,768]{1,0:T(8,128)(2,1)} %get-tuple-element.63.qw_ref, bf16[512,768]{1,0:T(8,128)(2,1)} %get-tuple-element.62.qp_ref, bf16[1024,768]{1,0:T(8,128)(2,1)} %convolution_convert_fusion.2.k_ref, bf16[1024,768]{1,0:T(8,128)(2,1)} %convolution_convert_fusion.1.v_ref, ...), custom_call_target="tpu_custom_call" | custom-call | flops 3221225472 | bytes 16777216 | tf_op jit(solution)/shard_map/attend_forward/pallas_call | solution.py:78
  191.8 8.9 %all-gather.8.cloned.1.call-done = bf16[64,96,768]{2,1,0:T(8,128)(2,1)} async-done(((bf16[2,96,768]{2,1,0:T(8,128)(2,1)}), bf16[64,96,768]{2,1,0:T(8,128)(2,1)}) %all-gather.8.cloned.1.call-update) | async-done | bytes 9437200 | tf_op jit(solution)/shard_map/all_gather | solution.py:376
  200.7 12.4 %copy.85 = bf16[8,4,2,96,768]{4,1,3,0,2:T(4,128)(2,1)} copy(bf16[8,4,2,96,768]{4,3,2,1,0:T(8,128)(2,1)} %bitcast.103) | data formatting | bytes 18874368 | tf_op jit(solution)/shard_map/reshape | solution.py:377
  213.1 10.9 %fusion.12 = (bf16[1,8,96,4,768]{4,3,2,1,0:T(4,128)(2,1)}, bf16[1,8,96,4,768]{4,3,2,1,0:T(4,128)(2,1)}) fusion(bf16[2,8,96,4,768]{4,3,2,1,0:T(4,128)(2,1)} %bitcast.95), kind=kLoop, calls=%fused_computation.87 | loop fusion | bytes 18874368 | tf_op jit(solution)/shard_map/slice | solution.py:379
  223.9 5.7 copy.82
  232.8 31.5 %feed.1 = (bf16[512,768]{1,0:T(8,128)(2,1)}, f32[512,768]{1,0:T(8,128)}, bf16[512,768]{1,0:T(8,128)(2,1)}, bf16[768,768]{1,0:T(8,128)(2,1)}, bf16[768,3072]{1,0:...) custom-call(bf16[512,768]{1,0:T(8,128)(2,1)} %get-tuple-element.34.vec_ref, ...), custom_call_target="tpu_custom_call" | custom-call | flops 14495514624 | bytes 37748736 | tf_op jit(solution)/shard_map/feed/pallas_call | solution.py:320
  264.4 33.1 %attend_backward.1 = (bf16[512,768]{1,0:T(8,128)(2,1)}, bf16[768,1024]{1,0:T(8,128)(2,1)}, bf16[768,1024]{1,0:T(8,128)(2,1)}, bf16[768,1536]{1,0:T(8,128)(2,1)}, f32[2,768]{1,0:T(2,128)}) custom-call(bf16[12,512,1024]{2,1,0:T(8,128)(2,1)} %get-tuple-element.37.prob_ref, bf16[512,768]{1,0:T(8,128)(2,1)} %get-tuple-element.38.gvec_ref, ...), custom_call_target="tpu_custom_call" | custom-call | flops 6442450944 | bytes 20971520 | tf_op jit(solution)/shard_map/attend_backward/pallas_call | solution.py:175
  297.5 4.7 convolution_convert_fusion.6
  308.9 4.6 stack.75
  313.6 4.2 convolution_convert_fusion.4
  321.5 4.5 stack.76
  334.6 4.8 copy.79
  339.5 10.1 %stack.81 = bf16[1,8,96,4,768]{4,3,2,1,0:T(4,128)(2,1)} reshape(bf16[768,3072]{1,0:T(8,128)(2,1)} %get-tuple-element.44) | data formatting | bytes 9437184 | tf_op jit(solution)/shard_map/stack | solution.py:385
  349.6 9.9 %stack.82 = bf16[1,8,96,4,768]{4,3,2,1,0:T(4,128)(2,1)} reshape(bf16[768,3072]{1,0:T(8,128)(2,1)} %get-tuple-element.45) | data formatting | bytes 9437184 | tf_op jit(solution)/shard_map/stack | solution.py:385
  359.4 9.8 %maximum_bitcast_fusion = bf16[8,4,2,96,768]{4,1,3,0,2:T(4,128)(2,1)} fusion(bf16[1,8,96,4,768]{4,3,2,1,0:T(4,128)(2,1)} %stack.82, bf16[1,8,96,4,768]{4,3,2,1,0:T(4,128)(2,1)} %stack.81), kind=kLoop, calls=%fused_computation.1 | loop fusion | flops 4718592 | bytes 18874368 | tf_op jit(solution)/shard_map/transpose | solution.py:386
  369.2 9.5 %copy.80 = bf16[8,4,2,96,768]{4,3,2,1,0:T(8,128)(2,1)} copy(bf16[8,4,2,96,768]{4,1,3,0,2:T(4,128)(2,1)} %maximum_bitcast_fusion) | data formatting | bytes 18874368 | tf_op jit(solution)/shard_map/transpose | solution.py:386
  391.7 35.7 %all-to-all-done.5 = bf16[4,128,768]{2,1,0:T(8,128)(2,1)S(1)} async-done(((bf16[4,128,768]{2,1,0:T(8,128)(2,1)}), bf16[4,128,768]{2,1,0:T(8,128)(2,1)S(1)}, u32[]{:S(2)}, u32[]{:S(2)}) %all-to-all-start.5) | async-done | bytes 786464 | tf_op jit(solution)/shard_map/all_to_all | solution.py:444
  431.0 47.8 %all-reduce.1 = (f32[6912]{0:T(1024)S(1)}, f32[2,768]{1,0:T(2,128)S(1)}) all-reduce(f32[6912]{0:T(1024)S(1)} %pad_maximum_fusion.7, f32[2,768]{1,0:T(2,128)S(1)} %copy-done.33), channel_id=1, replica_groups=mesh['dp'=8,'tensor'=4] {'dp','tensor'}, use_global_device_ids=true, to_apply=%region_3.4 | all-reduce | flops 8448 | bytes 67584 | tf_op jit(solution)/shard_map/psum | solution.py:526
  486.2 132.0 %reduce-scatter.5.cloned.1.call-done = bf16[1,2,96,768]{3,2,1,0:T(8,128)(2,1)} async-done(((bf16[32,2,96,768]{3,2,1,0:T(8,128)(2,1)}), bf16[1,2,96,768]{3,2,1,0:T(8,128)(2,1)}) %reduce-scatter.5.cloned.1.call-update) | async-done | bytes 294928 | tf_op jit(solution)/shard_map/reduce_scatter | solution.py:387
  (216 shorter events, 97.0 us)
Async XLA Ops:
  7.2 110.7 %all-gather.6.cloned.1.call-start = ((), (), s32[]{:S(2)}) async-start(), calls=%async_computation.11 | async-start | bytes 8110080 | tf_op jit(solution)/shard_map/all_gather | solution.py:376
  8.1 12.0 %copy-start.10 = (bf16[2,128,768]{2,1,0:T(8,128)(2,1)S(1)}, bf16[2,128,768]{2,1,0:T(8,128)(2,1)}, u32[]{:S(2)}) copy-start(bf16[2,128,768]{2,1,0:T(8,128)(2,1)} %param.24) | copy-start | bytes 1179652
  8.1 12.0 %copy-start.11 = (bf16[2,128,768]{2,1,0:T(8,128)(2,1)S(1)}, bf16[2,128,768]{2,1,0:T(8,128)(2,1)}, u32[]{:S(2)}) copy-start(bf16[2,128,768]{2,1,0:T(8,128)(2,1)} %param.25) | copy-start | bytes 1179652
  12.1 188.6 %all-gather.8.cloned.1.call-start = ((), (), s32[]{:S(2)}) async-start(), calls=%async_computation.12 | async-start | bytes 9732096 | tf_op jit(solution)/shard_map/all_gather | solution.py:376
  13.9 74.3 %collective-permute-start.3 = (s32[2,512]{1,0:T(2,128)}, s32[2,512]{1,0:T(2,128)}, u32[]{:S(2)}, u32[]{:S(2)}) collective-permute-start(s32[2,512]{1,0:T(2,128)} %param.30), channel_id=1, source_target_pairs={{0,4},{4,0},{8,12},{12,8},{16,20},{20,16},{24,28},{28,24},{1,5},{5... | collective-permute-start | bytes 12296 | tf_op jit(solution)/shard_map/ppermute | solution.py:432
  15.2 14.9 %all-to-all-start.1 = ((bf16[2,8,16,768]{3,2,0,1:T(8,128)(2,1)}), bf16[2,8,16,768]{3,2,0,1:T(8,128)(2,1)S(1)}, u32[]{:S(2)}, u32[]{:S(2)}) async-start(bf16[2,8,16,768]{3,2,0,1:T(8,128)(2,1)} %copy.73), calls=%async_computation.1 | async-start | bytes 786432 | tf_op jit(solution)/shard_map/all_to_all | solution.py:473
  20.1 31.7 %collective-permute-start = (bf16[2,128,768]{2,1,0:T(8,128)(2,1)S(1)}, bf16[2,128,768]{2,1,0:T(8,128)(2,1)S(1)}, u32[]{:S(2)}, u32[]{:S(2)}) collective-permute-start(bf16[2,128,768]{2,1,0:T(8,128)(2,1)S(1)} %broadcast_select_fusion.12), channel_id=1, source_target_pairs={{0,4},{4,0},{8,12},{12,8},{16,20},{20,16},{24,28},{28,24},{1,5},{5... | collective-permute-start | bytes 1179656 | tf_op jit(solution)/shard_map/ppermute | solution.py:432
  31.6 14.4 %all-to-all-start.2 = ((bf16[8,4,8,768]{3,2,1,0:T(8,128)(2,1)}), bf16[8,4,8,768]{3,2,1,0:T(8,128)(2,1)S(1)}, u32[]{:S(2)}, u32[]{:S(2)}) async-start(bf16[8,4,8,768]{3,2,1,0:T(8,128)(2,1)} %bitcast.15), calls=%async_computation.2 | async-start | bytes 786432 | tf_op jit(solution)/shard_map/all_to_all | solution.py:479
  35.9 72.9 %collective-permute-start.4 = (bf16[2,128,768]{2,1,0:T(8,128)(2,1)}, bf16[2,128,768]{2,1,0:T(8,128)(2,1)S(1)}, u32[]{:S(2)}, u32[]{:S(2)}) collective-permute-start(bf16[2,128,768]{2,1,0:T(8,128)(2,1)} %broadcast_select_fusion.9), channel_id=1, source_target_pairs={{0,4},{4,0},{8,12},{12,8},{16,20},{20,16},{24,28},{28,24},{1,5},{5... | collective-permute-start | bytes 1179656 | tf_op jit(solution)/shard_map/ppermute | solution.py:432
  46.9 19.7 %all-to-all-start.3 = ((bf16[8,4,8,768]{3,2,0,1:T(8,128)(2,1)}), bf16[8,4,8,768]{3,2,0,1:T(8,128)(2,1)S(1)}, u32[]{:S(2)}, u32[]{:S(2)}) async-start(bf16[8,4,8,768]{3,2,0,1:T(8,128)(2,1)} %copy.75), calls=%async_computation.3 | async-start | bytes 786432 | tf_op jit(solution)/shard_map/all_to_all | solution.py:486
  66.6 42.2 %all-to-all-start = ((bf16[4,128,768]{2,1,0:T(8,128)(2,1)}), bf16[4,128,768]{2,1,0:T(8,128)(2,1)S(1)}, u32[]{:S(2)}, u32[]{:S(2)}) async-start(bf16[4,128,768]{2,1,0:T(8,128)(2,1)} %pad_maximum_fusion.4), calls=%async_computation | async-start | bytes 1572864 | tf_op jit(solution)/shard_map/all_to_all | solution.py:439
  70.2 10.4 %copy-start.40 = (s32[16]{0:T(128)S(1)}, s32[16]{0:T(128)}, u32[]{:S(2)}) copy-start(s32[16]{0:T(128)} %copy-done.39) | copy-start | bytes 196
  70.2 12.3 %copy-start.34 = (f32[768]{0:T(1024)S(1)}, f32[768]{0:T(1024)}, u32[]{:S(2)}) copy-start(f32[768]{0:T(1024)} %param.41) | copy-start | bytes 9220
  70.2 12.9 %copy-start.35 = (f32[768]{0:T(1024)S(1)}, f32[768]{0:T(1024)}, u32[]{:S(2)}) copy-start(f32[768]{0:T(1024)} %param.44) | copy-start | bytes 9220
  70.2 13.4 %copy-start.36 = (f32[768]{0:T(1024)S(1)}, f32[768]{0:T(1024)}, u32[]{:S(2)}) copy-start(f32[768]{0:T(1024)} %param.45) | copy-start | bytes 9220
  70.2 14.0 %copy-start.37 = (f32[768]{0:T(1024)S(1)}, f32[768]{0:T(1024)}, u32[]{:S(2)}) copy-start(f32[768]{0:T(1024)} %param.46) | copy-start | bytes 9220
  70.2 14.6 %copy-start.38 = (f32[768]{0:T(1024)S(1)}, f32[768]{0:T(1024)}, u32[]{:S(2)}) copy-start(f32[768]{0:T(1024)} %param.47) | copy-start | bytes 9220
  70.2 15.1 %copy-start.31 = (f32[12,64]{1,0:T(8,128)S(1)}, f32[12,64]{1,0:T(8,128)}, u32[]{:S(2)}) copy-start(f32[12,64]{1,0:T(8,128)} %param.42) | copy-start | bytes 9220
  70.3 15.2 %copy-start.32 = (f32[12,64]{1,0:T(8,128)S(1)}, f32[12,64]{1,0:T(8,128)}, u32[]{:S(2)}) copy-start(f32[12,64]{1,0:T(8,128)} %param.43) | copy-start | bytes 9220
  91.0 23.7 %collective-permute-start.1 = (bf16[8,4,8,768]{3,2,0,1:T(8,128)(2,1)S(1)}, bf16[8,4,8,768]{3,2,0,1:T(8,128)(2,1)}, u32[]{:S(2)}, u32[]{:S(2)}) collective-permute-start(bf16[8,4,8,768]{3,2,0,1:T(8,128)(2,1)S(1)} %all-to-all-done.3), channel_id=1, source_target_pairs={{0,4},{4,0},{8,12},{12,8},{16,20},{20,16},{24,28},{28,24},{1,5},{5... | collective-permute-start | bytes 1179656 | tf_op jit(solution)/shard_map/ppermute | solution.py:432
  108.8 8.1 %collective-permute-start.2 = (bf16[512,768]{1,0:T(8,128)(2,1)S(1)}, bf16[512,768]{1,0:T(8,128)(2,1)S(1)}, u32[]{:S(2)}, u32[]{:S(2)}) collective-permute-start(bf16[512,768]{1,0:T(8,128)(2,1)S(1)} %bitcast.107), channel_id=1, source_target_pairs={{0,4},{4,0},{8,12},{12,8},{16,20},{20,16},{24,28},{28,24},{1,5},{5... | collective-permute-start | bytes 2359304 | tf_op jit(solution)/shard_map/ppermute | solution.py:432
  110.0 122.9 %all-to-all-start.4 = ((bf16[4,128,768]{2,1,0:T(8,128)(2,1)}), bf16[4,128,768]{2,1,0:T(8,128)(2,1)}, u32[]{:S(2)}, u32[]{:S(2)}) async-start(bf16[4,128,768]{2,1,0:T(8,128)(2,1)} %pad_maximum_fusion.5), calls=%async_computation.4 | async-start | bytes 1572864 | tf_op jit(solution)/shard_map/all_to_all | solution.py:439
  114.2 370.3 %reduce-scatter.3.cloned.1.call-start = ((), (), s32[]{:S(2)}) async-start(), calls=%async_computation.9 | async-start | bytes 8110080 | tf_op jit(solution)/shard_map/reduce_scatter | solution.py:387
  339.4 278.8 %reduce-scatter.5.cloned.1.call-start = ((), (), s32[]{:S(2)}) async-start(), calls=%async_computation.10 | async-start | bytes 9732096 | tf_op jit(solution)/shard_map/reduce_scatter | solution.py:387
  384.0 3.8 collective-permute-start.6
  384.3 43.1 %all-to-all-start.5 = ((bf16[4,128,768]{2,1,0:T(8,128)(2,1)}), bf16[4,128,768]{2,1,0:T(8,128)(2,1)S(1)}, u32[]{:S(2)}, u32[]{:S(2)}) async-start(bf16[4,128,768]{2,1,0:T(8,128)(2,1)} %bitcast.114), calls=%async_computation.5 | async-start | bytes 1572864 | tf_op jit(solution)/shard_map/all_to_all | solution.py:444
  391.7 39.2 %copy-start.29 = (f32[8,768]{1,0:T(8,128)S(1)}, f32[8,768]{1,0:T(8,128)}, u32[]{:S(2)}) copy-start(f32[8,768]{1,0:T(8,128)} %get-tuple-element.47) | copy-start | bytes 73732
  391.7 39.2 %copy-start.30 = (f32[1,3072]{1,0:T(1,128)S(1)}, f32[1,3072]{1,0:T(1,128)}, u32[]{:S(2)}) copy-start(f32[1,3072]{1,0:T(1,128)} %get-tuple-element.46) | copy-start | bytes 36868
  391.7 39.2 %copy-start.33 = (f32[2,768]{1,0:T(2,128)S(1)}, f32[2,768]{1,0:T(2,128)}, u32[]{:S(2)}) copy-start(f32[2,768]{1,0:T(2,128)} %get-tuple-element.48) | copy-start | bytes 18436
  427.4 53.5 %all-to-all-start.6 = ((bf16[4,128,768]{2,1,0:T(8,128)(2,1)}), bf16[4,128,768]{2,1,0:T(8,128)(2,1)S(1)}, u32[]{:S(2)}, u32[]{:S(2)}) async-start(bf16[4,128,768]{2,1,0:T(8,128)(2,1)} %bitcast.111), calls=%async_computation.6 | async-start | bytes 1572864 | tf_op jit(solution)/shard_map/all_to_all | solution.py:444
  480.8 1.8 collective-permute-start.5
  480.9 2.6 collective-permute-start.7
  (35 other events, 133.7 us)
Sparse Core Ops, SparseCore 0:
  12.2 99.8 all-gather.5
  115.5 85.1 all-gather.7
  339.6 137.7 reduce-scatter.2
  483.1 135.0 reduce-scatter.4

commit v2 on v1

--- a/solution.py
+++ b/solution.py
@@ -216,53 +216,91 @@
     return jnp.sum(value, axis=0, keepdims=True)
 
 
-def feed_kernel(
-    steps,
-    vec_ref,
-    x_ref,
-    tan_ref,
-    wo_ref,
-    up_ref,
-    dn_ref,
-    upb_ref,
-    dnb_ref,
-    g1_ref,
-    s1_ref,
-    g2_ref,
-    s2_ref,
-    out_ref,
-    dmix_ref,
-    gvec_ref,
-    go_ref,
-    gup_ref,
-    gdn_ref,
-    gupb_ref,
-    small_ref,
-    n1_ref,
-    r1_ref,
-    fb_ref,
-    fbt_ref,
-    acc_ref,
-    act_ref,
-    slope_ref,
-    gd_ref,
-    gdt_ref,
-):
+def load_pieces(refs, offs_ref, dst_ref, sems):
+    copies = []
+    for i, ref in enumerate(refs):
+        rows = ref.shape[1]
+        at = pl.multiple_of(offs_ref[i], 16) if len(refs) > 1 else 0
+        copies.append(pltpu.make_async_copy(ref, dst_ref.at[:, pl.ds(at, rows), :], sems.at[i]))
+    for copy in copies:
+        copy.start()
+    return copies
+
+
+def reorder_rows(value, order_ref, tmp_ref, dst_ref):
+    blocks = order_ref.shape[0]
+    if blocks == 1:
+        dst_ref[...] = jnp.transpose(value).astype(BF)
+        return
+    tmp_ref[...] = jnp.transpose(value)
+    rows = tmp_ref.shape[0] // blocks
+    for i in range(blocks):
+        at = pl.multiple_of(order_ref[i] * rows, 8)
+        dst_ref[i * rows : (i + 1) * rows, :] = tmp_ref[pl.ds(at, rows), :].astype(BF)
+
+
+def feed_kernel(steps, pieces, *refs):
+    offs_ref, order_ref = refs[:2]
+    ud_refs = refs[2 : 2 + pieces]
+    wo_refs = refs[2 + pieces : 2 + 2 * pieces]
+    (
+        vec_ref,
+        x_ref,
+        tan_ref,
+        upb_ref,
+        dnb_ref,
+        g1_ref,
+        s1_ref,
+        g2_ref,
+        s2_ref,
+        out_ref,
+        dmix_ref,
+        gvec_ref,
+        goe_ref,
+        goo_ref,
+        ge_ref,
+        gd2_ref,
+        gupb_ref,
+        small_ref,
+        ud_ref,
+        wo_ref,
+        n1_ref,
+        r1_ref,
+        fb_ref,
+        fbt_ref,
+        acc_ref,
+        act_ref,
+        slope_ref,
+        gd_ref,
+        gdt_ref,
+        tmp_ref,
+        ud_sems,
+        wo_sems,
+    ) = refs[2 + 2 * pieces :]
     step = pl.program_id(0)
+    chunk = act_ref.shape[2]
+    half_rows = goe_ref.shape[0]
+    cols = pl.ds(pl.multiple_of(lax.rem(step, steps) * chunk, chunk), chunk)
 
     @pl.when(step == 0)
     def _():
-        normed, scale = norm_parts(nt(vec_ref[...], wo_ref[...]) + x_ref[...].astype(F32))
+        out_copies = load_pieces(wo_refs, offs_ref, wo_ref, wo_sems)
+        copies = load_pieces(ud_refs, offs_ref, ud_ref, ud_sems)
+        for copy in out_copies:
+            copy.wait()
+        normed, scale = norm_parts(nt(vec_ref[...], wo_ref[0]) + x_ref[...].astype(F32))
         n1_ref[...] = normed
         r1_ref[...] = scale
         first = normed * g1_ref[...] + s1_ref[...]
         fb_ref[...] = first.astype(BF)
-        fbt_ref[...] = jnp.transpose(first).astype(BF)
+        reorder_rows(first, order_ref, tmp_ref, fbt_ref)
         acc_ref[...] = first + dnb_ref[...]
+        for copy in copies:
+            copy.wait()
 
     @pl.when(step < steps)
     def _():
-        upper = nn(fb_ref[...], up_ref[...]) + upb_ref[...]
+        upper = nn(fb_ref[...], ud_ref[0, :, cols]) + upb_ref[...]
         square = upper * upper
         root = 0.7978845608028654
         bend = jnp.tanh(root * (upper + 0.044715 * (square * upper)))
@@ -272,7 +310,7 @@
         slope_ref[step] = half + 0.5 * upper * (1.0 - bend * bend) * (
             root + (3 * 0.044715 * root) * square
         )
-        acc_ref[...] += nt(act, dn_ref[...])
+        acc_ref[...] += nt(act, ud_ref[1, :, cols])
 
     @pl.when(step == steps - 1)
     def _():
@@ -284,18 +322,21 @@
         small_ref[3:4, :] = sum_rows(tan * normed)
         small_ref[4:5, :] = sum_rows(tan)
         gd_ref[...] = d_down.astype(BF)
-        gdt_ref[...] = jnp.transpose(d_down).astype(BF)
+        reorder_rows(d_down, order_ref, tmp_ref, gdt_ref)
         acc_ref[...] = d_down
 
     @pl.when(step >= steps)
     def _():
         at = step - steps
-        d_up = nn(gd_ref[...], dn_ref[...]) * slope_ref[at]
+        d_up = nn(gd_ref[...], ud_ref[1, :, cols]) * slope_ref[at]
         gupb_ref[...] = sum_rows(d_up)
         g_up = d_up.astype(BF)
-        gdn_ref[...] = nn(gdt_ref[...], act_ref[at]).astype(BF)
-        gup_ref[...] = nn(fbt_ref[...], g_up).astype(BF)
-        acc_ref[...] += nt(g_up, up_ref[...])
+        acc_ref[...] += nt(g_up, ud_ref[0, :, cols])
+        act = act_ref[at]
+        for side, dst in ((0, ge_ref), (half_rows, gd2_ref)):
+            rows = slice(side, side + half_rows)
+            dst[0] = nn(fbt_ref[rows, :], g_up).astype(BF)
+            dst[1] = nn(gdt_ref[rows, :], act).astype(BF)
 
     @pl.when(step == 2 * steps - 1)
     def _():
@@ -304,53 +345,59 @@
         small_ref[2:3, :] = sum_rows(d_first)
         d_mixed = norm_pull(normed, r1_ref[...], d_first * g1_ref[...])
         dmix_ref[...] = d_mixed
-        g_mixed = d_mixed.astype(BF)
-        go_ref[...] = nn(jnp.transpose(d_mixed).astype(BF), vec_ref[...]).astype(BF)
-        gvec_ref[...] = nn(g_mixed, wo_ref[...]).astype(BF)
-
-
-def feed(vec, x, tan, wo, up, dn, upb, dnb, g1, s1, g2, s2):
+        gvec_ref[...] = nn(d_mixed.astype(BF), wo_ref[0]).astype(BF)
+        reorder_rows(d_mixed, order_ref, tmp_ref, gdt_ref)
+        goe_ref[...] = nn(gdt_ref[:half_rows, :], vec_ref[...]).astype(BF)
+        goo_ref[...] = nn(gdt_ref[half_rows:, :], vec_ref[...]).astype(BF)
+
+
+SMEM_SPEC = pl.BlockSpec(memory_space=pltpu.SMEM)
+ANY_SPEC = pl.BlockSpec(memory_space=pl.ANY)
+
+
+def feed(offs, order, ud_pieces, out_pieces, vec, x, tan, upb, dnb, g1, s1, g2, s2):
     rows, width = vec.shape
-    inner = up.shape[1]
+    inner = upb.shape[1]
     chunk = 512
     steps = inner // chunk
+    half = width // 2
+    count = len(ud_pieces)
     whole = lambda a, b: pl.BlockSpec((a, b), lambda i: (0, 0))
-    cols = lambda a: pl.BlockSpec((a, chunk), lambda i: (0, lax.rem(i, steps)))
-    late = lambda a: pl.BlockSpec((a, chunk), lambda i: (0, jnp.maximum(i - steps, 0)))
+    late = lambda i: jnp.maximum(i - steps, 0)
+    grads = pl.BlockSpec((2, half, chunk), lambda i: (0, 0, late(i)))
     return pl.pallas_call(
-        functools.partial(feed_kernel, steps),
+        functools.partial(feed_kernel, steps, count),
         grid=(2 * steps,),
-        in_specs=[
-            whole(rows, width),
-            whole(rows, width),
-            whole(rows, width),
-            whole(width, width),
-            cols(width),
-            cols(width),
-            cols(1),
-        ]
+        in_specs=[SMEM_SPEC, SMEM_SPEC]
+        + [ANY_SPEC] * (2 * count)
+        + [whole(rows, width)] * 3
+        + [pl.BlockSpec((1, chunk), lambda i: (0, lax.rem(i, steps)))]
         + [whole(1, width)] * 5,
         out_specs=[
             whole(rows, width),
             whole(rows, width),
             whole(rows, width),
-            whole(width, width),
-            late(width),
-            late(width),
-            late(1),
+            whole(half, width),
+            whole(half, width),
+            grads,
+            grads,
+            pl.BlockSpec((1, chunk), lambda i: (0, late(i))),
             whole(8, width),
         ],
         out_shape=[
             jax.ShapeDtypeStruct((rows, width), BF),
             jax.ShapeDtypeStruct((rows, width), F32),
             jax.ShapeDtypeStruct((rows, width), BF),
-            jax.ShapeDtypeStruct((width, width), BF),
-            jax.ShapeDtypeStruct((width, inner), BF),
-            jax.ShapeDtypeStruct((width, inner), BF),
+            jax.ShapeDtypeStruct((half, width), BF),
+            jax.ShapeDtypeStruct((half, width), BF),
+            jax.ShapeDtypeStruct((2, half, inner), BF),
+            jax.ShapeDtypeStruct((2, half, inner), BF),
             jax.ShapeDtypeStruct((1, inner), F32),
             jax.ShapeDtypeStruct((8, width), F32),
         ],
         scratch_shapes=[
+            pltpu.VMEM((2, width, inner), BF),
+            pltpu.VMEM((1, width, width), BF),
             pltpu.VMEM((rows, width), F32),
             pltpu.VMEM((rows, 1), F32),
             pltpu.VMEM((rows, width), BF),
@@ -360,33 +407,219 @@
             pltpu.VMEM((steps, rows, chunk), F32),
             pltpu.VMEM((rows, width), BF),
             pltpu.VMEM((width, rows), BF),
+            pltpu.VMEM((width, rows), F32),
+            pltpu.SemaphoreType.DMA((count,)),
+            pltpu.SemaphoreType.DMA((count,)),
         ],
         compiler_params=pltpu.CompilerParams(vmem_limit_bytes=LIMIT),
         cost_estimate=pl.CostEstimate(
             flops=12 * rows * width * inner, bytes_accessed=36 << 20, transcendentals=rows * inner
         ),
         name="feed",
-    )(vec, x, tan, wo, up, dn, upb, dnb, g1, s1, g2, s2)
-
-
-def gather_weights(shards):
-    rows, cols = shards[0].shape
+    )(offs, order, *ud_pieces, *out_pieces, vec, x, tan, upb, dnb, g1, s1, g2, s2)
+
+
+def project_kernel(pieces, *refs):
+    offs_ref = refs[0]
+    piece_refs = refs[1 : 1 + pieces]
+    ctx_ref, x_ref, table_ref, wb_ref, pb_ref = refs[1 + pieces : 6 + pieces]
+    k_ref, v_ref, rel_ref, qw_ref, qp_ref, w_ref, sems = refs[6 + pieces :]
+    for copy in load_pieces(piece_refs, offs_ref, w_ref, sems):
+        copy.wait()
+    block = 256
+
+    def loop(count, step):
+        def run(i, carry):
+            step(pl.ds(pl.multiple_of(i * block, block), block))
+            return carry
+
+        lax.fori_loop(0, count // block, run, 0)
+
+    def context_step(at):
+        k_ref[at, :] = nn(ctx_ref[at, :], w_ref[0]).astype(BF)
+        v_ref[at, :] = nn(ctx_ref[at, :], w_ref[1]).astype(BF)
+
+    def stream_step(at):
+        proj = nn(x_ref[at, :], w_ref[2])
+        qw_ref[at, :] = (0.125 * (proj + wb_ref[...]).astype(BF).astype(F32)).astype(BF)
+        qp_ref[at, :] = (0.125 * (proj + pb_ref[...]).astype(BF).astype(F32)).astype(BF)
+
+    def table_step(at):
+        rel_ref[at, :] = nn(table_ref[at, :], w_ref[3]).astype(BF)
+
+    loop(table_ref.shape[0], table_step)
+    loop(x_ref.shape[0], stream_step)
+    loop(ctx_ref.shape[0], context_step)
+
+
+def project(offs, pieces, context, stream, table, wb, pb):
+    rows, width = stream.shape
+    klen, span = context.shape[0], table.shape[0]
+    vmem = pl.BlockSpec(memory_space=pltpu.VMEM)
+    return pl.pallas_call(
+        functools.partial(project_kernel, len(pieces)),
+        in_specs=[SMEM_SPEC] + [ANY_SPEC] * len(pieces) + [vmem] * 5,
+        out_specs=[vmem] * 6,
+        out_shape=[
+            jax.ShapeDtypeStruct((klen, width), BF),
+            jax.ShapeDtypeStruct((klen, width), BF),
+            jax.ShapeDtypeStruct((span, width), BF),
+            jax.ShapeDtypeStruct((rows, width), BF),
+            jax.ShapeDtypeStruct((rows, width), BF),
+            jax.ShapeDtypeStruct((4, width, width), BF),
+        ],
+        scratch_shapes=[pltpu.SemaphoreType.DMA((len(pieces),))],
+        compiler_params=pltpu.CompilerParams(vmem_limit_bytes=LIMIT),
+        cost_estimate=pl.CostEstimate(
+            flops=2 * (2 * klen + rows + span) * width * width,
+            bytes_accessed=20 << 20,
+            transcendentals=0,
+        ),
+        name="project",
+    )(offs, *pieces, context, stream, table, wb, pb)
+
+
+def weight_grads_kernel(xt_ref, ct_ref, tt_ref, dp_ref, dk_ref, dv_ref, dr_ref, ge_ref, go_ref):
+    half = ge_ref.shape[1]
+    for side, dst in ((0, ge_ref), (half, go_ref)):
+        rows = slice(side, side + half)
+        dst[0] = nt(ct_ref[rows, :], dk_ref[...]).astype(BF)
+        dst[1] = nt(ct_ref[rows, :], dv_ref[...]).astype(BF)
+        dst[2] = nn(xt_ref[rows, :], dp_ref[...]).astype(BF)
+        dst[3] = nt(tt_ref[rows, :], dr_ref[...]).astype(BF)
+
+
+def weight_grads(x_t, ctx_t, table_t, d_proj, dk_t, dv_t, drel_t):
+    width, rows = x_t.shape
+    klen, span = ctx_t.shape[1], table_t.shape[1]
+    half, chunk = width // 2, 256
+    whole = lambda a, b: pl.BlockSpec((a, b), lambda i: (0, 0))
+    out = pl.BlockSpec((4, half, chunk), lambda i: (0, 0, i))
+    rowb = lambda b: pl.BlockSpec((chunk, b), lambda i: (i, 0))
+    return pl.pallas_call(
+        weight_grads_kernel,
+        grid=(width // chunk,),
+        in_specs=[
+            whole(width, rows),
+            whole(width, klen),
+            whole(width, span),
+            pl.BlockSpec((rows, chunk), lambda i: (0, i)),
+            rowb(klen),
+            rowb(klen),
+            rowb(span),
+        ],
+        out_specs=[out, out],
+        out_shape=[jax.ShapeDtypeStruct((4, half, width), BF)] * 2,
+        compiler_params=pltpu.CompilerParams(vmem_limit_bytes=LIMIT),
+        cost_estimate=pl.CostEstimate(
+            flops=2 * (rows + 2 * klen + span) * width * width,
+            bytes_accessed=20 << 20,
+            transcendentals=0,
+        ),
+        name="weight_grads",
+    )(x_t, ctx_t, table_t, d_proj, dk_t, dv_t, drel_t)
+
+
+CORE, XBIT, YBIT = 1, 2, 4
+ORDER = (0, 2, 4, 6, 1, 3, 5, 7)
+
+
+def flip(arr, bit):
+    return lax.ppermute(arr, "dp", [(i, i ^ bit) for i in range(lax.axis_size("dp"))])
+
+
+def flip_z(arr, bit):
+    return lax.ppermute(arr, "tensor", [(i, i ^ bit) for i in range(lax.axis_size("tensor"))])
+
+
+def by_bits(parts, bits):
+    step = 1
+    for bit in bits:
+        parts = [
+            jnp.where(bit == 1, parts[i ^ step], parts[i]) for i in range(len(parts))
+        ]
+        step *= 2
+    return parts
+
+
+def gather_columns(shard):
+    tensors, lane = lax.axis_size("tensor"), lax.axis_index("tensor")
+    assert tensors == 4
+    parts = [shard] + [flip_z(shard, bit) for bit in (1, 2, 3)]
+    return jnp.concatenate(by_bits(parts, (lane & 1, lane >> 1)), axis=2)
+
+
+def gather_pieces(shard):
+    rows = shard.shape[1]
+    if lax.axis_size("dp") != 8:
+        return [lax.all_gather(shard, "dp", axis=1, tiled=True)]
+    one, two = shard[:, : rows // 2], shard[:, rows // 2 :]
+    pieces = []
+    for part, first, second in ((one, XBIT, YBIT), (two, YBIT, XBIT)):
+        near = flip(part, first)
+        mine = [part, near, flip(part, second), flip(near, second)]
+        pieces += mine + [flip(p, CORE) for p in mine]
+    return pieces
+
+
+def piece_offsets(rows):
+    if lax.axis_size("dp") != 8:
+        return jnp.zeros((1,), jnp.int32)
+    here = lax.axis_index("dp")
+    offs = []
+    for start, first, second in ((0, XBIT, YBIT), (rows // 2, YBIT, XBIT)):
+        for core in (0, CORE):
+            for bits in (0, first, second, first | second):
+                offs.append((here ^ (bits | core)) * rows + start)
+    return jnp.stack(offs)
+
+
+def row_order():
+    if lax.axis_size("dp") != 8:
+        return jnp.zeros((1,), jnp.int32)
+    return lax.axis_index("dp") ^ jnp.asarray(ORDER, jnp.int32)
+
+
+def reorder_blocks(array, order):
+    turned = jnp.transpose(array)
+    if order.shape[0] == 1:
+        return turned
+    blocks = turned.reshape(order.shape[0], -1, turned.shape[1])
+    return jnp.take(blocks, order, axis=0).reshape(turned.shape)
+
+
+def scatter_sum(even, odd):
+    count, half, cols = even.shape
     groups, tensors = lax.axis_size("dp"), lax.axis_size("tensor")
-    stack = jnp.stack(shards)
-    both = lax.all_gather(stack, ("dp", "tensor"), axis=0, tiled=False)
-    both = both.reshape(groups, tensors, len(shards), rows, cols)
-    both = both.transpose(2, 0, 3, 1, 4).reshape(len(shards), groups * rows, tensors * cols)
-    return [both[i] for i in range(len(shards))]
-
-
-def scatter_grads(grads):
-    groups, tensors = lax.axis_size("dp"), lax.axis_size("tensor")
-    rows, cols = grads[0].shape[0] // groups, grads[0].shape[1] // tensors
-    stack = jnp.stack(grads).reshape(len(grads), groups, rows, tensors, cols)
-    stack = stack.transpose(1, 3, 0, 2, 4).reshape(groups * tensors, len(grads), rows, cols)
-    mine = lax.psum_scatter(stack, ("dp", "tensor"), scatter_dimension=0, tiled=True)
-    mine = mine.reshape(len(grads), rows, cols).astype(F32)
-    return [mine[i] for i in range(len(grads))]
+    rows = 2 * half // groups
+    if groups != 8:
+        full = jnp.concatenate([even, odd], axis=1)
+        mine = lax.psum_scatter(full, "dp", scatter_dimension=1, tiled=True)
+    else:
+        add = lambda a, b: (a.astype(F32) + b.astype(F32)).astype(BF)
+        got = flip(odd, CORE).reshape(count, 4, rows, cols)
+        own = even.reshape(count, 4, rows, cols)
+        parts = []
+        for at, first, second in ((slice(0, rows // 2), 1, 2), (slice(rows // 2, rows), 2, 1)):
+            block = lambda i: add(own[:, i, at], got[:, i, at])
+            send = jnp.stack([block(first), block(3)])
+            near = flip(send, 2 * first)
+            keep, last = add(block(0), near[0]), add(block(second), near[1])
+            parts.append(add(keep, flip(last, 2 * second)))
+        mine = jnp.concatenate(parts, axis=1)
+    mine = mine.reshape(count, rows, tensors, cols // tensors).transpose(2, 0, 1, 3)
+    mine = lax.all_to_all(mine, "tensor", split_axis=0, concat_axis=0, tiled=True)
+    return jnp.sum(mine.astype(F32), axis=0)
+
+
+def sum_all(value):
+    if lax.axis_size("dp") != 8:
+        return lax.psum(value, ("dp", "tensor"))
+    for bit in (1, 2, 4):
+        value = value + flip(value, bit)
+    for bit in (1, 2):
+        value = value + flip_z(value, bit)
+    return value
 
 
 def body(
@@ -426,10 +659,9 @@
     lead = core == 0
     block = 256
     assert 2 * micro == tensors
-    pairs = [(i, i ^ 1) for i in range(groups)]
 
     def swap(arr):
-        return lax.ppermute(arr, "dp", pairs)
+        return flip(arr, CORE)
 
     def to_unit(first, second):
         got = swap(jnp.where(lead, second, first))
@@ -449,11 +681,16 @@
     seq_id = (here // 2) * tensors + lane
     ids = jnp.arange(count, dtype=jnp.int32)
     slot_of = jnp.sum(jnp.where(slot_sequence[None, :] == ids[:, None], ids[None, :], 0), axis=1)
-    lengths = lax.all_gather(
-        jnp.concatenate([seq_lengths, memory_lengths]), "dp", axis=0, tiled=False
-    )
-    length = lengths[:, :micro].reshape(count)[seq_id]
-    mem_valid = lengths[:, micro:].reshape(count)[slot_of[seq_id]]
+    counts = jnp.concatenate([seq_lengths, memory_lengths])
+    if groups == 8:
+        lengths = jnp.stack([counts] + [flip(counts, bit) for bit in range(1, groups)])
+        turn = here
+    else:
+        lengths = lax.all_gather(counts, "dp", axis=0, tiled=False)
+        turn = 0
+    slot = slot_of[seq_id]
+    length = lengths[turn ^ (seq_id // micro), seq_id % micro]
+    mem_valid = lengths[turn ^ (slot // micro), micro + slot % micro]
     other = swap(factor_order)
     orders = jnp.concatenate(
         [jnp.where(lead, factor_order, other), jnp.where(lead, other, factor_order)], 0
@@ -490,30 +727,33 @@
 
     tangent = to_unit(content_tangent, query_tangent)
 
-    key_mat, value_mat, query_mat, pos_mat, out_mat = gather_weights(
-        [key_weight, value_weight, query_weight, pos_weight, out_weight]
-    )
-    up_mat, down_mat = gather_weights([up_weight, down_weight])
+    rows = key_weight.shape[0]
+    offs, order = piece_offsets(rows), row_order()
+    pieces = gather_pieces(
+        gather_columns(jnp.stack([key_weight, value_weight, query_weight, pos_weight]))
+    )
+    out_pieces = gather_pieces(gather_columns(out_weight[None]))
+    ud_pieces = gather_pieces(gather_columns(jnp.stack([up_weight, down_weight])))
 
     context = jnp.concatenate([mem_rows, content], 0)
     table = reversed_table(span, klen, width)
-    keys = nn(context, key_mat).astype(BF)
-    values = nn(context, value_mat).astype(BF)
-    rel = nn(table, pos_mat).astype(BF)
-    proj = nn(stream, query_mat)
-    scale = jnp.asarray(0.125, BF)
-    q_word = (proj + word_bias.reshape(1, width)).astype(BF) * scale
-    q_pos = (proj + pos_bias.reshape(1, width)).astype(BF) * scale
+    row = lambda v: v.reshape(1, -1)
+    keys, values, rel, q_word, q_pos, mats = project(
+        offs, pieces, context, stream, table, row(word_bias), row(pos_bias)
+    )
+    stream_t = reorder_blocks(stream, order)
+    context_t = reorder_blocks(context, order)
+    table_t = reorder_blocks(table, order)
 
     vec, prob = attend_forward(q_word, q_pos, keys, values, rel, thr, key_rank, block)
-    row = lambda v: v.reshape(1, -1)
-    out, d_mixed, g_vec, g_out, g_up, g_down, g_upb, small = feed(
+    out, d_mixed, g_vec, g_out_e, g_out_o, g_ud_e, g_ud_o, g_upb, small = feed(
+        offs,
+        order,
+        ud_pieces,
+        out_pieces,
         vec,
         stream,
         tangent,
-        out_mat,
-        up_mat,
-        down_mat,
         row(up_bias),
         row(down_bias),
         row(first_gain),
@@ -522,28 +762,21 @@
         row(second_shift),
     )
     content_out, query_out = from_unit(out)
-    grad_up, grad_down = scatter_grads([g_up, g_down])
-    early = lax.psum(
-        jnp.concatenate([g_upb.reshape(-1), small[:5].reshape(-1)]), ("dp", "tensor")
-    )
+    grad_up, grad_down = scatter_sum(g_ud_e, g_ud_o)
+    (grad_out,) = scatter_sum(g_out_e[None], g_out_o[None])
+    early = sum_all(jnp.concatenate([g_upb.reshape(-1), small[:5].reshape(-1)]))
 
     d_proj, dk_t, dv_t, drel_t, biases = attend_backward(
         prob, g_vec, q_word, q_pos, keys, values, rel, block
     )
-    late = lax.psum(biases, ("dp", "tensor"))
-    d_context = tt(dk_t[:, mem_total:], key_mat) + tt(dv_t[:, mem_total:], value_mat)
+    late = sum_all(biases)
+    d_context = tt(dk_t[:, mem_total:], mats[0]) + tt(dv_t[:, mem_total:], mats[1])
     partner = swap(d_context.astype(BF))
-    d_stream = d_mixed + nt(d_proj, query_mat)
+    d_stream = d_mixed + nt(d_proj, mats[2])
     d_stream = d_stream + jnp.where(lead, d_context + partner.astype(F32), 0.0)
     content_grad, query_grad = from_unit(d_stream.astype(BF))
-    grad_query, grad_key, grad_value, grad_pos, grad_out = scatter_grads(
-        [
-            tn(stream, d_proj).astype(BF),
-            tt(context, dk_t).astype(BF),
-            tt(context, dv_t).astype(BF),
-            tt(table, drel_t).astype(BF),
-            g_out,
-        ]
+    grad_key, grad_value, grad_query, grad_pos = scatter_sum(
+        *weight_grads(stream_t, context_t, table_t, d_proj, dk_t, dv_t, drel_t)
     )
     inner = up_bias.shape[0]
     rest = early[inner:].reshape(5, width)

time: 633 us -> 504 us (0.80)
  local copies, waits for them, and re-layouts: 149 us -> 40.4 us
  waiting for transfers between devices: 218 us -> 116 us
  starting transfers between devices: 31.2 us -> 131 us
  blocking collectives: 56.1 us -> 0 us
  other arithmetic: 33.2 us -> 73.5 us
  Pallas kernels: 91.3 us -> 121 us
  matrix products: 30.5 us -> 8.77 us
  between operations: 18 us -> 5.21 us
    reduce_scatter x2 -> x0, waiting for transfers between devices: 132 us -> none  [scatter_grads(): lax.psum_scatter(stack, ('dp', 'tensor'), scatter_dimension=0, tiled=True)]
    ppermute x8 -> x91, waiting for transfers between devices: 0.5 us -> 95.4 us  [the longest x78 75.3 us: flip(): lax.ppermute(arr, 'dp', [(i, i ^ bit) for i in range(lax.axis_size('dp'))])]
    ppermute x8 -> x91, starting transfers between devices: 2.35 us -> 83.7 us  [the longest x78 54.2 us: flip(): lax.ppermute(arr, 'dp', [(i, i ^ bit) for i in range(lax.axis_size('dp'))])]
    psum x1 -> x0, blocking collectives: 47.8 us -> none  [body(): lax.psum(jnp.concatenate([g_upb.reshape(-1), small[:5].reshape(-1)]), ('d...]
    another operation x9 -> x4, local copies, waits for them, and re-layouts: 38.7 us -> 3.01 us  [the longest x1 0.85 us: body(): grad_up, grad_down = scatter_sum(g_ud_e, g_ud_o)]
    all_to_all x2, waiting for transfers between devices: 35.7 us -> 0.01 us  [from_unit(): lax.all_to_all(both, 'tensor', split_axis=0, concat_axis=0, tiled=True)]
    pallas_call x1 -> x3, Pallas kernels: 31.5 us -> 61.4 us  [the longest x1 36.1 us: feed(): pl.pallas_call(functools.partial(feed_kernel, steps, count), grid=(2 * st...]
    reshape x5 -> x4, local copies, waits for them, and re-layouts: 26.4 us -> 3.34 us  [the longest x3 2.6 us: scatter_sum(): mine.reshape(count, rows, tensors, cols // tensors).transpose(2, 0, 1, 3)]
  transfers between devices with their start and end apart: 19 -> 101, of which waited for: 7 -> 28; matrix products, arithmetic and copies ran while one was open for 26% -> 23% of each run, Pallas kernels for 4% -> 17%
where the time goes in v2:
time: 504 us; the launch traced here: 495 us
  starting transfers between devices  131 us (26%)
  Pallas kernels  121 us (24%)
  waiting for transfers between devices  116 us (23%)
  other arithmetic  73.5 us (15%)
  local copies, waits for them, and re-layouts  40.4 us (8%)
  matrix products  8.77 us (2%)
  between operations  5.21 us (1%)
    ppermute x78, waiting for transfers between devices, flip(): lax.ppermute(arr, 'dp', [(i, i ^ bit) for i in range(lax.axis_size('dp'))])  75.3 us
    ppermute x78, starting transfers between devices, flip(): lax.ppermute(arr, 'dp', [(i, i ^ bit) for i in range(lax.axis_size('dp'))])  54.2 us
    pallas_call x1, Pallas kernels, feed(): pl.pallas_call(functools.partial(feed_kernel, steps, count), grid=(2 * st...  36.1 us
    pallas_call x1, Pallas kernels, attend_backward(): pl.pallas_call(functools.partial(attend_backward_kernel, block), grid=(wi...  33.1 us
    ppermute x13, starting transfers between devices, flip_z(): lax.ppermute(arr, 'tensor', [(i, i ^ bit) for i in range(lax.axis_size('t...  29.5 us
    pallas_call x1, Pallas kernels, attend_forward(): pl.pallas_call(functools.partial(attend_forward_kernel, block), grid=(wid...  26.4 us
    all_to_all x3, waiting for transfers between devices, scatter_sum(): lax.all_to_all(mine, 'tensor', split_axis=0, concat_axis=0, tiled=True)  20.2 us
    ppermute x13, waiting for transfers between devices, flip_z(): lax.ppermute(arr, 'tensor', [(i, i ^ bit) for i in range(lax.axis_size('t...  20.1 us
  transfers between devices with their start and end apart: 101, of which 28 were waited for; matrix products, arithmetic and copies ran while one was open for 23% of the time, Pallas kernels for 17%

profile of v2, /device:TPU:0, one launch (start us, length us, event | category | flops | bytes accessed | tf_op | source)
XLA Modules:
  0.0 495.0 jit_solution(14047340147674491995)
XLA Ops:
  5.0 3.6 collective-permute-start.17
  11.2 3.5 all-to-all-start
  17.7 9.1 %fusion = (bf16[1536,384]{1,0:T(8,128)(2,1)S(1)}, bf16[1536,384]{1,0:T(8,128)(2,1)S(1)}) fusion(f32[384]{0:T(512)S(1)} %negate_power_fusion, f32[1536]{0:T(1024)S(1)} %iota_subtract_fusion), kind=kLoop, calls=%fused_computation.6 | loop fusion | flops 1769472 | bytes 2366976 | tf_op jit(solution)/shard_map/convert.24
  55.0 3.6 collective-permute-start.34
  66.7 7.1 %collective-permute-start.2 = (bf16[2,96,768]{2,1,0:T(8,128)(2,1)}, bf16[2,96,768]{2,1,0:T(8,128)(2,1)}, u32[]{:S(2)}, u32[]{:S(2)}) collective-permute-start(bf16[2,96,768]{2,1,0:T(8,128)(2,1)} %pad_maximum_fusion.12), channel_id=1, source_target_pairs={{0,1},{1,0},{2,3},{3,2},{4,5},{5,4},{6,7},{7,6},{8,9},{9,8},{10,11... | collective-permute-start | bytes 884744 | tf_op jit(solution)/shard_map/ppermute | solution.py:532
  73.8 15.0 %collective-permute-done.35 = bf16[4,96,192]{2,1,0:T(8,128)(2,1)S(1)} collective-permute-done((bf16[4,96,192]{2,1,0:T(8,128)(2,1)}, bf16[4,96,192]{2,1,0:T(8,128)(2,1)S(1)}, u32[]{:S(2)}, u32[]{:S(2)}) %collective-permute-start.35) | collective-permute-done | bytes 147488 | tf_op jit(solution)/shard_map/ppermute | solution.py:532
  95.8 3.5 all-to-all-start.1
  103.5 4.7 collective-permute-done.21.refs_20_
  114.0 4.2 all-to-all-start.2
  131.6 5.0 %all-to-all-start.3 = ((bf16[4,128,768]{2,1,0:T(8,128)(2,1)}), bf16[4,128,768]{2,1,0:T(8,128)(2,1)S(1)}, u32[]{:S(2)}, u32[]{:S(2)}) async-start(bf16[4,128,768]{2,1,0:T(8,128)(2,1)} %pad_maximum_fusion.6), calls=%async_computation.3 | async-start | bytes 1572864 | tf_op jit(solution)/shard_map/all_to_all | solution.py:671
  145.5 3.7 collective-permute-done.39.refs_4_
  155.1 6.8 %collective-permute-done.10.refs_11_ = bf16[2,48,3072]{2,1,0:T(8,128)(2,1)} collective-permute-done((bf16[2,48,3072]{2,1,0:T(8,128)(2,1)}, bf16[2,48,3072]{2,1,0:T(8,128)(2,1)}, u32[]{:S(2)}, u32[]{:S(2)}) %collective-permute-start.10) | collective-permute-done | bytes 589856 | tf_op jit(solution)/shard_map/ppermute | solution.py:528
  165.3 5.3 %all-to-all-start.4 = ((bf16[4,128,768]{2,1,0:T(8,128)(2,1)}), bf16[4,128,768]{2,1,0:T(8,128)(2,1)}, u32[]{:S(2)}, u32[]{:S(2)}) async-start(bf16[4,128,768]{2,1,0:T(8,128)(2,1)} %pad_maximum_fusion.7), calls=%async_computation.4 | async-start | bytes 1572864 | tf_op jit(solution)/shard_map/all_to_all | solution.py:671
  180.7 6.5 %collective-permute-done.12.refs_13_ = bf16[2,48,3072]{2,1,0:T(8,128)(2,1)} collective-permute-done((bf16[2,48,3072]{2,1,0:T(8,128)(2,1)}, bf16[2,48,3072]{2,1,0:T(8,128)(2,1)}, u32[]{:S(2)}, u32[]{:S(2)}) %collective-permute-start.12) | collective-permute-done | bytes 589856 | tf_op jit(solution)/shard_map/ppermute | solution.py:528
  187.2 3.5 collective-permute-done.5.refs_5_
  191.3 15.5 %project.1 = (bf16[1024,768]{1,0:T(8,128)(2,1)}, bf16[1024,768]{1,0:T(8,128)(2,1)}, bf16[1536,768]{1,0:T(8,128)(2,1)}, bf16[512,768]{1,0:T(8,128)(2,1)}, bf16[51...) custom-call(s32[16]{0:T(128)} %stack.157.refs_0_, bf16[4,48,768]{2,1,0:T(8,128)(2,1)} %get-tuple-element.119.refs_1_, ...), custom_call_target="tpu_custom_call" | custom-call | flops 4831838208 | bytes 20971520 | tf_op jit(solution)/shard_map/project/pallas_call | solution.py:459
  206.8 26.4 %attend_forward.1 = (bf16[512,768]{1,0:T(8,128)(2,1)}, bf16[12,512,1024]{2,1,0:T(8,128)(2,1)}) custom-call(bf16[512,768]{1,0:T(8,128)(2,1)} %get-tuple-element.43.qw_ref, bf16[512,768]{1,0:T(8,128)(2,1)} %get-tuple-element.44.qp_ref, bf16[1024,768]{1,0:T(8,128)(2,1)} %get-tuple-element.45.k_ref, bf16[1024,768]{1,0:T(8,128)(2,1)} %get-tuple-element.46.v_ref, ...), custom_call_target="tpu_custom_call" | custom-call | flops 3221225472 | bytes 16777216 | tf_op jit(solution)/shard_map/attend_forward/pallas_call | solution.py:78
  234.2 36.1 %feed.1 = (bf16[512,768]{1,0:T(8,128)(2,1)}, f32[512,768]{1,0:T(8,128)}, bf16[512,768]{1,0:T(8,128)(2,1)}, bf16[384,768]{1,0:T(8,128)(2,1)}, bf16[384,768]{1,0:T...) custom-call(s32[16]{0:T(128)} %stack.157.refs_0_, ...), custom_call_target="tpu_custom_call" | custom-call | flops 14495514624 | bytes 37748736 | tf_op jit(solution)/shard_map/feed/pallas_call | solution.py:368
  277.5 33.1 %attend_backward.1 = (bf16[512,768]{1,0:T(8,128)(2,1)}, bf16[768,1024]{1,0:T(8,128)(2,1)}, bf16[768,1024]{1,0:T(8,128)(2,1)}, bf16[768,1536]{1,0:T(8,128)(2,1)}, f32[2,768]{1,0:T(2,128)}) custom-call(bf16[12,512,1024]{2,1,0:T(8,128)(2,1)} %get-tuple-element.51.prob_ref, bf16[512,768]{1,0:T(8,128)(2,1)} %get-tuple-element.52.gvec_ref, ...), custom_call_target="tpu_custom_call" | custom-call | flops 6442450944 | bytes 20971520 | tf_op jit(solution)/shard_map/attend_backward/pallas_call | solution.py:175
  310.7 9.9 %weight_grads.1 = (bf16[4,384,768]{2,1,0:T(8,128)(2,1)}, bf16[4,384,768]{2,1,0:T(8,128)(2,1)}) custom-call(bf16[768,512]{1,0:T(8,128)(2,1)} %bitcast_select_fusion.2.xt_ref, bf16[768,1024]{1,0:T(8,128)(2,1)} %bitcast_select_fusion.1.ct_ref, bf16[768,1536]{1,0:T(8,128)(2,1)} %bitcast_select_fusion.tt_ref, bf16[512,768]{1,0:T(8,128)(2,1)} %get-tuple-element.53.dp_ref, ...), custom_call_target="tpu_custom_call" | custom-call | flops 4831838208 | bytes 20971520 | tf_op jit(solution)/shard_map/weight_grads/pallas_call | solution.py:499
  321.6 4.7 collective-permute-done.71
  340.7 5.0 %all-to-all-start.8 = ((bf16[4,1,96,192]{3,2,1,0:T(8,128)(2,1)}), bf16[4,1,96,192]{3,2,1,0:T(8,128)(2,1)S(1)}, u32[]{:S(2)}, u32[]{:S(2)}) async-start(bf16[4,1,96,192]{3,2,1,0:T(8,128)(2,1)} %copy.246), calls=%async_computation.8 | async-start | bytes 393216 | tf_op jit(solution)/shard_map/all_to_all | solution.py:611
  358.1 5.3 %all-to-all-start.5 = ((bf16[4,128,768]{2,1,0:T(8,128)(2,1)}), bf16[4,128,768]{2,1,0:T(8,128)(2,1)S(1)}, u32[]{:S(2)}, u32[]{:S(2)}) async-start(bf16[4,128,768]{2,1,0:T(8,128)(2,1)} %bitcast.383), calls=%async_computation.5 | async-start | bytes 1572864 | tf_op jit(solution)/shard_map/all_to_all | solution.py:676
  366.8 3.6 fusion.9
  377.6 19.4 %collective-permute-done.67 = bf16[2,4,48,768]{3,2,1,0:T(8,128)(2,1)} collective-permute-done((bf16[2,4,48,768]{3,2,1,0:T(8,128)(2,1)}, bf16[2,4,48,768]{3,2,1,0:T(8,128)(2,1)}, u32[]{:S(2)}, u32[]{:S(2)}) %collective-permute-start.67) | collective-permute-done | bytes 589856 | tf_op jit(solution)/shard_map/ppermute | solution.py:528
  399.9 4.8 all-to-all-start.6
  406.2 3.4 fusion.4
  413.8 10.9 %collective-permute-done.82 = f32[6912]{0:T(1024)S(1)} collective-permute-done((f32[6912]{0:T(1024)S(1)}, f32[6912]{0:T(1024)S(1)}, u32[]{:S(2)}, u32[]{:S(2)}) %collective-permute-start.82) | collective-permute-done | bytes 27680 | tf_op jit(solution)/shard_map/ppermute | solution.py:528
  448.4 3.6 all-to-all-start.7
  459.2 10.5 %all-to-all-done.7 = bf16[4,4,96,192]{3,2,1,0:T(8,128)(2,1)S(1)} async-done(((bf16[4,4,96,192]{3,2,1,0:T(8,128)(2,1)}), bf16[4,4,96,192]{3,2,1,0:T(8,128)(2,1)S(1)}, u32[]{:S(2)}, u32[]{:S(2)}) %all-to-all-start.7) | async-done | bytes 589856 | tf_op jit(solution)/shard_map/all_to_all | solution.py:611
  469.7 6.8 %all-to-all-start.9 = ((bf16[4,2,96,768]{3,2,1,0:T(8,128)(2,1)}), bf16[4,2,96,768]{3,2,1,0:T(8,128)(2,1)S(1)}, u32[]{:S(2)}, u32[]{:S(2)}) async-start(bf16[4,2,96,768]{3,2,1,0:T(8,128)(2,1)} %copy.263), calls=%async_computation.9 | async-start | bytes 2359296 | tf_op jit(solution)/shard_map/all_to_all | solution.py:611
  484.0 9.7 %all-to-all-done.9 = bf16[4,2,96,768]{3,2,1,0:T(8,128)(2,1)S(1)} async-done(((bf16[4,2,96,768]{3,2,1,0:T(8,128)(2,1)}), bf16[4,2,96,768]{3,2,1,0:T(8,128)(2,1)S(1)}, u32[]{:S(2)}, u32[]{:S(2)}) %all-to-all-start.9) | async-done | bytes 1179680 | tf_op jit(solution)/shard_map/all_to_all | solution.py:611
  (420 shorter events, 196.0 us)
Async XLA Ops:
  2.0 43.2 %collective-permute-start.55 = (s32[4]{0:T(128)}, s32[4]{0:T(128)}, u32[]{:S(2)}, u32[]{:S(2)}) collective-permute-start(s32[4]{0:T(128)} %pad_add_fusion.1), channel_id=1, source_target_pairs={{0,4},{4,0},{8,12},{12,8},{16,20},{20,16},{24,28},{28,24},{1,5},{5... | collective-permute-start | bytes 56 | tf_op jit(solution)/shard_map/ppermute | solution.py:528
  2.5 44.3 %collective-permute-start.56 = (s32[4]{0:T(128)}, s32[4]{0:T(128)}, u32[]{:S(2)}, u32[]{:S(2)}) collective-permute-start(s32[4]{0:T(128)} %pad_add_fusion.1), channel_id=1, source_target_pairs={{0,8},{4,12},{8,0},{12,4},{16,24},{20,28},{24,16},{28,20},{1,9},{5... | collective-permute-start | bytes 56 | tf_op jit(solution)/shard_map/ppermute | solution.py:528
  5.0 55.5 %collective-permute-start.17 = (bf16[1,96,192]{2,1,0:T(8,128)(2,1)}, bf16[1,96,192]{2,1,0:T(8,128)(2,1)}, u32[]{:S(2)}, u32[]{:S(2)}) collective-permute-start(bf16[1,96,192]{2,1,0:T(8,128)(2,1)} %bitcast.408), channel_id=1, source_target_pairs={{0,3},{1,2},{2,1},{3,0},{4,7},{5,6},{6,5},{7,4},{8,11},{9,10},{10,... | collective-permute-start | bytes 110600 | tf_op jit(solution)/shard_map/ppermute | solution.py:532
  8.6 53.6 %collective-permute-start.18 = (bf16[1,96,192]{2,1,0:T(8,128)(2,1)}, bf16[1,96,192]{2,1,0:T(8,128)(2,1)}, u32[]{:S(2)}, u32[]{:S(2)}) collective-permute-start(bf16[1,96,192]{2,1,0:T(8,128)(2,1)} %bitcast.409), channel_id=1, source_target_pairs={{0,2},{1,3},{2,0},{3,1},{4,6},{5,7},{6,4},{7,5},{8,10},{9,11},{10,... | collective-permute-start | bytes 110600 | tf_op jit(solution)/shard_map/ppermute | solution.py:532
  8.6 56.4 %collective-permute-start.19 = (bf16[1,96,192]{2,1,0:T(8,128)(2,1)}, bf16[1,96,192]{2,1,0:T(8,128)(2,1)}, u32[]{:S(2)}, u32[]{:S(2)}) collective-permute-start(bf16[1,96,192]{2,1,0:T(8,128)(2,1)} %bitcast.410), channel_id=1, source_target_pairs={{0,1},{1,0},{2,3},{3,2},{4,5},{5,4},{6,7},{7,6},{8,9},{9,8},{10,11... | collective-permute-start | bytes 110600 | tf_op jit(solution)/shard_map/ppermute | solution.py:532
  11.2 80.7 %all-to-all-start = ((bf16[2,8,16,768]{3,2,0,1:T(8,128)(2,1)}), bf16[2,8,16,768]{3,2,0,1:T(8,128)(2,1)S(1)}, u32[]{:S(2)}, u32[]{:S(2)}) async-start(bf16[2,8,16,768]{3,2,0,1:T(8,128)(2,1)} %copy.221), calls=%async_computation | async-start | bytes 786432 | tf_op jit(solution)/shard_map/all_to_all | solution.py:710
  58.6 30.2 %collective-permute-start.35 = (bf16[4,96,192]{2,1,0:T(8,128)(2,1)}, bf16[4,96,192]{2,1,0:T(8,128)(2,1)S(1)}, u32[]{:S(2)}, u32[]{:S(2)}) collective-permute-start(bf16[4,96,192]{2,1,0:T(8,128)(2,1)} %pad_maximum_fusion.13), channel_id=1, source_target_pairs={{0,2},{1,3},{2,0},{3,1},{4,6},{5,7},{6,4},{7,5},{8,10},{9,11},{10,... | collective-permute-start | bytes 442376 | tf_op jit(solution)/shard_map/ppermute | solution.py:532
  60.5 28.3 %collective-permute-start.36 = (bf16[4,96,192]{2,1,0:T(8,128)(2,1)}, bf16[4,96,192]{2,1,0:T(8,128)(2,1)S(1)}, u32[]{:S(2)}, u32[]{:S(2)}) collective-permute-start(bf16[4,96,192]{2,1,0:T(8,128)(2,1)} %pad_maximum_fusion.13), channel_id=1, source_target_pairs={{0,1},{1,0},{2,3},{3,2},{4,5},{5,4},{6,7},{7,6},{8,9},{9,8},{10,11... | collective-permute-start | bytes 442376 | tf_op jit(solution)/shard_map/ppermute | solution.py:532
  62.2 46.5 %collective-permute-start = (bf16[2,96,768]{2,1,0:T(8,128)(2,1)}, bf16[2,96,768]{2,1,0:T(8,128)(2,1)}, u32[]{:S(2)}, u32[]{:S(2)}) collective-permute-start(bf16[2,96,768]{2,1,0:T(8,128)(2,1)} %pad_maximum_fusion.12), channel_id=1, source_target_pairs={{0,3},{1,2},{2,1},{3,0},{4,7},{5,6},{6,5},{7,4},{8,11},{9,10},{10,... | collective-permute-start | bytes 884744 | tf_op jit(solution)/shard_map/ppermute | solution.py:532
  65.0 43.8 %collective-permute-start.1 = (bf16[2,96,768]{2,1,0:T(8,128)(2,1)}, bf16[2,96,768]{2,1,0:T(8,128)(2,1)}, u32[]{:S(2)}, u32[]{:S(2)}) collective-permute-start(bf16[2,96,768]{2,1,0:T(8,128)(2,1)} %pad_maximum_fusion.12), channel_id=1, source_target_pairs={{0,2},{1,3},{2,0},{3,1},{4,6},{5,7},{6,4},{7,5},{8,10},{9,11},{10,... | collective-permute-start | bytes 884744 | tf_op jit(solution)/shard_map/ppermute | solution.py:532
  66.7 43.6 %collective-permute-start.2 = (bf16[2,96,768]{2,1,0:T(8,128)(2,1)}, bf16[2,96,768]{2,1,0:T(8,128)(2,1)}, u32[]{:S(2)}, u32[]{:S(2)}) collective-permute-start(bf16[2,96,768]{2,1,0:T(8,128)(2,1)} %pad_maximum_fusion.12), channel_id=1, source_target_pairs={{0,1},{1,0},{2,3},{3,2},{4,5},{5,4},{6,7},{7,6},{8,9},{9,8},{10,11... | collective-permute-start | bytes 884744 | tf_op jit(solution)/shard_map/ppermute | solution.py:532
  131.6 31.0 %all-to-all-start.3 = ((bf16[4,128,768]{2,1,0:T(8,128)(2,1)}), bf16[4,128,768]{2,1,0:T(8,128)(2,1)S(1)}, u32[]{:S(2)}, u32[]{:S(2)}) async-start(bf16[4,128,768]{2,1,0:T(8,128)(2,1)} %pad_maximum_fusion.6), calls=%async_computation.3 | async-start | bytes 1572864 | tf_op jit(solution)/shard_map/all_to_all | solution.py:671
  165.3 67.9 %all-to-all-start.4 = ((bf16[4,128,768]{2,1,0:T(8,128)(2,1)}), bf16[4,128,768]{2,1,0:T(8,128)(2,1)}, u32[]{:S(2)}, u32[]{:S(2)}) async-start(bf16[4,128,768]{2,1,0:T(8,128)(2,1)} %pad_maximum_fusion.7), calls=%async_computation.4 | async-start | bytes 1572864 | tf_op jit(solution)/shard_map/all_to_all | solution.py:671
  178.8 54.4 %collective-permute-start.7 = (bf16[2,48,3072]{2,1,0:T(8,128)(2,1)}, bf16[2,48,3072]{2,1,0:T(8,128)(2,1)S(1)}, u32[]{:S(2)}, u32[]{:S(2)}) collective-permute-start(bf16[2,48,3072]{2,1,0:T(8,128)(2,1)} %collective-permute-done.3.refs_3_), channel_id=1, source_target_pairs={{0,4},{4,0},{8,12},{12,8},{16,20},{20,16},{24,28},{28,24},{1,5},{5... | collective-permute-start | bytes 1769480 | tf_op jit(solution)/shard_map/ppermute | solution.py:528
  180.0 53.2 %collective-permute-start.15 = (bf16[2,48,3072]{2,1,0:T(8,128)(2,1)}, bf16[2,48,3072]{2,1,0:T(8,128)(2,1)S(1)}, u32[]{:S(2)}, u32[]{:S(2)}) collective-permute-start(bf16[2,48,3072]{2,1,0:T(8,128)(2,1)} %collective-permute-done.11.refs_12_), channel_id=1, source_target_pairs={{0,4},{4,0},{8,12},{12,8},{16,20},{20,16},{24,28},{28,24},{1,5},{5... | collective-permute-start | bytes 1769480 | tf_op jit(solution)/shard_map/ppermute | solution.py:528
  187.2 46.0 %collective-permute-start.8 = (bf16[2,48,3072]{2,1,0:T(8,128)(2,1)}, bf16[2,48,3072]{2,1,0:T(8,128)(2,1)}, u32[]{:S(2)}, u32[]{:S(2)}) collective-permute-start(bf16[2,48,3072]{2,1,0:T(8,128)(2,1)} %collective-permute-done.4.refs_4_), channel_id=1, source_target_pairs={{0,4},{4,0},{8,12},{12,8},{16,20},{20,16},{24,28},{28,24},{1,5},{5... | collective-permute-start | bytes 1769480 | tf_op jit(solution)/shard_map/ppermute | solution.py:528
  190.7 42.5 %collective-permute-start.16 = (bf16[2,48,3072]{2,1,0:T(8,128)(2,1)}, bf16[2,48,3072]{2,1,0:T(8,128)(2,1)}, u32[]{:S(2)}, u32[]{:S(2)}) collective-permute-start(bf16[2,48,3072]{2,1,0:T(8,128)(2,1)} %collective-permute-done.12.refs_13_), channel_id=1, source_target_pairs={{0,4},{4,0},{8,12},{12,8},{16,20},{20,16},{24,28},{28,24},{1,5},{5... | collective-permute-start | bytes 1769480 | tf_op jit(solution)/shard_map/ppermute | solution.py:528
  190.7 42.5 %collective-permute-start.9 = (bf16[2,48,3072]{2,1,0:T(8,128)(2,1)}, bf16[2,48,3072]{2,1,0:T(8,128)(2,1)}, u32[]{:S(2)}, u32[]{:S(2)}) collective-permute-start(bf16[2,48,3072]{2,1,0:T(8,128)(2,1)} %collective-permute-done.5.refs_5_), channel_id=1, source_target_pairs={{0,4},{4,0},{8,12},{12,8},{16,20},{20,16},{24,28},{28,24},{1,5},{5... | collective-permute-start | bytes 1769480 | tf_op jit(solution)/shard_map/ppermute | solution.py:528
  270.3 79.5 %collective-permute-start.76 = (bf16[2,384,3072]{2,1,0:T(8,128)(2,1)}, bf16[2,384,3072]{2,1,0:T(8,128)(2,1)}, u32[]{:S(2)}, u32[]{:S(2)}) collective-permute-start(bf16[2,384,3072]{2,1,0:T(8,128)(2,1)} %get-tuple-element.63), channel_id=1, source_target_pairs={{0,4},{4,0},{8,12},{12,8},{16,20},{20,16},{24,28},{28,24},{1,5},{5... | collective-permute-start | bytes 14155784 | tf_op jit(solution)/shard_map/ppermute | solution.py:528
  338.1 35.7 %collective-permute-start.64 = (bf16[512,768]{1,0:T(8,128)(2,1)}, bf16[512,768]{1,0:T(8,128)(2,1)}, u32[]{:S(2)}, u32[]{:S(2)}) collective-permute-start(bf16[512,768]{1,0:T(8,128)(2,1)} %get-tuple-element.147), channel_id=1, source_target_pairs={{0,4},{4,0},{8,12},{12,8},{16,20},{20,16},{24,28},{28,24},{1,5},{5... | collective-permute-start | bytes 2359304 | tf_op jit(solution)/shard_map/ppermute | solution.py:528
  354.2 50.5 %collective-permute-start.79 = (bf16[2,2,48,3072]{3,2,1,0:T(8,128)(2,1)}, bf16[2,2,48,3072]{3,2,1,0:T(8,128)(2,1)S(1)}, u32[]{:S(2)}, u32[]{:S(2)}) collective-permute-start(bf16[2,2,48,3072]{3,2,1,0:T(8,128)(2,1)} %pad_maximum_fusion.4), channel_id=1, source_target_pairs={{0,16},{4,20},{8,24},{12,28},{16,0},{20,4},{24,8},{28,12},{1,17},{... | collective-permute-start | bytes 3538952 | tf_op jit(solution)/shard_map/ppermute | solution.py:528
  356.8 49.4 %collective-permute-start.77 = (bf16[2,2,48,3072]{3,2,1,0:T(8,128)(2,1)}, bf16[2,2,48,3072]{3,2,1,0:T(8,128)(2,1)}, u32[]{:S(2)}, u32[]{:S(2)}) collective-permute-start(bf16[2,2,48,3072]{3,2,1,0:T(8,128)(2,1)} %pad_maximum_fusion.3), channel_id=1, source_target_pairs={{0,8},{4,12},{8,0},{12,4},{16,24},{20,28},{24,16},{28,20},{1,9},{5... | collective-permute-start | bytes 3538952 | tf_op jit(solution)/shard_map/ppermute | solution.py:528
  358.1 41.8 %all-to-all-start.5 = ((bf16[4,128,768]{2,1,0:T(8,128)(2,1)}), bf16[4,128,768]{2,1,0:T(8,128)(2,1)S(1)}, u32[]{:S(2)}, u32[]{:S(2)}) async-start(bf16[4,128,768]{2,1,0:T(8,128)(2,1)} %bitcast.383), calls=%async_computation.5 | async-start | bytes 1572864 | tf_op jit(solution)/shard_map/all_to_all | solution.py:676
  365.4 31.7 %collective-permute-start.67 = (bf16[2,4,48,768]{3,2,1,0:T(8,128)(2,1)}, bf16[2,4,48,768]{3,2,1,0:T(8,128)(2,1)}, u32[]{:S(2)}, u32[]{:S(2)}) collective-permute-start(bf16[2,4,48,768]{3,2,1,0:T(8,128)(2,1)} %pad_maximum_fusion.9), channel_id=1, source_target_pairs={{0,8},{4,12},{8,0},{12,4},{16,24},{20,28},{24,16},{28,20},{1,9},{5... | collective-permute-start | bytes 1769480 | tf_op jit(solution)/shard_map/ppermute | solution.py:528
  373.8 36.6 %collective-permute-start.81 = (f32[6912]{0:T(1024)}, f32[6912]{0:T(1024)}, u32[]{:S(2)}, u32[]{:S(2)}) collective-permute-start(f32[6912]{0:T(1024)} %pad_maximum_fusion.18), channel_id=1, source_target_pairs={{0,4},{4,0},{8,12},{12,8},{16,20},{20,16},{24,28},{28,24},{1,5},{5... | collective-permute-start | bytes 82952 | tf_op jit(solution)/shard_map/ppermute | solution.py:528
  377.2 35.4 %collective-permute-start.88 = (f32[2,768]{1,0:T(2,128)}, f32[2,768]{1,0:T(2,128)S(1)}, u32[]{:S(2)}, u32[]{:S(2)}) collective-permute-start(f32[2,768]{1,0:T(2,128)} %add.501), channel_id=1, source_target_pairs={{0,16},{4,20},{8,24},{12,28},{16,0},{20,4},{24,8},{28,12},{1,17},{... | collective-permute-start | bytes 18440 | tf_op jit(solution)/shard_map/ppermute | solution.py:528
  399.4 44.8 %collective-permute-start.68 = (bf16[4,48,768]{2,1,0:T(8,128)(2,1)}, bf16[4,48,768]{2,1,0:T(8,128)(2,1)S(1)}, u32[]{:S(2)}, u32[]{:S(2)}) collective-permute-start(bf16[4,48,768]{2,1,0:T(8,128)(2,1)} %get-tuple-element.83), channel_id=1, source_target_pairs={{0,16},{4,20},{8,24},{12,28},{16,0},{20,4},{24,8},{28,12},{1,17},{... | collective-permute-start | bytes 884744 | tf_op jit(solution)/shard_map/ppermute | solution.py:528
  399.9 48.6 %all-to-all-start.6 = ((bf16[4,128,768]{2,1,0:T(8,128)(2,1)}), bf16[4,128,768]{2,1,0:T(8,128)(2,1)S(1)}, u32[]{:S(2)}, u32[]{:S(2)}) async-start(bf16[4,128,768]{2,1,0:T(8,128)(2,1)} %bitcast.56), calls=%async_computation.6 | async-start | bytes 1572864 | tf_op jit(solution)/shard_map/all_to_all | solution.py:676
  404.7 40.2 %collective-permute-start.70 = (bf16[4,48,768]{2,1,0:T(8,128)(2,1)S(1)}, bf16[4,48,768]{2,1,0:T(8,128)(2,1)S(1)}, u32[]{:S(2)}, u32[]{:S(2)}) collective-permute-start(bf16[4,48,768]{2,1,0:T(8,128)(2,1)S(1)} %get-tuple-element.84), channel_id=1, source_target_pairs={{0,8},{4,12},{8,0},{12,4},{16,24},{20,28},{24,16},{28,20},{1,9},{5... | collective-permute-start | bytes 884744 | tf_op jit(solution)/shard_map/ppermute | solution.py:528
  409.7 42.4 %collective-permute-start.78 = (bf16[2,48,3072]{2,1,0:T(8,128)(2,1)}, bf16[2,48,3072]{2,1,0:T(8,128)(2,1)}, u32[]{:S(2)}, u32[]{:S(2)}) collective-permute-start(bf16[2,48,3072]{2,1,0:T(8,128)(2,1)} %get-tuple-element.75), channel_id=1, source_target_pairs={{0,16},{4,20},{8,24},{12,28},{16,0},{20,4},{24,8},{28,12},{1,17},{... | collective-permute-start | bytes 1769480 | tf_op jit(solution)/shard_map/ppermute | solution.py:528
  410.3 41.7 %collective-permute-start.80 = (bf16[2,48,3072]{2,1,0:T(8,128)(2,1)}, bf16[2,48,3072]{2,1,0:T(8,128)(2,1)}, u32[]{:S(2)}, u32[]{:S(2)}) collective-permute-start(bf16[2,48,3072]{2,1,0:T(8,128)(2,1)} %get-tuple-element.76), channel_id=1, source_target_pairs={{0,8},{4,12},{8,0},{12,4},{16,24},{20,28},{24,16},{28,20},{1,9},{5... | collective-permute-start | bytes 1769480 | tf_op jit(solution)/shard_map/ppermute | solution.py:528
  441.2 36.6 %collective-permute-start.85 = (f32[6912]{0:T(1024)}, f32[6912]{0:T(1024)}, u32[]{:S(2)}, u32[]{:S(2)}) collective-permute-start(f32[6912]{0:T(1024)} %add.498), channel_id=1, source_target_pairs={{0,2},{1,3},{2,0},{3,1},{4,6},{5,7},{6,4},{7,5},{8,10},{9,11},{10,... | collective-permute-start | bytes 82952 | tf_op jit(solution)/shard_map/ppermute | solution.py:532
  (130 other events, 1084.4 us)

commit v3 on v2

v3 whole, which is shorter than its diff:
```python
import functools

import jax
import jax.numpy as jnp
import numpy as np
from jax import lax
from jax.experimental import pallas as pl
from jax.experimental.pallas import tpu as pltpu
from jax.sharding import PartitionSpec as P

HEADS = 12
DH = 64
PAIR = 2 * DH
EPS = 1e-06
BF = jnp.bfloat16
F32 = jnp.float32
LIMIT = 60 * 1024 * 1024
SMEM_SPEC = pl.BlockSpec(memory_space=pltpu.SMEM)
ANY_SPEC = pl.BlockSpec(memory_space=pl.ANY)


def nn(left, right):
    return jnp.dot(left, right, preferred_element_type=F32)


def nt(left, right):
    return lax.dot_general(left, right, (((1,), (1,)), ((), ())), preferred_element_type=F32)


def tn(left, right):
    return lax.dot_general(left, right, (((0,), (0,)), ((), ())), preferred_element_type=F32)


def tt(left, right):
    return lax.dot_general(left, right, (((0,), (1,)), ((), ())), preferred_element_type=F32)


def reversed_table(count, first, width):
    dist = (first - np.arange(count)).astype(np.float32)
    half = width // 2
    power = np.arange(half).astype(np.float32) * np.float32(2.0 / width)
    freq = np.float32(1.0) / np.float32(10000.0) ** power
    angle = (dist[:, None] * freq[None, :]).astype(np.float64)
    return np.concatenate([np.sin(angle), np.cos(angle)], axis=1).astype(np.float32).astype(BF)


MESH = pl.DeviceIdType.MESH
CORE, XBIT, YBIT = 1, 2, 4


class Place:
    def __init__(self):
        self.d, self.z = lax.axis_index("dp"), lax.axis_index("tensor")
        self.core = lax.rem(self.d, 2)
        self.x = lax.rem(lax.div(self.d, 2), 2)
        self.y = lax.div(self.d, 4)

    def dp(self, bits):
        at = self.d
        if bits & CORE:
            at = at + (1 - 2 * self.core)
        if bits & XBIT:
            at = at + (2 - 4 * self.x)
        if bits & YBIT:
            at = at + (4 - 8 * self.y)
        return at

    def up(self, step):
        return lax.rem(self.z + step, 4) if step else self.z


def push(src, dst, send, recv, dp, z):
    return pltpu.make_async_remote_copy(
        src_ref=src,
        dst_ref=dst,
        send_sem=send,
        recv_sem=recv,
        device_id=(dp, z),
        device_id_type=MESH,
    )


def settle(ref, sem):
    pltpu.make_async_copy(ref, ref, sem).wait()


def greet(partners):
    barrier = pltpu.get_barrier_semaphore()
    for partner in partners:
        pl.semaphore_signal(barrier, inc=1, device_id=partner, device_id_type=MESH)
    pl.semaphore_wait(barrier, len(partners))


GATHER = (
    (0, 0, XBIT),
    (0, 1, YBIT),
    (0, 0, YBIT),
    (0, 1, XBIT),
    (XBIT, 0, YBIT),
    (YBIT, 1, XBIT),
    (0, 0, CORE),
    (0, 1, CORE),
    (XBIT, 0, CORE),
    (YBIT, 1, CORE),
    (YBIT, 0, CORE),
    (XBIT, 1, CORE),
    (XBIT | YBIT, 0, CORE),
    (XBIT | YBIT, 1, CORE),
)


class Gather:
    def __init__(self, place, dst, own, send, recv):
        self.place, self.dst, self.own = place, dst, own
        self.send, self.recv = send, recv
        self.half = dst.shape[1] // 16

    def region(self, owner, half):
        at = self.place.dp(owner) * (2 * self.half) + half * self.half
        return self.dst.at[:, pl.ds(pl.multiple_of(at, 16), self.half), :]

    def copy(self, i):
        owner, half, to = GATHER[i]
        src = self.region(owner, half)
        if owner == 0:
            src = self.own.at[:, half * self.half : (half + 1) * self.half, :]
        place = self.place
        return push(
            src, self.region(owner, half), self.send.at[i], self.recv.at[i], place.dp(to), place.z
        )

    def begin(self):
        for i in (0, 1, 2, 3, 6, 7):
            self.copy(i).start()

    def after(self, arrived, started):
        for i, more in zip(arrived, started):
            self.copy(i).wait_recv()
            for j in more:
                self.copy(j).start()

    def middle(self):
        self.after((0, 1), ((4, 8), (5, 9)))

    def late(self):
        self.after((2, 3), ((10,), (11,)))

    def last(self):
        self.after((4, 5), ((12,), (13,)))

    def end(self):
        for i in range(6, 14):
            self.copy(i).wait_recv()
        for i in range(14):
            self.copy(i).wait_send()


def exchange_kernel(
    slot_ref,
    content,
    query,
    memory,
    ints,
    *refs,
):
    mats, (upw, dnw) = refs[:5], refs[5:7]
    context, stream, all_ints, whole, out_slab, ud_slab = refs[7:13]
    (
        spread,
        picked,
        shards,
        slab,
        mat_send,
        ud_send,
        int_send,
        spread_send,
        pick_send,
        stream_send,
        gather_send,
        gather_recv,
        recv,
    ) = refs[13:]
    place = Place()
    d, z, core = place.d, place.z, place.core
    part = content.shape[1]
    mem_total = part * 4
    piece = part // 8
    greet([(place.dp(r), place.up(k)) for r in range(8) for k in range(4) if r or k])

    spread_copies = []
    for r in range(8):
        to = place.dp(r)
        src = memory.at[:, pl.ds(pl.multiple_of(to * piece, 16), piece), :]
        dst = spread.at[pl.ds(2 * d, 2)]
        if r == 0:
            pltpu.make_async_copy(src, dst, recv.at[0]).start()
        else:
            spread_copies.append(push(src, dst, spread_send.at[r - 1], recv.at[0], to, z))
    mat_copies = []
    for m, mat in enumerate(mats):
        pltpu.make_async_copy(mat, shards.at[m, z], recv.at[1]).start()
        for k in range(1, 4):
            at = mat_send.at[3 * m + k - 1]
            mat_copies.append(push(mat, shards.at[m, z], at, recv.at[1], d, place.up(k)))
    int_copies = []
    for r in range(8):
        if r == 0:
            pltpu.make_async_copy(ints, all_ints.at[d], recv.at[2]).start()
        else:
            int_copies.append(
                push(ints, all_ints.at[d], int_send.at[r - 1], recv.at[2], place.dp(r), z)
            )
    for copy in mat_copies + spread_copies + int_copies:
        copy.start()

    def stream_copy(i, act):
        j, kind = i // 3, i % 3
        to, row = 2 * core + j, pl.multiple_of(z * part, 16)
        if kind < 2:
            dp = d - core + kind
            src, dst, sem = content.at[j], context.at[pl.ds(mem_total + row, part), :], recv.at[3]
        else:
            dp = d - core + 1
            src, dst, sem = query.at[j], stream.at[pl.ds(row, part), :], recv.at[4]
        here = jnp.logical_and(dp == d, to == z)
        local = pltpu.make_async_copy(src, dst, sem)
        remote = push(src, dst, stream_send.at[i], sem, dp, to)
        if act == "start":
            pl.when(here)(local.start)
            pl.when(jnp.logical_not(here))(remote.start)
        else:
            pl.when(jnp.logical_not(here))(remote.wait_send)

    for i in range(6):
        stream_copy(i, "start")

    settle(shards, recv.at[1])
    for m in range(5):
        slab[m] = jnp.concatenate([shards[m, k] for k in range(4)], axis=1)
    rows = slab.shape[1]
    own_rows = pl.ds(pl.multiple_of(d * rows, 16), rows)
    gather = Gather(place, whole, slab.at[0:4], gather_send, gather_recv)
    gather.begin()
    pltpu.make_async_copy(slab.at[0:4], whole.at[:, own_rows, :], recv.at[6]).start()
    pltpu.make_async_copy(slab.at[4:5], out_slab, recv.at[7]).start()

    settle(spread, recv.at[0])
    for q in range(16):
        picked[q] = spread[slot_ref[q]]
    pick_copies = []
    row = pl.multiple_of(z * part + d * piece, 16)
    for r in range(8):
        for k in range(4):
            to, lane = place.dp(r), place.up(k)
            src = picked.at[4 * lax.div(to, 2) + lane]
            dst = context.at[pl.ds(row, piece), :]
            if r or k:
                copy = push(src, dst, pick_send.at[4 * r + k - 1], recv.at[5], to, lane)
                pick_copies.append(copy)
            else:
                copy = pltpu.make_async_copy(src, dst, recv.at[5])
            copy.start()

    width = upw.shape[1]
    cols = pl.ds(pl.multiple_of(z * width, 128), width)
    ud_copies = []
    for m, mat in enumerate((upw, dnw)):
        pltpu.make_async_copy(mat, ud_slab.at[m, :, cols], recv.at[8]).start()
        for k in range(1, 4):
            at = ud_send.at[3 * m + k - 1]
            ud_copies.append(push(mat, ud_slab.at[m, :, cols], at, recv.at[8], d, place.up(k)))
            ud_copies[-1].start()

    gather.middle()
    gather.late()
    gather.last()
    gather.end()
    settle(whole.at[:, own_rows, :], recv.at[6])
    settle(out_slab, recv.at[7])
    settle(ud_slab, recv.at[8])
    settle(all_ints, recv.at[2])
    settle(context.at[mem_total:, :], recv.at[3])
    settle(context.at[:mem_total, :], recv.at[5])

    @pl.when(core == 1)
    def _():
        settle(stream, recv.at[4])

    for i in range(6):
        stream_copy(i, "wait")
    for copy in mat_copies + spread_copies + int_copies + pick_copies + ud_copies:
        copy.wait_send()


def exchange(slot_of, content, query, memory, ints, mats, upw, dnw):
    micro, part, width = content.shape
    rows = mats[0].shape[0]
    inner = upw.shape[1] * 4
    vmem = pl.BlockSpec(memory_space=pltpu.VMEM)
    dma = lambda n: pltpu.SemaphoreType.DMA((n,))
    return pl.pallas_call(
        exchange_kernel,
        in_specs=[SMEM_SPEC] + [ANY_SPEC] * 3 + [vmem] * 8,
        out_specs=[ANY_SPEC] * 6,
        out_shape=[
            jax.ShapeDtypeStruct((8 * part, width), BF),
            jax.ShapeDtypeStruct((4 * part, width), BF),
            jax.ShapeDtypeStruct((8,) + ints.shape, jnp.int32),
            jax.ShapeDtypeStruct((4, 8 * rows, width), BF),
            jax.ShapeDtypeStruct((1, rows, width), BF),
            jax.ShapeDtypeStruct((2, rows, inner), BF),
        ],
        scratch_shapes=[
            pltpu.VMEM((16, part // 8, width), BF),
            pltpu.VMEM((16, part // 8, width), BF),
            pltpu.VMEM((5, 4, rows, width // 4), BF),
            pltpu.VMEM((5, rows, width), BF),
            dma(15),
            dma(6),
            dma(7),
            dma(7),
            dma(31),
            dma(6),
            dma(14),
            dma(14),
            dma(9),
        ],
        compiler_params=pltpu.CompilerParams(
            collective_id=1, has_side_effects=True, vmem_limit_bytes=LIMIT
        ),
        cost_estimate=pl.CostEstimate(flops=0, bytes_accessed=64 << 20, transcendentals=0),
        name="exchange",
    )(slot_of, content, query, memory, ints, *mats, upw, dnw)


def head_lanes(array, head):
    lane = lax.broadcasted_iota(jnp.int32, array.shape, 1)
    return jnp.where((lane >= DH) == (head == 1), array, jnp.zeros_like(array))


def attend_forward_step(
    block, qw_ref, qp_ref, k_ref, v_ref, rel_ref, thr_ref, kr_ref, vec_ref, prob_ref
):
    rows, klen = qw_ref.shape[0], k_ref.shape[0]
    width = klen + block
    keys, values = k_ref[...], v_ref[...]
    for part in range(rows // block):
        at = slice(part * block, (part + 1) * block)
        first = rows - (part + 1) * block
        qw, qp = qw_ref[at, :], qp_ref[at, :]
        rel = rel_ref[first : first + width, :]
        seen = kr_ref[...] < thr_ref[at, :]
        vecs = []
        for head in range(2):
            raw = nt(head_lanes(qp, head), rel)
            moved = pltpu.roll(raw, 0, 1, stride=1, stride_axis=0)[:, block:]
            score = nt(head_lanes(qw, head), keys) + moved
            score = jnp.where(seen, score, -1e30)
            expo = jnp.exp(score - jnp.max(score, axis=1, keepdims=True))
            prob = (expo * (1.0 / jnp.sum(expo, axis=1, keepdims=True))).astype(BF)
            prob_ref[head, at, :] = prob
            vecs.append(nn(prob, values))
        lane = lax.broadcasted_iota(jnp.int32, vecs[0].shape, 1)
        vec_ref[at, :] = jnp.where(lane < DH, vecs[0], vecs[1]).astype(BF)


def attend_forward_kernel(block, wired, *refs):
    if not wired:
        attend_forward_step(block, *refs)
        return
    ins, (out_slab, ud_slab, ctan, qtan) = refs[:7], refs[7:11]
    outs, (wo, ud, tangent) = refs[11:13], refs[13:16]
    out_send, out_recv, ud_send, ud_recv, tan_send, recv = refs[16:]
    step, steps = pl.program_id(0), pl.num_programs(0)
    place = Place()
    d, z, core = place.d, place.z, place.core
    gathers = (
        Gather(place, ud, ud_slab, ud_send, ud_recv),
        Gather(place, wo, out_slab, out_send, out_recv),
    )
    rows, part = out_slab.shape[1], ctan.shape[1]
    own_rows = pl.ds(pl.multiple_of(d * rows, 16), rows)

    def tan_copy(i, act):
        j, kind = i // 2, i % 2
        to, dp = 2 * core + j, d - core + kind
        src = (ctan, qtan)[kind].at[j]
        dst = tangent.at[pl.ds(pl.multiple_of(z * part, 16), part), :]
        here = jnp.logical_and(dp == d, to == z)
        local = pltpu.make_async_copy(src, dst, recv.at[0])
        remote = push(src, dst, tan_send.at[i], recv.at[0], dp, to)
        if act == "start":
            pl.when(here)(local.start)
            pl.when(jnp.logical_not(here))(remote.start)
        else:
            pl.when(jnp.logical_not(here))(remote.wait_send)

    @pl.when(step == 0)
    def _():
        partners = [(place.dp(r), z) for r in (CORE, XBIT, YBIT)]
        partners += [(place.dp(r), place.up(k)) for k in (1, 2, 3) for r in (0, CORE)]
        greet(partners)
        for gather in gathers:
            gather.begin()
        pltpu.make_async_copy(ud_slab, ud.at[:, own_rows, :], recv.at[1]).start()
        pltpu.make_async_copy(out_slab, wo.at[:, own_rows, :], recv.at[2]).start()
        for i in range(4):
            tan_copy(i, "start")

    @pl.when(step == 3)
    def _():
        for gather in gathers:
            gather.middle()

    attend_forward_step(block, *ins, *outs)

    @pl.when(step == steps - 1)
    def _():
        for gather in gathers:
            gather.late()
        for gather in gathers:
            gather.last()
        for gather in gathers:
            gather.end()
        settle(ud.at[:, own_rows, :], recv.at[1])
        settle(wo.at[:, own_rows, :], recv.at[2])
        settle(tangent, recv.at[0])
        for i in range(4):
            tan_copy(i, "wait")


def attend_forward(qw, qp, keys, values, rel, thr, key_rank, block, wires=()):
    rows, width = qw.shape
    klen, span = keys.shape[0], rel.shape[0]
    col = lambda count: pl.BlockSpec((count, PAIR), lambda p: (0, p))
    in_specs = [
        col(rows),
        col(rows),
        col(klen),
        col(klen),
        col(span),
        pl.BlockSpec((rows, 1), lambda p: (0, 0)),
        pl.BlockSpec((1, klen), lambda p: (0, 0)),
    ]
    out_specs = [col(rows), pl.BlockSpec((2, rows, klen), lambda p: (p, 0, 0))]
    out_shape = [
        jax.ShapeDtypeStruct((rows, width), BF),
        jax.ShapeDtypeStruct((width // DH, rows, klen), BF),
    ]
    params = dict(vmem_limit_bytes=LIMIT)
    scratch = []
    if wires:
        vmem = pl.BlockSpec(memory_space=pltpu.VMEM)
        in_specs += [vmem, vmem, ANY_SPEC, ANY_SPEC]
        out_specs += [ANY_SPEC] * 3
        inner = wires[1].shape[2]
        out_shape += [
            jax.ShapeDtypeStruct((1, width, width), BF),
            jax.ShapeDtypeStruct((2, width, inner), BF),
            jax.ShapeDtypeStruct((rows, width), BF),
        ]
        scratch = [pltpu.SemaphoreType.DMA((n,)) for n in (14, 14, 14, 14, 4, 3)]
        params.update(collective_id=2, has_side_effects=True)
    return pl.pallas_call(
        functools.partial(attend_forward_kernel, block, bool(wires)),
        grid=(width // PAIR,),
        in_specs=in_specs,
        out_specs=out_specs,
        out_shape=out_shape,
        scratch_shapes=scratch,
        compiler_params=pltpu.CompilerParams(**params),
        cost_estimate=pl.CostEstimate(
            flops=8 * rows * klen * width, bytes_accessed=16 << 20, transcendentals=12 * rows * klen
        ),
        name="attend_forward",
    )(qw, qp, keys, values, rel, thr, key_rank, *wires)


def attend_backward_kernel(
    block,
    prob_ref,
    gvec_ref,
    qw_ref,
    qp_ref,
    k_ref,
    v_ref,
    rel_ref,
    dproj_ref,
    dk_ref,
    dv_ref,
    drel_ref,
    bias_ref,
    rel_acc,
):
    rows, klen = qw_ref.shape[0], k_ref.shape[0]
    width = klen + block
    keys, values = k_ref[...], v_ref[...]
    row = lax.broadcasted_iota(jnp.int32, (block, block), 0)
    col = lax.broadcasted_iota(jnp.int32, (block, block), 1)
    mirror = (row + col == block - 1).astype(BF)
    rel_acc[...] = jnp.zeros_like(rel_acc)
    d_keys, d_values = [None, None], [None, None]
    word_sum = jnp.zeros((1, PAIR), F32)
    pos_sum = jnp.zeros((1, PAIR), F32)
    for part in range(rows // block):
        at = slice(part * block, (part + 1) * block)
        first = rows - (part + 1) * block
        gvec, qw = gvec_ref[at, :], qw_ref[at, :]
        gvec_t = jnp.transpose(gvec.astype(F32)).astype(BF)
        qw_t = jnp.transpose(qw.astype(F32)).astype(BF)
        qp_t = jnp.transpose(nn(mirror, qp_ref[at, :])).astype(BF)
        rel = rel_ref[first : first + width, :]
        word_parts, pos_parts = [], []
        for head in range(2):
            own = slice(head * DH, (head + 1) * DH)
            prob = prob_ref[head, at, :]
            d_prob = nt(head_lanes(gvec, head), values)
            weight = prob.astype(F32)
            inner = jnp.sum(weight * d_prob, axis=1, keepdims=True)
            g_sum = (weight * (d_prob - inner) * 0.125).astype(BF)
            dv = nn(gvec_t[own, :], prob)
            dk = nn(qw_t[own, :], g_sum)
            d_values[head] = dv if part == 0 else d_values[head] + dv
            d_keys[head] = dk if part == 0 else d_keys[head] + dk
            turned = nn(mirror, g_sum)
            padded = jnp.concatenate([jnp.zeros((block, block), F32), turned], axis=1)
            moved = pltpu.roll(padded, width - block + 1, 1, stride=1, stride_axis=0).astype(BF)
            word_parts.append(nn(turned.astype(BF), keys))
            pos_parts.append(nn(moved, rel))
            rel_acc[own, first : first + width] += nn(qp_t[own, :], moved)
        lane = lax.broadcasted_iota(jnp.int32, word_parts[0].shape, 1)
        word = jnp.where(lane < DH, word_parts[0], word_parts[1])
        pos = jnp.where(lane < DH, pos_parts[0], pos_parts[1])
        word_sum = word_sum + jnp.sum(word, axis=0, keepdims=True)
        pos_sum = pos_sum + jnp.sum(pos, axis=0, keepdims=True)
        dproj_ref[at, :] = nn(mirror, (word + pos).astype(BF)).astype(BF)
    for head in range(2):
        own = slice(head * DH, (head + 1) * DH)
        dv_ref[own, :] = d_values[head].astype(BF)
        dk_ref[own, :] = (8.0 * d_keys[head]).astype(BF)
    drel_ref[...] = (8.0 * rel_acc[...]).astype(BF)
    bias_ref[0:1, :] = word_sum
    bias_ref[1:2, :] = pos_sum


def attend_backward(prob, gvec, qw, qp, keys, values, rel, block):
    rows, width = qw.shape
    klen, span = keys.shape[0], rel.shape[0]
    col = lambda count: pl.BlockSpec((count, PAIR), lambda p: (0, p))
    rowb = lambda count: pl.BlockSpec((PAIR, count), lambda p: (p, 0))
    return pl.pallas_call(
        functools.partial(attend_backward_kernel, block),
        grid=(width // PAIR,),
        in_specs=[
            pl.BlockSpec((2, rows, klen), lambda p: (p, 0, 0)),
            col(rows),
            col(rows),
            col(rows),
            col(klen),
            col(klen),
            col(span),
        ],
        out_specs=[col(rows), rowb(klen), rowb(klen), rowb(span), col(2)],
        out_shape=[
            jax.ShapeDtypeStruct((rows, width), BF),
            jax.ShapeDtypeStruct((width, klen), BF),
            jax.ShapeDtypeStruct((width, klen), BF),
            jax.ShapeDtypeStruct((width, span), BF),
            jax.ShapeDtypeStruct((2, width), F32),
        ],
        scratch_shapes=[pltpu.VMEM((PAIR, span), F32)],
        compiler_params=pltpu.CompilerParams(vmem_limit_bytes=LIMIT),
        cost_estimate=pl.CostEstimate(
            flops=16 * rows * klen * width, bytes_accessed=20 << 20, transcendentals=0
        ),
        name="attend_backward",
    )(prob, gvec, qw, qp, keys, values, rel)


def norm_parts(value):
    center = value - jnp.mean(value, axis=1, keepdims=True)
    scale = lax.rsqrt(jnp.mean(center * center, axis=1, keepdims=True) + EPS)
    return center * scale, scale


def norm_pull(normed, scale, err):
    inner = jnp.mean(err * normed, axis=1, keepdims=True)
    return (err - jnp.mean(err, axis=1, keepdims=True) - normed * inner) * scale


def sum_rows(value):
    return jnp.sum(value, axis=0, keepdims=True)


def feed_kernel(steps, *refs):
    (
        ud_hbm,
        wo_hbm,
        vec_ref,
        x_ref,
        tan_ref,
        upb_ref,
        dnb_ref,
        g1_ref,
        s1_ref,
        g2_ref,
        s2_ref,
        out_ref,
        dmix_ref,
        gvec_ref,
        go_ref,
        gud_ref,
        gupb_ref,
        small_ref,
        ud_ref,
        wo_ref,
        n1_ref,
        r1_ref,
        fb_ref,
        fbt_ref,
        acc_ref,
        act_ref,
        slope_ref,
        gd_ref,
        gdt_ref,
        sems,
    ) = refs
    step = pl.program_id(0)
    chunk = act_ref.shape[2]
    cols = pl.ds(pl.multiple_of(lax.rem(step, steps) * chunk, chunk), chunk)

    @pl.when(step == 0)
    def _():
        wo_copy = pltpu.make_async_copy(wo_hbm, wo_ref, sems.at[0])
        ud_copy = pltpu.make_async_copy(ud_hbm, ud_ref, sems.at[1])
        wo_copy.start()
        ud_copy.start()
        wo_copy.wait()
        normed, scale = norm_parts(nt(vec_ref[...], wo_ref[0]) + x_ref[...].astype(F32))
        n1_ref[...] = normed
        r1_ref[...] = scale
        first = normed * g1_ref[...] + s1_ref[...]
        fb_ref[...] = first.astype(BF)
        fbt_ref[...] = jnp.transpose(first).astype(BF)
        acc_ref[...] = first + dnb_ref[...]
        ud_copy.wait()

    @pl.when(step < steps)
    def _():
        upper = nn(fb_ref[...], ud_ref[0, :, cols]) + upb_ref[...]
        square = upper * upper
        root = 0.7978845608028654
        bend = jnp.tanh(root * (upper + 0.044715 * (square * upper)))
        half = 0.5 * (1.0 + bend)
        act = (upper * half).astype(BF)
        act_ref[step] = act
        slope_ref[step] = half + 0.5 * upper * (1.0 - bend * bend) * (
            root + (3 * 0.044715 * root) * square
        )
        acc_ref[...] += nt(act, ud_ref[1, :, cols])

    @pl.when(step == steps - 1)
    def _():
        normed, scale = norm_parts(acc_ref[...])
        out_ref[...] = (normed * g2_ref[...] + s2_ref[...]).astype(BF)
        tan = tan_ref[...].astype(F32)
        d_down = norm_pull(normed, scale, tan * g2_ref[...])
        small_ref[0:1, :] = sum_rows(d_down)
        small_ref[3:4, :] = sum_rows(tan * normed)
        small_ref[4:5, :] = sum_rows(tan)
        gd_ref[...] = d_down.astype(BF)
        gdt_ref[...] = jnp.transpose(d_down).astype(BF)
        acc_ref[...] = d_down

    @pl.when(step >= steps)
    def _():
        at = step - steps
        d_up = nn(gd_ref[...], ud_ref[1, :, cols]) * slope_ref[at]
        gupb_ref[...] = sum_rows(d_up)
        g_up = d_up.astype(BF)
        acc_ref[...] += nt(g_up, ud_ref[0, :, cols])
        gud_ref[0] = nn(fbt_ref[...], g_up).astype(BF)
        gud_ref[1] = nn(gdt_ref[...], act_ref[at]).astype(BF)

    @pl.when(step == 2 * steps - 1)
    def _():
        d_first, normed = acc_ref[...], n1_ref[...]
        small_ref[1:2, :] = sum_rows(d_first * normed)
        small_ref[2:3, :] = sum_rows(d_first)
        d_mixed = norm_pull(normed, r1_ref[...], d_first * g1_ref[...])
        dmix_ref[...] = d_mixed
        gvec_ref[...] = nn(d_mixed.astype(BF), wo_ref[0]).astype(BF)
        gdt_ref[...] = jnp.transpose(d_mixed).astype(BF)
        go_ref[...] = nn(gdt_ref[...], vec_ref[...]).astype(BF)


def feed(ud, wo, vec, x, tan, upb, dnb, g1, s1, g2, s2):
    rows, width = vec.shape
    inner = upb.shape[1]
    chunk = 512
    steps = inner // chunk
    whole = lambda a, b: pl.BlockSpec((a, b), lambda i: (0, 0))
    late = lambda i: jnp.maximum(i - steps, 0)
    grads = pl.BlockSpec((2, width, chunk), lambda i: (0, 0, late(i)))
    return pl.pallas_call(
        functools.partial(feed_kernel, steps),
        grid=(2 * steps,),
        in_specs=[ANY_SPEC] * 2
        + [whole(rows, width)] * 3
        + [pl.BlockSpec((1, chunk), lambda i: (0, lax.rem(i, steps)))]
        + [whole(1, width)] * 5,
        out_specs=[
            whole(rows, width),
            whole(rows, width),
            whole(rows, width),
            whole(width, width),
            grads,
            pl.BlockSpec((1, chunk), lambda i: (0, late(i))),
            whole(8, width),
        ],
        out_shape=[
            jax.ShapeDtypeStruct((rows, width), BF),
            jax.ShapeDtypeStruct((rows, width), F32),
            jax.ShapeDtypeStruct((rows, width), BF),
            jax.ShapeDtypeStruct((width, width), BF),
            jax.ShapeDtypeStruct((2, width, inner), BF),
            jax.ShapeDtypeStruct((1, inner), F32),
            jax.ShapeDtypeStruct((8, width), F32),
        ],
        scratch_shapes=[
            pltpu.VMEM((2, width, inner), BF),
            pltpu.VMEM((1, width, width), BF),
            pltpu.VMEM((rows, width), F32),
            pltpu.VMEM((rows, 1), F32),
            pltpu.VMEM((rows, width), BF),
            pltpu.VMEM((width, rows), BF),
            pltpu.VMEM((rows, width), F32),
            pltpu.VMEM((steps, rows, chunk), BF),
            pltpu.VMEM((steps, rows, chunk), F32),
            pltpu.VMEM((rows, width), BF),
            pltpu.VMEM((width, rows), BF),
            pltpu.SemaphoreType.DMA((2,)),
        ],
        compiler_params=pltpu.CompilerParams(vmem_limit_bytes=LIMIT),
        cost_estimate=pl.CostEstimate(
            flops=12 * rows * width * inner, bytes_accessed=36 << 20, transcendentals=rows * inner
        ),
        name="feed",
    )(ud, wo, vec, x, tan, upb, dnb, g1, s1, g2, s2)


def project_kernel(
    w_ref, ctx_ref, q_ref, table_ref, wb_ref, pb_ref, k_ref, v_ref, rel_ref, qw_ref, qp_ref, x_ref
):
    lead = lax.rem(lax.axis_index("dp"), 2) == 0
    back = ctx_ref.shape[0] - q_ref.shape[0]
    block = 256

    def loop(count, step):
        def run(i, carry):
            step(pl.ds(pl.multiple_of(i * block, block), block))
            return carry

        lax.fori_loop(0, count // block, run, 0)

    def context_step(at):
        k_ref[at, :] = nn(ctx_ref[at, :], w_ref[0]).astype(BF)
        v_ref[at, :] = nn(ctx_ref[at, :], w_ref[1]).astype(BF)

    def stream_step(at):
        own = ctx_ref[pl.ds(pl.multiple_of(at.start + back, block), block), :]
        x_ref[at, :] = jnp.where(lead, own, q_ref[at, :])
        proj = nn(x_ref[at, :], w_ref[2])
        qw_ref[at, :] = (0.125 * (proj + wb_ref[...]).astype(BF).astype(F32)).astype(BF)
        qp_ref[at, :] = (0.125 * (proj + pb_ref[...]).astype(BF).astype(F32)).astype(BF)

    def table_step(at):
        rel_ref[at, :] = nn(table_ref[at, :], w_ref[3]).astype(BF)

    loop(table_ref.shape[0], table_step)
    loop(q_ref.shape[0], stream_step)
    loop(ctx_ref.shape[0], context_step)


def project(mats, context, query, table, wb, pb):
    rows, width = query.shape
    klen, span = context.shape[0], table.shape[0]
    vmem = pl.BlockSpec(memory_space=pltpu.VMEM)
    return pl.pallas_call(
        project_kernel,
        in_specs=[vmem] * 6,
        out_specs=[vmem] * 6,
        out_shape=[
            jax.ShapeDtypeStruct((klen, width), BF),
            jax.ShapeDtypeStruct((klen, width), BF),
            jax.ShapeDtypeStruct((span, width), BF),
            jax.ShapeDtypeStruct((rows, width), BF),
            jax.ShapeDtypeStruct((rows, width), BF),
            jax.ShapeDtypeStruct((rows, width), BF),
        ],
        compiler_params=pltpu.CompilerParams(vmem_limit_bytes=LIMIT),
        cost_estimate=pl.CostEstimate(
            flops=2 * (2 * klen + rows + span) * width * width,
            bytes_accessed=20 << 20,
            transcendentals=0,
        ),
        name="project",
    )(mats, context, query, table, wb, pb)


def weight_grads_kernel(xt_ref, ct_ref, tt_ref, dp_ref, dk_ref, dv_ref, dr_ref, g_ref):
    g_ref[0] = nt(ct_ref[...], dk_ref[...]).astype(BF)
    g_ref[1] = nt(ct_ref[...], dv_ref[...]).astype(BF)
    g_ref[2] = nn(xt_ref[...], dp_ref[...]).astype(BF)
    g_ref[3] = nt(tt_ref[...], dr_ref[...]).astype(BF)


def weight_grads(x_t, ctx_t, table_t, d_proj, dk_t, dv_t, drel_t):
    width, rows = x_t.shape
    klen, span = ctx_t.shape[1], table_t.shape[1]
    chunk = 256
    whole = lambda a, b: pl.BlockSpec((a, b), lambda i: (0, 0))
    rowb = lambda b: pl.BlockSpec((chunk, b), lambda i: (i, 0))
    return pl.pallas_call(
        weight_grads_kernel,
        grid=(width // chunk,),
        in_specs=[
            whole(width, rows),
            whole(width, klen),
            whole(width, span),
            pl.BlockSpec((rows, chunk), lambda i: (0, i)),
            rowb(klen),
            rowb(klen),
            rowb(span),
        ],
        out_specs=pl.BlockSpec((4, width, chunk), lambda i: (0, 0, i)),
        out_shape=jax.ShapeDtypeStruct((4, width, width), BF),
        compiler_params=pltpu.CompilerParams(vmem_limit_bytes=LIMIT),
        cost_estimate=pl.CostEstimate(
            flops=2 * (rows + 2 * klen + span) * width * width,
            bytes_accessed=20 << 20,
            transcendentals=0,
        ),
        name="weight_grads",
    )(x_t, ctx_t, table_t, d_proj, dk_t, dv_t, drel_t)


def flip(arr, bit):
    return lax.ppermute(arr, "dp", [(i, i ^ bit) for i in range(lax.axis_size("dp"))])


def flip_z(arr, bit):
    return lax.ppermute(arr, "tensor", [(i, i ^ bit) for i in range(lax.axis_size("tensor"))])


def by_bits(parts, bits):
    step = 1
    for bit in bits:
        parts = [
            jnp.where(bit == 1, parts[i ^ step], parts[i]) for i in range(len(parts))
        ]
        step *= 2
    return parts


def scatter_sum(grads):
    mine = lax.psum_scatter(grads, "dp", scatter_dimension=1, tiled=True)
    return lax.psum_scatter(mine, "tensor", scatter_dimension=2, tiled=True).astype(F32)


def sum_all(value):
    if lax.axis_size("dp") != 8:
        return lax.psum(value, ("dp", "tensor"))
    for bit in (1, 2, 4):
        value = value + flip(value, bit)
    for bit in (1, 2):
        value = value + flip_z(value, bit)
    return value


def body(
    content_stream,
    query_stream,
    memory,
    content_tangent,
    query_tangent,
    seq_lengths,
    factor_order,
    memory_lengths,
    slot_sequence,
    query_weight,
    key_weight,
    value_weight,
    pos_weight,
    out_weight,
    up_weight,
    up_bias,
    down_weight,
    down_bias,
    word_bias,
    pos_bias,
    first_gain,
    first_shift,
    second_gain,
    second_shift,
):
    groups, tensors = lax.axis_size("dp"), lax.axis_size("tensor")
    micro, part_len, width = content_stream.shape
    mem_part = memory.shape[1]
    seq_len, mem_total = part_len * tensors, mem_part * tensors
    klen, span = mem_total + seq_len, mem_total + 2 * seq_len
    count = micro * groups
    here, lane = lax.axis_index("dp"), lax.axis_index("tensor")
    core = here % 2
    lead = core == 0
    block = 256
    assert 2 * micro == tensors

    def swap(arr):
        return flip(arr, CORE)

    def to_unit(first, second):
        got = swap(jnp.where(lead, second, first))
        low = jnp.where(lead, first, got)
        high = jnp.where(lead, got, second)
        both = jnp.concatenate([low, high], 0)
        both = lax.all_to_all(both, "tensor", split_axis=0, concat_axis=0, tiled=True)
        return both.reshape(seq_len, width)

    def from_unit(arr):
        both = arr.reshape(tensors, part_len, width)
        both = lax.all_to_all(both, "tensor", split_axis=0, concat_axis=0, tiled=True)
        low, high = both[:micro], both[micro:]
        got = swap(jnp.where(lead, high, low))
        return jnp.where(lead, low, got), jnp.where(lead, got, high)

    seq_id = (here // 2) * tensors + lane
    ids = jnp.arange(count, dtype=jnp.int32)
    slot_of = jnp.sum(jnp.where(slot_sequence[None, :] == ids[:, None], ids[None, :], 0), axis=1)
    counts = jnp.concatenate([seq_lengths, memory_lengths])
    slot = slot_of[seq_id]
    mats = [key_weight, value_weight, query_weight, pos_weight, out_weight]
    table = jnp.asarray(reversed_table(span, klen, width))
    wires = ()
    if groups == 8:
        ints = jnp.pad(factor_order, ((0, 6), (0, 0)))
        ints = lax.dynamic_update_slice(ints, counts[None, :], (micro, 0))
        context, query, all_ints, weights, out_slab, ud_slab = exchange(
            slot_of, content_stream, query_stream, memory, ints, mats, up_weight, down_weight
        )
        wires = (out_slab, ud_slab, content_tangent, query_tangent)
        lengths = all_ints[:, micro, : 2 * micro]
        orders = all_ints[seq_id // micro, :micro]
    else:
        lengths = lax.all_gather(counts, "dp", axis=0, tiled=False)
        orders = lax.all_gather(factor_order, "dp", axis=0, tiled=False)[seq_id // micro]
        stream = to_unit(content_stream, query_stream)
        content, query = jnp.where(lead, stream, swap(stream)), stream
        tangent = to_unit(content_tangent, query_tangent)
        piece = mem_part // groups
        spread = lax.all_to_all(
            memory.reshape(micro, groups, piece, width), "dp", split_axis=1, concat_axis=1, tiled=True
        )
        spread = spread.transpose(1, 0, 2, 3).reshape(count, piece, width)
        spread = jnp.take(spread, slot_of, axis=0)
        spread = spread.reshape(groups // 2, tensors, 2, piece // 2, width).transpose(0, 2, 1, 3, 4)
        spread = lax.all_to_all(
            spread.reshape(groups, tensors, piece // 2, width),
            "dp",
            split_axis=0,
            concat_axis=0,
            tiled=True,
        )
        spread = lax.all_to_all(spread, "tensor", split_axis=1, concat_axis=1, tiled=True)
        got = swap(spread)
        mem_rows = jnp.stack([jnp.where(lead, spread, got), jnp.where(lead, got, spread)])
        mem_rows = mem_rows.transpose(2, 1, 0, 3, 4).reshape(mem_total, width)
        context = jnp.concatenate([mem_rows, content], 0)

        def whole(mat):
            mat = lax.all_gather(mat, "tensor", axis=1, tiled=True)
            return lax.all_gather(mat, "dp", axis=0, tiled=True)

        weights = jnp.stack([whole(mat) for mat in mats[:4]])
        wo = whole(out_weight)[None]
        ud = jnp.stack([whole(up_weight), whole(down_weight)])

    length = lengths[seq_id // micro, seq_id % micro]
    mem_valid = lengths[slot // micro, micro + slot % micro]
    rank = orders[seq_id % micro]
    key_pos = jnp.arange(klen, dtype=jnp.int32)
    hidden = jnp.int32(1 << 20)
    mem_rank = jnp.where(key_pos[:mem_total] >= mem_total - mem_valid, -1, hidden)
    own_rank = jnp.where(key_pos[:seq_len] < length, rank, hidden)
    key_rank = jnp.concatenate([mem_rank, own_rank])[None, :]
    thr = (rank + jnp.where(lead, 1, 0))[:, None]

    row = lambda v: v.reshape(1, -1)
    keys, values, rel, q_word, q_pos, stream = project(
        weights, context, query, table, row(word_bias), row(pos_bias)
    )
    vec, prob, *arrived = attend_forward(
        q_word, q_pos, keys, values, rel, thr, key_rank, block, wires
    )
    if wires:
        wo, ud, tangent = arrived
    out, d_mixed, g_vec, g_out, g_ud, g_upb, small = feed(
        ud,
        wo,
        vec,
        stream,
        tangent,
        row(up_bias),
        row(down_bias),
        row(first_gain),
        row(first_shift),
        row(second_gain),
        row(second_shift),
    )
    content_out, query_out = from_unit(out)
    grad_up, grad_down = scatter_sum(g_ud)
    (grad_out,) = scatter_sum(g_out[None])
    early = sum_all(jnp.concatenate([g_upb.reshape(-1), small[:5].reshape(-1)]))

    d_proj, dk_t, dv_t, drel_t, biases = attend_backward(
        prob, g_vec, q_word, q_pos, keys, values, rel, block
    )
    late = sum_all(biases)
    d_context = tt(dk_t[:, mem_total:], weights[0]) + tt(dv_t[:, mem_total:], weights[1])
    partner = swap(d_context.astype(BF))
    d_stream = d_mixed + nt(d_proj, weights[2])
    d_stream = d_stream + jnp.where(lead, d_context + partner.astype(F32), 0.0)
    content_grad, query_grad = from_unit(d_stream.astype(BF))
    grad_key, grad_value, grad_query, grad_pos = scatter_sum(
        weight_grads(
            jnp.transpose(stream), jnp.transpose(context), jnp.transpose(table), d_proj, dk_t, dv_t, drel_t
        )
    )
    inner = up_bias.shape[0]
    rest = early[inner:].reshape(5, width)
    return (
        content_out,
        query_out,
        content_grad,
        query_grad,
        grad_query,
        grad_key,
        grad_value,
        grad_pos,
        grad_out,
        grad_up,
        early[:inner],
        grad_down,
        rest[0],
        late[0].reshape(HEADS, DH),
        late[1].reshape(HEADS, DH),
        rest[1],
        rest[2],
        rest[3],
        rest[4],
    )


def solution(mesh):
    rows = P("dp", "tensor", None)
    mat = P("dp", "tensor")
    return jax.shard_map(
        body,
        mesh=mesh,
        in_specs=(rows,) * 5
        + (P("dp"), P("dp", None), P("dp"), P())
        + (mat,) * 6
        + (P(), mat)
        + (P(),) * 7,
        out_specs=(rows,) * 4 + (mat,) * 6 + (P(), mat) + (P(),) * 7,
        check_vma=False,
    )
```

time: 504 us -> 485 us (0.962); the launches traced: 495 us -> 484 us
  Pallas kernels: 121 us -> 242 us
  starting transfers between devices: 131 us -> 22.3 us
  other arithmetic: 73.5 us -> 7.19 us
  waiting for transfers between devices: 116 us -> 159 us
  local copies, waits for them, and re-layouts: 40.4 us -> 23.5 us
  between operations: 5.21 us -> 17.8 us
    reduce_scatter x0 -> x4, waiting for transfers between devices: none -> 133 us  [the longest x3 106 us: scatter_sum(): mine = lax.psum_scatter(grads, 'dp', scatter_dimension=1, tiled=True)]
    pallas_call x3 -> x4, Pallas kernels: 78 us -> 199 us  [the longest x1 98.2 us: exchange(): pl.pallas_call(exchange_kernel, in_specs=[SMEM_SPEC] + [ANY_SPEC] * 3 + [...]
    ppermute x78 -> x9, waiting for transfers between devices: 75.3 us -> 10.8 us  [flip(): lax.ppermute(arr, 'dp', [(i, i ^ bit) for i in range(lax.axis_size('dp'))])]
    ppermute x78 -> x9, starting transfers between devices: 54.2 us -> 7.05 us  [flip(): lax.ppermute(arr, 'dp', [(i, i ^ bit) for i in range(lax.axis_size('dp'))])]
    all_to_all x8 -> x0, starting transfers between devices: 36.9 us -> none  [the longest x3 15.5 us: scatter_sum(): lax.all_to_all(mine, 'tensor', split_axis=0, concat_axis=0, tiled=True)]
    ppermute x13 -> x4, starting transfers between devices: 29.5 us -> 6.81 us  [flip_z(): lax.ppermute(arr, 'tensor', [(i, i ^ bit) for i in range(lax.axis_size('t...]
    all_to_all x8 -> x0, waiting for transfers between devices: 20.2 us -> none  [the longest x3 20.2 us: scatter_sum(): lax.all_to_all(mine, 'tensor', split_axis=0, concat_axis=0, tiled=True)]
    convert_element_type x10 -> x2, other arithmetic: 20 us -> 1.03 us  [scatter_sum(): lax.psum_scatter(mine, 'tensor', scatter_dimension=2, tiled=True)]
  transfers between devices with their start and end apart: 101 -> 21, of which waited for: 28 -> 13; matrix products, arithmetic and copies ran while one was open for 23% -> 6% of each run, Pallas kernels for 17% -> 9%
where the time goes in v3:
time: 485 us; the launch traced here: 484 us
  Pallas kernels  242 us (50%)
  waiting for transfers between devices  159 us (33%)
  local copies, waits for them, and re-layouts  23.5 us (5%)
  starting transfers between devices  22.3 us (5%)
  between operations  17.8 us (4%)
  matrix products  11.4 us (2%)
  other arithmetic  7.19 us (1%)
    reduce_scatter x3, waiting for transfers between devices, scatter_sum(): mine = lax.psum_scatter(grads, 'dp', scatter_dimension=1, tiled=True)  106 us
    pallas_call x1, Pallas kernels, exchange(): pl.pallas_call(exchange_kernel, in_specs=[SMEM_SPEC] + [ANY_SPEC] * 3 + [...  98.2 us
    pallas_call x1, Pallas kernels, attend_forward(): pl.pallas_call(functools.partial(attend_forward_kernel, block, bool(wires...  53.6 us
    pallas_call x1, Pallas kernels, feed(): pl.pallas_call(functools.partial(feed_kernel, steps), grid=(2 * steps,),...  34 us
    pallas_call x1, Pallas kernels, attend_backward(): pl.pallas_call(functools.partial(attend_backward_kernel, block), grid=(wi...  33 us
    reduce_scatter x1, waiting for transfers between devices, scatter_sum(): lax.psum_scatter(mine, 'tensor', scatter_dimension=2, tiled=True)  27.9 us
    pallas_call x1, Pallas kernels, project(): pl.pallas_call(project_kernel, in_specs=[vmem] * 6, out_specs=[vmem] * 6,...  13.2 us
    ppermute x9, waiting for transfers between devices, flip(): lax.ppermute(arr, 'dp', [(i, i ^ bit) for i in range(lax.axis_size('dp'))])  10.8 us
  transfers between devices with their start and end apart: 21, of which 13 were waited for; matrix products, arithmetic and copies ran while one was open for 6% of the time, Pallas kernels for 9%

profile of v3, /device:TPU:0, one launch (start us, length us, event | category | flops | bytes accessed | tf_op | source)
XLA Modules:
  0.0 483.7 jit_solution(12119450447206681056)
XLA Ops:
  13.6 98.2 %exchange.1 = (bf16[1024,768]{1,0:T(8,128)(2,1)}, bf16[512,768]{1,0:T(8,128)(2,1)}, s32[8,8,512]{2,1,0:T(8,128)}, bf16[4,768,768]{2,1,0:T(8,128)(2,1)}, bf16[1,9...) custom-call(s32[16]{0:T(128)} %copy-done.13, bf16[2,128,768]{2,1,0:T(8,128)(2,1)} %content.1, ...), custom_call_target="tpu_custom_call" | custom-call | bytes 67108864 | tf_op jit(solution)/shard_map/exchange/pallas_call | solution.py:301
  120.9 13.2 %project.1 = (bf16[1024,768]{1,0:T(8,128)(2,1)}, bf16[1024,768]{1,0:T(8,128)(2,1)}, bf16[1536,768]{1,0:T(8,128)(2,1)}, bf16[512,768]{1,0:T(8,128)(2,1)}, bf16[51...) custom-call(bf16[4,768,768]{2,1,0:T(8,128)(2,1)} %get-tuple-element.48.w_ref, bf16[1024,768]{1,0:T(8,128)(2,1)} %get-tuple-element.49.ctx_ref, ...), custom_call_target="tpu_custom_call" | custom-call | flops 4831838208 | bytes 20971520 | tf_op jit(solution)/shard_map/project/pallas_call | solution.py:789
  134.1 53.6 %attend_forward.1 = (bf16[512,768]{1,0:T(8,128)(2,1)}, bf16[12,512,1024]{2,1,0:T(8,128)(2,1)}, bf16[1,768,768]{2,1,0:T(8,128)(2,1)}, bf16[2,768,3072]{2,1,0:T(8,128)(2,1)}, bf16[512,768]{1,0:T(8,128)(2,1)}) custom-call(bf16[512,768]{1,0:T(8,128)(2,1)} %get-tuple-element.51.refs_0_.qw_ref, bf16[512,768]{1,0:T(8,128)(2,1)} %get-tuple-element.52.refs_1_.qp_ref, ...), custom_call_target="tpu_custom_call" | custom-call | flops 3221225472 | bytes 16777216 | tf_op jit(solution)/shard_map/attend_forward/pallas_call | solution.py:464
  187.7 34.0 %feed.1 = (bf16[512,768]{1,0:T(8,128)(2,1)}, f32[512,768]{1,0:T(8,128)}, bf16[512,768]{1,0:T(8,128)(2,1)}, bf16[768,768]{1,0:T(8,128)(2,1)}, bf16[2,768,3072]{2,...) custom-call(bf16[2,768,3072]{2,1,0:T(8,128)(2,1)} %get-tuple-element.59.refs_0_, ...), custom_call_target="tpu_custom_call" | custom-call | flops 14495514624 | bytes 37748736 | tf_op jit(solution)/shard_map/feed/pallas_call | solution.py:705
  223.3 1.6 copy.54
  224.9 33.0 %attend_backward.1 = (bf16[512,768]{1,0:T(8,128)(2,1)}, bf16[768,1024]{1,0:T(8,128)(2,1)}, bf16[768,1024]{1,0:T(8,128)(2,1)}, bf16[768,1536]{1,0:T(8,128)(2,1)}, f32[2,768]{1,0:T(2,128)}) custom-call(bf16[12,512,1024]{2,1,0:T(8,128)(2,1)} %get-tuple-element.66.prob_ref, bf16[512,768]{1,0:T(8,128)(2,1)} %get-tuple-element.67.gvec_ref, ...), custom_call_target="tpu_custom_call" | custom-call | flops 6442450944 | bytes 20971520 | tf_op jit(solution)/shard_map/attend_backward/pallas_call | solution.py:551
  257.9 10.3 %weight_grads.1 = bf16[4,768,768]{2,1,0:T(8,128)(2,1)} custom-call(bf16[768,512]{1,0:T(8,128)(2,1)} %bitcast.56, bf16[768,1024]{1,0:T(8,128)(2,1)} %bitcast.53, bf16[768,1536]{1,0:T(8,128)(2,1)} %constant.109.tt_ref, bf16[512,768]{1,0:T(8,128)(2,1)} %get-tuple-element.68.dp_ref, bf16[768,1024]{1,0:T(8,128)(2,1)} %get-tuple-element.69.dk_ref, ...), custom_call_target="tpu_custom_call" | custom-call | flops 4831838208 | bytes 20971520 | tf_op jit(solution)/shard_map/weight_grads/pallas_call | solution.py:824
  269.7 3.2 fusion.1
  274.9 4.2 fusion.11
  279.5 3.5 all-to-all-start
  283.1 36.9 %reduce-scatter.11.cloned.1.call-done = bf16[4,96,768]{2,1,0:T(8,128)(2,1)} async-done(((bf16[4,768,768]{2,1,0:T(8,128)(2,1)}), bf16[4,96,768]{2,1,0:T(8,128)(2,1)}) %reduce-scatter.11.cloned.1.call-update) | async-done | bytes 589840 | tf_op jit(solution)/shard_map/reduce_scatter | solution.py:867
  320.0 1.5 copy.55
  321.5 1.4 reshape.119
  322.9 4.0 add_convert_fusion
  326.8 4.8 all-to-all-start.1
  331.6 68.6 %reduce-scatter.15.cloned.1.call-done = bf16[2,96,3072]{2,1,0:T(8,128)(2,1)} async-done(((bf16[2,768,3072]{2,1,0:T(8,128)(2,1)}), bf16[2,96,3072]{2,1,0:T(8,128)(2,1)}) %reduce-scatter.15.cloned.1.call-update) | async-done | bytes 1179664 | tf_op jit(solution)/shard_map/reduce_scatter | solution.py:867
  401.5 1.5 collective-permute-start.4
  403.0 2.4 collective-permute-done.4
  405.4 1.5 collective-permute-start.5
  406.9 2.4 collective-permute-done.5
  409.3 1.5 collective-permute-start.6
  410.8 1.5 collective-permute-start.9
  412.3 2.1 collective-permute-done.9
  414.5 1.5 collective-permute-start.10
  415.9 2.2 collective-permute-done.10
  418.7 3.1 collective-permute-done.11
  421.8 2.4 collective-permute-start.12
  424.2 2.2 collective-permute-done.12
  426.4 2.4 collective-permute-start.7
  430.1 1.4 collective-permute-done.7
  437.5 7.7 %reduce-scatter.19.cloned.1.call-done = bf16[192,384]{1,0:T(8,128)(2,1)} async-done(((bf16[768,384]{1,0:T(8,128)(2,1)}), bf16[192,384]{1,0:T(8,128)(2,1)}) %reduce-scatter.19.cloned.1.call-update) | async-done | bytes 147472
  447.2 27.9 %reduce-scatter.17.cloned.1.call-done = bf16[2,96,768]{2,1,0:T(8,128)(2,1)} async-done(((bf16[2,96,3072]{2,1,0:T(8,128)(2,1)}), bf16[2,96,768]{2,1,0:T(8,128)(2,1)}) %reduce-scatter.17.cloned.1.call-update) | async-done | bytes 294928 | tf_op jit(solution)/shard_map/reduce_scatter | solution.py:868
  (110 shorter events, 30.5 us)
Async XLA Ops:
  7.2 107.0 %copy-start.5 = (f32[12,64]{1,0:T(8,128)S(1)}, f32[12,64]{1,0:T(8,128)}, u32[]{:S(2)}) copy-start(f32[12,64]{1,0:T(8,128)} %param.43) | copy-start | bytes 9220
  7.2 107.6 %copy-start.6 = (f32[12,64]{1,0:T(8,128)S(1)}, f32[12,64]{1,0:T(8,128)}, u32[]{:S(2)}) copy-start(f32[12,64]{1,0:T(8,128)} %param.44) | copy-start | bytes 9220
  7.2 108.3 %copy-start.8 = (f32[768]{0:T(1024)S(1)}, f32[768]{0:T(1024)}, u32[]{:S(2)}) copy-start(f32[768]{0:T(1024)} %param.42) | copy-start | bytes 9220
  7.2 108.9 %copy-start.9 = (f32[768]{0:T(1024)S(1)}, f32[768]{0:T(1024)}, u32[]{:S(2)}) copy-start(f32[768]{0:T(1024)} %param.45) | copy-start | bytes 9220
  7.2 109.4 %copy-start.10 = (f32[768]{0:T(1024)S(1)}, f32[768]{0:T(1024)}, u32[]{:S(2)}) copy-start(f32[768]{0:T(1024)} %param.46) | copy-start | bytes 9220
  7.2 110.0 %copy-start.11 = (f32[768]{0:T(1024)S(1)}, f32[768]{0:T(1024)}, u32[]{:S(2)}) copy-start(f32[768]{0:T(1024)} %param.47) | copy-start | bytes 9220
  7.3 110.6 %copy-start.12 = (f32[768]{0:T(1024)S(1)}, f32[768]{0:T(1024)}, u32[]{:S(2)}) copy-start(f32[768]{0:T(1024)} %param.48) | copy-start | bytes 9220
  7.3 265.7 %reduce-scatter.13.cloned.1.call-start = ((), (), s32[]{:S(2)}) async-start(), calls=%async_computation.9 | async-start | bytes 1327104 | tf_op jit(solution)/shard_map/reduce_scatter | solution.py:867
  8.1 4.9 %copy-start.13 = (s32[16]{0:T(128)}, s32[16]{0:T(128)S(1)}, u32[]{:S(2)}) copy-start(s32[16]{0:T(128)S(1)} %select_reduce_fusion.slot_ref) | copy-start | bytes 196
  187.7 34.1 %copy-start.1 = (bf16[512,768]{1,0:T(8,128)(2,1)S(1)}, bf16[512,768]{1,0:T(8,128)(2,1)}, u32[]{:S(2)}) copy-start(bf16[512,768]{1,0:T(8,128)(2,1)} %get-tuple-element.62.refs_3_) | copy-start | bytes 2359300
  221.7 98.3 %reduce-scatter.11.cloned.1.call-start = ((), (), s32[]{:S(2)}) async-start(), calls=%async_computation.8 | async-start | bytes 5308416 | tf_op jit(solution)/shard_map/reduce_scatter | solution.py:867
  268.2 132.0 %reduce-scatter.15.cloned.1.call-start = ((), (), s32[]{:S(2)}) async-start(), calls=%async_computation.10 | async-start | bytes 10616832 | tf_op jit(solution)/shard_map/reduce_scatter | solution.py:867
  269.0 166.0 %reduce-scatter.21.cloned.1.call-start = ((), (), s32[]{:S(2)}) async-start(), calls=%async_computation.13 | async-start | bytes 245760
  279.1 43.8 %collective-permute-start.1 = (bf16[512,768]{1,0:T(8,128)(2,1)}, bf16[512,768]{1,0:T(8,128)(2,1)}, u32[]{:S(2)}, u32[]{:S(2)}) collective-permute-start(bf16[512,768]{1,0:T(8,128)(2,1)} %get-tuple-element.100), channel_id=1, source_target_pairs={{0,4},{4,0},{8,12},{12,8},{16,20},{20,16},{24,28},{28,24},{1,5},{5... | collective-permute-start | bytes 2359304 | tf_op jit(solution)/shard_map/ppermute | solution.py:849
  279.5 47.3 %all-to-all-start = ((bf16[4,128,768]{2,1,0:T(8,128)(2,1)}), bf16[4,128,768]{2,1,0:T(8,128)(2,1)S(1)}, u32[]{:S(2)}, u32[]{:S(2)}) async-start(bf16[4,128,768]{2,1,0:T(8,128)(2,1)} %bitcast.8), calls=%async_computation | async-start | bytes 1572864 | tf_op jit(solution)/shard_map/all_to_all | solution.py:932
  283.0 162.1 %reduce-scatter.19.cloned.1.call-start = ((), (), s32[]{:S(2)}) async-start(), calls=%async_computation.12 | async-start | bytes 737280
  326.8 73.4 %copy-start.3 = (f32[1,3072]{1,0:T(1,128)S(1)}, f32[1,3072]{1,0:T(1,128)}, u32[]{:S(2)}) copy-start(f32[1,3072]{1,0:T(1,128)} %get-tuple-element.74) | copy-start | bytes 36868
  326.8 80.1 %copy-start.7 = (f32[2,768]{1,0:T(2,128)S(1)}, f32[2,768]{1,0:T(2,128)}, u32[]{:S(2)}) copy-start(f32[2,768]{1,0:T(2,128)} %get-tuple-element.76) | copy-start | bytes 18436
  326.8 106.1 %all-to-all-start.1 = ((bf16[4,128,768]{2,1,0:T(8,128)(2,1)}), bf16[4,128,768]{2,1,0:T(8,128)(2,1)S(1)}, u32[]{:S(2)}, u32[]{:S(2)}) async-start(bf16[4,128,768]{2,1,0:T(8,128)(2,1)} %bitcast.12), calls=%async_computation.1 | async-start | bytes 1572864 | tf_op jit(solution)/shard_map/all_to_all | solution.py:932
  331.6 143.5 %reduce-scatter.17.cloned.1.call-start = ((), (), s32[]{:S(2)}) async-start(), calls=%async_computation.11 | async-start | bytes 1474560 | tf_op jit(solution)/shard_map/reduce_scatter | solution.py:868
  400.3 1.3 collective-permute-start.3
  401.5 3.9 collective-permute-start.4
  405.4 3.9 collective-permute-start.5
  406.9 3.9 collective-permute-start.8
  409.3 17.0 %collective-permute-start.6 = (f32[6912]{0:T(1024)S(1)}, f32[6912]{0:T(1024)S(1)}, u32[]{:S(2)}, u32[]{:S(2)}) collective-permute-start(f32[6912]{0:T(1024)S(1)} %add.136), channel_id=1, source_target_pairs={{0,1},{1,0},{2,3},{3,2},{4,5},{5,4},{6,7},{7,6},{8,9},{9,8},{10,11... | collective-permute-start | bytes 82952 | tf_op jit(solution)/shard_map/ppermute | solution.py:853
  410.8 3.7 collective-permute-start.9
  414.5 3.6 collective-permute-start.10
  418.1 3.7 collective-permute-start.11
  421.8 4.5 collective-permute-start.12
  426.4 5.2 %collective-permute-start.7 = (f32[6912]{0:T(1024)S(1)}, f32[6912]{0:T(1024)S(1)}, u32[]{:S(2)}, u32[]{:S(2)}) collective-permute-start(f32[6912]{0:T(1024)S(1)} %add.137), channel_id=1, source_target_pairs={{0,2},{1,3},{2,0},{3,1},{4,6},{5,7},{6,4},{7,5},{8,10},{9,11},{10,... | collective-permute-start | bytes 82952 | tf_op jit(solution)/shard_map/ppermute | solution.py:853
  432.2 1.8 collective-permute-start
  432.9 3.6 collective-permute-start.2
  (4 other events, 8.4 us)
Sparse Core Ops, SparseCore 0:
  221.8 34.5 reduce-scatter.12
  268.3 51.5 reduce-scatter.10
  323.5 76.6 reduce-scatter.14
  402.9 19.6 reduce-scatter.20
  424.8 20.3 reduce-scatter.18
  447.3 27.6 reduce-scatter.16

commit v4 on v3

--- a/solution.py
+++ b/solution.py
@@ -153,6 +153,264 @@
             self.copy(i).wait_recv()
         for i in range(14):
             self.copy(i).wait_send()
+
+
+def chip_bits(j):
+    return (XBIT if j & 1 else 0) | (YBIT if j & 2 else 0)
+
+
+def add_into(dst, src):
+    def run(i, carry):
+        at = pl.ds(pl.multiple_of(i * 16, 16), 16)
+        dst[:, at, :] = (dst[:, at, :].astype(F32) + src[:, at, :].astype(F32)).astype(BF)
+        return carry
+
+    lax.fori_loop(0, dst.shape[1] // 16, run, 0)
+
+
+class Reduce:
+    def __init__(self, place, sources, scratch, out):
+        self.place, self.sources, self.out = place, sources, out
+        self.total, self.pair, self.near, self.far, self.quarter, self.stage = scratch[:6]
+        self.pair_send, self.pair_recv, self.load, self.send, self.recv, self.z_send, self.z_recv = scratch[6:]
+        self.rows = self.total.shape[2]
+
+    @staticmethod
+    def scratch(count, n, rows, cols):
+        part = cols // 4
+        dma = lambda k: pltpu.SemaphoreType.DMA((k,))
+        return [
+            pltpu.VMEM((n, 4, rows, cols), BF),
+            pltpu.VMEM((n, 4, rows, cols), BF),
+            pltpu.VMEM((n, 2, 2, rows // 2, cols), BF),
+            pltpu.VMEM((n, 2, rows // 2, cols), BF),
+            pltpu.VMEM((4, n, rows, part), BF),
+            pltpu.VMEM((4, n, rows, part) if part % 128 else (8, 128), BF),
+            dma(4 * count),
+            dma(4 * count),
+            dma(4 * count),
+            dma(6),
+            dma(6),
+            dma(3),
+            dma(1),
+        ]
+
+    def pair_copies(self, j):
+        place, rows = self.place, self.rows
+        copies, at = [], 0
+        for i, src in enumerate(self.sources):
+            slot, n = len(self.sources) * j + i, src.shape[0]
+            block = lambda bits: src.at[:, pl.ds(pl.multiple_of(place.dp(bits) * rows, 16), rows), :]
+            remote = push(
+                block(chip_bits(j) | CORE),
+                self.pair.at[at : at + n, j],
+                self.pair_send.at[slot],
+                self.pair_recv.at[slot],
+                place.dp(CORE),
+                place.z,
+            )
+            local = pltpu.make_async_copy(
+                block(chip_bits(j)), self.total.at[at : at + n, j], self.load.at[slot]
+            )
+            copies.append((remote, local))
+            at += n
+        return copies
+
+    def half(self, j, h):
+        size = self.rows // 2
+        return self.total.at[:, j, h * size : (h + 1) * size, :]
+
+    MOVES = ((3, 0, XBIT, 1), (3, 1, YBIT, 1), (1, 0, XBIT, 0), (2, 1, YBIT, 0), (2, 0, YBIT, 0), (1, 1, XBIT, 1))
+
+    def move(self, i):
+        j, h, to, where = self.MOVES[i]
+        dst = self.near.at[:, h, where] if i < 4 else self.far.at[:, where]
+        place = self.place
+        return push(self.half(j, h), dst, self.send.at[i], self.recv.at[i], place.dp(to), place.z)
+
+    def z_copy(self, k):
+        place, part = self.place, self.quarter.shape[3]
+        to = place.up(k)
+        if part % 128:
+            src = self.stage.at[to]
+        else:
+            src = self.total.at[:, 0, :, pl.ds(pl.multiple_of(to * part, 128), part)]
+        dst = self.quarter.at[place.z]
+        if k == 0:
+            return pltpu.make_async_copy(src, dst, self.z_recv.at[0])
+        return push(src, dst, self.z_send.at[k - 1], self.z_recv.at[0], place.d, to)
+
+    def begin(self):
+        for j in (3, 1, 2, 0):
+            for remote, local in self.pair_copies(j):
+                remote.start()
+                local.start()
+
+    def pairs(self):
+        for j, moves in ((3, (0, 1)), (1, (2,)), (2, (3,)), (0, ())):
+            for remote, local in self.pair_copies(j):
+                local.wait()
+                remote.wait_recv()
+            add_into(self.total.at[:, j], self.pair.at[:, j])
+            for i in moves:
+                self.move(i).start()
+
+    def middle(self):
+        for i, j, h, where, more in ((0, 2, 0, 1, 4), (1, 1, 1, 1, 5), (2, 0, 0, 0, None), (3, 0, 1, 0, None)):
+            self.move(i).wait_recv()
+            add_into(self.half(j, h), self.near.at[:, h, where])
+            if more is not None:
+                self.move(more).start()
+
+    def late(self):
+        for i, h in ((4, 0), (5, 1)):
+            self.move(i).wait_recv()
+            add_into(self.half(0, h), self.far.at[:, h])
+        part = self.quarter.shape[3]
+        if part % 128:
+            for k in range(4):
+                for m in range(self.total.shape[0]):
+                    self.stage[k, m] = self.total[m, 0, :, k * part : (k + 1) * part]
+        for k in (2, 1, 3, 0):
+            self.z_copy(k).start()
+
+    def end(self):
+        settle(self.quarter, self.z_recv.at[0])
+        parts = [self.quarter[k].astype(F32) for k in range(4)]
+        self.out[...] = (parts[0] + parts[1]) + (parts[2] + parts[3])
+        for j in range(4):
+            for remote, _ in self.pair_copies(j):
+                remote.wait_send()
+        for i in range(6):
+            self.move(i).wait_send()
+        for k in range(1, 4):
+            self.z_copy(k).wait_send()
+
+
+class Homeward:
+    def __init__(self, place, src, home, send, recv):
+        self.place, self.src, self.home, self.send, self.recv = place, src, home, send, recv
+        self.part = home.shape[2]
+
+    def act(self, what):
+        place, part = self.place, self.part
+        for k in (2, 1, 3, 0):
+            to, dp = place.up(k), place.d - place.core + lax.div(place.z, 2)
+            src = self.src.at[pl.ds(pl.multiple_of(to * part, 16), part), :]
+            dst = self.home.at[place.core, lax.rem(place.z, 2)]
+            here = jnp.logical_and(dp == place.d, to == place.z)
+            remote = push(src, dst, self.send.at[k], self.recv, dp, to)
+            if what == "start":
+                pl.when(here)(pltpu.make_async_copy(src, dst, self.recv).start)
+                pl.when(jnp.logical_not(here))(remote.start)
+            else:
+                pl.when(jnp.logical_not(here))(remote.wait_send)
+
+    def start(self):
+        self.act("start")
+
+    def end(self):
+        settle(self.home, self.recv)
+        self.act("wait")
+
+
+def pair_and_z(place):
+    return [(place.dp(r), place.up(k)) for k in range(4) for r in (0, CORE) if r or k]
+
+
+def near_partners(place):
+    return pair_and_z(place) + [(place.dp(r), place.z) for r in (XBIT, YBIT)]
+
+
+def finish_kernel(g_ref, go_ref, base_ref, ctx_ref, small_ref, *refs):
+    grads_ref, home_ref, sums_ref = refs[:3]
+    stream, partner, slots, part_sum, chips = refs[3:8]
+    home_send, slot_send, chip_send, one_send, recv = refs[8:13]
+    place = Place()
+    d, z, core = place.d, place.z, place.core
+    greet(near_partners(place) + [(place.dp(XBIT | YBIT), z)])
+    reduce = Reduce(place, (g_ref, go_ref), refs[13:], grads_ref)
+    swap = push(ctx_ref, partner, one_send.at[0], recv.at[0], place.dp(CORE), z)
+    swap.start()
+    reduce.begin()
+    slot_copies = []
+    others = [(r, k) for k in range(4) for r in (0, CORE) if r or k]
+    for i, (r, k) in enumerate(others):
+        copy = push(small_ref, slots.at[4 * core + z], slot_send.at[i], recv.at[1], place.dp(r), place.up(k))
+        copy.start()
+        slot_copies.append(copy)
+    pltpu.make_async_copy(small_ref, slots.at[4 * core + z], recv.at[1]).start()
+
+    home = Homeward(place, stream, home_ref, home_send, recv.at[2])
+    swap.wait()
+    block = 64
+
+    def add_partner(i, carry):
+        at = pl.ds(pl.multiple_of(i * block, block), block)
+        more = jnp.where(core == 0, partner[at, :].astype(F32), 0.0)
+        stream[at, :] = (base_ref[at, :] + more).astype(BF)
+        return carry
+
+    lax.fori_loop(0, stream.shape[0] // block, add_partner, 0)
+    home.start()
+    reduce.pairs()
+
+    settle(slots, recv.at[1])
+    total = slots[0]
+    for i in range(1, 8):
+        total = total + slots[i]
+    part_sum[...] = total
+    chip = lax.div(d, 2)
+    chip_copies = []
+    for i, r in enumerate((XBIT, YBIT, XBIT | YBIT)):
+        copy = push(part_sum, chips.at[chip], chip_send.at[i], recv.at[3], place.dp(r), z)
+        copy.start()
+        chip_copies.append(copy)
+    pltpu.make_async_copy(part_sum, chips.at[chip], recv.at[3]).start()
+
+    reduce.middle()
+    settle(chips, recv.at[3])
+    sums_ref[...] = (chips[0] + chips[1]) + (chips[2] + chips[3])
+    reduce.late()
+    reduce.end()
+    home.end()
+    for copy in slot_copies + chip_copies:
+        copy.wait_send()
+
+
+def finish(grads, g_out, base, ctx, small):
+    n, width, cols = grads.shape
+    rows, total = width // 8, base.shape[0]
+    vmem = pl.BlockSpec(memory_space=pltpu.VMEM)
+    dma = lambda k: pltpu.SemaphoreType.DMA((k,))
+    return pl.pallas_call(
+        finish_kernel,
+        in_specs=[ANY_SPEC] * 2 + [vmem] * 3,
+        out_specs=[vmem, ANY_SPEC, vmem],
+        out_shape=[
+            jax.ShapeDtypeStruct((n + 1, rows, cols // 4), F32),
+            jax.ShapeDtypeStruct((2, 2, total // 4, width), BF),
+            jax.ShapeDtypeStruct(small.shape, F32),
+        ],
+        scratch_shapes=[
+            pltpu.VMEM((total, width), BF),
+            pltpu.VMEM((total, width), BF),
+            pltpu.VMEM((8,) + small.shape, F32),
+            pltpu.VMEM(small.shape, F32),
+            pltpu.VMEM((4,) + small.shape, F32),
+            dma(4),
+            dma(7),
+            dma(3),
+            dma(1),
+            dma(4),
+        ]
+        + Reduce.scratch(2, n + 1, rows, cols),
+        compiler_params=pltpu.CompilerParams(
+            collective_id=4, has_side_effects=True, vmem_limit_bytes=LIMIT
+        ),
+        cost_estimate=pl.CostEstimate(flops=0, bytes_accessed=64 << 20, transcendentals=0),
+        name="finish",
+    )(grads, g_out, base, ctx, small)
 
 
 def exchange_kernel(
@@ -476,7 +734,54 @@
     )(qw, qp, keys, values, rel, thr, key_rank, *wires)
 
 
-def attend_backward_kernel(
+def attend_backward_kernel(block, wired, *refs):
+    if not wired:
+        attend_backward_step(block, *refs)
+        return
+    ins, (g_ud, src) = refs[:7], refs[7:9]
+    outs, (grads_ref, home_ref) = refs[9:14], refs[14:16]
+    rel_acc, home_send, home_recv = refs[16:19]
+    step, steps = pl.program_id(0), pl.num_programs(0)
+    place = Place()
+    count = len(refs[19:]) // 2
+    reduces = [
+        Reduce(place, (g_ud.at[m : m + 1],), refs[19 + m * count : 19 + (m + 1) * count], grads_ref.at[m : m + 1])
+        for m in range(2)
+    ]
+    home = Homeward(place, src, home_ref, home_send, home_recv.at[0])
+
+    @pl.when(step == 0)
+    def _():
+        greet(near_partners(place))
+        for reduce in reduces:
+            reduce.begin()
+        home.start()
+
+    @pl.when(step == 2)
+    def _():
+        reduces[0].pairs()
+
+    @pl.when(step == 3)
+    def _():
+        reduces[1].pairs()
+
+    @pl.when(step == 5)
+    def _():
+        reduces[0].middle()
+
+    attend_backward_step(block, *ins, *outs, rel_acc)
+
+    @pl.when(step == steps - 1)
+    def _():
+        reduces[0].late()
+        reduces[1].middle()
+        reduces[1].late()
+        reduces[0].end()
+        reduces[1].end()
+        home.end()
+
+
+def attend_backward_step(
     block,
     prob_ref,
     gvec_ref,
@@ -543,38 +848,54 @@
     bias_ref[1:2, :] = pos_sum
 
 
-def attend_backward(prob, gvec, qw, qp, keys, values, rel, block):
+def attend_backward(prob, gvec, qw, qp, keys, values, rel, block, wires=()):
     rows, width = qw.shape
     klen, span = keys.shape[0], rel.shape[0]
     col = lambda count: pl.BlockSpec((count, PAIR), lambda p: (0, p))
     rowb = lambda count: pl.BlockSpec((PAIR, count), lambda p: (p, 0))
+    in_specs = [
+        pl.BlockSpec((2, rows, klen), lambda p: (p, 0, 0)),
+        col(rows),
+        col(rows),
+        col(rows),
+        col(klen),
+        col(klen),
+        col(span),
+    ]
+    out_specs = [col(rows), rowb(klen), rowb(klen), rowb(span), col(2)]
+    out_shape = [
+        jax.ShapeDtypeStruct((rows, width), BF),
+        jax.ShapeDtypeStruct((width, klen), BF),
+        jax.ShapeDtypeStruct((width, klen), BF),
+        jax.ShapeDtypeStruct((width, span), BF),
+        jax.ShapeDtypeStruct((2, width), F32),
+    ]
+    scratch = [pltpu.VMEM((PAIR, span), F32)]
+    params = dict(vmem_limit_bytes=LIMIT)
+    if wires:
+        inner, mine = wires[0].shape[2], width // 8
+        in_specs += [ANY_SPEC, ANY_SPEC]
+        out_specs += [pl.BlockSpec(memory_space=pltpu.VMEM), ANY_SPEC]
+        out_shape += [
+            jax.ShapeDtypeStruct((2, mine, inner // 4), F32),
+            jax.ShapeDtypeStruct((2, 2, rows // 4, width), BF),
+        ]
+        scratch += [pltpu.SemaphoreType.DMA((4,)), pltpu.SemaphoreType.DMA((1,))]
+        scratch += 2 * Reduce.scratch(1, 1, mine, inner)
+        params.update(collective_id=3, has_side_effects=True)
     return pl.pallas_call(
-        functools.partial(attend_backward_kernel, block),
+        functools.partial(attend_backward_kernel, block, bool(wires)),
         grid=(width // PAIR,),
-        in_specs=[
-            pl.BlockSpec((2, rows, klen), lambda p: (p, 0, 0)),
-            col(rows),
-            col(rows),
-            col(rows),
-            col(klen),
-            col(klen),
-            col(span),
-        ],
-        out_specs=[col(rows), rowb(klen), rowb(klen), rowb(span), col(2)],
-        out_shape=[
-            jax.ShapeDtypeStruct((rows, width), BF),
-            jax.ShapeDtypeStruct((width, klen), BF),
-            jax.ShapeDtypeStruct((width, klen), BF),
-            jax.ShapeDtypeStruct((width, span), BF),
-            jax.ShapeDtypeStruct((2, width), F32),
-        ],
-        scratch_shapes=[pltpu.VMEM((PAIR, span), F32)],
-        compiler_params=pltpu.CompilerParams(vmem_limit_bytes=LIMIT),
+        in_specs=in_specs,
+        out_specs=out_specs,
+        out_shape=out_shape,
+        scratch_shapes=scratch,
+        compiler_params=pltpu.CompilerParams(**params),
         cost_estimate=pl.CostEstimate(
             flops=16 * rows * klen * width, bytes_accessed=20 << 20, transcendentals=0
         ),
         name="attend_backward",
-    )(prob, gvec, qw, qp, keys, values, rel)
+    )(prob, gvec, qw, qp, keys, values, rel, *wires)
 
 
 def norm_parts(value):
@@ -849,33 +1170,9 @@
     return lax.ppermute(arr, "dp", [(i, i ^ bit) for i in range(lax.axis_size("dp"))])
 
 
-def flip_z(arr, bit):
-    return lax.ppermute(arr, "tensor", [(i, i ^ bit) for i in range(lax.axis_size("tensor"))])
-
-
-def by_bits(parts, bits):
-    step = 1
-    for bit in bits:
-        parts = [
-            jnp.where(bit == 1, parts[i ^ step], parts[i]) for i in range(len(parts))
-        ]
-        step *= 2
-    return parts
-
-
 def scatter_sum(grads):
     mine = lax.psum_scatter(grads, "dp", scatter_dimension=1, tiled=True)
     return lax.psum_scatter(mine, "tensor", scatter_dimension=2, tiled=True).astype(F32)
-
-
-def sum_all(value):
-    if lax.axis_size("dp") != 8:
-        return lax.psum(value, ("dp", "tensor"))
-    for bit in (1, 2, 4):
-        value = value + flip(value, bit)
-    for bit in (1, 2):
-        value = value + flip_z(value, bit)
-    return value
 
 
 def body(
@@ -1017,27 +1314,45 @@
         row(second_gain),
         row(second_shift),
     )
-    content_out, query_out = from_unit(out)
-    grad_up, grad_down = scatter_sum(g_ud)
-    (grad_out,) = scatter_sum(g_out[None])
-    early = sum_all(jnp.concatenate([g_upb.reshape(-1), small[:5].reshape(-1)]))
-
-    d_proj, dk_t, dv_t, drel_t, biases = attend_backward(
-        prob, g_vec, q_word, q_pos, keys, values, rel, block
-    )
-    late = sum_all(biases)
+    backward = (prob, g_vec, q_word, q_pos, keys, values, rel, block)
+    if groups == 8:
+        d_proj, dk_t, dv_t, drel_t, biases, (grad_up, grad_down), outs = attend_backward(
+            *backward, (g_ud, out)
+        )
+        content_out, query_out = outs[0], outs[1]
+    else:
+        d_proj, dk_t, dv_t, drel_t, biases = attend_backward(*backward)
+        content_out, query_out = from_unit(out)
+        grad_up, grad_down = scatter_sum(g_ud)
+    small = jnp.concatenate([g_upb.reshape(-1), small[:5].reshape(-1), biases.reshape(-1)])
     d_context = tt(dk_t[:, mem_total:], weights[0]) + tt(dv_t[:, mem_total:], weights[1])
-    partner = swap(d_context.astype(BF))
     d_stream = d_mixed + nt(d_proj, weights[2])
-    d_stream = d_stream + jnp.where(lead, d_context + partner.astype(F32), 0.0)
-    content_grad, query_grad = from_unit(d_stream.astype(BF))
-    grad_key, grad_value, grad_query, grad_pos = scatter_sum(
-        weight_grads(
-            jnp.transpose(stream), jnp.transpose(context), jnp.transpose(table), d_proj, dk_t, dv_t, drel_t
-        )
+    d_stream = d_stream + jnp.where(lead, d_context, 0.0)
+    grads = weight_grads(
+        jnp.transpose(stream),
+        jnp.transpose(context),
+        jnp.transpose(table),
+        d_proj,
+        dk_t,
+        dv_t,
+        drel_t,
     )
     inner = up_bias.shape[0]
-    rest = early[inner:].reshape(5, width)
+    if groups == 8:
+        size = small.shape[0]
+        small = jnp.pad(small, (0, -size % 1024)).reshape(-1, 128)
+        grads, homes, small = finish(grads, g_out[None], d_stream, d_context.astype(BF), small)
+        grad_key, grad_value, grad_query, grad_pos, grad_out = grads
+        content_grad, query_grad = homes[0], homes[1]
+        small = small.reshape(-1)[:size]
+    else:
+        partner = swap(d_context.astype(BF)).astype(F32)
+        d_stream = d_stream + jnp.where(lead, partner, 0.0)
+        content_grad, query_grad = from_unit(d_stream.astype(BF))
+        grad_key, grad_value, grad_query, grad_pos = scatter_sum(grads)
+        (grad_out,) = scatter_sum(g_out[None])
+        small = lax.psum(small, ("dp", "tensor"))
+    rest = small[inner:].reshape(7, width)
     return (
         content_out,
         query_out,
@@ -1049,11 +1364,11 @@
         grad_pos,
         grad_out,
         grad_up,
-        early[:inner],
+        small[:inner],
         grad_down,
         rest[0],
-        late[0].reshape(HEADS, DH),
-        late[1].reshape(HEADS, DH),
+        rest[5].reshape(HEADS, DH),
+        rest[6].reshape(HEADS, DH),
         rest[1],
         rest[2],
         rest[3],

time: 485 us -> 379 us (0.78)
  waiting for transfers between devices: 159 us -> 0 us
  Pallas kernels: 242 us -> 340 us
  starting transfers between devices: 22.3 us -> 0 us
  between operations: 17.8 us -> 4.26 us
    reduce_scatter x4 -> x0, waiting for transfers between devices: 133 us -> none  [the longest x3 106 us: scatter_sum(): mine = lax.psum_scatter(grads, 'dp', scatter_dimension=1, tiled=True)]
    pallas_call x1 -> x2, Pallas kernels: 33 us -> 131 us  [the longest x1 75.3 us: attend_backward(): pl.pallas_call(functools.partial(attend_backward_kernel, block, bool(wire...]
    ppermute x13 -> x0, waiting for transfers between devices: 17.5 us -> none  [the longest x9 10.8 us: flip(): lax.ppermute(arr, 'dp', [(i, i ^ bit) for i in range(lax.axis_size('dp'))])]
    ppermute x13 -> x0, starting transfers between devices: 13.9 us -> none  [the longest x9 7.05 us: flip(): lax.ppermute(arr, 'dp', [(i, i ^ bit) for i in range(lax.axis_size('dp'))])]
    unnamed x8 -> x0, waiting for transfers between devices: 8.42 us -> none
    all_to_all x2 -> x0, starting transfers between devices: 8.26 us -> none  [from_unit(): lax.all_to_all(both, 'tensor', split_axis=0, concat_axis=0, tiled=True)]
    unnamed x38 -> x40, local copies, waits for them, and re-layouts: 8.64 us -> 1.22 us
  transfers between devices with their start and end apart: 21 -> 0, of which waited for: 13 -> 0; matrix products, arithmetic and copies ran while one was open for 6% -> 0% of each run, Pallas kernels for 9% -> 0%
where the time goes in v4:
time: 379 us; the launch traced here: 376 us
  Pallas kernels  340 us (90%)
  local copies, waits for them, and re-layouts  19.1 us (5%)
  matrix products  9.03 us (2%)
  between operations  4.26 us (1%)
  other arithmetic  4.12 us (1%)
    pallas_call x1, Pallas kernels, exchange(): pl.pallas_call(exchange_kernel, in_specs=[SMEM_SPEC] + [ANY_SPEC] * 3 + [...  98.2 us
    pallas_call x1, Pallas kernels, attend_backward(): pl.pallas_call(functools.partial(attend_backward_kernel, block, bool(wire...  75.3 us
    pallas_call x1, Pallas kernels, finish(): pl.pallas_call(finish_kernel, in_specs=[ANY_SPEC] * 2 + [vmem] * 3, out_s...  55.3 us
    pallas_call x1, Pallas kernels, attend_forward(): pl.pallas_call(functools.partial(attend_forward_kernel, block, bool(wires...  53.7 us
    pallas_call x1, Pallas kernels, feed(): pl.pallas_call(functools.partial(feed_kernel, steps), grid=(2 * steps,),...  33.8 us
    pallas_call x1, Pallas kernels, project(): pl.pallas_call(project_kernel, in_specs=[vmem] * 6, out_specs=[vmem] * 6,...  13.2 us
    pallas_call x1, Pallas kernels, weight_grads(): pl.pallas_call(weight_grads_kernel, grid=(width // chunk,), in_specs=[who...  10.2 us

profile of v4, /device:TPU:0, one launch (start us, length us, event | category | flops | bytes accessed | tf_op | source)
XLA Modules:
  0.0 376.1 jit_solution(1894177937331915449)
XLA Ops:
  0.7 0.8 select_reduce_fusion.slot_ref
  4.7 0.7 pad.8
  5.4 0.7 add_bitcast_fusion.1
  6.4 0.6 copy-done.8
  6.9 98.2 %exchange.1 = (bf16[1024,768]{1,0:T(8,128)(2,1)}, bf16[512,768]{1,0:T(8,128)(2,1)}, s32[8,8,512]{2,1,0:T(8,128)}, bf16[4,768,768]{2,1,0:T(8,128)(2,1)}, bf16[1,9...) custom-call(s32[16]{0:T(128)} %copy-done.19, bf16[2,128,768]{2,1,0:T(8,128)(2,1)} %content.1, ...), custom_call_target="tpu_custom_call" | custom-call | bytes 67108864 | tf_op jit(solution)/shard_map/exchange/pallas_call | solution.py:559
  105.2 0.8 slice.87
  107.2 0.7 add_bitcast_fusion
  108.0 0.6 compare_select_fusion.1
  108.6 0.6 pad_add_fusion
  109.2 0.9 copy.49.refs_5_
  110.1 0.7 reshape.115.wb_ref
  110.7 0.7 reshape.116.pb_ref
  111.4 13.2 %project.1 = (bf16[1024,768]{1,0:T(8,128)(2,1)}, bf16[1024,768]{1,0:T(8,128)(2,1)}, bf16[1536,768]{1,0:T(8,128)(2,1)}, bf16[512,768]{1,0:T(8,128)(2,1)}, bf16[51...) custom-call(bf16[4,768,768]{2,1,0:T(8,128)(2,1)} %get-tuple-element.53.w_ref, bf16[1024,768]{1,0:T(8,128)(2,1)} %get-tuple-element.54.ctx_ref, ...), custom_call_target="tpu_custom_call" | custom-call | flops 4831838208 | bytes 20971520 | tf_op jit(solution)/shard_map/project/pallas_call | solution.py:1110
  124.7 53.7 %attend_forward.1 = (bf16[512,768]{1,0:T(8,128)(2,1)}, bf16[12,512,1024]{2,1,0:T(8,128)(2,1)}, bf16[1,768,768]{2,1,0:T(8,128)(2,1)}, bf16[2,768,3072]{2,1,0:T(8,128)(2,1)}, bf16[512,768]{1,0:T(8,128)(2,1)}) custom-call(bf16[512,768]{1,0:T(8,128)(2,1)} %get-tuple-element.56.refs_0_.refs_2_, bf16[512,768]{1,0:T(8,128)(2,1)} %get-tuple-element.57.refs_1_.refs_3_, ...), custom_call_target="tpu_custom_call" | custom-call | flops 3221225472 | bytes 16777216 | tf_op jit(solution)/shard_map/attend_forward/pallas_call | solution.py:722
  181.3 33.8 %feed.1 = (bf16[512,768]{1,0:T(8,128)(2,1)}, f32[512,768]{1,0:T(8,128)}, bf16[512,768]{1,0:T(8,128)(2,1)}, bf16[768,768]{1,0:T(8,128)(2,1)}, bf16[2,768,3072]{2,...) custom-call(bf16[2,768,3072]{2,1,0:T(8,128)(2,1)} %get-tuple-element.65.refs_0_, ...), custom_call_target="tpu_custom_call" | custom-call | flops 14495514624 | bytes 37748736 | tf_op jit(solution)/shard_map/feed/pallas_call | solution.py:1026
  215.1 75.3 %attend_backward.1 = (bf16[512,768]{1,0:T(8,128)(2,1)}, bf16[768,1024]{1,0:T(8,128)(2,1)}, bf16[768,1024]{1,0:T(8,128)(2,1)}, bf16[768,1536]{1,0:T(8,128)(2,1)},...) custom-call(bf16[12,512,1024]{2,1,0:T(8,128)(2,1)} %get-tuple-element.64.refs_0_, ...), custom_call_target="tpu_custom_call" | custom-call | flops 6442450944 | bytes 20971520 | tf_op jit(solution)/shard_map/attend_backward/pallas_call | solution.py:886
  290.3 0.7 reshape.125
  291.0 0.6 fusion.9.small_ref
  291.7 2.5 fusion.1
  294.1 3.2 fusion.10
  297.3 3.4 select_add_fusion.base_ref
  300.7 1.1 copy.50
  302.4 1.6 copy.51
  304.0 10.2 %weight_grads.1.g_ref = bf16[4,768,768]{2,1,0:T(8,128)(2,1)} custom-call(bf16[768,512]{1,0:T(8,128)(2,1)} %bitcast.65, bf16[768,1024]{1,0:T(8,128)(2,1)} %bitcast.63, bf16[768,1536]{1,0:T(8,128)(2,1)} %constant.112.tt_ref, bf16[512,768]{1,0:T(8,128)(2,1)} %get-tuple-element.74.dp_ref, bf16[768,1024]{1,0:T(8,128)(2,1)} %get-tuple-element.75.dk_ref, ...), custom_call_target="tpu_custom_call" | custom-call | flops 4831838208 | bytes 20971520 | tf_op jit(solution)/shard_map/weight_grads/pallas_call | solution.py:1145
  314.2 55.3 %finish.1 = (f32[5,96,192]{2,1,0:T(8,128)}, bf16[2,2,128,768]{3,2,1,0:T(8,128)(2,1)}, f32[72,128]{1,0:T(8,128)}) custom-call(bf16[4,768,768]{2,1,0:T(8,128)(2,1)} %weight_grads.1.g_ref, bf16[1,768,768]{2,1,0:T(8,128)(2,1)} %bitcast.64, f32[512,768]{1,0:T(8,128)} %select_add_fusion.base_ref, bf16[512,768]{1,0:T(8,128)(2,1)} %get-tuple-element.111.ctx_ref, ...), custom_call_target="tpu_custom_call" | custom-call | bytes 67108864 | tf_op jit(solution)/shard_map/finish/pallas_call | solution.py:386
  369.6 2.4 slice_bitcast_fusion
  372.0 0.8 slice_bitcast_fusion.6
  372.7 0.6 slice_bitcast_fusion.12
  373.4 0.7 reshape_squeeze.6
  374.0 0.7 reshape_squeeze.7
  374.7 0.6 slice_bitcast_fusion.11
  375.3 0.8 slice_bitcast_fusion.4
  (49 shorter events, 4.9 us)
Async XLA Ops:
  0.7 109.4 %copy-start.12 = (f32[12,64]{1,0:T(8,128)S(1)}, f32[12,64]{1,0:T(8,128)}, u32[]{:S(2)}) copy-start(f32[12,64]{1,0:T(8,128)} %param.43) | copy-start | bytes 9220
  0.7 110.1 %copy-start.13 = (f32[12,64]{1,0:T(8,128)S(1)}, f32[12,64]{1,0:T(8,128)}, u32[]{:S(2)}) copy-start(f32[12,64]{1,0:T(8,128)} %param.44) | copy-start | bytes 9220
  1.5 4.9 %copy-start.19 = (s32[16]{0:T(128)}, s32[16]{0:T(128)S(1)}, u32[]{:S(2)}) copy-start(s32[16]{0:T(128)S(1)} %select_reduce_fusion.slot_ref) | copy-start | bytes 196
  6.3 0.6 copy-start.8
  124.6 53.7 %copy-start.14 = (f32[768]{0:T(1024)S(1)}, f32[768]{0:T(1024)}, u32[]{:S(2)}) copy-start(f32[768]{0:T(1024)} %param.42) | copy-start | bytes 9220
  124.6 54.3 %copy-start.15 = (f32[768]{0:T(1024)S(1)}, f32[768]{0:T(1024)}, u32[]{:S(2)}) copy-start(f32[768]{0:T(1024)} %param.45) | copy-start | bytes 9220
  124.6 54.9 %copy-start.16 = (f32[768]{0:T(1024)S(1)}, f32[768]{0:T(1024)}, u32[]{:S(2)}) copy-start(f32[768]{0:T(1024)} %param.46) | copy-start | bytes 9220
  124.7 55.4 %copy-start.17 = (f32[768]{0:T(1024)S(1)}, f32[768]{0:T(1024)}, u32[]{:S(2)}) copy-start(f32[768]{0:T(1024)} %param.47) | copy-start | bytes 9220
  124.7 56.0 %copy-start.18 = (f32[768]{0:T(1024)S(1)}, f32[768]{0:T(1024)}, u32[]{:S(2)}) copy-start(f32[768]{0:T(1024)} %param.48) | copy-start | bytes 9220
  215.0 76.0 %copy-start.10 = (f32[8,768]{1,0:T(8,128)S(1)}, f32[8,768]{1,0:T(8,128)}, u32[]{:S(2)}) copy-start(f32[8,768]{1,0:T(8,128)} %get-tuple-element.81) | copy-start | bytes 73732
  215.0 76.0 %copy-start.11 = (f32[1,3072]{1,0:T(1,128)S(1)}, f32[1,3072]{1,0:T(1,128)}, u32[]{:S(2)}) copy-start(f32[1,3072]{1,0:T(1,128)} %get-tuple-element.80) | copy-start | bytes 36868
  291.7 2.5 copy-start.7
  294.1 3.2 copy-start.1
  294.1 3.2 copy-start.4
  297.3 3.4 copy-start.2
  300.7 1.7 copy-start
  314.2 55.3 %copy-start.3 = (bf16[2,2,128,768]{3,2,1,0:T(8,128)(2,1)S(1)}, bf16[2,2,128,768]{3,2,1,0:T(8,128)(2,1)}, u32[]{:S(2)}) copy-start(bf16[2,2,128,768]{3,2,1,0:T(8,128)(2,1)} %get-tuple-element.73) | copy-start | bytes 2359300
  369.6 2.4 copy-start.6
  369.6 3.2 copy-start.9
  369.6 5.7 %copy-start.5 = (f32[2,96,768]{2,1,0:T(8,128)S(1)}, f32[2,96,768]{2,1,0:T(8,128)}, u32[]{:S(2)}) copy-start(f32[2,96,768]{2,1,0:T(8,128)} %get-tuple-element.85) | copy-start | bytes 1769476

commit v5 on v4

--- a/solution.py
+++ b/solution.py
@@ -122,16 +122,22 @@
     def copy(self, i):
         owner, half, to = GATHER[i]
         src = self.region(owner, half)
-        if owner == 0:
+        if owner == 0 and self.own is not None:
             src = self.own.at[:, half * self.half : (half + 1) * self.half, :]
         place = self.place
         return push(
             src, self.region(owner, half), self.send.at[i], self.recv.at[i], place.dp(to), place.z
         )
 
-    def begin(self):
-        for i in (0, 1, 2, 3, 6, 7):
+    def start(self, *which):
+        for i in which:
             self.copy(i).start()
+
+    def wait(self, received, sent):
+        for i in received:
+            self.copy(i).wait_recv()
+        for i in sent:
+            self.copy(i).wait_send()
 
     def after(self, arrived, started):
         for i, more in zip(arrived, started):
@@ -142,17 +148,8 @@
     def middle(self):
         self.after((0, 1), ((4, 8), (5, 9)))
 
-    def late(self):
-        self.after((2, 3), ((10,), (11,)))
-
     def last(self):
-        self.after((4, 5), ((12,), (13,)))
-
-    def end(self):
-        for i in range(6, 14):
-            self.copy(i).wait_recv()
-        for i in range(14):
-            self.copy(i).wait_send()
+        self.after((2, 3, 4, 5), ((10,), (11,), (12,), (13,)))
 
 
 def chip_bits(j):
@@ -413,14 +410,18 @@
     )(grads, g_out, base, ctx, small)
 
 
-def exchange_kernel(
-    slot_ref,
-    content,
-    query,
-    memory,
-    ints,
-    *refs,
-):
+def pack(mat):
+    half = mat.shape[0] // 2
+    return jnp.concatenate([mat[:, :128], jnp.concatenate([mat[:half, 128:], mat[half:, 128:]], axis=1)], axis=0)
+
+
+def unpack(packed):
+    rows = packed.shape[0] * 2 // 3
+    rest = packed[rows:, :]
+    return jnp.concatenate([packed[:rows, :], jnp.concatenate([rest[:, :64], rest[:, 64:]], axis=0)], axis=1)
+
+
+def exchange_kernel(slot_ref, content, query, memory, ints, *refs):
     mats, (upw, dnw) = refs[:5], refs[5:7]
     context, stream, all_ints, whole, out_slab, ud_slab = refs[7:13]
     (
@@ -429,20 +430,25 @@
         shards,
         slab,
         mat_send,
+        mat_recv,
         ud_send,
+        ud_recv,
         int_send,
         spread_send,
         pick_send,
         stream_send,
+        pair_send,
         gather_send,
         gather_recv,
         recv,
     ) = refs[13:]
     place = Place()
     d, z, core = place.d, place.z, place.core
-    part = content.shape[1]
-    mem_total = part * 4
-    piece = part // 8
+    up, down, far = place.up(1), place.up(3), place.up(2)
+    part = query.shape[1]
+    piece = spread.shape[1]
+    blocks = part // piece // 2
+    first = 4 * blocks
     greet([(place.dp(r), place.up(k)) for r in range(8) for k in range(4) if r or k])
 
     spread_copies = []
@@ -454,99 +460,143 @@
             pltpu.make_async_copy(src, dst, recv.at[0]).start()
         else:
             spread_copies.append(push(src, dst, spread_send.at[r - 1], recv.at[0], to, z))
-    mat_copies = []
+            spread_copies[-1].start()
+
     for m, mat in enumerate(mats):
-        pltpu.make_async_copy(mat, shards.at[m, z], recv.at[1]).start()
-        for k in range(1, 4):
-            at = mat_send.at[3 * m + k - 1]
-            mat_copies.append(push(mat, shards.at[m, z], at, recv.at[1], d, place.up(k)))
+        shards[z, m] = pack(mat[...])
+    cutoff = shards.shape[2] * 5 // 9
+
+    def mat_copy(i):
+        own = shards.at[z]
+        low, high = shards.at[down, :, :cutoff], shards.at[up, :, cutoff:]
+        src = (own, own, low, high)[i]
+        return push(src, src, mat_send.at[i], mat_recv.at[i], d, (up, down, up, down)[i])
+
+    mat_copy(0).start()
+    mat_copy(1).start()
     int_copies = []
     for r in range(8):
         if r == 0:
             pltpu.make_async_copy(ints, all_ints.at[d], recv.at[2]).start()
         else:
-            int_copies.append(
-                push(ints, all_ints.at[d], int_send.at[r - 1], recv.at[2], place.dp(r), z)
-            )
-    for copy in mat_copies + spread_copies + int_copies:
-        copy.start()
+            copy = push(ints, all_ints.at[d], int_send.at[r - 1], recv.at[2], place.dp(r), z)
+            int_copies.append(copy)
+            copy.start()
 
     def stream_copy(i, act):
-        j, kind = i // 3, i % 3
-        to, row = 2 * core + j, pl.multiple_of(z * part, 16)
-        if kind < 2:
-            dp = d - core + kind
-            src, dst, sem = content.at[j], context.at[pl.ds(mem_total + row, part), :], recv.at[3]
+        j, kind = i // 2, i % 2
+        to, dp = 2 * core + j, d - core + kind
+        if kind == 0:
+            src, sem = content.at[j], recv.at[3]
+            dst = context.at[pl.ds(first + blocks * z, blocks)]
         else:
-            dp = d - core + 1
-            src, dst, sem = query.at[j], stream.at[pl.ds(row, part), :], recv.at[4]
+            src, sem = query.at[j], recv.at[4]
+            dst = stream.at[pl.ds(pl.multiple_of(z * part, 16), part), :]
         here = jnp.logical_and(dp == d, to == z)
-        local = pltpu.make_async_copy(src, dst, sem)
         remote = push(src, dst, stream_send.at[i], sem, dp, to)
         if act == "start":
-            pl.when(here)(local.start)
+            pl.when(here)(pltpu.make_async_copy(src, dst, sem).start)
             pl.when(jnp.logical_not(here))(remote.start)
         else:
             pl.when(jnp.logical_not(here))(remote.wait_send)
 
-    for i in range(6):
+    mat_copy(0).wait_recv()
+    mat_copy(2).start()
+    mat_copy(1).wait_recv()
+    mat_copy(3).start()
+    for i in range(4):
         stream_copy(i, "start")
-
-    settle(shards, recv.at[1])
-    for m in range(5):
-        slab[m] = jnp.concatenate([shards[m, k] for k in range(4)], axis=1)
-    rows = slab.shape[1]
-    own_rows = pl.ds(pl.multiple_of(d * rows, 16), rows)
-    gather = Gather(place, whole, slab.at[0:4], gather_send, gather_recv)
-    gather.begin()
-    pltpu.make_async_copy(slab.at[0:4], whole.at[:, own_rows, :], recv.at[6]).start()
-    pltpu.make_async_copy(slab.at[4:5], out_slab, recv.at[7]).start()
 
     settle(spread, recv.at[0])
     for q in range(16):
         picked[q] = spread[slot_ref[q]]
     pick_copies = []
-    row = pl.multiple_of(z * part + d * piece, 16)
-    for r in range(8):
+    for r in (YBIT | XBIT, XBIT, YBIT, 0):
         for k in range(4):
             to, lane = place.dp(r), place.up(k)
             src = picked.at[4 * lax.div(to, 2) + lane]
-            dst = context.at[pl.ds(row, piece), :]
+            dst = context.at[blocks * z + lax.div(d, 2), core]
             if r or k:
-                copy = push(src, dst, pick_send.at[4 * r + k - 1], recv.at[5], to, lane)
+                copy = push(src, dst, pick_send.at[2 * r + k - 1], recv.at[5], to, lane)
                 pick_copies.append(copy)
             else:
                 copy = pltpu.make_async_copy(src, dst, recv.at[5])
             copy.start()
 
+    mat_copy(2).wait_recv()
+    mat_copy(3).wait_recv()
+    for m in range(5):
+        slab[m] = jnp.concatenate([unpack(shards[k, m]) for k in range(4)], axis=1)
+    rows = slab.shape[1]
+    own_rows = pl.ds(pl.multiple_of(d * rows, 16), rows)
+    gather = Gather(place, whole, slab.at[0:4], gather_send, gather_recv)
+    gather.start(0, 1, 2, 3, 6, 7)
+    pltpu.make_async_copy(slab.at[0:4], whole.at[:, own_rows, :], recv.at[6]).start()
+    pltpu.make_async_copy(slab.at[4:5], out_slab, recv.at[7]).start()
+
     width = upw.shape[1]
-    cols = pl.ds(pl.multiple_of(z * width, 128), width)
-    ud_copies = []
+
+    def columns(at, rows=slice(None)):
+        return ud_slab.at[:, rows, pl.ds(pl.multiple_of(at * width, 128), width)]
+
+    def ud_copy(i):
+        if i < 4:
+            src, dst = (upw, dnw)[i % 2], columns(z).at[i % 2]
+            return push(src, dst, ud_send.at[i], ud_recv.at[i // 2], d, (up, down)[i // 2])
+        half = rows // 2
+        src = columns(down, slice(0, half)) if i == 4 else columns(up, slice(half, rows))
+        return push(src, src, ud_send.at[i], ud_recv.at[i - 2], d, (up, down)[i - 4])
+
+    for i in range(4):
+        ud_copy(i).start()
     for m, mat in enumerate((upw, dnw)):
-        pltpu.make_async_copy(mat, ud_slab.at[m, :, cols], recv.at[8]).start()
-        for k in range(1, 4):
-            at = ud_send.at[3 * m + k - 1]
-            ud_copies.append(push(mat, ud_slab.at[m, :, cols], at, recv.at[8], d, place.up(k)))
-            ud_copies[-1].start()
-
+        pltpu.make_async_copy(mat, columns(z).at[m], recv.at[8]).start()
+
+    pick_pair = push(
+        context.at[0:first, core], context.at[0:first, core], pair_send.at[0], recv.at[1], place.dp(CORE), z
+    )
+    settle(context.at[0:first, core], recv.at[5])
+    pick_pair.start()
     gather.middle()
-    gather.late()
+    settle(columns(down), ud_recv.at[0])
+    ud_copy(4).start()
+    settle(columns(up), ud_recv.at[1])
+    ud_copy(5).start()
+
+    lead_copy = push(
+        context.at[first:], context.at[first:], pair_send.at[1], recv.at[3], place.dp(CORE), z
+    )
+
+    @pl.when(core == 0)
+    def _():
+        settle(context.at[first:], recv.at[3])
+        lead_copy.start()
+
     gather.last()
-    gather.end()
+    gather.wait(range(6, 14), range(14))
     settle(whole.at[:, own_rows, :], recv.at[6])
     settle(out_slab, recv.at[7])
-    settle(ud_slab, recv.at[8])
+    settle(columns(z), recv.at[8])
+    ud_copy(4).wait_recv()
+    ud_copy(5).wait_recv()
     settle(all_ints, recv.at[2])
-    settle(context.at[mem_total:, :], recv.at[3])
-    settle(context.at[:mem_total, :], recv.at[5])
+    pick_pair.wait()
+
+    @pl.when(core == 0)
+    def _():
+        lead_copy.wait_send()
 
     @pl.when(core == 1)
     def _():
+        settle(context.at[first:], recv.at[3])
         settle(stream, recv.at[4])
 
+    for i in range(4):
+        stream_copy(i, "wait")
+        mat_copy(i).wait_send()
     for i in range(6):
-        stream_copy(i, "wait")
-    for copy in mat_copies + spread_copies + int_copies + pick_copies + ud_copies:
+        ud_copy(i).wait_send()
+    for copy in spread_copies + int_copies + pick_copies:
         copy.wait_send()
 
 
@@ -554,14 +604,15 @@
     micro, part, width = content.shape
     rows = mats[0].shape[0]
     inner = upw.shape[1] * 4
+    piece = part // 8
     vmem = pl.BlockSpec(memory_space=pltpu.VMEM)
     dma = lambda n: pltpu.SemaphoreType.DMA((n,))
-    return pl.pallas_call(
+    context, *rest = pl.pallas_call(
         exchange_kernel,
         in_specs=[SMEM_SPEC] + [ANY_SPEC] * 3 + [vmem] * 8,
         out_specs=[ANY_SPEC] * 6,
         out_shape=[
-            jax.ShapeDtypeStruct((8 * part, width), BF),
+            jax.ShapeDtypeStruct((32, 2, piece, width), BF),
             jax.ShapeDtypeStruct((4 * part, width), BF),
             jax.ShapeDtypeStruct((8,) + ints.shape, jnp.int32),
             jax.ShapeDtypeStruct((4, 8 * rows, width), BF),
@@ -569,16 +620,19 @@
             jax.ShapeDtypeStruct((2, rows, inner), BF),
         ],
         scratch_shapes=[
-            pltpu.VMEM((16, part // 8, width), BF),
-            pltpu.VMEM((16, part // 8, width), BF),
-            pltpu.VMEM((5, 4, rows, width // 4), BF),
+            pltpu.VMEM((16, piece, width), BF),
+            pltpu.VMEM((16, piece, width), BF),
+            pltpu.VMEM((4, 5, rows * 3 // 2, 128), BF),
             pltpu.VMEM((5, rows, width), BF),
-            dma(15),
+            dma(4),
+            dma(4),
             dma(6),
+            dma(4),
             dma(7),
             dma(7),
-            dma(31),
-            dma(6),
+            dma(15),
+            dma(4),
+            dma(2),
             dma(14),
             dma(14),
             dma(9),
@@ -588,7 +642,8 @@
         ),
         cost_estimate=pl.CostEstimate(flops=0, bytes_accessed=64 << 20, transcendentals=0),
         name="exchange",
-    )(slot_of, content, query, memory, ints, *mats, upw, dnw)
+    )(slot_of, content.reshape(micro, 4, 2, piece, width), query, memory, ints, *mats, upw, dnw)
+    return [context.reshape(8 * part, width)] + rest
 
 
 def head_lanes(array, head):
@@ -626,18 +681,17 @@
     if not wired:
         attend_forward_step(block, *refs)
         return
-    ins, (out_slab, ud_slab, ctan, qtan) = refs[:7], refs[7:11]
+    ins, (ctan, qtan) = refs[:7], refs[9:11]
     outs, (wo, ud, tangent) = refs[11:13], refs[13:16]
     out_send, out_recv, ud_send, ud_recv, tan_send, recv = refs[16:]
     step, steps = pl.program_id(0), pl.num_programs(0)
     place = Place()
     d, z, core = place.d, place.z, place.core
     gathers = (
-        Gather(place, ud, ud_slab, ud_send, ud_recv),
-        Gather(place, wo, out_slab, out_send, out_recv),
+        Gather(place, ud, None, ud_send, ud_recv),
+        Gather(place, wo, None, out_send, out_recv),
     )
-    rows, part = out_slab.shape[1], ctan.shape[1]
-    own_rows = pl.ds(pl.multiple_of(d * rows, 16), rows)
+    part = ctan.shape[1]
 
     def tan_copy(i, act):
         j, kind = i // 2, i % 2
@@ -655,33 +709,20 @@
 
     @pl.when(step == 0)
     def _():
-        partners = [(place.dp(r), z) for r in (CORE, XBIT, YBIT)]
-        partners += [(place.dp(r), place.up(k)) for k in (1, 2, 3) for r in (0, CORE)]
-        greet(partners)
+        greet(near_partners(place))
         for gather in gathers:
-            gather.begin()
-        pltpu.make_async_copy(ud_slab, ud.at[:, own_rows, :], recv.at[1]).start()
-        pltpu.make_async_copy(out_slab, wo.at[:, own_rows, :], recv.at[2]).start()
+            gather.start(2, 3, 4, 5, 8, 9)
         for i in range(4):
             tan_copy(i, "start")
-
-    @pl.when(step == 3)
-    def _():
-        for gather in gathers:
-            gather.middle()
 
     attend_forward_step(block, *ins, *outs)
 
     @pl.when(step == steps - 1)
     def _():
         for gather in gathers:
-            gather.late()
-        for gather in gathers:
             gather.last()
         for gather in gathers:
-            gather.end()
-        settle(ud.at[:, own_rows, :], recv.at[1])
-        settle(wo.at[:, own_rows, :], recv.at[2])
+            gather.wait(range(8, 14), (2, 3, 4, 5) + tuple(range(8, 14)))
         settle(tangent, recv.at[0])
         for i in range(4):
             tan_copy(i, "wait")
@@ -708,16 +749,14 @@
     params = dict(vmem_limit_bytes=LIMIT)
     scratch = []
     if wires:
-        vmem = pl.BlockSpec(memory_space=pltpu.VMEM)
-        in_specs += [vmem, vmem, ANY_SPEC, ANY_SPEC]
+        in_specs += [ANY_SPEC] * 4
         out_specs += [ANY_SPEC] * 3
-        inner = wires[1].shape[2]
         out_shape += [
-            jax.ShapeDtypeStruct((1, width, width), BF),
-            jax.ShapeDtypeStruct((2, width, inner), BF),
+            jax.ShapeDtypeStruct(wires[0].shape, BF),
+            jax.ShapeDtypeStruct(wires[1].shape, BF),
             jax.ShapeDtypeStruct((rows, width), BF),
         ]
-        scratch = [pltpu.SemaphoreType.DMA((n,)) for n in (14, 14, 14, 14, 4, 3)]
+        scratch = [pltpu.SemaphoreType.DMA((n,)) for n in (14, 14, 14, 14, 4, 1)]
         params.update(collective_id=2, has_side_effects=True)
     return pl.pallas_call(
         functools.partial(attend_forward_kernel, block, bool(wires)),
@@ -726,6 +765,7 @@
         out_specs=out_specs,
         out_shape=out_shape,
         scratch_shapes=scratch,
+        input_output_aliases={7: 2, 8: 3} if wires else {},
         compiler_params=pltpu.CompilerParams(**params),
         cost_estimate=pl.CostEstimate(
             flops=8 * rows * klen * width, bytes_accessed=16 << 20, transcendentals=12 * rows * klen
@@ -1070,7 +1110,37 @@
     )(ud, wo, vec, x, tan, upb, dnb, g1, s1, g2, s2)
 
 
-def project_kernel(
+def project_kernel(wired, *refs):
+    if not wired:
+        project_step(*refs)
+        return
+    ins, (out_slab, ud_slab) = refs[:6], refs[6:8]
+    outs, (wo, ud) = refs[8:14], refs[14:16]
+    out_send, out_recv, ud_send, ud_recv, own = refs[16:]
+    place = Place()
+    gathers = (
+        Gather(place, ud, ud_slab, ud_send, ud_recv),
+        Gather(place, wo, out_slab, out_send, out_recv),
+    )
+    rows = out_slab.shape[1]
+    own_rows = pl.ds(pl.multiple_of(place.d * rows, 16), rows)
+    locals_ = (
+        pltpu.make_async_copy(ud_slab, ud.at[:, own_rows, :], own.at[0]),
+        pltpu.make_async_copy(out_slab, wo.at[:, own_rows, :], own.at[1]),
+    )
+    greet([(place.dp(r), place.z) for r in (CORE, XBIT, YBIT)])
+    for gather in gathers:
+        gather.start(0, 1, 6, 7)
+    for copy in locals_:
+        copy.start()
+    project_step(*ins, *outs)
+    for gather in gathers:
+        gather.wait((0, 1, 6, 7), (0, 1, 6, 7))
+    for copy in locals_:
+        copy.wait()
+
+
+def project_step(
     w_ref, ctx_ref, q_ref, table_ref, wb_ref, pb_ref, k_ref, v_ref, rel_ref, qw_ref, qp_ref, x_ref
 ):
     lead = lax.rem(lax.axis_index("dp"), 2) == 0
@@ -1103,30 +1173,40 @@
     loop(ctx_ref.shape[0], context_step)
 
 
-def project(mats, context, query, table, wb, pb):
+def project(mats, context, query, table, wb, pb, wires=()):
     rows, width = query.shape
     klen, span = context.shape[0], table.shape[0]
     vmem = pl.BlockSpec(memory_space=pltpu.VMEM)
+    out_shape = [
+        jax.ShapeDtypeStruct((klen, width), BF),
+        jax.ShapeDtypeStruct((klen, width), BF),
+        jax.ShapeDtypeStruct((span, width), BF),
+        jax.ShapeDtypeStruct((rows, width), BF),
+        jax.ShapeDtypeStruct((rows, width), BF),
+        jax.ShapeDtypeStruct((rows, width), BF),
+    ]
+    params = dict(vmem_limit_bytes=LIMIT)
+    scratch = []
+    if wires:
+        params.update(collective_id=5, has_side_effects=True)
+        scratch = [pltpu.SemaphoreType.DMA((n,)) for n in (14, 14, 14, 14, 2)]
+        out_shape += [
+            jax.ShapeDtypeStruct((slab.shape[0], width, slab.shape[2]), BF) for slab in wires
+        ]
     return pl.pallas_call(
-        project_kernel,
-        in_specs=[vmem] * 6,
-        out_specs=[vmem] * 6,
-        out_shape=[
-            jax.ShapeDtypeStruct((klen, width), BF),
-            jax.ShapeDtypeStruct((klen, width), BF),
-            jax.ShapeDtypeStruct((span, width), BF),
-            jax.ShapeDtypeStruct((rows, width), BF),
-            jax.ShapeDtypeStruct((rows, width), BF),
-            jax.ShapeDtypeStruct((rows, width), BF),
-        ],
-        compiler_params=pltpu.CompilerParams(vmem_limit_bytes=LIMIT),
+        functools.partial(project_kernel, bool(wires)),
+        in_specs=[vmem] * (6 + len(wires)),
+        out_specs=[vmem] * 6 + [ANY_SPEC] * len(wires),
+        out_shape=out_shape,
+        scratch_shapes=scratch,
+        compiler_params=pltpu.CompilerParams(**params),
         cost_estimate=pl.CostEstimate(
             flops=2 * (2 * klen + rows + span) * width * width,
             bytes_accessed=20 << 20,
             transcendentals=0,
         ),
         name="project",
-    )(mats, context, query, table, wb, pb)
+    )(mats, context, query, table, wb, pb, *wires)
 
 
 def weight_grads_kernel(xt_ref, ct_ref, tt_ref, dp_ref, dk_ref, dv_ref, dr_ref, g_ref):
@@ -1245,7 +1325,7 @@
         context, query, all_ints, weights, out_slab, ud_slab = exchange(
             slot_of, content_stream, query_stream, memory, ints, mats, up_weight, down_weight
         )
-        wires = (out_slab, ud_slab, content_tangent, query_tangent)
+        wires = (out_slab, ud_slab)
         lengths = all_ints[:, micro, : 2 * micro]
         orders = all_ints[seq_id // micro, :micro]
     else:
@@ -1293,9 +1373,11 @@
     thr = (rank + jnp.where(lead, 1, 0))[:, None]
 
     row = lambda v: v.reshape(1, -1)
-    keys, values, rel, q_word, q_pos, stream = project(
-        weights, context, query, table, row(word_bias), row(pos_bias)
+    keys, values, rel, q_word, q_pos, stream, *wires = project(
+        weights, context, query, table, row(word_bias), row(pos_bias), wires
     )
+    if wires:
+        wires += [content_tangent, query_tangent]
     vec, prob, *arrived = attend_forward(
         q_word, q_pos, keys, values, rel, thr, key_rank, block, wires
     )

time: 379 us -> 345 us (0.910)
  Pallas kernels: 340 us -> 306 us
    pallas_call x1, Pallas kernels: 98.2 us -> 66.8 us  [exchange(): pl.pallas_call(exchange_kernel, in_specs=[SMEM_SPEC] + [ANY_SPEC] * 3 + [...]
    pallas_call x1, Pallas kernels: 53.7 us -> 39.8 us  [attend_forward(): pl.pallas_call(functools.partial(attend_forward_kernel, block, bool(wires...]
    pallas_call x1, Pallas kernels: 13.2 us -> 25.1 us  [project(): pl.pallas_call(functools.partial(project_kernel, bool(wires)), in_specs=[...]
where the time goes in v5:
time: 345 us; the launch traced here: 343 us
  Pallas kernels  306 us (89%)
  local copies, waits for them, and re-layouts  19.1 us (6%)
  matrix products  9.03 us (3%)
  between operations  4.28 us (1%)
  other arithmetic  4.12 us (1%)
    pallas_call x1, Pallas kernels, attend_backward(): pl.pallas_call(functools.partial(attend_backward_kernel, block, bool(wire...  74.1 us
    pallas_call x1, Pallas kernels, exchange(): pl.pallas_call(exchange_kernel, in_specs=[SMEM_SPEC] + [ANY_SPEC] * 3 + [...  66.8 us
    pallas_call x1, Pallas kernels, finish(): pl.pallas_call(finish_kernel, in_specs=[ANY_SPEC] * 2 + [vmem] * 3, out_s...  56.4 us
    pallas_call x1, Pallas kernels, attend_forward(): pl.pallas_call(functools.partial(attend_forward_kernel, block, bool(wires...  39.8 us
    pallas_call x1, Pallas kernels, feed(): pl.pallas_call(functools.partial(feed_kernel, steps), grid=(2 * steps,),...  33.8 us
    pallas_call x1, Pallas kernels, project(): pl.pallas_call(functools.partial(project_kernel, bool(wires)), in_specs=[...  25.1 us
    pallas_call x1, Pallas kernels, weight_grads(): pl.pallas_call(weight_grads_kernel, grid=(width // chunk,), in_specs=[who...  10.2 us

profile of v5, /device:TPU:0, one launch (start us, length us, event | category | flops | bytes accessed | tf_op | source)
XLA Modules:
  0.0 342.8 jit_solution(16830180178880221669)
XLA Ops:
  0.7 0.8 select_reduce_fusion.slot_ref
  1.5 0.6 dynamic_slice.14
  4.7 0.7 pad.8
  5.4 0.7 add_bitcast_fusion.1
  6.9 66.8 %exchange.1 = (bf16[32,2,16,768]{3,2,1,0:T(8,128)(2,1)}, bf16[512,768]{1,0:T(8,128)(2,1)}, s32[8,8,512]{2,1,0:T(8,128)}, bf16[4,768,768]{2,1,0:T(8,128)(2,1)}, b...) custom-call(s32[16]{0:T(128)} %copy-done.19, bf16[2,4,2,16,768]{4,3,2,1,0:T(8,128)(2,1)} %bitcast.70, ...), custom_call_target="tpu_custom_call" | custom-call | bytes 67108864 | tf_op jit(solution)/shard_map/exchange/pallas_call | solution.py:610
  73.8 0.8 slice.87
  75.8 0.7 add_bitcast_fusion
  76.5 0.6 compare_select_fusion.1
  77.2 0.6 pad_add_fusion
  77.8 0.9 copy.52.refs_5_
  78.7 0.7 reshape.123.refs_4_
  79.3 0.7 reshape.124.refs_5_
  80.0 25.1 %project.1 = (bf16[1024,768]{1,0:T(8,128)(2,1)}, bf16[1024,768]{1,0:T(8,128)(2,1)}, bf16[1536,768]{1,0:T(8,128)(2,1)}, bf16[512,768]{1,0:T(8,128)(2,1)}, bf16[51...) custom-call(bf16[4,768,768]{2,1,0:T(8,128)(2,1)} %get-tuple-element., ...), custom_call_target="tpu_custom_call" | custom-call | flops 4831838208 | bytes 20971520 | tf_op jit(solution)/shard_map/project/pallas_call | solution.py:1196
  105.1 39.8 %attend_forward.1 = (bf16[512,768]{1,0:T(8,128)(2,1)}, bf16[12,512,1024]{2,1,0:T(8,128)(2,1)}, bf16[1,768,768]{2,1,0:T(8,128)(2,1)}, bf16[2,768,3072]{2,1,0:T(8,128)(2,1)}, bf16[512,768]{1,0:T(8,128)(2,1)}) custom-call(bf16[512,768]{1,0:T(8,128)(2,1)} %get-tuple-element.60.refs_0_.refs_2_, ...), custom_call_target="tpu_custom_call", output_to_operand_aliasing={{2}: (7, {}), {3}: (8, {})} | custom-call | flops 3221225472 | bytes 16777216 | tf_op jit(solution)/shard_map/attend_forward/pallas_call | solution.py:761
  147.9 33.8 %feed.1 = (bf16[512,768]{1,0:T(8,128)(2,1)}, f32[512,768]{1,0:T(8,128)}, bf16[512,768]{1,0:T(8,128)(2,1)}, bf16[768,768]{1,0:T(8,128)(2,1)}, bf16[2,768,3072]{2,...) custom-call(bf16[2,768,3072]{2,1,0:T(8,128)(2,1)} %get-tuple-element.69.refs_0_, ...), custom_call_target="tpu_custom_call" | custom-call | flops 14495514624 | bytes 37748736 | tf_op jit(solution)/shard_map/feed/pallas_call | solution.py:1066
  181.7 74.1 %attend_backward.1 = (bf16[512,768]{1,0:T(8,128)(2,1)}, bf16[768,1024]{1,0:T(8,128)(2,1)}, bf16[768,1024]{1,0:T(8,128)(2,1)}, bf16[768,1536]{1,0:T(8,128)(2,1)},...) custom-call(bf16[12,512,1024]{2,1,0:T(8,128)(2,1)} %get-tuple-element.68.refs_0_, ...), custom_call_target="tpu_custom_call" | custom-call | flops 6442450944 | bytes 20971520 | tf_op jit(solution)/shard_map/attend_backward/pallas_call | solution.py:926
  255.8 0.7 reshape.133
  256.5 0.6 fusion.9.small_ref
  257.2 2.5 fusion.1
  259.7 3.2 fusion.10
  262.9 3.4 select_add_fusion.base_ref
  266.2 1.1 copy.53
  267.9 1.6 copy.54
  269.6 10.2 %weight_grads.1.g_ref = bf16[4,768,768]{2,1,0:T(8,128)(2,1)} custom-call(bf16[768,512]{1,0:T(8,128)(2,1)} %bitcast.69, bf16[768,1024]{1,0:T(8,128)(2,1)} %bitcast.67, bf16[768,1536]{1,0:T(8,128)(2,1)} %constant.112.tt_ref, bf16[512,768]{1,0:T(8,128)(2,1)} %get-tuple-element.78.dp_ref, bf16[768,1024]{1,0:T(8,128)(2,1)} %get-tuple-element.79.dk_ref, ...), custom_call_target="tpu_custom_call" | custom-call | flops 4831838208 | bytes 20971520 | tf_op jit(solution)/shard_map/weight_grads/pallas_call | solution.py:1225
  279.7 56.4 %finish.1 = (f32[5,96,192]{2,1,0:T(8,128)}, bf16[2,2,128,768]{3,2,1,0:T(8,128)(2,1)}, f32[72,128]{1,0:T(8,128)}) custom-call(bf16[4,768,768]{2,1,0:T(8,128)(2,1)} %weight_grads.1.g_ref, bf16[1,768,768]{2,1,0:T(8,128)(2,1)} %bitcast.68, f32[512,768]{1,0:T(8,128)} %select_add_fusion.base_ref, bf16[512,768]{1,0:T(8,128)(2,1)} %get-tuple-element.115.ctx_ref, ...), custom_call_target="tpu_custom_call" | custom-call | bytes 67108864 | tf_op jit(solution)/shard_map/finish/pallas_call | solution.py:383
  336.2 2.4 slice_bitcast_fusion
  338.6 0.8 slice_bitcast_fusion.6
  339.4 0.6 slice_bitcast_fusion.12
  340.0 0.7 reshape_squeeze.6
  340.6 0.7 reshape_squeeze.7
  341.3 0.6 slice_bitcast_fusion.11
  341.9 0.8 slice_bitcast_fusion.4
  (49 shorter events, 4.9 us)
Async XLA Ops:
  0.7 78.0 %copy-start.12 = (f32[12,64]{1,0:T(8,128)S(1)}, f32[12,64]{1,0:T(8,128)}, u32[]{:S(2)}) copy-start(f32[12,64]{1,0:T(8,128)} %param.43) | copy-start | bytes 9220
  0.7 78.7 %copy-start.13 = (f32[12,64]{1,0:T(8,128)S(1)}, f32[12,64]{1,0:T(8,128)}, u32[]{:S(2)}) copy-start(f32[12,64]{1,0:T(8,128)} %param.44) | copy-start | bytes 9220
  1.5 4.9 %copy-start.19 = (s32[16]{0:T(128)}, s32[16]{0:T(128)S(1)}, u32[]{:S(2)}) copy-start(s32[16]{0:T(128)S(1)} %select_reduce_fusion.slot_ref) | copy-start | bytes 196
  6.3 0.6 copy-start.8
  105.1 39.9 %copy-start.14 = (f32[768]{0:T(1024)S(1)}, f32[768]{0:T(1024)}, u32[]{:S(2)}) copy-start(f32[768]{0:T(1024)} %param.42) | copy-start | bytes 9220
  105.1 40.5 %copy-start.15 = (f32[768]{0:T(1024)S(1)}, f32[768]{0:T(1024)}, u32[]{:S(2)}) copy-start(f32[768]{0:T(1024)} %param.45) | copy-start | bytes 9220
  105.1 41.0 %copy-start.16 = (f32[768]{0:T(1024)S(1)}, f32[768]{0:T(1024)}, u32[]{:S(2)}) copy-start(f32[768]{0:T(1024)} %param.46) | copy-start | bytes 9220
  105.1 41.6 %copy-start.17 = (f32[768]{0:T(1024)S(1)}, f32[768]{0:T(1024)}, u32[]{:S(2)}) copy-start(f32[768]{0:T(1024)} %param.47) | copy-start | bytes 9220
  105.1 42.2 %copy-start.18 = (f32[768]{0:T(1024)S(1)}, f32[768]{0:T(1024)}, u32[]{:S(2)}) copy-start(f32[768]{0:T(1024)} %param.48) | copy-start | bytes 9220
  181.6 74.9 %copy-start.10 = (f32[8,768]{1,0:T(8,128)S(1)}, f32[8,768]{1,0:T(8,128)}, u32[]{:S(2)}) copy-start(f32[8,768]{1,0:T(8,128)} %get-tuple-element.85) | copy-start | bytes 73732
  181.7 74.9 %copy-start.11 = (f32[1,3072]{1,0:T(1,128)S(1)}, f32[1,3072]{1,0:T(1,128)}, u32[]{:S(2)}) copy-start(f32[1,3072]{1,0:T(1,128)} %get-tuple-element.84) | copy-start | bytes 36868
  257.2 2.5 copy-start.7
  259.6 3.2 copy-start.1
  259.6 3.2 copy-start.4
  262.9 3.4 copy-start.2
  266.2 1.7 copy-start
  279.7 56.4 %copy-start.3 = (bf16[2,2,128,768]{3,2,1,0:T(8,128)(2,1)S(1)}, bf16[2,2,128,768]{3,2,1,0:T(8,128)(2,1)}, u32[]{:S(2)}) copy-start(bf16[2,2,128,768]{3,2,1,0:T(8,128)(2,1)} %get-tuple-element.77) | copy-start | bytes 2359300
  336.2 2.4 copy-start.6
  336.2 3.2 copy-start.9
  336.2 5.7 %copy-start.5 = (f32[2,96,768]{2,1,0:T(8,128)S(1)}, f32[2,96,768]{2,1,0:T(8,128)}, u32[]{:S(2)}) copy-start(f32[2,96,768]{2,1,0:T(8,128)} %get-tuple-element.89) | copy-start | bytes 1769476

commit v6 on v5

--- a/solution.py
+++ b/solution.py
@@ -319,17 +319,36 @@
     return pair_and_z(place) + [(place.dp(r), place.z) for r in (XBIT, YBIT)]
 
 
-def finish_kernel(g_ref, go_ref, base_ref, ctx_ref, small_ref, *refs):
-    grads_ref, home_ref, sums_ref = refs[:3]
-    stream, partner, slots, part_sum, chips = refs[3:8]
-    home_send, slot_send, chip_send, one_send, recv = refs[8:13]
+INPUTS = 11
+
+
+def finish_kernel(*refs):
+    hbm, (go_ref, small_ref) = refs[:INPUTS], refs[INPUTS : INPUTS + 2]
+    grads_ref, home_ref, sums_ref = refs[INPUTS + 2 : INPUTS + 5]
+    refs = refs[INPUTS + 5 :]
+    held, refs = refs[:INPUTS], refs[INPUTS:]
+    loads, g_ref, base, ctx, partner, stream, slots, part_sum, chips = refs[:9]
+    home_send, slot_send, chip_send, one_send, recv = refs[9:14]
+    refs = refs[14:]
+    count = len(refs) // 5
     place = Place()
     d, z, core = place.d, place.z, place.core
+    copies = [pltpu.make_async_copy(a, b, loads.at[i]) for i, (a, b) in enumerate(zip(hbm, held))]
+    for copy in copies:
+        copy.start()
+
+    def need(*which):
+        for i in which:
+            copies[i].wait()
+        return [held[i] for i in which]
+
     greet(near_partners(place) + [(place.dp(XBIT | YBIT), z)])
-    reduce = Reduce(place, (g_ref, go_ref), refs[13:], grads_ref)
-    swap = push(ctx_ref, partner, one_send.at[0], recv.at[0], place.dp(CORE), z)
-    swap.start()
-    reduce.begin()
+    sources = [g_ref.at[m : m + 1] for m in range(4)] + [go_ref]
+    key, value, query, pos, out = [
+        Reduce(place, (src,), refs[m * count : (m + 1) * count], grads_ref.at[m : m + 1])
+        for m, src in enumerate(sources)
+    ]
+    out.begin()
     slot_copies = []
     others = [(r, k) for k in range(4) for r in (0, CORE) if r or k]
     for i, (r, k) in enumerate(others):
@@ -338,19 +357,72 @@
         slot_copies.append(copy)
     pltpu.make_async_copy(small_ref, slots.at[4 * core + z], recv.at[1]).start()
 
+    width, block = g_ref.shape[1], 256
+
+    def product(m, left, right, dot):
+        def run(i, carry):
+            at = pl.ds(pl.multiple_of(i * block, block), block)
+            g_ref[m, at, :] = dot(left[at, :], right[...]).astype(BF)
+            return carry
+
+        lax.fori_loop(0, width // block, run, 0)
+
+    x_t, d_proj = need(0, 1)
+    product(2, x_t, d_proj, nn)
+    query.begin()
+    ctx_t, dk_t = need(2, 3)
+    product(0, ctx_t, dk_t, nt)
+    key.begin()
+    out.pairs()
+
+    dv_t, w_key, w_value, w_query, d_mixed = need(4, 5, 6, 7, 8)
+    back = dk_t.shape[1] - base.shape[0]
+
+    def from_context(i, carry):
+        at = pl.ds(pl.multiple_of(i * block, block), block)
+        cols = pl.ds(pl.multiple_of(i * block + back, block), block)
+        turned = nn(w_key[...], dk_t[:, cols]) + nn(w_value[...], dv_t[:, cols])
+        turned = jnp.transpose(turned)
+        base[at, :] = turned
+        ctx[at, :] = turned.astype(BF)
+        return carry
+
+    lax.fori_loop(0, base.shape[0] // block, from_context, 0)
+    swap = push(ctx, partner, one_send.at[0], recv.at[0], place.dp(CORE), z)
+    swap.start()
+
+    def from_proj(i, carry):
+        at = pl.ds(pl.multiple_of(i * block, block), block)
+        own = d_mixed[at, :] + nt(d_proj[at, :], w_query[...])
+        base[at, :] = own + jnp.where(core == 0, base[at, :], 0.0)
+        return carry
+
+    lax.fori_loop(0, base.shape[0] // block, from_proj, 0)
+    query.pairs()
+    product(1, ctx_t, dv_t, nt)
+    value.begin()
+    key.pairs()
+
+    swap.wait()
+    small_block = 64
+
+    def add_partner(i, carry):
+        at = pl.ds(pl.multiple_of(i * small_block, small_block), small_block)
+        more = jnp.where(core == 0, partner[at, :].astype(F32), 0.0)
+        stream[at, :] = (base[at, :] + more).astype(BF)
+        return carry
+
+    lax.fori_loop(0, stream.shape[0] // small_block, add_partner, 0)
     home = Homeward(place, stream, home_ref, home_send, recv.at[2])
-    swap.wait()
-    block = 64
-
-    def add_partner(i, carry):
-        at = pl.ds(pl.multiple_of(i * block, block), block)
-        more = jnp.where(core == 0, partner[at, :].astype(F32), 0.0)
-        stream[at, :] = (base_ref[at, :] + more).astype(BF)
-        return carry
-
-    lax.fori_loop(0, stream.shape[0] // block, add_partner, 0)
     home.start()
-    reduce.pairs()
+    out.middle()
+
+    table_t, dr_t = need(9, 10)
+    product(3, table_t, dr_t, nt)
+    pos.begin()
+    value.pairs()
+    query.middle()
+    out.late()
 
     settle(slots, recv.at[1])
     total = slots[0]
@@ -365,49 +437,63 @@
         chip_copies.append(copy)
     pltpu.make_async_copy(part_sum, chips.at[chip], recv.at[3]).start()
 
-    reduce.middle()
+    pos.pairs()
+    key.middle()
+    query.late()
+    value.middle()
+    key.late()
+    pos.middle()
+    value.late()
     settle(chips, recv.at[3])
     sums_ref[...] = (chips[0] + chips[1]) + (chips[2] + chips[3])
-    reduce.late()
-    reduce.end()
+    pos.late()
+    for reduce in (out, query, key, value, pos):
+        reduce.end()
     home.end()
     for copy in slot_copies + chip_copies:
         copy.wait_send()
 
 
-def finish(grads, g_out, base, ctx, small):
-    n, width, cols = grads.shape
-    rows, total = width // 8, base.shape[0]
+def finish(arrays, g_out, small):
+    x_t, d_proj = arrays[:2]
+    width, total = x_t.shape
+    rows = width // 8
     vmem = pl.BlockSpec(memory_space=pltpu.VMEM)
     dma = lambda k: pltpu.SemaphoreType.DMA((k,))
+    scratch = [pltpu.VMEM(a.shape, a.dtype) for a in arrays] + [
+        dma(INPUTS),
+        pltpu.VMEM((4, width, width), BF),
+        pltpu.VMEM((total, width), F32),
+        pltpu.VMEM((total, width), BF),
+        pltpu.VMEM((total, width), BF),
+        pltpu.VMEM((total, width), BF),
+        pltpu.VMEM((8,) + small.shape, F32),
+        pltpu.VMEM(small.shape, F32),
+        pltpu.VMEM((4,) + small.shape, F32),
+        dma(4),
+        dma(7),
+        dma(3),
+        dma(1),
+        dma(4),
+    ]
+    for _ in range(5):
+        scratch += Reduce.scratch(1, 1, rows, width)
     return pl.pallas_call(
         finish_kernel,
-        in_specs=[ANY_SPEC] * 2 + [vmem] * 3,
+        in_specs=[ANY_SPEC] * (INPUTS + 1) + [vmem],
         out_specs=[vmem, ANY_SPEC, vmem],
         out_shape=[
-            jax.ShapeDtypeStruct((n + 1, rows, cols // 4), F32),
+            jax.ShapeDtypeStruct((5, rows, width // 4), F32),
             jax.ShapeDtypeStruct((2, 2, total // 4, width), BF),
             jax.ShapeDtypeStruct(small.shape, F32),
         ],
-        scratch_shapes=[
-            pltpu.VMEM((total, width), BF),
-            pltpu.VMEM((total, width), BF),
-            pltpu.VMEM((8,) + small.shape, F32),
-            pltpu.VMEM(small.shape, F32),
-            pltpu.VMEM((4,) + small.shape, F32),
-            dma(4),
-            dma(7),
-            dma(3),
-            dma(1),
-            dma(4),
-        ]
-        + Reduce.scratch(2, n + 1, rows, cols),
+        scratch_shapes=scratch,
         compiler_params=pltpu.CompilerParams(
             collective_id=4, has_side_effects=True, vmem_limit_bytes=LIMIT
         ),
-        cost_estimate=pl.CostEstimate(flops=0, bytes_accessed=64 << 20, transcendentals=0),
+        cost_estimate=pl.CostEstimate(flops=20 << 30, bytes_accessed=64 << 20, transcendentals=0),
         name="finish",
-    )(grads, g_out, base, ctx, small)
+    )(*arrays, g_out, small)
 
 
 def pack(mat):
@@ -1407,31 +1493,25 @@
         content_out, query_out = from_unit(out)
         grad_up, grad_down = scatter_sum(g_ud)
     small = jnp.concatenate([g_upb.reshape(-1), small[:5].reshape(-1), biases.reshape(-1)])
-    d_context = tt(dk_t[:, mem_total:], weights[0]) + tt(dv_t[:, mem_total:], weights[1])
-    d_stream = d_mixed + nt(d_proj, weights[2])
-    d_stream = d_stream + jnp.where(lead, d_context, 0.0)
-    grads = weight_grads(
-        jnp.transpose(stream),
-        jnp.transpose(context),
-        jnp.transpose(table),
-        d_proj,
-        dk_t,
-        dv_t,
-        drel_t,
-    )
     inner = up_bias.shape[0]
+    stream_t, context_t, table_t = (jnp.transpose(a) for a in (stream, context, table))
     if groups == 8:
         size = small.shape[0]
         small = jnp.pad(small, (0, -size % 1024)).reshape(-1, 128)
-        grads, homes, small = finish(grads, g_out[None], d_stream, d_context.astype(BF), small)
+        arrays = [stream_t, d_proj, context_t, dk_t, dv_t, weights[0], weights[1], weights[2]]
+        arrays += [d_mixed, table_t, drel_t]
+        grads, homes, small = finish(arrays, g_out[None], small)
         grad_key, grad_value, grad_query, grad_pos, grad_out = grads
         content_grad, query_grad = homes[0], homes[1]
         small = small.reshape(-1)[:size]
     else:
+        d_context = tt(dk_t[:, mem_total:], weights[0]) + tt(dv_t[:, mem_total:], weights[1])
         partner = swap(d_context.astype(BF)).astype(F32)
-        d_stream = d_stream + jnp.where(lead, partner, 0.0)
+        d_stream = d_mixed + nt(d_proj, weights[2]) + jnp.where(lead, d_context + partner, 0.0)
         content_grad, query_grad = from_unit(d_stream.astype(BF))
-        grad_key, grad_value, grad_query, grad_pos = scatter_sum(grads)
+        grad_key, grad_value, grad_query, grad_pos = scatter_sum(
+            weight_grads(stream_t, context_t, table_t, d_proj, dk_t, dv_t, drel_t)
+        )
         (grad_out,) = scatter_sum(g_out[None])
         small = lax.psum(small, ("dp", "tensor"))
     rest = small[inner:].reshape(7, width)

time: 345 us -> 335 us (0.971)
  local copies, waits for them, and re-layouts: 19.1 us -> 29.2 us
  matrix products: 9.03 us -> 0 us
  Pallas kernels: 306 us -> 297 us
    pallas_call x2 -> x1, Pallas kernels: 66.6 us -> 56.9 us  [finish(): pl.pallas_call(finish_kernel, in_specs=[ANY_SPEC] * (INPUTS + 1) + [vmem]...]
    dot_general x3 -> x0, matrix products: 9.03 us -> none  [the longest x2 5.64 us: tt(): lax.dot_general(left, right, (((0,), (1,)), ((), ())), preferred_element_...]
    reshape x7, local copies, waits for them, and re-layouts: 4.21 us -> 9.03 us  [body(): row = lambda v: v.reshape(1, -1)]
    squeeze x0 -> x1, local copies, waits for them, and re-layouts: none -> 3.83 us  [body(): weights[2]]
where the time goes in v6:
time: 335 us; the launch traced here: 334 us
  Pallas kernels  297 us (89%)
  local copies, waits for them, and re-layouts  29.2 us (9%)
  between operations  4.16 us (1%)
  other arithmetic  4.13 us (1%)
    pallas_call x1, Pallas kernels, attend_backward(): pl.pallas_call(functools.partial(attend_backward_kernel, block, bool(wire...  74.2 us
    pallas_call x1, Pallas kernels, exchange(): pl.pallas_call(exchange_kernel, in_specs=[SMEM_SPEC] + [ANY_SPEC] * 3 + [...  66.8 us
    pallas_call x1, Pallas kernels, finish(): pl.pallas_call(finish_kernel, in_specs=[ANY_SPEC] * (INPUTS + 1) + [vmem]...  56.9 us
    pallas_call x1, Pallas kernels, attend_forward(): pl.pallas_call(functools.partial(attend_forward_kernel, block, bool(wires...  39.8 us
    pallas_call x1, Pallas kernels, feed(): pl.pallas_call(functools.partial(feed_kernel, steps), grid=(2 * steps,),...  33.9 us
    pallas_call x1, Pallas kernels, project(): pl.pallas_call(functools.partial(project_kernel, bool(wires)), in_specs=[...  25.1 us
    reshape x7, local copies, waits for them, and re-layouts, body(): row = lambda v: v.reshape(1, -1)  9.03 us

profile of v6, /device:TPU:0, one launch (start us, length us, event | category | flops | bytes accessed | tf_op | source)
XLA Modules:
  0.0 334.2 jit_solution(11423485261932550234)
XLA Ops:
  0.7 0.8 select_reduce_fusion.slot_ref
  4.7 0.7 add_bitcast_fusion.1
  5.5 1.3 reshape.126.refs_6_
  6.7 1.4 reshape.123.refs_4_
  8.1 1.4 reshape.124.refs_5_
  9.4 1.3 reshape.127.refs_7_
  10.7 1.3 reshape.128.refs_8_
  12.0 1.3 reshape.129.refs_9_
  13.2 1.3 reshape.130.refs_10_
  14.5 0.7 pad.8
  15.9 66.8 %exchange.1 = (bf16[32,2,16,768]{3,2,1,0:T(8,128)(2,1)}, bf16[512,768]{1,0:T(8,128)(2,1)}, s32[8,8,512]{2,1,0:T(8,128)}, bf16[4,768,768]{2,1,0:T(8,128)(2,1)}, b...) custom-call(s32[16]{0:T(128)} %copy-done.7, bf16[2,4,2,16,768]{4,3,2,1,0:T(8,128)(2,1)} %bitcast.63, ...), custom_call_target="tpu_custom_call" | custom-call | bytes 67108864 | tf_op jit(solution)/shard_map/exchange/pallas_call | solution.py:696
  82.8 0.7 add_bitcast_fusion
  83.5 0.8 slice.81
  85.5 0.7 compare_select_fusion.1
  86.8 0.9 copy.52.refs_5_
  87.6 2.6 copy.54
  90.2 3.8 %slice_bitcast_fusion = (bf16[768,768]{1,0:T(8,128)(2,1)}, bf16[768,768]{1,0:T(8,128)(2,1)}, bf16[768,768]{1,0:T(8,128)(2,1)}) fusion(bf16[4,768,768]{2,1,0:T(8,128)(2,1)} %get-tuple-element.55.refs_0_), kind=kLoop, calls=%fused_computation | loop fusion | bytes 7077888 | tf_op jit(solution)/shard_map/squeeze | solution.py:1501
  94.1 25.1 %project.1 = (bf16[1024,768]{1,0:T(8,128)(2,1)}, bf16[1024,768]{1,0:T(8,128)(2,1)}, bf16[1536,768]{1,0:T(8,128)(2,1)}, bf16[512,768]{1,0:T(8,128)(2,1)}, bf16[51...) custom-call(bf16[4,768,768]{2,1,0:T(8,128)(2,1)} %get-tuple-element., ...), custom_call_target="tpu_custom_call" | custom-call | flops 4831838208 | bytes 20971520 | tf_op jit(solution)/shard_map/project/pallas_call | solution.py:1282
  119.2 2.3 copy.53
  121.5 39.8 %attend_forward.1 = (bf16[512,768]{1,0:T(8,128)(2,1)}, bf16[12,512,1024]{2,1,0:T(8,128)(2,1)}, bf16[1,768,768]{2,1,0:T(8,128)(2,1)}, bf16[2,768,3072]{2,1,0:T(8,128)(2,1)}, bf16[512,768]{1,0:T(8,128)(2,1)}) custom-call(bf16[512,768]{1,0:T(8,128)(2,1)} %get-tuple-element.60.refs_0_.refs_2_, ...), custom_call_target="tpu_custom_call", output_to_operand_aliasing={{2}: (7, {}), {3}: (8, {})} | custom-call | flops 3221225472 | bytes 16777216 | tf_op jit(solution)/shard_map/attend_forward/pallas_call | solution.py:847
  161.3 33.9 %feed.1 = (bf16[512,768]{1,0:T(8,128)(2,1)}, f32[512,768]{1,0:T(8,128)}, bf16[512,768]{1,0:T(8,128)(2,1)}, bf16[768,768]{1,0:T(8,128)(2,1)}, bf16[2,768,3072]{2,...) custom-call(bf16[2,768,3072]{2,1,0:T(8,128)(2,1)} %get-tuple-element.69.refs_0_, ...), custom_call_target="tpu_custom_call" | custom-call | flops 14495514624 | bytes 37748736 | tf_op jit(solution)/shard_map/feed/pallas_call | solution.py:1152
  195.2 74.2 %attend_backward.1 = (bf16[512,768]{1,0:T(8,128)(2,1)}, bf16[768,1024]{1,0:T(8,128)(2,1)}, bf16[768,1024]{1,0:T(8,128)(2,1)}, bf16[768,1536]{1,0:T(8,128)(2,1)},...) custom-call(bf16[12,512,1024]{2,1,0:T(8,128)(2,1)} %get-tuple-element.68.refs_0_, ...), custom_call_target="tpu_custom_call" | custom-call | flops 6442450944 | bytes 20971520 | tf_op jit(solution)/shard_map/attend_backward/pallas_call | solution.py:1012
  269.4 0.7 reshape.133
  270.1 0.6 fusion.refs_12_
  270.7 56.9 %finish.1 = (f32[5,96,192]{2,1,0:T(8,128)}, bf16[2,2,128,768]{3,2,1,0:T(8,128)(2,1)}, f32[72,128]{1,0:T(8,128)}) custom-call(bf16[768,512]{1,0:T(8,128)(2,1)} %bitcast.62, bf16[512,768]{1,0:T(8,128)(2,1)} %get-tuple-element.78.refs_1_, bf16[768,1024]{1,0:T(8,128)(2,1)} %bitcast.59, bf16[768,1024]{1,0:T(8,128)(2,1)} %get-tuple-element.79.refs_3_, ...), custom_call_target="tpu_custom_call" | custom-call | flops 21474836480 | bytes 67108864 | tf_op jit(solution)/shard_map/finish/pallas_call | solution.py:481
  327.7 2.4 slice_bitcast_fusion.3
  330.0 0.6 slice_bitcast_fusion.14
  330.6 0.6 slice_bitcast_fusion.15
  331.3 0.7 reshape_squeeze.7
  331.9 0.7 reshape_squeeze.6
  332.6 0.8 slice_bitcast_fusion.9
  333.4 0.8 slice_bitcast_fusion.7
  (22 shorter events, 2.5 us)
Async XLA Ops:
  1.5 13.8 %copy-start.7 = (s32[16]{0:T(128)}, s32[16]{0:T(128)S(1)}, u32[]{:S(2)}) copy-start(s32[16]{0:T(128)S(1)} %select_reduce_fusion.slot_ref) | copy-start | bytes 196
  15.3 0.6 copy-start.3
  195.1 74.9 %copy-start.5 = (f32[8,768]{1,0:T(8,128)S(1)}, f32[8,768]{1,0:T(8,128)}, u32[]{:S(2)}) copy-start(f32[8,768]{1,0:T(8,128)} %get-tuple-element.85) | copy-start | bytes 73732
  195.1 74.9 %copy-start.6 = (f32[1,3072]{1,0:T(1,128)S(1)}, f32[1,3072]{1,0:T(1,128)}, u32[]{:S(2)}) copy-start(f32[1,3072]{1,0:T(1,128)} %get-tuple-element.84) | copy-start | bytes 36868
  270.7 56.9 %copy-start = (bf16[2,2,128,768]{3,2,1,0:T(8,128)(2,1)S(1)}, bf16[2,2,128,768]{3,2,1,0:T(8,128)(2,1)}, u32[]{:S(2)}) copy-start(bf16[2,2,128,768]{3,2,1,0:T(8,128)(2,1)} %get-tuple-element.77) | copy-start | bytes 2359300
  327.6 2.4 copy-start.4
  327.7 4.9 %copy-start.2 = (f32[5,96,192]{2,1,0:T(8,128)S(1)}, f32[5,96,192]{2,1,0:T(8,128)}, u32[]{:S(2)}) copy-start(f32[5,96,192]{2,1,0:T(8,128)} %get-tuple-element.88) | copy-start | bytes 1105924
  327.7 5.7 %copy-start.1 = (f32[2,96,768]{2,1,0:T(8,128)S(1)}, f32[2,96,768]{2,1,0:T(8,128)}, u32[]{:S(2)}) copy-start(f32[2,96,768]{2,1,0:T(8,128)} %get-tuple-element.89) | copy-start | bytes 1769476

commit v7 on v6

--- a/solution.py
+++ b/solution.py
@@ -274,7 +274,8 @@
     def end(self):
         settle(self.quarter, self.z_recv.at[0])
         parts = [self.quarter[k].astype(F32) for k in range(4)]
-        self.out[...] = (parts[0] + parts[1]) + (parts[2] + parts[3])
+        total = (parts[0] + parts[1]) + (parts[2] + parts[3])
+        self.out[...] = total.reshape(self.out.shape)
         for j in range(4):
             for remote, _ in self.pair_copies(j):
                 remote.wait_send()
@@ -285,29 +286,35 @@
 
 
 class Homeward:
-    def __init__(self, place, src, home, send, recv):
-        self.place, self.src, self.home, self.send, self.recv = place, src, home, send, recv
-        self.part = home.shape[2]
+    def __init__(self, place, src, homes, send, recv):
+        self.place, self.src, self.homes, self.send, self.recv = place, src, homes, send, recv
+        self.part = homes[0].shape[1]
 
     def act(self, what):
         place, part = self.place, self.part
-        for k in (2, 1, 3, 0):
-            to, dp = place.up(k), place.d - place.core + lax.div(place.z, 2)
-            src = self.src.at[pl.ds(pl.multiple_of(to * part, 16), part), :]
-            dst = self.home.at[place.core, lax.rem(place.z, 2)]
-            here = jnp.logical_and(dp == place.d, to == place.z)
-            remote = push(src, dst, self.send.at[k], self.recv, dp, to)
-            if what == "start":
-                pl.when(here)(pltpu.make_async_copy(src, dst, self.recv).start)
-                pl.when(jnp.logical_not(here))(remote.start)
-            else:
-                pl.when(jnp.logical_not(here))(remote.wait_send)
+        for u in range(2):
+
+            @pl.when(place.core == u)
+            def _():
+                for k in (2, 1, 3, 0):
+                    to, dp = place.up(k), place.d - place.core + lax.div(place.z, 2)
+                    src = self.src.at[pl.ds(pl.multiple_of(to * part, 16), part), :]
+                    dst = self.homes[u].at[lax.rem(place.z, 2)]
+                    recv = self.recv.at[u]
+                    here = jnp.logical_and(dp == place.d, to == place.z)
+                    remote = push(src, dst, self.send.at[k], recv, dp, to)
+                    if what == "start":
+                        pl.when(here)(pltpu.make_async_copy(src, dst, recv).start)
+                        pl.when(jnp.logical_not(here))(remote.start)
+                    else:
+                        pl.when(jnp.logical_not(here))(remote.wait_send)
 
     def start(self):
         self.act("start")
 
     def end(self):
-        settle(self.home, self.recv)
+        for u in range(2):
+            settle(self.homes[u], self.recv.at[u])
         self.act("wait")
 
 
@@ -319,21 +326,24 @@
     return pair_and_z(place) + [(place.dp(r), place.z) for r in (XBIT, YBIT)]
 
 
-INPUTS = 11
+INPUTS = 8
 
 
 def finish_kernel(*refs):
-    hbm, (go_ref, small_ref) = refs[:INPUTS], refs[INPUTS : INPUTS + 2]
-    grads_ref, home_ref, sums_ref = refs[INPUTS + 2 : INPUTS + 5]
-    refs = refs[INPUTS + 5 :]
+    hbm, (go_ref, mixed_ref, small_ref) = refs[:INPUTS], refs[INPUTS : INPUTS + 3]
+    grad_refs, home_refs, sums_ref = refs[INPUTS + 3 : INPUTS + 8], refs[INPUTS + 8 : INPUTS + 10], refs[INPUTS + 10]
+    refs = refs[INPUTS + 11 :]
     held, refs = refs[:INPUTS], refs[INPUTS:]
-    loads, g_ref, base, ctx, partner, stream, slots, part_sum, chips = refs[:9]
-    home_send, slot_send, chip_send, one_send, recv = refs[9:14]
-    refs = refs[14:]
+    loads, x_t, ctx_t, g_ref, base, ctx, partner, stream, slots, part_sum, chips = refs[:11]
+    home_send, slot_send, chip_send, one_send, recv = refs[11:16]
+    refs = refs[16:]
     count = len(refs) // 5
     place = Place()
     d, z, core = place.d, place.z, place.core
-    copies = [pltpu.make_async_copy(a, b, loads.at[i]) for i, (a, b) in enumerate(zip(hbm, held))]
+    copies = [
+        pltpu.make_async_copy(a.at[0:3] if i == 5 else a, b, loads.at[i])
+        for i, (a, b) in enumerate(zip(hbm, held))
+    ]
     for copy in copies:
         copy.start()
 
@@ -345,7 +355,7 @@
     greet(near_partners(place) + [(place.dp(XBIT | YBIT), z)])
     sources = [g_ref.at[m : m + 1] for m in range(4)] + [go_ref]
     key, value, query, pos, out = [
-        Reduce(place, (src,), refs[m * count : (m + 1) * count], grads_ref.at[m : m + 1])
+        Reduce(place, (src,), refs[m * count : (m + 1) * count], grad_refs[m])
         for m, src in enumerate(sources)
     ]
     out.begin()
@@ -367,21 +377,31 @@
 
         lax.fori_loop(0, width // block, run, 0)
 
-    x_t, d_proj = need(0, 1)
+    def turn(src, dst):
+        def run(i, carry):
+            at = pl.ds(pl.multiple_of(i * block, block), block)
+            dst[:, at] = jnp.transpose(src[at, :].astype(F32)).astype(BF)
+            return carry
+
+        lax.fori_loop(0, src.shape[0] // block, run, 0)
+
+    x_ref, d_proj = need(0, 1)
+    turn(x_ref, x_t)
     product(2, x_t, d_proj, nn)
     query.begin()
-    ctx_t, dk_t = need(2, 3)
+    ctx_ref, dk_t = need(2, 3)
+    turn(ctx_ref, ctx_t)
     product(0, ctx_t, dk_t, nt)
     key.begin()
     out.pairs()
 
-    dv_t, w_key, w_value, w_query, d_mixed = need(4, 5, 6, 7, 8)
+    dv_t, mats = need(4, 5)
     back = dk_t.shape[1] - base.shape[0]
 
     def from_context(i, carry):
         at = pl.ds(pl.multiple_of(i * block, block), block)
         cols = pl.ds(pl.multiple_of(i * block + back, block), block)
-        turned = nn(w_key[...], dk_t[:, cols]) + nn(w_value[...], dv_t[:, cols])
+        turned = nn(mats[0], dk_t[:, cols]) + nn(mats[1], dv_t[:, cols])
         turned = jnp.transpose(turned)
         base[at, :] = turned
         ctx[at, :] = turned.astype(BF)
@@ -393,7 +413,7 @@
 
     def from_proj(i, carry):
         at = pl.ds(pl.multiple_of(i * block, block), block)
-        own = d_mixed[at, :] + nt(d_proj[at, :], w_query[...])
+        own = mixed_ref[at, :] + nt(d_proj[at, :], mats[2])
         base[at, :] = own + jnp.where(core == 0, base[at, :], 0.0)
         return carry
 
@@ -413,11 +433,11 @@
         return carry
 
     lax.fori_loop(0, stream.shape[0] // small_block, add_partner, 0)
-    home = Homeward(place, stream, home_ref, home_send, recv.at[2])
+    home = Homeward(place, stream, home_refs, home_send, recv.at[2:4])
     home.start()
     out.middle()
 
-    table_t, dr_t = need(9, 10)
+    table_t, dr_t = need(6, 7)
     product(3, table_t, dr_t, nt)
     pos.begin()
     value.pairs()
@@ -432,10 +452,10 @@
     chip = lax.div(d, 2)
     chip_copies = []
     for i, r in enumerate((XBIT, YBIT, XBIT | YBIT)):
-        copy = push(part_sum, chips.at[chip], chip_send.at[i], recv.at[3], place.dp(r), z)
+        copy = push(part_sum, chips.at[chip], chip_send.at[i], recv.at[4], place.dp(r), z)
         copy.start()
         chip_copies.append(copy)
-    pltpu.make_async_copy(part_sum, chips.at[chip], recv.at[3]).start()
+    pltpu.make_async_copy(part_sum, chips.at[chip], recv.at[4]).start()
 
     pos.pairs()
     key.middle()
@@ -444,7 +464,7 @@
     key.late()
     pos.middle()
     value.late()
-    settle(chips, recv.at[3])
+    settle(chips, recv.at[4])
     sums_ref[...] = (chips[0] + chips[1]) + (chips[2] + chips[3])
     pos.late()
     for reduce in (out, query, key, value, pos):
@@ -454,14 +474,17 @@
         copy.wait_send()
 
 
-def finish(arrays, g_out, small):
-    x_t, d_proj = arrays[:2]
-    width, total = x_t.shape
+def finish(arrays, g_out, mixed, small):
+    total, width = arrays[0].shape
+    klen = arrays[2].shape[0]
     rows = width // 8
     vmem = pl.BlockSpec(memory_space=pltpu.VMEM)
     dma = lambda k: pltpu.SemaphoreType.DMA((k,))
-    scratch = [pltpu.VMEM(a.shape, a.dtype) for a in arrays] + [
+    scratch = [pltpu.VMEM((3,) + a.shape[1:] if a.ndim == 3 else a.shape, BF) for a in arrays]
+    scratch += [
         dma(INPUTS),
+        pltpu.VMEM((width, total), BF),
+        pltpu.VMEM((width, klen), BF),
         pltpu.VMEM((4, width, width), BF),
         pltpu.VMEM((total, width), F32),
         pltpu.VMEM((total, width), BF),
@@ -474,17 +497,17 @@
         dma(7),
         dma(3),
         dma(1),
-        dma(4),
+        dma(5),
     ]
     for _ in range(5):
         scratch += Reduce.scratch(1, 1, rows, width)
     return pl.pallas_call(
         finish_kernel,
-        in_specs=[ANY_SPEC] * (INPUTS + 1) + [vmem],
-        out_specs=[vmem, ANY_SPEC, vmem],
-        out_shape=[
-            jax.ShapeDtypeStruct((5, rows, width // 4), F32),
-            jax.ShapeDtypeStruct((2, 2, total // 4, width), BF),
+        in_specs=[ANY_SPEC] * (INPUTS + 1) + [vmem] * 2,
+        out_specs=[vmem] * 5 + [ANY_SPEC] * 2 + [vmem],
+        out_shape=[jax.ShapeDtypeStruct((rows, width // 4), F32)] * 5
+        + [jax.ShapeDtypeStruct((2, total // 4, width), BF)] * 2
+        + [
             jax.ShapeDtypeStruct(small.shape, F32),
         ],
         scratch_shapes=scratch,
@@ -493,7 +516,7 @@
         ),
         cost_estimate=pl.CostEstimate(flops=20 << 30, bytes_accessed=64 << 20, transcendentals=0),
         name="finish",
-    )(*arrays, g_out, small)
+    )(*arrays, g_out, mixed, small)
 
 
 def pack(mat):
@@ -507,10 +530,14 @@
     return jnp.concatenate([packed[:rows, :], jnp.concatenate([rest[:, :64], rest[:, 64:]], axis=0)], axis=1)
 
 
-def exchange_kernel(slot_ref, content, query, memory, ints, *refs):
-    mats, (upw, dnw) = refs[:5], refs[5:7]
-    context, stream, all_ints, whole, out_slab, ud_slab = refs[7:13]
+def enter_kernel(slot_ref, content, query, memory, table_hbm, ints, *refs):
+    mats, (upw, dnw), (wb_ref, pb_ref) = refs[:5], refs[5:7], refs[7:9]
+    outs, (all_ints, whole_out, context_out, wo, ud) = refs[9:15], refs[15:20]
     (
+        whole,
+        context,
+        stream,
+        table,
         spread,
         picked,
         shards,
@@ -526,12 +553,18 @@
         pair_send,
         gather_send,
         gather_recv,
+        wo_send,
+        wo_recv,
+        far_send,
+        far_recv,
         recv,
-    ) = refs[13:]
+        local,
+    ) = refs[20:]
     place = Place()
     d, z, core = place.d, place.z, place.core
     up, down, far = place.up(1), place.up(3), place.up(2)
     part = query.shape[1]
+    pltpu.make_async_copy(table_hbm, table, local.at[0]).start()
     piece = spread.shape[1]
     blocks = part // piece // 2
     first = 4 * blocks
@@ -618,19 +651,20 @@
     gather = Gather(place, whole, slab.at[0:4], gather_send, gather_recv)
     gather.start(0, 1, 2, 3, 6, 7)
     pltpu.make_async_copy(slab.at[0:4], whole.at[:, own_rows, :], recv.at[6]).start()
-    pltpu.make_async_copy(slab.at[4:5], out_slab, recv.at[7]).start()
+    pltpu.make_async_copy(slab.at[4:5], wo.at[:, own_rows, :], recv.at[7]).start()
 
     width = upw.shape[1]
 
-    def columns(at, rows=slice(None)):
-        return ud_slab.at[:, rows, pl.ds(pl.multiple_of(at * width, 128), width)]
+    def columns(at, start=0, size=rows):
+        mine = pl.ds(pl.multiple_of(d * rows + start, 16), size)
+        return ud.at[:, mine, pl.ds(pl.multiple_of(at * width, 128), width)]
 
     def ud_copy(i):
         if i < 4:
             src, dst = (upw, dnw)[i % 2], columns(z).at[i % 2]
             return push(src, dst, ud_send.at[i], ud_recv.at[i // 2], d, (up, down)[i // 2])
         half = rows // 2
-        src = columns(down, slice(0, half)) if i == 4 else columns(up, slice(half, rows))
+        src = columns(down, 0, half) if i == 4 else columns(up, half, half)
         return push(src, src, ud_send.at[i], ud_recv.at[i - 2], d, (up, down)[i - 4])
 
     for i in range(4):
@@ -659,24 +693,52 @@
         lead_copy.start()
 
     gather.last()
-    gather.wait(range(6, 14), range(14))
+    wo_gather = Gather(place, wo, slab.at[4:5], wo_send, wo_recv)
+    ud_gather = Gather(place, ud, None, far_send, far_recv)
+    wo_gather.start(0, 1, 2, 3, 6, 7)
+    gather.wait(range(6, 14), ())
     settle(whole.at[:, own_rows, :], recv.at[6])
-    settle(out_slab, recv.at[7])
+    keep_whole = pltpu.make_async_copy(whole, whole_out, local.at[1])
+    keep_whole.start()
     settle(columns(z), recv.at[8])
     ud_copy(4).wait_recv()
     ud_copy(5).wait_recv()
+    ud_gather.start(0, 1, 2, 3, 6, 7)
+    gathers = (ud_gather, wo_gather)
+
+    keep_context = pltpu.make_async_copy(context, context_out, local.at[2])
+
+    def before_stream():
+        pick_pair.wait()
+
+        @pl.when(core == 0)
+        def _():
+            lead_copy.wait_send()
+
+        @pl.when(core == 1)
+        def _():
+            settle(context.at[first:], recv.at[3])
+            settle(stream, recv.at[4])
+
+        keep_context.start()
+
+    def before_context():
+        for one in gathers:
+            one.after((0, 1), ((8,), (9,)))
+
+    pltpu.make_async_copy(table_hbm, table, local.at[0]).wait()
+    project_step(
+        whole, context, stream, table, wb_ref, pb_ref, *outs, hooks=(before_stream, before_context)
+    )
+    for one in gathers:
+        one.after((2, 3), ((10,), (11,)))
+    settle(wo.at[:, own_rows, :], recv.at[7])
     settle(all_ints, recv.at[2])
-    pick_pair.wait()
-
-    @pl.when(core == 0)
-    def _():
-        lead_copy.wait_send()
-
-    @pl.when(core == 1)
-    def _():
-        settle(context.at[first:], recv.at[3])
-        settle(stream, recv.at[4])
-
+    gather.wait((), range(14))
+    for one in gathers:
+        one.wait(range(6, 12), (0, 1, 2, 3) + tuple(range(6, 12)))
+    keep_whole.wait()
+    keep_context.wait()
     for i in range(4):
         stream_copy(i, "wait")
         mat_copy(i).wait_send()
@@ -686,26 +748,37 @@
         copy.wait_send()
 
 
-def exchange(slot_of, content, query, memory, ints, mats, upw, dnw):
+def enter(slot_of, content, query, memory, table, ints, mats, upw, dnw, wb, pb):
     micro, part, width = content.shape
     rows = mats[0].shape[0]
     inner = upw.shape[1] * 4
     piece = part // 8
+    klen, span, seq = 8 * part, table.shape[0], 4 * part
     vmem = pl.BlockSpec(memory_space=pltpu.VMEM)
     dma = lambda n: pltpu.SemaphoreType.DMA((n,))
-    context, *rest = pl.pallas_call(
-        exchange_kernel,
-        in_specs=[SMEM_SPEC] + [ANY_SPEC] * 3 + [vmem] * 8,
-        out_specs=[ANY_SPEC] * 6,
+    bf = lambda *shape: jax.ShapeDtypeStruct(shape, BF)
+    return pl.pallas_call(
+        enter_kernel,
+        in_specs=[SMEM_SPEC] + [ANY_SPEC] * 4 + [vmem] * 10,
+        out_specs=[vmem] * 6 + [ANY_SPEC] * 5,
         out_shape=[
-            jax.ShapeDtypeStruct((32, 2, piece, width), BF),
-            jax.ShapeDtypeStruct((4 * part, width), BF),
+            bf(klen, width),
+            bf(klen, width),
+            bf(span, width),
+            bf(seq, width),
+            bf(seq, width),
+            bf(seq, width),
             jax.ShapeDtypeStruct((8,) + ints.shape, jnp.int32),
-            jax.ShapeDtypeStruct((4, 8 * rows, width), BF),
-            jax.ShapeDtypeStruct((1, rows, width), BF),
-            jax.ShapeDtypeStruct((2, rows, inner), BF),
+            bf(4, 8 * rows, width),
+            bf(32, 2, piece, width),
+            bf(1, 8 * rows, width),
+            bf(2, 8 * rows, inner),
         ],
         scratch_shapes=[
+            pltpu.VMEM((4, 8 * rows, width), BF),
+            pltpu.VMEM((32, 2, piece, width), BF),
+            pltpu.VMEM((seq, width), BF),
+            pltpu.VMEM((span, width), BF),
             pltpu.VMEM((16, piece, width), BF),
             pltpu.VMEM((16, piece, width), BF),
             pltpu.VMEM((4, 5, rows * 3 // 2, 128), BF),
@@ -721,15 +794,31 @@
             dma(2),
             dma(14),
             dma(14),
+            dma(14),
+            dma(14),
+            dma(14),
+            dma(14),
             dma(9),
+            dma(3),
         ],
         compiler_params=pltpu.CompilerParams(
             collective_id=1, has_side_effects=True, vmem_limit_bytes=LIMIT
         ),
         cost_estimate=pl.CostEstimate(flops=0, bytes_accessed=64 << 20, transcendentals=0),
-        name="exchange",
-    )(slot_of, content.reshape(micro, 4, 2, piece, width), query, memory, ints, *mats, upw, dnw)
-    return [context.reshape(8 * part, width)] + rest
+        name="enter",
+    )(
+        slot_of,
+        content.reshape(micro, 4, 2, piece, width),
+        query,
+        memory,
+        table,
+        ints,
+        *mats,
+        upw,
+        dnw,
+        wb,
+        pb,
+    )
 
 
 def head_lanes(array, head):
@@ -797,18 +886,21 @@
     def _():
         greet(near_partners(place))
         for gather in gathers:
-            gather.start(2, 3, 4, 5, 8, 9)
+            gather.start(4, 5)
         for i in range(4):
             tan_copy(i, "start")
-
-    attend_forward_step(block, *ins, *outs)
 
     @pl.when(step == steps - 1)
     def _():
         for gather in gathers:
-            gather.last()
+            gather.after((4, 5), ((12,), (13,)))
+
+    attend_forward_step(block, *ins, *outs)
+
+    @pl.when(step == steps - 1)
+    def _():
         for gather in gathers:
-            gather.wait(range(8, 14), (2, 3, 4, 5) + tuple(range(8, 14)))
+            gather.wait((12, 13), (4, 5, 12, 13))
         settle(tangent, recv.at[0])
         for i in range(4):
             tan_copy(i, "wait")
@@ -865,16 +957,16 @@
         attend_backward_step(block, *refs)
         return
     ins, (g_ud, src) = refs[:7], refs[7:9]
-    outs, (grads_ref, home_ref) = refs[9:14], refs[14:16]
-    rel_acc, home_send, home_recv = refs[16:19]
+    outs, grad_refs, home_refs = refs[9:14], refs[14:16], refs[16:18]
+    rel_acc, home_send, home_recv = refs[18:21]
     step, steps = pl.program_id(0), pl.num_programs(0)
     place = Place()
-    count = len(refs[19:]) // 2
+    count = len(refs[21:]) // 2
     reduces = [
-        Reduce(place, (g_ud.at[m : m + 1],), refs[19 + m * count : 19 + (m + 1) * count], grads_ref.at[m : m + 1])
+        Reduce(place, (g_ud.at[m : m + 1],), refs[21 + m * count : 21 + (m + 1) * count], grad_refs[m])
         for m in range(2)
     ]
-    home = Homeward(place, src, home_ref, home_send, home_recv.at[0])
+    home = Homeward(place, src, home_refs, home_send, home_recv)
 
     @pl.when(step == 0)
     def _():
@@ -1001,12 +1093,10 @@
     if wires:
         inner, mine = wires[0].shape[2], width // 8
         in_specs += [ANY_SPEC, ANY_SPEC]
-        out_specs += [pl.BlockSpec(memory_space=pltpu.VMEM), ANY_SPEC]
-        out_shape += [
-            jax.ShapeDtypeStruct((2, mine, inner // 4), F32),
-            jax.ShapeDtypeStruct((2, 2, rows // 4, width), BF),
-        ]
-        scratch += [pltpu.SemaphoreType.DMA((4,)), pltpu.SemaphoreType.DMA((1,))]
+        out_specs += [pl.BlockSpec(memory_space=pltpu.VMEM)] * 2 + [ANY_SPEC] * 2
+        out_shape += [jax.ShapeDtypeStruct((mine, inner // 4), F32)] * 2
+        out_shape += [jax.ShapeDtypeStruct((2, rows // 4, width), BF)] * 2
+        scratch += [pltpu.SemaphoreType.DMA((4,)), pltpu.SemaphoreType.DMA((2,))]
         scratch += 2 * Reduce.scratch(1, 1, mine, inner)
         params.update(collective_id=3, has_side_effects=True)
     return pl.pallas_call(
@@ -1047,11 +1137,7 @@
         x_ref,
         tan_ref,
         upb_ref,
-        dnb_ref,
-        g1_ref,
-        s1_ref,
-        g2_ref,
-        s2_ref,
+        rows_ref,
         out_ref,
         dmix_ref,
         gvec_ref,
@@ -1074,6 +1160,7 @@
     ) = refs
     step = pl.program_id(0)
     chunk = act_ref.shape[2]
+    dnb_ref, g1_ref, s1_ref, g2_ref, s2_ref = (rows_ref.at[i : i + 1] for i in range(5))
     cols = pl.ds(pl.multiple_of(lax.rem(step, steps) * chunk, chunk), chunk)
 
     @pl.when(step == 0)
@@ -1141,7 +1228,7 @@
         go_ref[...] = nn(gdt_ref[...], vec_ref[...]).astype(BF)
 
 
-def feed(ud, wo, vec, x, tan, upb, dnb, g1, s1, g2, s2):
+def feed(ud, wo, vec, x, tan, upb, vecs):
     rows, width = vec.shape
     inner = upb.shape[1]
     chunk = 512
@@ -1155,7 +1242,7 @@
         in_specs=[ANY_SPEC] * 2
         + [whole(rows, width)] * 3
         + [pl.BlockSpec((1, chunk), lambda i: (0, lax.rem(i, steps)))]
-        + [whole(1, width)] * 5,
+        + [whole(5, width)],
         out_specs=[
             whole(rows, width),
             whole(rows, width),
@@ -1193,44 +1280,32 @@
             flops=12 * rows * width * inner, bytes_accessed=36 << 20, transcendentals=rows * inner
         ),
         name="feed",
-    )(ud, wo, vec, x, tan, upb, dnb, g1, s1, g2, s2)
-
-
-def project_kernel(wired, *refs):
-    if not wired:
-        project_step(*refs)
-        return
-    ins, (out_slab, ud_slab) = refs[:6], refs[6:8]
-    outs, (wo, ud) = refs[8:14], refs[14:16]
-    out_send, out_recv, ud_send, ud_recv, own = refs[16:]
-    place = Place()
-    gathers = (
-        Gather(place, ud, ud_slab, ud_send, ud_recv),
-        Gather(place, wo, out_slab, out_send, out_recv),
-    )
-    rows = out_slab.shape[1]
-    own_rows = pl.ds(pl.multiple_of(place.d * rows, 16), rows)
-    locals_ = (
-        pltpu.make_async_copy(ud_slab, ud.at[:, own_rows, :], own.at[0]),
-        pltpu.make_async_copy(out_slab, wo.at[:, own_rows, :], own.at[1]),
-    )
-    greet([(place.dp(r), place.z) for r in (CORE, XBIT, YBIT)])
-    for gather in gathers:
-        gather.start(0, 1, 6, 7)
-    for copy in locals_:
-        copy.start()
-    project_step(*ins, *outs)
-    for gather in gathers:
-        gather.wait((0, 1, 6, 7), (0, 1, 6, 7))
-    for copy in locals_:
-        copy.wait()
+    )(ud, wo, vec, x, tan, upb, vecs)
 
 
 def project_step(
-    w_ref, ctx_ref, q_ref, table_ref, wb_ref, pb_ref, k_ref, v_ref, rel_ref, qw_ref, qp_ref, x_ref
+    w_ref,
+    ctx_ref,
+    q_ref,
+    table_ref,
+    wb_ref,
+    pb_ref,
+    k_ref,
+    v_ref,
+    rel_ref,
+    qw_ref,
+    qp_ref,
+    x_ref,
+    hooks=(),
 ):
     lead = lax.rem(lax.axis_index("dp"), 2) == 0
-    back = ctx_ref.shape[0] - q_ref.shape[0]
+    klen, width = k_ref.shape
+    back = klen - q_ref.shape[0]
+
+    def context_rows(start):
+        at = pl.ds(lax.div(start, 32), block // 32)
+        return ctx_ref[at].reshape(block, width)
+
     block = 256
 
     def loop(count, step):
@@ -1241,12 +1316,12 @@
         lax.fori_loop(0, count // block, run, 0)
 
     def context_step(at):
-        k_ref[at, :] = nn(ctx_ref[at, :], w_ref[0]).astype(BF)
-        v_ref[at, :] = nn(ctx_ref[at, :], w_ref[1]).astype(BF)
+        rows = context_rows(at.start)
+        k_ref[at, :] = nn(rows, w_ref[0]).astype(BF)
+        v_ref[at, :] = nn(rows, w_ref[1]).astype(BF)
 
     def stream_step(at):
-        own = ctx_ref[pl.ds(pl.multiple_of(at.start + back, block), block), :]
-        x_ref[at, :] = jnp.where(lead, own, q_ref[at, :])
+        x_ref[at, :] = jnp.where(lead, context_rows(at.start + back), q_ref[at, :])
         proj = nn(x_ref[at, :], w_ref[2])
         qw_ref[at, :] = (0.125 * (proj + wb_ref[...]).astype(BF).astype(F32)).astype(BF)
         qp_ref[at, :] = (0.125 * (proj + pb_ref[...]).astype(BF).astype(F32)).astype(BF)
@@ -1255,44 +1330,38 @@
         rel_ref[at, :] = nn(table_ref[at, :], w_ref[3]).astype(BF)
 
     loop(table_ref.shape[0], table_step)
+    if hooks:
+        hooks[0]()
     loop(q_ref.shape[0], stream_step)
-    loop(ctx_ref.shape[0], context_step)
-
-
-def project(mats, context, query, table, wb, pb, wires=()):
+    if hooks:
+        hooks[1]()
+    loop(klen, context_step)
+
+
+def project(mats, context, query, table, wb, pb):
     rows, width = query.shape
     klen, span = context.shape[0], table.shape[0]
     vmem = pl.BlockSpec(memory_space=pltpu.VMEM)
-    out_shape = [
-        jax.ShapeDtypeStruct((klen, width), BF),
-        jax.ShapeDtypeStruct((klen, width), BF),
-        jax.ShapeDtypeStruct((span, width), BF),
-        jax.ShapeDtypeStruct((rows, width), BF),
-        jax.ShapeDtypeStruct((rows, width), BF),
-        jax.ShapeDtypeStruct((rows, width), BF),
-    ]
-    params = dict(vmem_limit_bytes=LIMIT)
-    scratch = []
-    if wires:
-        params.update(collective_id=5, has_side_effects=True)
-        scratch = [pltpu.SemaphoreType.DMA((n,)) for n in (14, 14, 14, 14, 2)]
-        out_shape += [
-            jax.ShapeDtypeStruct((slab.shape[0], width, slab.shape[2]), BF) for slab in wires
-        ]
     return pl.pallas_call(
-        functools.partial(project_kernel, bool(wires)),
-        in_specs=[vmem] * (6 + len(wires)),
-        out_specs=[vmem] * 6 + [ANY_SPEC] * len(wires),
-        out_shape=out_shape,
-        scratch_shapes=scratch,
-        compiler_params=pltpu.CompilerParams(**params),
+        project_step,
+        in_specs=[vmem] * 6,
+        out_specs=[vmem] * 6,
+        out_shape=[
+            jax.ShapeDtypeStruct((klen, width), BF),
+            jax.ShapeDtypeStruct((klen, width), BF),
+            jax.ShapeDtypeStruct((span, width), BF),
+            jax.ShapeDtypeStruct((rows, width), BF),
+            jax.ShapeDtypeStruct((rows, width), BF),
+            jax.ShapeDtypeStruct((rows, width), BF),
+        ],
+        compiler_params=pltpu.CompilerParams(vmem_limit_bytes=LIMIT),
         cost_estimate=pl.CostEstimate(
             flops=2 * (2 * klen + rows + span) * width * width,
             bytes_accessed=20 << 20,
             transcendentals=0,
         ),
         name="project",
-    )(mats, context, query, table, wb, pb, *wires)
+    )(mats, context.reshape(klen // 32, 2, 16, width), query, table, wb, pb)
 
 
 def weight_grads_kernel(xt_ref, ct_ref, tt_ref, dp_ref, dk_ref, dv_ref, dr_ref, g_ref):
@@ -1404,14 +1473,26 @@
     slot = slot_of[seq_id]
     mats = [key_weight, value_weight, query_weight, pos_weight, out_weight]
     table = jnp.asarray(reversed_table(span, klen, width))
+    row = lambda v: v.reshape(1, -1)
     wires = ()
     if groups == 8:
         ints = jnp.pad(factor_order, ((0, 6), (0, 0)))
         ints = lax.dynamic_update_slice(ints, counts[None, :], (micro, 0))
-        context, query, all_ints, weights, out_slab, ud_slab = exchange(
-            slot_of, content_stream, query_stream, memory, ints, mats, up_weight, down_weight
+        keys, values, rel, q_word, q_pos, stream, all_ints, weights, context, *wires = enter(
+            slot_of,
+            content_stream,
+            query_stream,
+            memory,
+            table,
+            ints,
+            mats,
+            up_weight,
+            down_weight,
+            row(word_bias),
+            row(pos_bias),
         )
-        wires = (out_slab, ud_slab)
+        wires += [content_tangent, query_tangent]
+        context = context.reshape(klen, width)
         lengths = all_ints[:, micro, : 2 * micro]
         orders = all_ints[seq_id // micro, :micro]
     else:
@@ -1447,6 +1528,9 @@
         weights = jnp.stack([whole(mat) for mat in mats[:4]])
         wo = whole(out_weight)[None]
         ud = jnp.stack([whole(up_weight), whole(down_weight)])
+        keys, values, rel, q_word, q_pos, stream = project(
+            weights, context, query, table, row(word_bias), row(pos_bias)
+        )
 
     length = lengths[seq_id // micro, seq_id % micro]
     mem_valid = lengths[slot // micro, micro + slot % micro]
@@ -1458,12 +1542,6 @@
     key_rank = jnp.concatenate([mem_rank, own_rank])[None, :]
     thr = (rank + jnp.where(lead, 1, 0))[:, None]
 
-    row = lambda v: v.reshape(1, -1)
-    keys, values, rel, q_word, q_pos, stream, *wires = project(
-        weights, context, query, table, row(word_bias), row(pos_bias), wires
-    )
-    if wires:
-        wires += [content_tangent, query_tangent]
     vec, prob, *arrived = attend_forward(
         q_word, q_pos, keys, values, rel, thr, key_rank, block, wires
     )
@@ -1476,33 +1554,34 @@
         stream,
         tangent,
         row(up_bias),
-        row(down_bias),
-        row(first_gain),
-        row(first_shift),
-        row(second_gain),
-        row(second_shift),
+        jnp.stack([down_bias, first_gain, first_shift, second_gain, second_shift]),
     )
     backward = (prob, g_vec, q_word, q_pos, keys, values, rel, block)
     if groups == 8:
-        d_proj, dk_t, dv_t, drel_t, biases, (grad_up, grad_down), outs = attend_backward(
-            *backward, (g_ud, out)
+        d_proj, dk_t, dv_t, drel_t, biases, grad_up, grad_down, content_out, query_out = (
+            attend_backward(*backward, (g_ud, out))
         )
-        content_out, query_out = outs[0], outs[1]
     else:
         d_proj, dk_t, dv_t, drel_t, biases = attend_backward(*backward)
         content_out, query_out = from_unit(out)
         grad_up, grad_down = scatter_sum(g_ud)
     small = jnp.concatenate([g_upb.reshape(-1), small[:5].reshape(-1), biases.reshape(-1)])
     inner = up_bias.shape[0]
-    stream_t, context_t, table_t = (jnp.transpose(a) for a in (stream, context, table))
+    table_t = jnp.asarray(np.ascontiguousarray(reversed_table(span, klen, width).T))
     if groups == 8:
         size = small.shape[0]
         small = jnp.pad(small, (0, -size % 1024)).reshape(-1, 128)
-        arrays = [stream_t, d_proj, context_t, dk_t, dv_t, weights[0], weights[1], weights[2]]
-        arrays += [d_mixed, table_t, drel_t]
-        grads, homes, small = finish(arrays, g_out[None], small)
-        grad_key, grad_value, grad_query, grad_pos, grad_out = grads
-        content_grad, query_grad = homes[0], homes[1]
+        arrays = [stream, d_proj, context, dk_t, dv_t, weights, table_t, drel_t]
+        (
+            grad_key,
+            grad_value,
+            grad_query,
+            grad_pos,
+            grad_out,
+            content_grad,
+            query_grad,
+            small,
+        ) = finish(arrays, g_out[None], d_mixed, small)
         small = small.reshape(-1)[:size]
     else:
         d_context = tt(dk_t[:, mem_total:], weights[0]) + tt(dv_t[:, mem_total:], weights[1])
@@ -1510,7 +1589,7 @@
         d_stream = d_mixed + nt(d_proj, weights[2]) + jnp.where(lead, d_context + partner, 0.0)
         content_grad, query_grad = from_unit(d_stream.astype(BF))
         grad_key, grad_value, grad_query, grad_pos = scatter_sum(
-            weight_grads(stream_t, context_t, table_t, d_proj, dk_t, dv_t, drel_t)
+            weight_grads(jnp.transpose(stream), jnp.transpose(context), table_t, d_proj, dk_t, dv_t, drel_t)
         )
         (grad_out,) = scatter_sum(g_out[None])
         small = lax.psum(small, ("dp", "tensor"))

time: 335 us -> 332 us (level)
  local copies, waits for them, and re-layouts: 29.2 us -> 24.5 us
    pallas_call x1, Pallas kernels: 39.8 us -> 30.6 us  [attend_forward(): pl.pallas_call(functools.partial(attend_forward_kernel, block, bool(wires...]
    pallas_call x2 -> x1, Pallas kernels: 91.9 us -> 101 us  [enter(): pl.pallas_call(enter_kernel, in_specs=[SMEM_SPEC] + [ANY_SPEC] * 4 + [vme...]
    unnamed x16 -> x39, local copies, waits for them, and re-layouts: 0.63 us -> 9.29 us
    reshape x7 -> x2, local copies, waits for them, and re-layouts: 9.03 us -> 2.7 us  [body(): row = lambda v: v.reshape(1, -1)]
    squeeze x2 -> x0, local copies, waits for them, and re-layouts: 6.19 us -> none  [the longest x1 3.83 us: body(): weights[2]]
where the time goes in v7:
time: 332 us; the launch traced here: 331 us
  Pallas kernels  298 us (90%)
  local copies, waits for them, and re-layouts  24.5 us (7%)
  between operations  4.18 us (1%)
  other arithmetic  4.13 us (1%)
    pallas_call x1, Pallas kernels, enter(): pl.pallas_call(enter_kernel, in_specs=[SMEM_SPEC] + [ANY_SPEC] * 4 + [vme...  101 us
    pallas_call x1, Pallas kernels, attend_backward(): pl.pallas_call(functools.partial(attend_backward_kernel, block, bool(wire...  74.7 us
    pallas_call x1, Pallas kernels, finish(): pl.pallas_call(finish_kernel, in_specs=[ANY_SPEC] * (INPUTS + 1) + [vmem]...  58.6 us
    pallas_call x1, Pallas kernels, feed(): pl.pallas_call(functools.partial(feed_kernel, steps), grid=(2 * steps,),...  33.7 us
    pallas_call x1, Pallas kernels, attend_forward(): pl.pallas_call(functools.partial(attend_forward_kernel, block, bool(wires...  30.6 us
    unnamed x39, local copies, waits for them, and re-layouts  9.29 us

profile of v7, /device:TPU:0, one launch (start us, length us, event | category | flops | bytes accessed | tf_op | source)
XLA Modules:
  0.0 331.2 jit_solution(11288457522101671881)
XLA Ops:
  0.7 0.8 select_reduce_fusion.slot_ref
  4.7 0.7 add_bitcast_fusion.1
  5.5 0.7 stack.18
  6.2 1.4 reshape.107.refs_7_
  7.5 1.4 reshape.108.refs_8_
  8.9 0.7 stack.19
  9.5 0.7 stack.20
  10.2 0.7 stack.21
  10.9 0.7 stack.22
  12.2 0.7 pad.8
  13.7 100.8 %enter.1 = (bf16[1024,768]{1,0:T(8,128)(2,1)}, bf16[1024,768]{1,0:T(8,128)(2,1)}, bf16[1536,768]{1,0:T(8,128)(2,1)}, bf16[512,768]{1,0:T(8,128)(2,1)}, bf16[512,...) custom-call(s32[16]{0:T(128)} %copy-done.13, ...), custom_call_target="tpu_custom_call" | custom-call | bytes 67108864 | tf_op jit(solution)/shard_map/enter/pallas_call | solution.py:760
  114.5 0.7 add_bitcast_fusion
  115.3 0.8 slice.60
  117.3 0.7 compare_select_fusion.1
  118.5 0.9 copy.48.refs_5_
  119.4 30.6 %attend_forward.1 = (bf16[512,768]{1,0:T(8,128)(2,1)}, bf16[12,512,1024]{2,1,0:T(8,128)(2,1)}, bf16[1,768,768]{2,1,0:T(8,128)(2,1)}, bf16[2,768,3072]{2,1,0:T(8,128)(2,1)}, bf16[512,768]{1,0:T(8,128)(2,1)}) custom-call(bf16[512,768]{1,0:T(8,128)(2,1)} %get-tuple-element.59.refs_0_.refs_2_, ...), custom_call_target="tpu_custom_call", output_to_operand_aliasing={{2}: (7, {}), {3}: (8, {})} | custom-call | flops 3221225472 | bytes 16777216 | tf_op jit(solution)/shard_map/attend_forward/pallas_call | solution.py:939
  150.0 33.7 %feed.1 = (bf16[512,768]{1,0:T(8,128)(2,1)}, f32[512,768]{1,0:T(8,128)}, bf16[512,768]{1,0:T(8,128)(2,1)}, bf16[768,768]{1,0:T(8,128)(2,1)}, bf16[2,768,3072]{2,...) custom-call(bf16[2,768,3072]{2,1,0:T(8,128)(2,1)} %get-tuple-element.68.refs_0_, ...), custom_call_target="tpu_custom_call" | custom-call | flops 14495514624 | bytes 37748736 | tf_op jit(solution)/shard_map/feed/pallas_call | solution.py:1239
  183.7 74.7 %attend_backward.1 = (bf16[512,768]{1,0:T(8,128)(2,1)}, bf16[768,1024]{1,0:T(8,128)(2,1)}, bf16[768,1024]{1,0:T(8,128)(2,1)}, bf16[768,1536]{1,0:T(8,128)(2,1)},...) custom-call(bf16[12,512,1024]{2,1,0:T(8,128)(2,1)} %get-tuple-elemen, ...), custom_call_target="tpu_custom_call" | custom-call | flops 6442450944 | bytes 20971520 | tf_op jit(solution)/shard_map/attend_backward/pallas_call | solution.py:1102
  258.4 0.7 reshape.113
  259.8 58.6 %finish.1 = (f32[96,192]{1,0:T(8,128)}, f32[96,192]{1,0:T(8,128)}, f32[96,192]{1,0:T(8,128)}, f32[96,192]{1,0:T(8,128)}, f32[96,192]{1,0:T(8,128)}, /*index=5*/b...) custom-call(bf16[512,768]{1,0:T(8,128)(2,1)} %get-tuple-element.71.refs_3_.refs_0_, ...), custom_call_target="tpu_custom_call" | custom-call | flops 21474836480 | bytes 67108864 | tf_op jit(solution)/shard_map/finish/pallas_call | solution.py:504
  318.5 1.4 slice_bitcast_fusion
  319.9 1.4 slice_bitcast_fusion.1
  321.2 0.7 reshape_squeeze.7
  321.9 0.7 reshape_squeeze.6
  322.6 0.7 copy.63
  323.3 0.7 copy.64
  324.1 1.8 copy.65
  325.8 0.7 copy.66
  326.6 0.6 copy.67
  329.2 0.6 copy.71
  329.8 0.7 copy.72
  330.5 0.7 copy.73
  (39 shorter events, 5.7 us)
Async XLA Ops:
  1.5 11.6 %copy-start.13 = (s32[16]{0:T(128)}, s32[16]{0:T(128)S(1)}, u32[]{:S(2)}) copy-start(s32[16]{0:T(128)S(1)} %select_reduce_fusion.slot_ref) | copy-start | bytes 196
  13.1 0.6 copy-start.10
  183.7 75.5 %copy-start.11 = (f32[8,768]{1,0:T(8,128)S(1)}, f32[8,768]{1,0:T(8,128)}, u32[]{:S(2)}) copy-start(f32[8,768]{1,0:T(8,128)} %get-tuple-element.87) | copy-start | bytes 73732
  183.7 75.5 %copy-start.12 = (f32[1,3072]{1,0:T(1,128)S(1)}, f32[1,3072]{1,0:T(1,128)}, u32[]{:S(2)}) copy-start(f32[1,3072]{1,0:T(1,128)} %get-tuple-element.86) | copy-start | bytes 36868
  259.8 62.8 %copy-start.1 = (bf16[2,128,768]{2,1,0:T(8,128)(2,1)S(1)}, bf16[2,128,768]{2,1,0:T(8,128)(2,1)}, u32[]{:S(2)}) copy-start(bf16[2,128,768]{2,1,0:T(8,128)(2,1)} %get-tuple-element.131) | copy-start | bytes 1179652
  259.8 63.6 %copy-start = (bf16[2,128,768]{2,1,0:T(8,128)(2,1)S(1)}, bf16[2,128,768]{2,1,0:T(8,128)(2,1)}, u32[]{:S(2)}) copy-start(bf16[2,128,768]{2,1,0:T(8,128)(2,1)} %get-tuple-element.132) | copy-start | bytes 1179652
  318.4 7.5 %copy-start.2 = (bf16[2,128,768]{2,1,0:T(8,128)(2,1)S(1)}, bf16[2,128,768]{2,1,0:T(8,128)(2,1)}, u32[]{:S(2)}) copy-start(bf16[2,128,768]{2,1,0:T(8,128)(2,1)} %get-tuple-element.134) | copy-start | bytes 1179652
  318.4 8.2 %copy-start.9 = (f32[96,192]{1,0:T(8,128)S(1)}, f32[96,192]{1,0:T(8,128)}, u32[]{:S(2)}) copy-start(f32[96,192]{1,0:T(8,128)} %get-tuple-element.135) | copy-start | bytes 221188
  318.4 8.8 %copy-start.8 = (f32[96,192]{1,0:T(8,128)S(1)}, f32[96,192]{1,0:T(8,128)}, u32[]{:S(2)}) copy-start(f32[96,192]{1,0:T(8,128)} %get-tuple-element.136) | copy-start | bytes 221188
  318.4 9.5 %copy-start.7 = (f32[96,192]{1,0:T(8,128)S(1)}, f32[96,192]{1,0:T(8,128)}, u32[]{:S(2)}) copy-start(f32[96,192]{1,0:T(8,128)} %get-tuple-element.137) | copy-start | bytes 221188
  318.4 10.1 %copy-start.6 = (f32[96,192]{1,0:T(8,128)S(1)}, f32[96,192]{1,0:T(8,128)}, u32[]{:S(2)}) copy-start(f32[96,192]{1,0:T(8,128)} %get-tuple-element.138) | copy-start | bytes 221188
  318.4 10.7 %copy-start.5 = (f32[96,192]{1,0:T(8,128)S(1)}, f32[96,192]{1,0:T(8,128)}, u32[]{:S(2)}) copy-start(f32[96,192]{1,0:T(8,128)} %get-tuple-element.139) | copy-start | bytes 221188
  318.5 11.4 %copy-start.4 = (f32[96,768]{1,0:T(8,128)S(1)}, f32[96,768]{1,0:T(8,128)}, u32[]{:S(2)}) copy-start(f32[96,768]{1,0:T(8,128)} %get-tuple-element.140) | copy-start | bytes 884740
  322.6 8.0 %copy-start.3 = (f32[96,768]{1,0:T(8,128)S(1)}, f32[96,768]{1,0:T(8,128)}, u32[]{:S(2)}) copy-start(f32[96,768]{1,0:T(8,128)} %get-tuple-element.142) | copy-start | bytes 884740

commit v8 on v7

--- a/solution.py
+++ b/solution.py
@@ -63,7 +63,7 @@
             at = at + (2 - 4 * self.x)
         if bits & YBIT:
             at = at + (4 - 8 * self.y)
-        return at
+        return jnp.minimum(at, 15)
 
     def up(self, step):
         return lax.rem(self.z + step, 4) if step else self.z
@@ -519,6 +519,41 @@
     )(*arrays, g_out, mixed, small)
 
 
+def emit_kernel(small_ref, *refs):
+    count = 11
+    for src, dst in zip(refs[:count], refs[count : 2 * count]):
+        dst[...] = src[...]
+    wide, *rows, word_ref, pos_ref = refs[2 * count :]
+    lanes = small_ref.shape[1]
+    size = wide.shape[0] // lanes
+    wide[...] = small_ref[0:size, :].reshape(wide.shape)
+    for ref in rows:
+        step = ref.shape[0] // lanes
+        ref[...] = small_ref[size : size + step, :].reshape(ref.shape)
+        size += step
+    for ref in (word_ref, pos_ref):
+        for h in range(HEADS):
+            at = size + h * DH // lanes
+            ref[h : h + 1, :] = small_ref[at : at + 1, h * DH % lanes : h * DH % lanes + DH]
+        size += HEADS * DH // lanes
+
+
+def emit(small, arrays, inner, width):
+    vmem = pl.BlockSpec(memory_space=pltpu.VMEM)
+    out_shape = [jax.ShapeDtypeStruct(a.shape, a.dtype) for a in arrays]
+    out_shape += [jax.ShapeDtypeStruct((inner,), F32)]
+    out_shape += [jax.ShapeDtypeStruct((width,), F32)] * 5
+    out_shape += [jax.ShapeDtypeStruct((HEADS, DH), F32)] * 2
+    return pl.pallas_call(
+        emit_kernel,
+        in_specs=[vmem] * (1 + len(arrays)),
+        out_specs=[vmem] * len(out_shape),
+        out_shape=out_shape,
+        compiler_params=pltpu.CompilerParams(vmem_limit_bytes=LIMIT),
+        name="emit",
+    )(small, *arrays)
+
+
 def pack(mat):
     half = mat.shape[0] // 2
     return jnp.concatenate([mat[:, :128], jnp.concatenate([mat[:half, 128:], mat[half:, 128:]], axis=1)], axis=0)
@@ -530,10 +565,12 @@
     return jnp.concatenate([packed[:rows, :], jnp.concatenate([rest[:, :64], rest[:, 64:]], axis=0)], axis=1)
 
 
-def enter_kernel(slot_ref, content, query, memory, table_hbm, ints, *refs):
+def enter_kernel(slot_ref, seq_ref, mem_ref, content, query, memory, table_hbm, orders, *refs):
     mats, (upw, dnw), (wb_ref, pb_ref) = refs[:5], refs[5:7], refs[7:9]
-    outs, (all_ints, whole_out, context_out, wo, ud) = refs[9:15], refs[15:20]
+    outs, (thr_ref, key_ref, whole_out, context_out, wo, ud) = refs[9:15], refs[15:21]
     (
+        ints,
+        all_ints,
         whole,
         context,
         stream,
@@ -559,11 +596,23 @@
         far_recv,
         recv,
         local,
-    ) = refs[20:]
+    ) = refs[21:]
     place = Place()
     d, z, core = place.d, place.z, place.core
     up, down, far = place.up(1), place.up(3), place.up(2)
     part = query.shape[1]
+    micro = orders.shape[0]
+    spot = lax.broadcasted_iota(jnp.int32, (1, ints.shape[1]), 1)
+    lengths = jnp.where(spot == 0, seq_ref[0], seq_ref[1])
+    lengths = jnp.where(spot < 2, lengths, jnp.where(spot == 2, mem_ref[0], mem_ref[1]))
+    ints[...] = jnp.concatenate([orders[...], jnp.broadcast_to(lengths, (6, ints.shape[1]))], axis=0)
+
+    def slot_of(seq):
+        at = jnp.int32(0)
+        for k in range(16):
+            at = at + jnp.where(slot_ref[k] == seq, k, 0)
+        return jnp.minimum(at, 15)
+
     pltpu.make_async_copy(table_hbm, table, local.at[0]).start()
     piece = spread.shape[1]
     blocks = part // piece // 2
@@ -593,6 +642,26 @@
 
     mat_copy(0).start()
     mat_copy(1).start()
+    rows = slab.shape[1]
+    width = upw.shape[1]
+
+    def columns(at, start=0, size=rows):
+        mine = pl.ds(pl.multiple_of(d * rows + start, 16), size)
+        return ud.at[:, mine, pl.ds(pl.multiple_of(at * width, 128), width)]
+
+    def ud_copy(i):
+        if i < 4:
+            src, dst = (upw, dnw)[i % 2], columns(z).at[i % 2]
+            return push(src, dst, ud_send.at[i], ud_recv.at[i // 2], d, (up, down)[i // 2])
+        half = rows // 2
+        src = columns(down, 0, half) if i == 4 else columns(up, half, half)
+        return push(src, src, ud_send.at[i], ud_recv.at[i - 2], d, (up, down)[i - 4])
+
+    for i in range(4):
+        ud_copy(i).start()
+    for m, mat in enumerate((upw, dnw)):
+        pltpu.make_async_copy(mat, columns(z).at[m], recv.at[8]).start()
+
     int_copies = []
     for r in range(8):
         if r == 0:
@@ -623,12 +692,26 @@
     mat_copy(2).start()
     mat_copy(1).wait_recv()
     mat_copy(3).start()
+    mat_copy(2).wait_recv()
+    mat_copy(3).wait_recv()
+    for m in range(5):
+        slab[m] = jnp.concatenate([unpack(shards[k, m]) for k in range(4)], axis=1)
+    own_rows = pl.ds(pl.multiple_of(d * rows, 16), rows)
+    gather = Gather(place, whole, slab.at[0:4], gather_send, gather_recv)
+    gather.start(0, 1, 2, 3, 6, 7)
+    pltpu.make_async_copy(slab.at[0:4], whole.at[:, own_rows, :], recv.at[6]).start()
+    pltpu.make_async_copy(slab.at[4:5], wo.at[:, own_rows, :], recv.at[7]).start()
+
+    settle(columns(down), ud_recv.at[0])
+    ud_copy(4).start()
+    settle(columns(up), ud_recv.at[1])
+    ud_copy(5).start()
     for i in range(4):
         stream_copy(i, "start")
 
     settle(spread, recv.at[0])
     for q in range(16):
-        picked[q] = spread[slot_ref[q]]
+        picked[q] = spread[slot_of(q)]
     pick_copies = []
     for r in (YBIT | XBIT, XBIT, YBIT, 0):
         for k in range(4):
@@ -642,47 +725,23 @@
                 copy = pltpu.make_async_copy(src, dst, recv.at[5])
             copy.start()
 
-    mat_copy(2).wait_recv()
-    mat_copy(3).wait_recv()
-    for m in range(5):
-        slab[m] = jnp.concatenate([unpack(shards[k, m]) for k in range(4)], axis=1)
-    rows = slab.shape[1]
-    own_rows = pl.ds(pl.multiple_of(d * rows, 16), rows)
-    gather = Gather(place, whole, slab.at[0:4], gather_send, gather_recv)
-    gather.start(0, 1, 2, 3, 6, 7)
-    pltpu.make_async_copy(slab.at[0:4], whole.at[:, own_rows, :], recv.at[6]).start()
-    pltpu.make_async_copy(slab.at[4:5], wo.at[:, own_rows, :], recv.at[7]).start()
-
-    width = upw.shape[1]
-
-    def columns(at, start=0, size=rows):
-        mine = pl.ds(pl.multiple_of(d * rows + start, 16), size)
-        return ud.at[:, mine, pl.ds(pl.multiple_of(at * width, 128), width)]
-
-    def ud_copy(i):
-        if i < 4:
-            src, dst = (upw, dnw)[i % 2], columns(z).at[i % 2]
-            return push(src, dst, ud_send.at[i], ud_recv.at[i // 2], d, (up, down)[i // 2])
-        half = rows // 2
-        src = columns(down, 0, half) if i == 4 else columns(up, half, half)
-        return push(src, src, ud_send.at[i], ud_recv.at[i - 2], d, (up, down)[i - 4])
-
-    for i in range(4):
-        ud_copy(i).start()
-    for m, mat in enumerate((upw, dnw)):
-        pltpu.make_async_copy(mat, columns(z).at[m], recv.at[8]).start()
+    gather.middle()
+    wo_gather = Gather(place, wo, slab.at[4:5], wo_send, wo_recv)
+    ud_gather = Gather(place, ud, None, far_send, far_recv)
+    gathers = (ud_gather, wo_gather)
+    settle(columns(z), recv.at[8])
+    ud_copy(4).wait_recv()
+    ud_copy(5).wait_recv()
+    for i in (0, 1, 2, 3, 6, 7):
+        for one in gathers:
+            one.start(i)
+    gather.last()
 
     pick_pair = push(
         context.at[0:first, core], context.at[0:first, core], pair_send.at[0], recv.at[1], place.dp(CORE), z
     )
     settle(context.at[0:first, core], recv.at[5])
     pick_pair.start()
-    gather.middle()
-    settle(columns(down), ud_recv.at[0])
-    ud_copy(4).start()
-    settle(columns(up), ud_recv.at[1])
-    ud_copy(5).start()
-
     lead_copy = push(
         context.at[first:], context.at[first:], pair_send.at[1], recv.at[3], place.dp(CORE), z
     )
@@ -692,19 +751,31 @@
         settle(context.at[first:], recv.at[3])
         lead_copy.start()
 
-    gather.last()
-    wo_gather = Gather(place, wo, slab.at[4:5], wo_send, wo_recv)
-    ud_gather = Gather(place, ud, None, far_send, far_recv)
-    wo_gather.start(0, 1, 2, 3, 6, 7)
+    settle(all_ints, recv.at[2])
+    seq = 4 * lax.div(d, 2) + z
+    slot = slot_of(seq)
+    odd = lax.rem(seq, micro)
+    own, other = all_ints[lax.div(seq, micro)], all_ints[lax.div(slot, micro)]
+
+    def pick(row, at):
+        return jnp.sum(jnp.where(spot == at, row.astype(F32), 0.0), axis=1, keepdims=True)
+
+    length = pick(own[2:3], odd)
+    mem_valid = pick(other[2:3], micro + lax.rem(slot, micro))
+    rank = jnp.where(odd == 0, own[0:1], own[1:2])
+    seq_len = rank.shape[1]
+    mem_total = key_ref.shape[1] - seq_len
+    where = spot.astype(F32)
+    hidden = jnp.int32(1 << 20)
+    key_ref[:, :mem_total] = jnp.where(where >= mem_total - mem_valid, -1, hidden)
+    key_ref[:, mem_total:] = jnp.where(where < length, rank, hidden)
+    ranks = jnp.transpose(jnp.broadcast_to(rank.astype(F32), (8, seq_len)))
+    thr_ref[...] = ranks[:, 0:1].astype(jnp.int32) + jnp.where(core == 0, 1, 0)
+
     gather.wait(range(6, 14), ())
     settle(whole.at[:, own_rows, :], recv.at[6])
     keep_whole = pltpu.make_async_copy(whole, whole_out, local.at[1])
     keep_whole.start()
-    settle(columns(z), recv.at[8])
-    ud_copy(4).wait_recv()
-    ud_copy(5).wait_recv()
-    ud_gather.start(0, 1, 2, 3, 6, 7)
-    gathers = (ud_gather, wo_gather)
 
     keep_context = pltpu.make_async_copy(context, context_out, local.at[2])
 
@@ -733,7 +804,6 @@
     for one in gathers:
         one.after((2, 3), ((10,), (11,)))
     settle(wo.at[:, own_rows, :], recv.at[7])
-    settle(all_ints, recv.at[2])
     gather.wait((), range(14))
     for one in gathers:
         one.wait(range(6, 12), (0, 1, 2, 3) + tuple(range(6, 12)))
@@ -748,7 +818,7 @@
         copy.wait_send()
 
 
-def enter(slot_of, content, query, memory, table, ints, mats, upw, dnw, wb, pb):
+def enter(slots, seqs, mems, content, query, memory, table, orders, mats, upw, dnw, wb, pb):
     micro, part, width = content.shape
     rows = mats[0].shape[0]
     inner = upw.shape[1] * 4
@@ -759,8 +829,8 @@
     bf = lambda *shape: jax.ShapeDtypeStruct(shape, BF)
     return pl.pallas_call(
         enter_kernel,
-        in_specs=[SMEM_SPEC] + [ANY_SPEC] * 4 + [vmem] * 10,
-        out_specs=[vmem] * 6 + [ANY_SPEC] * 5,
+        in_specs=[SMEM_SPEC] * 3 + [ANY_SPEC] * 4 + [vmem] * 10,
+        out_specs=[vmem] * 8 + [ANY_SPEC] * 4,
         out_shape=[
             bf(klen, width),
             bf(klen, width),
@@ -768,13 +838,16 @@
             bf(seq, width),
             bf(seq, width),
             bf(seq, width),
-            jax.ShapeDtypeStruct((8,) + ints.shape, jnp.int32),
+            jax.ShapeDtypeStruct((seq, 1), jnp.int32),
+            jax.ShapeDtypeStruct((1, klen), jnp.int32),
             bf(4, 8 * rows, width),
             bf(32, 2, piece, width),
             bf(1, 8 * rows, width),
             bf(2, 8 * rows, inner),
         ],
         scratch_shapes=[
+            pltpu.VMEM((8, seq), jnp.int32),
+            pltpu.VMEM((8, 8, seq), jnp.int32),
             pltpu.VMEM((4, 8 * rows, width), BF),
             pltpu.VMEM((32, 2, piece, width), BF),
             pltpu.VMEM((seq, width), BF),
@@ -807,12 +880,14 @@
         cost_estimate=pl.CostEstimate(flops=0, bytes_accessed=64 << 20, transcendentals=0),
         name="enter",
     )(
-        slot_of,
+        slots,
+        seqs,
+        mems,
         content.reshape(micro, 4, 2, piece, width),
         query,
         memory,
         table,
-        ints,
+        orders,
         *mats,
         upw,
         dnw,
@@ -1137,7 +1212,11 @@
         x_ref,
         tan_ref,
         upb_ref,
-        rows_ref,
+        dnb_ref,
+        g1_ref,
+        s1_ref,
+        g2_ref,
+        s2_ref,
         out_ref,
         dmix_ref,
         gvec_ref,
@@ -1160,7 +1239,7 @@
     ) = refs
     step = pl.program_id(0)
     chunk = act_ref.shape[2]
-    dnb_ref, g1_ref, s1_ref, g2_ref, s2_ref = (rows_ref.at[i : i + 1] for i in range(5))
+    row = lambda ref: ref[...].reshape(1, -1)
     cols = pl.ds(pl.multiple_of(lax.rem(step, steps) * chunk, chunk), chunk)
 
     @pl.when(step == 0)
@@ -1173,15 +1252,15 @@
         normed, scale = norm_parts(nt(vec_ref[...], wo_ref[0]) + x_ref[...].astype(F32))
         n1_ref[...] = normed
         r1_ref[...] = scale
-        first = normed * g1_ref[...] + s1_ref[...]
+        first = normed * row(g1_ref) + row(s1_ref)
         fb_ref[...] = first.astype(BF)
         fbt_ref[...] = jnp.transpose(first).astype(BF)
-        acc_ref[...] = first + dnb_ref[...]
+        acc_ref[...] = first + row(dnb_ref)
         ud_copy.wait()
 
     @pl.when(step < steps)
     def _():
-        upper = nn(fb_ref[...], ud_ref[0, :, cols]) + upb_ref[...]
+        upper = nn(fb_ref[...], ud_ref[0, :, cols]) + row(upb_ref)
         square = upper * upper
         root = 0.7978845608028654
         bend = jnp.tanh(root * (upper + 0.044715 * (square * upper)))
@@ -1196,9 +1275,9 @@
     @pl.when(step == steps - 1)
     def _():
         normed, scale = norm_parts(acc_ref[...])
-        out_ref[...] = (normed * g2_ref[...] + s2_ref[...]).astype(BF)
+        out_ref[...] = (normed * row(g2_ref) + row(s2_ref)).astype(BF)
         tan = tan_ref[...].astype(F32)
-        d_down = norm_pull(normed, scale, tan * g2_ref[...])
+        d_down = norm_pull(normed, scale, tan * row(g2_ref))
         small_ref[0:1, :] = sum_rows(d_down)
         small_ref[3:4, :] = sum_rows(tan * normed)
         small_ref[4:5, :] = sum_rows(tan)
@@ -1221,7 +1300,7 @@
         d_first, normed = acc_ref[...], n1_ref[...]
         small_ref[1:2, :] = sum_rows(d_first * normed)
         small_ref[2:3, :] = sum_rows(d_first)
-        d_mixed = norm_pull(normed, r1_ref[...], d_first * g1_ref[...])
+        d_mixed = norm_pull(normed, r1_ref[...], d_first * row(g1_ref))
         dmix_ref[...] = d_mixed
         gvec_ref[...] = nn(d_mixed.astype(BF), wo_ref[0]).astype(BF)
         gdt_ref[...] = jnp.transpose(d_mixed).astype(BF)
@@ -1230,7 +1309,7 @@
 
 def feed(ud, wo, vec, x, tan, upb, vecs):
     rows, width = vec.shape
-    inner = upb.shape[1]
+    inner = upb.shape[0]
     chunk = 512
     steps = inner // chunk
     whole = lambda a, b: pl.BlockSpec((a, b), lambda i: (0, 0))
@@ -1241,8 +1320,8 @@
         grid=(2 * steps,),
         in_specs=[ANY_SPEC] * 2
         + [whole(rows, width)] * 3
-        + [pl.BlockSpec((1, chunk), lambda i: (0, lax.rem(i, steps)))]
-        + [whole(5, width)],
+        + [pl.BlockSpec((chunk,), lambda i: (lax.rem(i, steps),))]
+        + [pl.BlockSpec((width,), lambda i: (0,))] * 5,
         out_specs=[
             whole(rows, width),
             whole(rows, width),
@@ -1280,7 +1359,7 @@
             flops=12 * rows * width * inner, bytes_accessed=36 << 20, transcendentals=rows * inner
         ),
         name="feed",
-    )(ud, wo, vec, x, tan, upb, vecs)
+    )(ud, wo, vec, x, tan, upb, *vecs)
 
 
 def project_step(
@@ -1299,6 +1378,8 @@
     hooks=(),
 ):
     lead = lax.rem(lax.axis_index("dp"), 2) == 0
+    flat = lambda ref: jnp.concatenate([ref[h : h + 1, :] for h in range(ref.shape[0])], axis=1)
+    word_bias, pos_bias = flat(wb_ref), flat(pb_ref)
     klen, width = k_ref.shape
     back = klen - q_ref.shape[0]
 
@@ -1323,8 +1404,8 @@
     def stream_step(at):
         x_ref[at, :] = jnp.where(lead, context_rows(at.start + back), q_ref[at, :])
         proj = nn(x_ref[at, :], w_ref[2])
-        qw_ref[at, :] = (0.125 * (proj + wb_ref[...]).astype(BF).astype(F32)).astype(BF)
-        qp_ref[at, :] = (0.125 * (proj + pb_ref[...]).astype(BF).astype(F32)).astype(BF)
+        qw_ref[at, :] = (0.125 * (proj + word_bias).astype(BF).astype(F32)).astype(BF)
+        qp_ref[at, :] = (0.125 * (proj + pos_bias).astype(BF).astype(F32)).astype(BF)
 
     def table_step(at):
         rel_ref[at, :] = nn(table_ref[at, :], w_ref[3]).astype(BF)
@@ -1467,35 +1548,32 @@
         return jnp.where(lead, low, got), jnp.where(lead, got, high)
 
     seq_id = (here // 2) * tensors + lane
-    ids = jnp.arange(count, dtype=jnp.int32)
-    slot_of = jnp.sum(jnp.where(slot_sequence[None, :] == ids[:, None], ids[None, :], 0), axis=1)
-    counts = jnp.concatenate([seq_lengths, memory_lengths])
-    slot = slot_of[seq_id]
     mats = [key_weight, value_weight, query_weight, pos_weight, out_weight]
     table = jnp.asarray(reversed_table(span, klen, width))
-    row = lambda v: v.reshape(1, -1)
     wires = ()
     if groups == 8:
-        ints = jnp.pad(factor_order, ((0, 6), (0, 0)))
-        ints = lax.dynamic_update_slice(ints, counts[None, :], (micro, 0))
-        keys, values, rel, q_word, q_pos, stream, all_ints, weights, context, *wires = enter(
-            slot_of,
+        keys, values, rel, q_word, q_pos, stream, thr, key_rank, weights, context, *wires = enter(
+            slot_sequence,
+            seq_lengths,
+            memory_lengths,
             content_stream,
             query_stream,
             memory,
             table,
-            ints,
+            factor_order,
             mats,
             up_weight,
             down_weight,
-            row(word_bias),
-            row(pos_bias),
+            word_bias,
+            pos_bias,
         )
         wires += [content_tangent, query_tangent]
         context = context.reshape(klen, width)
-        lengths = all_ints[:, micro, : 2 * micro]
-        orders = all_ints[seq_id // micro, :micro]
     else:
+        ids = jnp.arange(count, dtype=jnp.int32)
+        slot_of = jnp.sum(jnp.where(slot_sequence[None, :] == ids[:, None], ids[None, :], 0), axis=1)
+        counts = jnp.concatenate([seq_lengths, memory_lengths])
+        slot = slot_of[seq_id]
         lengths = lax.all_gather(counts, "dp", axis=0, tiled=False)
         orders = lax.all_gather(factor_order, "dp", axis=0, tiled=False)[seq_id // micro]
         stream = to_unit(content_stream, query_stream)
@@ -1529,18 +1607,17 @@
         wo = whole(out_weight)[None]
         ud = jnp.stack([whole(up_weight), whole(down_weight)])
         keys, values, rel, q_word, q_pos, stream = project(
-            weights, context, query, table, row(word_bias), row(pos_bias)
+            weights, context, query, table, word_bias, pos_bias
         )
-
-    length = lengths[seq_id // micro, seq_id % micro]
-    mem_valid = lengths[slot // micro, micro + slot % micro]
-    rank = orders[seq_id % micro]
-    key_pos = jnp.arange(klen, dtype=jnp.int32)
-    hidden = jnp.int32(1 << 20)
-    mem_rank = jnp.where(key_pos[:mem_total] >= mem_total - mem_valid, -1, hidden)
-    own_rank = jnp.where(key_pos[:seq_len] < length, rank, hidden)
-    key_rank = jnp.concatenate([mem_rank, own_rank])[None, :]
-    thr = (rank + jnp.where(lead, 1, 0))[:, None]
+        length = lengths[seq_id // micro, seq_id % micro]
+        mem_valid = lengths[slot // micro, micro + slot % micro]
+        rank = orders[seq_id % micro]
+        key_pos = jnp.arange(klen, dtype=jnp.int32)
+        hidden = jnp.int32(1 << 20)
+        mem_rank = jnp.where(key_pos[:mem_total] >= mem_total - mem_valid, -1, hidden)
+        own_rank = jnp.where(key_pos[:seq_len] < length, rank, hidden)
+        key_rank = jnp.concatenate([mem_rank, own_rank])[None, :]
+        thr = (rank + jnp.where(lead, 1, 0))[:, None]
 
     vec, prob, *arrived = attend_forward(
         q_word, q_pos, keys, values, rel, thr, key_rank, block, wires
@@ -1553,8 +1630,8 @@
         vec,
         stream,
         tangent,
-        row(up_bias),
-        jnp.stack([down_bias, first_gain, first_shift, second_gain, second_shift]),
+        up_bias,
+        (down_bias, first_gain, first_shift, second_gain, second_shift),
     )
     backward = (prob, g_vec, q_word, q_pos, keys, values, rel, block)
     if groups == 8:
@@ -1569,8 +1646,7 @@
     inner = up_bias.shape[0]
     table_t = jnp.asarray(np.ascontiguousarray(reversed_table(span, klen, width).T))
     if groups == 8:
-        size = small.shape[0]
-        small = jnp.pad(small, (0, -size % 1024)).reshape(-1, 128)
+        small = jnp.pad(small, (0, -small.shape[0] % 1024)).reshape(-1, 128)
         arrays = [stream, d_proj, context, dk_t, dv_t, weights, table_t, drel_t]
         (
             grad_key,
@@ -1582,7 +1658,12 @@
             query_grad,
             small,
         ) = finish(arrays, g_out[None], d_mixed, small)
-        small = small.reshape(-1)[:size]
+        arrays = [content_out, query_out, content_grad, query_grad, grad_query, grad_key]
+        arrays += [grad_value, grad_pos, grad_out, grad_up, grad_down]
+        *arrays, up_sum, down_sum, a1, b1, a2, b2, word_sum, pos_sum = emit(
+            small, arrays, inner, width
+        )
+        return *arrays[:10], up_sum, arrays[10], down_sum, word_sum, pos_sum, a1, b1, a2, b2
     else:
         d_context = tt(dk_t[:, mem_total:], weights[0]) + tt(dv_t[:, mem_total:], weights[1])
         partner = swap(d_context.astype(BF)).astype(F32)

time: 332 us -> 299 us (0.901)
  local copies, waits for them, and re-layouts: 24.5 us -> 0.72 us
  other arithmetic: 4.13 us -> 0.62 us
    unnamed x39 -> x4, local copies, waits for them, and re-layouts: 9.29 us -> 0.01 us
    another operation x8 -> x0, local copies, waits for them, and re-layouts: 5.41 us -> none  [the longest x6 4.08 us: body(): jnp.stack([down_bias, first_gain, first_shift, second_gain, second_shift])]
    pallas_call x1 -> x2, Pallas kernels: 101 us -> 97.9 us  [the longest x1 94.6 us: enter(): pl.pallas_call(enter_kernel, in_specs=[SMEM_SPEC] * 3 + [ANY_SPEC] * 4 +...]
where the time goes in v8:
time: 299 us
  Pallas kernels  296 us (99%)
    pallas_call x1, Pallas kernels, enter(): pl.pallas_call(enter_kernel, in_specs=[SMEM_SPEC] * 3 + [ANY_SPEC] * 4 +...  94.6 us
    pallas_call x1, Pallas kernels, attend_backward(): pl.pallas_call(functools.partial(attend_backward_kernel, block, bool(wire...  75.3 us
    pallas_call x1, Pallas kernels, finish(): pl.pallas_call(finish_kernel, in_specs=[ANY_SPEC] * (INPUTS + 1) + [vmem]...  58.6 us
    pallas_call x1, Pallas kernels, feed(): pl.pallas_call(functools.partial(feed_kernel, steps), grid=(2 * steps,),...  33.9 us
    pallas_call x1, Pallas kernels, attend_forward(): pl.pallas_call(functools.partial(attend_forward_kernel, block, bool(wires...  30.9 us

profile of v8, /device:TPU:0, one launch (start us, length us, event | category | flops | bytes accessed | tf_op | source)
XLA Modules:
  0.0 298.7 jit_solution(5488653705981606408)
XLA Ops:
  0.7 94.6 %enter.1 = (bf16[1024,768]{1,0:T(8,128)(2,1)}, bf16[1024,768]{1,0:T(8,128)(2,1)}, bf16[1536,768]{1,0:T(8,128)(2,1)}, bf16[512,768]{1,0:T(8,128)(2,1)}, bf16[512,...) custom-call(s32[16]{0:T(128)} %slot_ref.1, ...), custom_call_target="tpu_custom_call" | custom-call | bytes 67108864 | tf_op jit(solution)/shard_map/enter/pallas_call | solution.py:830
  95.2 30.9 %attend_forward.1 = (bf16[512,768]{1,0:T(8,128)(2,1)}, bf16[12,512,1024]{2,1,0:T(8,128)(2,1)}, bf16[1,768,768]{2,1,0:T(8,128)(2,1)}, bf16[2,768,3072]{2,1,0:T(8,128)(2,1)}, bf16[512,768]{1,0:T(8,128)(2,1)}) custom-call(bf16[512,768]{1,0:T(8,128)(2,1)} %get-tuple-element.80.refs_0_.refs_2_, ...), custom_call_target="tpu_custom_call", output_to_operand_aliasing={{2}: (7, {}), {3}: (8, {})} | custom-call | flops 3221225472 | bytes 16777216 | tf_op jit(solution)/shard_map/attend_forward/pallas_call | solution.py:1014
  126.1 33.9 %feed.1 = (bf16[512,768]{1,0:T(8,128)(2,1)}, f32[512,768]{1,0:T(8,128)}, bf16[512,768]{1,0:T(8,128)(2,1)}, bf16[768,768]{1,0:T(8,128)(2,1)}, bf16[2,768,3072]{2,...) custom-call(bf16[2,768,3072]{2,1,0:T(8,128)(2,1)} %get-tuple-element.90.refs_0_, ...), custom_call_target="tpu_custom_call" | custom-call | flops 14495514624 | bytes 37748736 | tf_op jit(solution)/shard_map/feed/pallas_call | solution.py:1318
  160.0 0.0 copy-start
  160.0 0.0 copy-start.1
  160.1 75.3 %attend_backward.1 = (bf16[512,768]{1,0:T(8,128)(2,1)}, bf16[768,1024]{1,0:T(8,128)(2,1)}, bf16[768,1024]{1,0:T(8,128)(2,1)}, bf16[768,1536]{1,0:T(8,128)(2,1)},...) custom-call(bf16[12,512,1024]{2,1,0:T(8,128)(2,1)} %get-tuple-elemen, ...), custom_call_target="tpu_custom_call" | custom-call | flops 6442450944 | bytes 20971520 | tf_op jit(solution)/shard_map/attend_backward/pallas_call | solution.py:1177
  235.3 0.7 reshape.60
  236.0 0.0 copy-done
  236.1 0.0 copy-done.1
  236.1 0.6 fusion.refs_10_
  236.7 58.6 %finish.1 = (f32[96,192]{1,0:T(8,128)}, f32[96,192]{1,0:T(8,128)}, f32[96,192]{1,0:T(8,128)}, f32[96,192]{1,0:T(8,128)}, f32[96,192]{1,0:T(8,128)}, /*index=5*/b...) custom-call(bf16[512,768]{1,0:T(8,128)(2,1)} %get-tuple-element.79.refs_3_.refs_0_, ...), custom_call_target="tpu_custom_call" | custom-call | flops 21474836480 | bytes 67108864 | tf_op jit(solution)/shard_map/finish/pallas_call | solution.py:504
  295.3 3.3 %emit.1 = (bf16[2,128,768]{2,1,0:T(8,128)(2,1)}, bf16[2,128,768]{2,1,0:T(8,128)(2,1)}, bf16[2,128,768]{2,1,0:T(8,128)(2,1)}, bf16[2,128,768]{2,1,0:T(8,128)(2,1)...) custom-call(f32[72,128]{1,0:T(8,128)} %get-tuple-element.108.small_r, ...), custom_call_target="tpu_custom_call" | custom-call | tf_op jit(solution)/shard_map/emit/pallas_call | solution.py:547
  (1 shorter events, 0.0 us)
Async XLA Ops:
  160.0 76.0 %copy-start = (f32[8,768]{1,0:T(8,128)S(1)}, f32[8,768]{1,0:T(8,128)}, u32[]{:S(2)}) copy-start(f32[8,768]{1,0:T(8,128)} %get-tuple-element.106) | copy-start | bytes 73732
  160.0 76.0 %copy-start.1 = (f32[1,3072]{1,0:T(1,128)S(1)}, f32[1,3072]{1,0:T(1,128)}, u32[]{:S(2)}) copy-start(f32[1,3072]{1,0:T(1,128)} %get-tuple-element.105) | copy-start | bytes 36868

commit v9 on v8

--- a/solution.py
+++ b/solution.py
@@ -63,7 +63,7 @@
             at = at + (2 - 4 * self.x)
         if bits & YBIT:
             at = at + (4 - 8 * self.y)
-        return jnp.minimum(at, 15)
+        return at
 
     def up(self, step):
         return lax.rem(self.z + step, 4) if step else self.z
@@ -166,19 +166,19 @@
 
 
 class Reduce:
-    def __init__(self, place, sources, scratch, out):
-        self.place, self.sources, self.out = place, sources, out
+    def __init__(self, place, sources, scratch, out, paired=False):
+        self.place, self.sources, self.out, self.paired = place, sources, out, paired
         self.total, self.pair, self.near, self.far, self.quarter, self.stage = scratch[:6]
         self.pair_send, self.pair_recv, self.load, self.send, self.recv, self.z_send, self.z_recv = scratch[6:]
         self.rows = self.total.shape[2]
 
     @staticmethod
-    def scratch(count, n, rows, cols):
+    def scratch(count, n, rows, cols, paired=False):
         part = cols // 4
         dma = lambda k: pltpu.SemaphoreType.DMA((k,))
         return [
             pltpu.VMEM((n, 4, rows, cols), BF),
-            pltpu.VMEM((n, 4, rows, cols), BF),
+            pltpu.VMEM((8, 128) if paired else (n, 4, rows, cols), BF),
             pltpu.VMEM((n, 2, 2, rows // 2, cols), BF),
             pltpu.VMEM((n, 2, rows // 2, cols), BF),
             pltpu.VMEM((4, n, rows, part), BF),
@@ -237,18 +237,27 @@
             return pltpu.make_async_copy(src, dst, self.z_recv.at[0])
         return push(src, dst, self.z_send.at[k - 1], self.z_recv.at[0], place.d, to)
 
+    def loaded(self, j):
+        return pltpu.make_async_copy(self.sources[0].at[:, j], self.total.at[:, j], self.load.at[j])
+
     def begin(self):
         for j in (3, 1, 2, 0):
+            if self.paired:
+                self.loaded(j).start()
+                continue
             for remote, local in self.pair_copies(j):
                 remote.start()
                 local.start()
 
     def pairs(self):
         for j, moves in ((3, (0, 1)), (1, (2,)), (2, (3,)), (0, ())):
-            for remote, local in self.pair_copies(j):
-                local.wait()
-                remote.wait_recv()
-            add_into(self.total.at[:, j], self.pair.at[:, j])
+            if self.paired:
+                self.loaded(j).wait()
+            else:
+                for remote, local in self.pair_copies(j):
+                    local.wait()
+                    remote.wait_recv()
+                add_into(self.total.at[:, j], self.pair.at[:, j])
             for i in moves:
                 self.move(i).start()
 
@@ -276,9 +285,10 @@
         parts = [self.quarter[k].astype(F32) for k in range(4)]
         total = (parts[0] + parts[1]) + (parts[2] + parts[3])
         self.out[...] = total.reshape(self.out.shape)
-        for j in range(4):
-            for remote, _ in self.pair_copies(j):
-                remote.wait_send()
+        if not self.paired:
+            for j in range(4):
+                for remote, _ in self.pair_copies(j):
+                    remote.wait_send()
         for i in range(6):
             self.move(i).wait_send()
         for k in range(1, 4):
@@ -657,8 +667,6 @@
         src = columns(down, 0, half) if i == 4 else columns(up, half, half)
         return push(src, src, ud_send.at[i], ud_recv.at[i - 2], d, (up, down)[i - 4])
 
-    for i in range(4):
-        ud_copy(i).start()
     for m, mat in enumerate((upw, dnw)):
         pltpu.make_async_copy(mat, columns(z).at[m], recv.at[8]).start()
 
@@ -692,6 +700,8 @@
     mat_copy(2).start()
     mat_copy(1).wait_recv()
     mat_copy(3).start()
+    for i in range(4):
+        ud_copy(i).start()
     mat_copy(2).wait_recv()
     mat_copy(3).wait_recv()
     for m in range(5):
@@ -1038,7 +1048,7 @@
     place = Place()
     count = len(refs[21:]) // 2
     reduces = [
-        Reduce(place, (g_ud.at[m : m + 1],), refs[21 + m * count : 21 + (m + 1) * count], grad_refs[m])
+        Reduce(place, (g_ud.at[m : m + 1],), refs[21 + m * count : 21 + (m + 1) * count], grad_refs[m], True)
         for m in range(2)
     ]
     home = Homeward(place, src, home_refs, home_send, home_recv)
@@ -1049,25 +1059,22 @@
         for reduce in reduces:
             reduce.begin()
         home.start()
-
-    @pl.when(step == 2)
-    def _():
-        reduces[0].pairs()
+        for reduce in reduces:
+            reduce.pairs()
 
     @pl.when(step == 3)
     def _():
-        reduces[1].pairs()
+        reduces[0].middle()
 
     @pl.when(step == 5)
     def _():
-        reduces[0].middle()
+        reduces[1].middle()
 
     attend_backward_step(block, *ins, *outs, rel_acc)
 
     @pl.when(step == steps - 1)
     def _():
         reduces[0].late()
-        reduces[1].middle()
         reduces[1].late()
         reduces[0].end()
         reduces[1].end()
@@ -1166,13 +1173,13 @@
     scratch = [pltpu.VMEM((PAIR, span), F32)]
     params = dict(vmem_limit_bytes=LIMIT)
     if wires:
-        inner, mine = wires[0].shape[2], width // 8
+        inner, mine = wires[0].shape[3], width // 8
         in_specs += [ANY_SPEC, ANY_SPEC]
         out_specs += [pl.BlockSpec(memory_space=pltpu.VMEM)] * 2 + [ANY_SPEC] * 2
         out_shape += [jax.ShapeDtypeStruct((mine, inner // 4), F32)] * 2
         out_shape += [jax.ShapeDtypeStruct((2, rows // 4, width), BF)] * 2
         scratch += [pltpu.SemaphoreType.DMA((4,)), pltpu.SemaphoreType.DMA((2,))]
-        scratch += 2 * Reduce.scratch(1, 1, mine, inner)
+        scratch += 2 * Reduce.scratch(1, 1, mine, inner, True)
         params.update(collective_id=3, has_side_effects=True)
     return pl.pallas_call(
         functools.partial(attend_backward_kernel, block, bool(wires)),
@@ -1204,7 +1211,7 @@
     return jnp.sum(value, axis=0, keepdims=True)
 
 
-def feed_kernel(steps, *refs):
+def feed_kernel(steps, wired, *refs):
     (
         ud_hbm,
         wo_hbm,
@@ -1236,11 +1243,55 @@
         gd_ref,
         gdt_ref,
         sems,
+        *pair_refs,
     ) = refs
     step = pl.program_id(0)
     chunk = act_ref.shape[2]
     row = lambda ref: ref[...].reshape(1, -1)
     cols = pl.ds(pl.multiple_of(lax.rem(step, steps) * chunk, chunk), chunk)
+
+    if wired:
+        own_ref, pair_ref, sum_ref, send, recv, keep = pair_refs
+        place = Place()
+        rows = pair_ref.shape[2]
+
+        def span(c):
+            return pl.ds(pl.multiple_of(c * chunk, chunk), chunk)
+
+        def block(bits):
+            return pl.ds(pl.multiple_of(place.dp(bits) * rows, 16), rows)
+
+        def pair_copy(c, j):
+            slot = lax.rem(c, 2)
+            return push(
+                own_ref.at[slot, :, block(chip_bits(j) | CORE), :],
+                pair_ref.at[:, j, :, span(c)],
+                send.at[slot, j],
+                recv.at[c],
+                place.dp(CORE),
+                place.z,
+            )
+
+        def keep_copy(c):
+            slot = lax.rem(c, 2)
+            return pltpu.make_async_copy(sum_ref.at[slot], gud_ref.at[:, :, :, span(c)], keep.at[slot])
+
+        def join(c):
+            slot = lax.rem(c, 2)
+            settle(pair_ref.at[:, :, :, span(c)], recv.at[c])
+            pl.when(c >= 2)(lambda: keep_copy(c - 2).wait())
+            for j in range(4):
+                mine = own_ref[slot, :, block(chip_bits(j)), :].astype(F32)
+                sum_ref[slot, :, j] = (mine + pair_ref[:, j, :, span(c)].astype(F32)).astype(BF)
+            keep_copy(c).start()
+
+        def send_wait(c):
+            for j in range(4):
+                pair_copy(c, j).wait_send()
+
+        @pl.when(step == 0)
+        def _():
+            greet([(place.dp(CORE), place.z)])
 
     @pl.when(step == 0)
     def _():
@@ -1292,8 +1343,17 @@
         gupb_ref[...] = sum_rows(d_up)
         g_up = d_up.astype(BF)
         acc_ref[...] += nt(g_up, ud_ref[0, :, cols])
-        gud_ref[0] = nn(fbt_ref[...], g_up).astype(BF)
-        gud_ref[1] = nn(gdt_ref[...], act_ref[at]).astype(BF)
+        if not wired:
+            gud_ref[0] = nn(fbt_ref[...], g_up).astype(BF)
+            gud_ref[1] = nn(gdt_ref[...], act_ref[at]).astype(BF)
+            return
+        pl.when(at >= 2)(lambda: send_wait(at - 2))
+        slot = lax.rem(at, 2)
+        own_ref[slot, 0] = nn(fbt_ref[...], g_up).astype(BF)
+        own_ref[slot, 1] = nn(gdt_ref[...], act_ref[at]).astype(BF)
+        for j in range(4):
+            pair_copy(at, j).start()
+        pl.when(at >= 1)(lambda: join(at - 1))
 
     @pl.when(step == 2 * steps - 1)
     def _():
@@ -1305,9 +1365,14 @@
         gvec_ref[...] = nn(d_mixed.astype(BF), wo_ref[0]).astype(BF)
         gdt_ref[...] = jnp.transpose(d_mixed).astype(BF)
         go_ref[...] = nn(gdt_ref[...], vec_ref[...]).astype(BF)
-
-
-def feed(ud, wo, vec, x, tan, upb, vecs):
+        if wired:
+            join(steps - 1)
+            for c in (steps - 2, steps - 1):
+                send_wait(c)
+                keep_copy(c).wait()
+
+
+def feed(ud, wo, vec, x, tan, upb, vecs, wired):
     rows, width = vec.shape
     inner = upb.shape[0]
     chunk = 512
@@ -1315,8 +1380,23 @@
     whole = lambda a, b: pl.BlockSpec((a, b), lambda i: (0, 0))
     late = lambda i: jnp.maximum(i - steps, 0)
     grads = pl.BlockSpec((2, width, chunk), lambda i: (0, 0, late(i)))
+    grad_shape = (2, width, inner)
+    params = dict(vmem_limit_bytes=LIMIT)
+    scratch = []
+    if wired:
+        mine = width // 8
+        grads, grad_shape = ANY_SPEC, (2, 4, mine, inner)
+        scratch = [
+            pltpu.VMEM((2, 2, width, chunk), BF),
+            pltpu.VMEM(grad_shape, BF),
+            pltpu.VMEM((2, 2, 4, mine, chunk), BF),
+            pltpu.SemaphoreType.DMA((2, 4)),
+            pltpu.SemaphoreType.DMA((steps,)),
+            pltpu.SemaphoreType.DMA((2,)),
+        ]
+        params.update(collective_id=6, has_side_effects=True)
     return pl.pallas_call(
-        functools.partial(feed_kernel, steps),
+        functools.partial(feed_kernel, steps, wired),
         grid=(2 * steps,),
         in_specs=[ANY_SPEC] * 2
         + [whole(rows, width)] * 3
@@ -1336,7 +1416,7 @@
             jax.ShapeDtypeStruct((rows, width), F32),
             jax.ShapeDtypeStruct((rows, width), BF),
             jax.ShapeDtypeStruct((width, width), BF),
-            jax.ShapeDtypeStruct((2, width, inner), BF),
+            jax.ShapeDtypeStruct(grad_shape, BF),
             jax.ShapeDtypeStruct((1, inner), F32),
             jax.ShapeDtypeStruct((8, width), F32),
         ],
@@ -1353,8 +1433,9 @@
             pltpu.VMEM((rows, width), BF),
             pltpu.VMEM((width, rows), BF),
             pltpu.SemaphoreType.DMA((2,)),
-        ],
-        compiler_params=pltpu.CompilerParams(vmem_limit_bytes=LIMIT),
+        ]
+        + scratch,
+        compiler_params=pltpu.CompilerParams(**params),
         cost_estimate=pl.CostEstimate(
             flops=12 * rows * width * inner, bytes_accessed=36 << 20, transcendentals=rows * inner
         ),
@@ -1632,6 +1713,7 @@
         tangent,
         up_bias,
         (down_bias, first_gain, first_shift, second_gain, second_shift),
+        groups == 8,
     )
     backward = (prob, g_vec, q_word, q_pos, keys, values, rel, block)
     if groups == 8:

time: 299 us -> 280 us (0.936)
  Pallas kernels: 296 us -> 278 us
    pallas_call x1, Pallas kernels: 94.6 us -> 82 us  [enter(): pl.pallas_call(enter_kernel, in_specs=[SMEM_SPEC] * 3 + [ANY_SPEC] * 4 +...]
    pallas_call x1, Pallas kernels: 75.3 us -> 65.9 us  [attend_backward(): pl.pallas_call(functools.partial(attend_backward_kernel, block, bool(wire...]
    pallas_call x1, Pallas kernels: 33.9 us -> 37 us  [feed(): pl.pallas_call(functools.partial(feed_kernel, steps, wired), grid=(2 * st...]
where the time goes in v9:
time: 280 us
  Pallas kernels  278 us (99%)
    pallas_call x1, Pallas kernels, enter(): pl.pallas_call(enter_kernel, in_specs=[SMEM_SPEC] * 3 + [ANY_SPEC] * 4 +...  82 us
    pallas_call x1, Pallas kernels, attend_backward(): pl.pallas_call(functools.partial(attend_backward_kernel, block, bool(wire...  65.9 us
    pallas_call x1, Pallas kernels, finish(): pl.pallas_call(finish_kernel, in_specs=[ANY_SPEC] * (INPUTS + 1) + [vmem]...  58.5 us
    pallas_call x1, Pallas kernels, feed(): pl.pallas_call(functools.partial(feed_kernel, steps, wired), grid=(2 * st...  37 us
    pallas_call x1, Pallas kernels, attend_forward(): pl.pallas_call(functools.partial(attend_forward_kernel, block, bool(wires...  31.1 us

profile of v9, /device:TPU:0, one launch (start us, length us, event | category | flops | bytes accessed | tf_op | source)
XLA Modules:
  0.0 280.0 jit_solution(4483188984212880109)
XLA Ops:
  0.7 82.0 %enter.1 = (bf16[1024,768]{1,0:T(8,128)(2,1)}, bf16[1024,768]{1,0:T(8,128)(2,1)}, bf16[1536,768]{1,0:T(8,128)(2,1)}, bf16[512,768]{1,0:T(8,128)(2,1)}, bf16[512,...) custom-call(s32[16]{0:T(128)} %slot_ref.1, ...), custom_call_target="tpu_custom_call" | custom-call | bytes 67108864 | tf_op jit(solution)/shard_map/enter/pallas_call | solution.py:840
  82.6 31.1 %attend_forward.1 = (bf16[512,768]{1,0:T(8,128)(2,1)}, bf16[12,512,1024]{2,1,0:T(8,128)(2,1)}, bf16[1,768,768]{2,1,0:T(8,128)(2,1)}, bf16[2,768,3072]{2,1,0:T(8,128)(2,1)}, bf16[512,768]{1,0:T(8,128)(2,1)}) custom-call(bf16[512,768]{1,0:T(8,128)(2,1)} %get-tuple-element.80.refs_0_.refs_2_, ...), custom_call_target="tpu_custom_call", output_to_operand_aliasing={{2}: (7, {}), {3}: (8, {})} | custom-call | flops 3221225472 | bytes 16777216 | tf_op jit(solution)/shard_map/attend_forward/pallas_call | solution.py:1024
  113.7 37.0 %feed.1 = (bf16[512,768]{1,0:T(8,128)(2,1)}, f32[512,768]{1,0:T(8,128)}, bf16[512,768]{1,0:T(8,128)(2,1)}, bf16[768,768]{1,0:T(8,128)(2,1)}, bf16[2,4,96,3072]{3...) custom-call(bf16[2,768,3072]{2,1,0:T(8,128)(2,1)} %get-tuple-element.90.refs_0_, ...), custom_call_target="tpu_custom_call" | custom-call | flops 14495514624 | bytes 37748736 | tf_op jit(solution)/shard_map/feed/pallas_call | solution.py:1398
  150.8 0.0 copy-start
  150.8 0.0 copy-start.1
  150.8 65.9 %attend_backward.1 = (bf16[512,768]{1,0:T(8,128)(2,1)}, bf16[768,1024]{1,0:T(8,128)(2,1)}, bf16[768,1024]{1,0:T(8,128)(2,1)}, bf16[768,1536]{1,0:T(8,128)(2,1)},...) custom-call(bf16[12,512,1024]{2,1,0:T(8,128)(2,1)} %get-tuple-elemen, ...), custom_call_target="tpu_custom_call" | custom-call | flops 6442450944 | bytes 20971520 | tf_op jit(solution)/shard_map/attend_backward/pallas_call | solution.py:1184
  216.7 0.7 reshape.60
  217.4 0.0 copy-done
  217.4 0.0 copy-done.1
  217.4 0.6 fusion.refs_10_
  218.0 58.5 %finish.1 = (f32[96,192]{1,0:T(8,128)}, f32[96,192]{1,0:T(8,128)}, f32[96,192]{1,0:T(8,128)}, f32[96,192]{1,0:T(8,128)}, f32[96,192]{1,0:T(8,128)}, /*index=5*/b...) custom-call(bf16[512,768]{1,0:T(8,128)(2,1)} %get-tuple-element.79.refs_3_.refs_0_, ...), custom_call_target="tpu_custom_call" | custom-call | flops 21474836480 | bytes 67108864 | tf_op jit(solution)/shard_map/finish/pallas_call | solution.py:514
  276.6 3.3 %emit.1 = (bf16[2,128,768]{2,1,0:T(8,128)(2,1)}, bf16[2,128,768]{2,1,0:T(8,128)(2,1)}, bf16[2,128,768]{2,1,0:T(8,128)(2,1)}, bf16[2,128,768]{2,1,0:T(8,128)(2,1)...) custom-call(f32[72,128]{1,0:T(8,128)} %get-tuple-element.108.small_r, ...), custom_call_target="tpu_custom_call" | custom-call | tf_op jit(solution)/shard_map/emit/pallas_call | solution.py:557
  (1 shorter events, 0.0 us)
Async XLA Ops:
  150.8 66.6 %copy-start = (f32[8,768]{1,0:T(8,128)S(1)}, f32[8,768]{1,0:T(8,128)}, u32[]{:S(2)}) copy-start(f32[8,768]{1,0:T(8,128)} %get-tuple-element.106) | copy-start | bytes 73732
  150.8 66.6 %copy-start.1 = (f32[1,3072]{1,0:T(1,128)S(1)}, f32[1,3072]{1,0:T(1,128)}, u32[]{:S(2)}) copy-start(f32[1,3072]{1,0:T(1,128)} %get-tuple-element.105) | copy-start | bytes 36868

commit v10 on v9

--- a/solution.py
+++ b/solution.py
@@ -238,7 +238,10 @@
         return push(src, dst, self.z_send.at[k - 1], self.z_recv.at[0], place.d, to)
 
     def loaded(self, j):
-        return pltpu.make_async_copy(self.sources[0].at[:, j], self.total.at[:, j], self.load.at[j])
+        src, near = self.sources
+        if j == 3:
+            return pltpu.make_async_copy(near, self.near, self.load.at[3])
+        return pltpu.make_async_copy(src.at[:, j], self.total.at[:, j], self.load.at[j])
 
     def begin(self):
         for j in (3, 1, 2, 0):
@@ -251,19 +254,20 @@
 
     def pairs(self):
         for j, moves in ((3, (0, 1)), (1, (2,)), (2, (3,)), (0, ())):
-            if self.paired:
-                self.loaded(j).wait()
-            else:
-                for remote, local in self.pair_copies(j):
-                    local.wait()
-                    remote.wait_recv()
-                add_into(self.total.at[:, j], self.pair.at[:, j])
+            for remote, local in self.pair_copies(j):
+                local.wait()
+                remote.wait_recv()
+            add_into(self.total.at[:, j], self.pair.at[:, j])
             for i in moves:
                 self.move(i).start()
 
     def middle(self):
         for i, j, h, where, more in ((0, 2, 0, 1, 4), (1, 1, 1, 1, 5), (2, 0, 0, 0, None), (3, 0, 1, 0, None)):
-            self.move(i).wait_recv()
+            if not self.paired:
+                self.move(i).wait_recv()
+            elif i == 0:
+                for k in range(4):
+                    self.loaded(k).wait()
             add_into(self.half(j, h), self.near.at[:, h, where])
             if more is not None:
                 self.move(more).start()
@@ -289,7 +293,7 @@
             for j in range(4):
                 for remote, _ in self.pair_copies(j):
                     remote.wait_send()
-        for i in range(6):
+        for i in range(4 if self.paired else 0, 6):
             self.move(i).wait_send()
         for k in range(1, 4):
             self.z_copy(k).wait_send()
@@ -340,14 +344,14 @@
 
 
 def finish_kernel(*refs):
-    hbm, (go_ref, mixed_ref, small_ref) = refs[:INPUTS], refs[INPUTS : INPUTS + 3]
-    grad_refs, home_refs, sums_ref = refs[INPUTS + 3 : INPUTS + 8], refs[INPUTS + 8 : INPUTS + 10], refs[INPUTS + 10]
-    refs = refs[INPUTS + 11 :]
+    hbm, (mixed_ref, small_ref) = refs[:INPUTS], refs[INPUTS : INPUTS + 2]
+    grad_refs, home_refs, sums_ref = refs[INPUTS + 2 : INPUTS + 6], refs[INPUTS + 6 : INPUTS + 8], refs[INPUTS + 8]
+    refs = refs[INPUTS + 9 :]
     held, refs = refs[:INPUTS], refs[INPUTS:]
     loads, x_t, ctx_t, g_ref, base, ctx, partner, stream, slots, part_sum, chips = refs[:11]
     home_send, slot_send, chip_send, one_send, recv = refs[11:16]
     refs = refs[16:]
-    count = len(refs) // 5
+    count = len(refs) // 4
     place = Place()
     d, z, core = place.d, place.z, place.core
     copies = [
@@ -363,12 +367,11 @@
         return [held[i] for i in which]
 
     greet(near_partners(place) + [(place.dp(XBIT | YBIT), z)])
-    sources = [g_ref.at[m : m + 1] for m in range(4)] + [go_ref]
-    key, value, query, pos, out = [
+    sources = [g_ref.at[m : m + 1] for m in range(4)]
+    key, value, query, pos = [
         Reduce(place, (src,), refs[m * count : (m + 1) * count], grad_refs[m])
         for m, src in enumerate(sources)
     ]
-    out.begin()
     slot_copies = []
     others = [(r, k) for k in range(4) for r in (0, CORE) if r or k]
     for i, (r, k) in enumerate(others):
@@ -403,7 +406,6 @@
     turn(ctx_ref, ctx_t)
     product(0, ctx_t, dk_t, nt)
     key.begin()
-    out.pairs()
 
     dv_t, mats = need(4, 5)
     back = dk_t.shape[1] - base.shape[0]
@@ -445,14 +447,12 @@
     lax.fori_loop(0, stream.shape[0] // small_block, add_partner, 0)
     home = Homeward(place, stream, home_refs, home_send, recv.at[2:4])
     home.start()
-    out.middle()
 
     table_t, dr_t = need(6, 7)
     product(3, table_t, dr_t, nt)
     pos.begin()
     value.pairs()
     query.middle()
-    out.late()
 
     settle(slots, recv.at[1])
     total = slots[0]
@@ -477,14 +477,14 @@
     settle(chips, recv.at[4])
     sums_ref[...] = (chips[0] + chips[1]) + (chips[2] + chips[3])
     pos.late()
-    for reduce in (out, query, key, value, pos):
+    for reduce in (query, key, value, pos):
         reduce.end()
     home.end()
     for copy in slot_copies + chip_copies:
         copy.wait_send()
 
 
-def finish(arrays, g_out, mixed, small):
+def finish(arrays, mixed, small):
     total, width = arrays[0].shape
     klen = arrays[2].shape[0]
     rows = width // 8
@@ -509,13 +509,13 @@
         dma(1),
         dma(5),
     ]
-    for _ in range(5):
+    for _ in range(4):
         scratch += Reduce.scratch(1, 1, rows, width)
     return pl.pallas_call(
         finish_kernel,
-        in_specs=[ANY_SPEC] * (INPUTS + 1) + [vmem] * 2,
-        out_specs=[vmem] * 5 + [ANY_SPEC] * 2 + [vmem],
-        out_shape=[jax.ShapeDtypeStruct((rows, width // 4), F32)] * 5
+        in_specs=[ANY_SPEC] * INPUTS + [vmem] * 2,
+        out_specs=[vmem] * 4 + [ANY_SPEC] * 2 + [vmem],
+        out_shape=[jax.ShapeDtypeStruct((rows, width // 4), F32)] * 4
         + [jax.ShapeDtypeStruct((2, total // 4, width), BF)] * 2
         + [
             jax.ShapeDtypeStruct(small.shape, F32),
@@ -526,7 +526,7 @@
         ),
         cost_estimate=pl.CostEstimate(flops=20 << 30, bytes_accessed=64 << 20, transcendentals=0),
         name="finish",
-    )(*arrays, g_out, mixed, small)
+    )(*arrays, mixed, small)
 
 
 def emit_kernel(small_ref, *refs):
@@ -1041,16 +1041,19 @@
     if not wired:
         attend_backward_step(block, *refs)
         return
-    ins, (g_ud, src) = refs[:7], refs[7:9]
-    outs, grad_refs, home_refs = refs[9:14], refs[14:16], refs[16:18]
-    rel_acc, home_send, home_recv = refs[18:21]
+    ins, (g_ud, near_ud, g_out, src) = refs[:7], refs[7:11]
+    outs, grad_refs, home_refs = refs[11:16], refs[16:19], refs[19:21]
+    rel_acc, home_send, home_recv = refs[21:24]
+    refs = refs[24:]
     step, steps = pl.program_id(0), pl.num_programs(0)
     place = Place()
-    count = len(refs[21:]) // 2
+    count = len(refs) // 3
+    held = [refs[m * count : (m + 1) * count] for m in range(3)]
     reduces = [
-        Reduce(place, (g_ud.at[m : m + 1],), refs[21 + m * count : 21 + (m + 1) * count], grad_refs[m], True)
+        Reduce(place, (g_ud.at[m : m + 1], near_ud.at[m : m + 1]), held[m], grad_refs[m], True)
         for m in range(2)
     ]
+    out = Reduce(place, (g_out,), held[2], grad_refs[2])
     home = Homeward(place, src, home_refs, home_send, home_recv)
 
     @pl.when(step == 0)
@@ -1058,26 +1061,35 @@
         greet(near_partners(place))
         for reduce in reduces:
             reduce.begin()
+        out.begin()
         home.start()
+
+    @pl.when(step == 1)
+    def _():
         for reduce in reduces:
-            reduce.pairs()
+            reduce.middle()
+        out.pairs()
 
     @pl.when(step == 3)
     def _():
-        reduces[0].middle()
+        reduces[0].late()
+
+    @pl.when(step == 4)
+    def _():
+        reduces[1].late()
+        out.middle()
 
     @pl.when(step == 5)
     def _():
-        reduces[1].middle()
+        out.late()
 
     attend_backward_step(block, *ins, *outs, rel_acc)
 
     @pl.when(step == steps - 1)
     def _():
-        reduces[0].late()
-        reduces[1].late()
-        reduces[0].end()
-        reduces[1].end()
+        for reduce in reduces:
+            reduce.end()
+        out.end()
         home.end()
 
 
@@ -1174,12 +1186,13 @@
     params = dict(vmem_limit_bytes=LIMIT)
     if wires:
         inner, mine = wires[0].shape[3], width // 8
-        in_specs += [ANY_SPEC, ANY_SPEC]
-        out_specs += [pl.BlockSpec(memory_space=pltpu.VMEM)] * 2 + [ANY_SPEC] * 2
+        in_specs += [ANY_SPEC] * 4
+        out_specs += [pl.BlockSpec(memory_space=pltpu.VMEM)] * 3 + [ANY_SPEC] * 2
         out_shape += [jax.ShapeDtypeStruct((mine, inner // 4), F32)] * 2
+        out_shape += [jax.ShapeDtypeStruct((mine, width // 4), F32)]
         out_shape += [jax.ShapeDtypeStruct((2, rows // 4, width), BF)] * 2
         scratch += [pltpu.SemaphoreType.DMA((4,)), pltpu.SemaphoreType.DMA((2,))]
-        scratch += 2 * Reduce.scratch(1, 1, mine, inner, True)
+        scratch += 2 * Reduce.scratch(1, 1, mine, inner, True) + Reduce.scratch(1, 1, mine, width)
         params.update(collective_id=3, has_side_effects=True)
     return pl.pallas_call(
         functools.partial(attend_backward_kernel, block, bool(wires)),
@@ -1231,6 +1244,10 @@
         gud_ref,
         gupb_ref,
         small_ref,
+        *refs,
+    ) = refs
+    near_ref, *refs = refs if wired else (None, *refs)
+    (
         ud_ref,
         wo_ref,
         n1_ref,
@@ -1251,7 +1268,7 @@
     cols = pl.ds(pl.multiple_of(lax.rem(step, steps) * chunk, chunk), chunk)
 
     if wired:
-        own_ref, pair_ref, sum_ref, send, recv, keep = pair_refs
+        own_ref, pair_ref, sum_ref, send, recv, keep, move_send, move_recv = pair_refs
         place = Place()
         rows = pair_ref.shape[2]
 
@@ -1273,16 +1290,27 @@
             )
 
         def keep_copy(c):
-            slot = lax.rem(c, 2)
-            return pltpu.make_async_copy(sum_ref.at[slot], gud_ref.at[:, :, :, span(c)], keep.at[slot])
+            return pltpu.make_async_copy(sum_ref.at[c], gud_ref.at[:, :, :, span(c)], keep.at[c])
+
+        def move(c, i):
+            j, h, to, where = Reduce.MOVES[i]
+            return push(
+                sum_ref.at[c, :, j, h * (rows // 2) : (h + 1) * (rows // 2), :],
+                near_ref.at[:, h, where, :, span(c)],
+                move_send.at[c, i],
+                move_recv.at[c],
+                place.dp(to),
+                place.z,
+            )
 
         def join(c):
             slot = lax.rem(c, 2)
             settle(pair_ref.at[:, :, :, span(c)], recv.at[c])
-            pl.when(c >= 2)(lambda: keep_copy(c - 2).wait())
-            for j in range(4):
+            for j in (3, 1, 2, 0):
                 mine = own_ref[slot, :, block(chip_bits(j)), :].astype(F32)
-                sum_ref[slot, :, j] = (mine + pair_ref[:, j, :, span(c)].astype(F32)).astype(BF)
+                sum_ref[c, :, j] = (mine + pair_ref[:, j, :, span(c)].astype(F32)).astype(BF)
+            for i in range(4):
+                move(c, i).start()
             keep_copy(c).start()
 
         def send_wait(c):
@@ -1291,7 +1319,7 @@
 
         @pl.when(step == 0)
         def _():
-            greet([(place.dp(CORE), place.z)])
+            greet([(place.dp(r), place.z) for r in (CORE, XBIT, YBIT)])
 
     @pl.when(step == 0)
     def _():
@@ -1369,7 +1397,11 @@
             join(steps - 1)
             for c in (steps - 2, steps - 1):
                 send_wait(c)
+            for c in range(steps):
                 keep_copy(c).wait()
+                settle(near_ref.at[:, :, :, :, span(c)], move_recv.at[c])
+                for i in range(4):
+                    move(c, i).wait_send()
 
 
 def feed(ud, wo, vec, x, tan, upb, vecs, wired):
@@ -1382,18 +1414,21 @@
     grads = pl.BlockSpec((2, width, chunk), lambda i: (0, 0, late(i)))
     grad_shape = (2, width, inner)
     params = dict(vmem_limit_bytes=LIMIT)
-    scratch = []
+    scratch, near_shape = [], []
     if wired:
         mine = width // 8
         grads, grad_shape = ANY_SPEC, (2, 4, mine, inner)
         scratch = [
             pltpu.VMEM((2, 2, width, chunk), BF),
             pltpu.VMEM(grad_shape, BF),
-            pltpu.VMEM((2, 2, 4, mine, chunk), BF),
+            pltpu.VMEM((steps, 2, 4, mine, chunk), BF),
             pltpu.SemaphoreType.DMA((2, 4)),
             pltpu.SemaphoreType.DMA((steps,)),
-            pltpu.SemaphoreType.DMA((2,)),
+            pltpu.SemaphoreType.DMA((steps,)),
+            pltpu.SemaphoreType.DMA((steps, 4)),
+            pltpu.SemaphoreType.DMA((steps,)),
         ]
+        near_shape = [jax.ShapeDtypeStruct((2, 2, 2, mine // 2, inner), BF)]
         params.update(collective_id=6, has_side_effects=True)
     return pl.pallas_call(
         functools.partial(feed_kernel, steps, wired),
@@ -1410,7 +1445,8 @@
             grads,
             pl.BlockSpec((1, chunk), lambda i: (0, late(i))),
             whole(8, width),
-        ],
+        ]
+        + [ANY_SPEC] * len(near_shape),
         out_shape=[
             jax.ShapeDtypeStruct((rows, width), BF),
             jax.ShapeDtypeStruct((rows, width), F32),
@@ -1419,7 +1455,8 @@
             jax.ShapeDtypeStruct(grad_shape, BF),
             jax.ShapeDtypeStruct((1, inner), F32),
             jax.ShapeDtypeStruct((8, width), F32),
-        ],
+        ]
+        + near_shape,
         scratch_shapes=[
             pltpu.VMEM((2, width, inner), BF),
             pltpu.VMEM((1, width, width), BF),
@@ -1705,7 +1742,7 @@
     )
     if wires:
         wo, ud, tangent = arrived
-    out, d_mixed, g_vec, g_out, g_ud, g_upb, small = feed(
+    out, d_mixed, g_vec, g_out, g_ud, g_upb, small, *near = feed(
         ud,
         wo,
         vec,
@@ -1717,8 +1754,8 @@
     )
     backward = (prob, g_vec, q_word, q_pos, keys, values, rel, block)
     if groups == 8:
-        d_proj, dk_t, dv_t, drel_t, biases, grad_up, grad_down, content_out, query_out = (
-            attend_backward(*backward, (g_ud, out))
+        d_proj, dk_t, dv_t, drel_t, biases, grad_up, grad_down, grad_out, content_out, query_out = (
+            attend_backward(*backward, (g_ud, *near, g_out[None], out))
         )
     else:
         d_proj, dk_t, dv_t, drel_t, biases = attend_backward(*backward)
@@ -1735,11 +1772,10 @@
             grad_value,
             grad_query,
             grad_pos,
-            grad_out,
             content_grad,
             query_grad,
             small,
-        ) = finish(arrays, g_out[None], d_mixed, small)
+        ) = finish(arrays, d_mixed, small)
         arrays = [content_out, query_out, content_grad, query_grad, grad_query, grad_key]
         arrays += [grad_value, grad_pos, grad_out, grad_up, grad_down]
         *arrays, up_sum, down_sum, a1, b1, a2, b2, word_sum, pos_sum = emit(

time: 280 us -> 278 us (level)
    pallas_call x1, Pallas kernels: 37 us -> 52.7 us  [feed(): pl.pallas_call(functools.partial(feed_kernel, steps, wired), grid=(2 * st...]
    pallas_call x1, Pallas kernels: 65.9 us -> 54.3 us  [attend_backward(): pl.pallas_call(functools.partial(attend_backward_kernel, block, bool(wire...]
    pallas_call x1, Pallas kernels: 58.5 us -> 52.5 us  [finish(): pl.pallas_call(finish_kernel, in_specs=[ANY_SPEC] * INPUTS + [vmem] * 2,...]
where the time goes in v10:
time: 278 us
  Pallas kernels  276 us (99%)
    pallas_call x1, Pallas kernels, enter(): pl.pallas_call(enter_kernel, in_specs=[SMEM_SPEC] * 3 + [ANY_SPEC] * 4 +...  82 us
    pallas_call x1, Pallas kernels, attend_backward(): pl.pallas_call(functools.partial(attend_backward_kernel, block, bool(wire...  54.3 us
    pallas_call x1, Pallas kernels, feed(): pl.pallas_call(functools.partial(feed_kernel, steps, wired), grid=(2 * st...  52.7 us
    pallas_call x1, Pallas kernels, finish(): pl.pallas_call(finish_kernel, in_specs=[ANY_SPEC] * INPUTS + [vmem] * 2,...  52.5 us
    pallas_call x1, Pallas kernels, attend_forward(): pl.pallas_call(functools.partial(attend_forward_kernel, block, bool(wires...  31.1 us

profile of v10, /device:TPU:0, one launch (start us, length us, event | category | flops | bytes accessed | tf_op | source)
XLA Modules:
  0.0 278.2 jit_solution(11568296097963460746)
XLA Ops:
  0.7 82.0 %enter.1 = (bf16[1024,768]{1,0:T(8,128)(2,1)}, bf16[1024,768]{1,0:T(8,128)(2,1)}, bf16[1536,768]{1,0:T(8,128)(2,1)}, bf16[512,768]{1,0:T(8,128)(2,1)}, bf16[512,...) custom-call(s32[16]{0:T(128)} %slot_ref.1, ...), custom_call_target="tpu_custom_call" | custom-call | bytes 67108864 | tf_op jit(solution)/shard_map/enter/pallas_call | solution.py:840
  82.7 31.1 %attend_forward.1 = (bf16[512,768]{1,0:T(8,128)(2,1)}, bf16[12,512,1024]{2,1,0:T(8,128)(2,1)}, bf16[1,768,768]{2,1,0:T(8,128)(2,1)}, bf16[2,768,3072]{2,1,0:T(8,128)(2,1)}, bf16[512,768]{1,0:T(8,128)(2,1)}) custom-call(bf16[512,768]{1,0:T(8,128)(2,1)} %get-tuple-element.81.refs_0_.refs_2_, ...), custom_call_target="tpu_custom_call", output_to_operand_aliasing={{2}: (7, {}), {3}: (8, {})} | custom-call | flops 3221225472 | bytes 16777216 | tf_op jit(solution)/shard_map/attend_forward/pallas_call | solution.py:1024
  113.8 52.7 %feed.1 = (bf16[512,768]{1,0:T(8,128)(2,1)}, f32[512,768]{1,0:T(8,128)}, bf16[512,768]{1,0:T(8,128)(2,1)}, bf16[768,768]{1,0:T(8,128)(2,1)}, bf16[2,4,96,3072]{3...) custom-call(bf16[2,768,3072]{2,1,0:T(8,128)(2,1)} %get-tuple-element.91.refs_0_, ...), custom_call_target="tpu_custom_call" | custom-call | flops 14495514624 | bytes 37748736 | tf_op jit(solution)/shard_map/feed/pallas_call | solution.py:1433
  166.5 0.0 copy-start
  166.5 0.0 copy-start.1
  166.5 54.3 %attend_backward.1 = (bf16[512,768]{1,0:T(8,128)(2,1)}, bf16[768,1024]{1,0:T(8,128)(2,1)}, bf16[768,1024]{1,0:T(8,128)(2,1)}, bf16[768,1536]{1,0:T(8,128)(2,1)},...) custom-call(bf16[12,512,1024]{2,1,0:T(8,128)(2,1)} %get-tuple-elemen, ...), custom_call_target="tpu_custom_call" | custom-call | flops 6442450944 | bytes 20971520 | tf_op jit(solution)/shard_map/attend_backward/pallas_call | solution.py:1197
  220.9 0.7 reshape.60
  221.6 0.0 copy-done
  221.6 0.0 copy-done.1
  221.6 0.6 fusion.refs_9_
  222.2 52.5 %finish.1 = (f32[96,192]{1,0:T(8,128)}, f32[96,192]{1,0:T(8,128)}, f32[96,192]{1,0:T(8,128)}, f32[96,192]{1,0:T(8,128)}, bf16[2,128,768]{2,1,0:T(8,128)(2,1)}, /...) custom-call(bf16[512,768]{1,0:T(8,128)(2,1)} %get-tuple-element.80.refs_3_.refs_0_, ...), custom_call_target="tpu_custom_call" | custom-call | flops 21474836480 | bytes 67108864 | tf_op jit(solution)/shard_map/finish/pallas_call | solution.py:514
  274.7 3.3 %emit.1 = (bf16[2,128,768]{2,1,0:T(8,128)(2,1)}, bf16[2,128,768]{2,1,0:T(8,128)(2,1)}, bf16[2,128,768]{2,1,0:T(8,128)(2,1)}, bf16[2,128,768]{2,1,0:T(8,128)(2,1)...) custom-call(f32[72,128]{1,0:T(8,128)} %get-tuple-element.110.small_r, ...), custom_call_target="tpu_custom_call" | custom-call | tf_op jit(solution)/shard_map/emit/pallas_call | solution.py:557
  (1 shorter events, 0.0 us)
Async XLA Ops:
  166.5 55.0 %copy-start = (f32[8,768]{1,0:T(8,128)S(1)}, f32[8,768]{1,0:T(8,128)}, u32[]{:S(2)}) copy-start(f32[8,768]{1,0:T(8,128)} %get-tuple-element.108) | copy-start | bytes 73732
  166.5 55.0 %copy-start.1 = (f32[1,3072]{1,0:T(1,128)S(1)}, f32[1,3072]{1,0:T(1,128)}, u32[]{:S(2)}) copy-start(f32[1,3072]{1,0:T(1,128)} %get-tuple-element.107) | copy-start | bytes 36868

commit v11 on v10

--- a/solution.py
+++ b/solution.py
@@ -742,7 +742,7 @@
     settle(columns(z), recv.at[8])
     ud_copy(4).wait_recv()
     ud_copy(5).wait_recv()
-    for i in (0, 1, 2, 3, 6, 7):
+    for i in (0, 1, 6, 7):
         for one in gathers:
             one.start(i)
     gather.last()
@@ -811,12 +811,10 @@
     project_step(
         whole, context, stream, table, wb_ref, pb_ref, *outs, hooks=(before_stream, before_context)
     )
-    for one in gathers:
-        one.after((2, 3), ((10,), (11,)))
     settle(wo.at[:, own_rows, :], recv.at[7])
     gather.wait((), range(14))
     for one in gathers:
-        one.wait(range(6, 12), (0, 1, 2, 3) + tuple(range(6, 12)))
+        one.wait(range(6, 10), (0, 1, 6, 7, 8, 9))
     keep_whole.wait()
     keep_context.wait()
     for i in range(4):
@@ -971,21 +969,25 @@
     def _():
         greet(near_partners(place))
         for gather in gathers:
+            gather.start(2, 3)
+        for gather in gathers:
             gather.start(4, 5)
         for i in range(4):
             tan_copy(i, "start")
+
+    @pl.when(step == 4)
+    def _():
+        for gather in gathers:
+            gather.after((2, 3), ((10,), (11,)))
+
+    attend_forward_step(block, *ins, *outs)
 
     @pl.when(step == steps - 1)
     def _():
         for gather in gathers:
             gather.after((4, 5), ((12,), (13,)))
-
-    attend_forward_step(block, *ins, *outs)
-
-    @pl.when(step == steps - 1)
-    def _():
         for gather in gathers:
-            gather.wait((12, 13), (4, 5, 12, 13))
+            gather.wait(range(10, 14), (2, 3, 4, 5) + tuple(range(10, 14)))
         settle(tangent, recv.at[0])
         for i in range(4):
             tan_copy(i, "wait")

time: 278 us -> 283 us (1.018)
  Pallas kernels: 276 us -> 280 us
    pallas_call x1, Pallas kernels: 31.1 us -> 38.5 us  [attend_forward(): pl.pallas_call(functools.partial(attend_forward_kernel, block, bool(wires...]
    pallas_call x1, Pallas kernels: 82 us -> 78.8 us  [enter(): pl.pallas_call(enter_kernel, in_specs=[SMEM_SPEC] * 3 + [ANY_SPEC] * 4 +...]
where the time goes in v11:
time: 283 us; the launch traced here: 282 us
  Pallas kernels  280 us (99%)
    pallas_call x1, Pallas kernels, enter(): pl.pallas_call(enter_kernel, in_specs=[SMEM_SPEC] * 3 + [ANY_SPEC] * 4 +...  78.8 us
    pallas_call x1, Pallas kernels, attend_backward(): pl.pallas_call(functools.partial(attend_backward_kernel, block, bool(wire...  54.3 us
    pallas_call x1, Pallas kernels, feed(): pl.pallas_call(functools.partial(feed_kernel, steps, wired), grid=(2 * st...  52.7 us
    pallas_call x1, Pallas kernels, finish(): pl.pallas_call(finish_kernel, in_specs=[ANY_SPEC] * INPUTS + [vmem] * 2,...  52.5 us
    pallas_call x1, Pallas kernels, attend_forward(): pl.pallas_call(functools.partial(attend_forward_kernel, block, bool(wires...  38.5 us

profile of v11, /device:TPU:0, one launch (start us, length us, event | category | flops | bytes accessed | tf_op | source)
XLA Modules:
  0.0 282.3 jit_solution(297295500596279125)
XLA Ops:
  0.7 78.8 %enter.1 = (bf16[1024,768]{1,0:T(8,128)(2,1)}, bf16[1024,768]{1,0:T(8,128)(2,1)}, bf16[1536,768]{1,0:T(8,128)(2,1)}, bf16[512,768]{1,0:T(8,128)(2,1)}, bf16[512,...) custom-call(s32[16]{0:T(128)} %slot_ref.1, ...), custom_call_target="tpu_custom_call" | custom-call | bytes 67108864 | tf_op jit(solution)/shard_map/enter/pallas_call | solution.py:838
  79.4 38.5 %attend_forward.1 = (bf16[512,768]{1,0:T(8,128)(2,1)}, bf16[12,512,1024]{2,1,0:T(8,128)(2,1)}, bf16[1,768,768]{2,1,0:T(8,128)(2,1)}, bf16[2,768,3072]{2,1,0:T(8,128)(2,1)}, bf16[512,768]{1,0:T(8,128)(2,1)}) custom-call(bf16[512,768]{1,0:T(8,128)(2,1)} %get-tuple-element.81.refs_0_.refs_2_, ...), custom_call_target="tpu_custom_call", output_to_operand_aliasing={{2}: (7, {}), {3}: (8, {})} | custom-call | flops 3221225472 | bytes 16777216 | tf_op jit(solution)/shard_map/attend_forward/pallas_call | solution.py:1026
  117.9 52.7 %feed.1 = (bf16[512,768]{1,0:T(8,128)(2,1)}, f32[512,768]{1,0:T(8,128)}, bf16[512,768]{1,0:T(8,128)(2,1)}, bf16[768,768]{1,0:T(8,128)(2,1)}, bf16[2,4,96,3072]{3...) custom-call(bf16[2,768,3072]{2,1,0:T(8,128)(2,1)} %get-tuple-element.91.refs_0_, ...), custom_call_target="tpu_custom_call" | custom-call | flops 14495514624 | bytes 37748736 | tf_op jit(solution)/shard_map/feed/pallas_call | solution.py:1435
  170.6 0.0 copy-start
  170.6 0.0 copy-start.1
  170.6 54.3 %attend_backward.1 = (bf16[512,768]{1,0:T(8,128)(2,1)}, bf16[768,1024]{1,0:T(8,128)(2,1)}, bf16[768,1024]{1,0:T(8,128)(2,1)}, bf16[768,1536]{1,0:T(8,128)(2,1)},...) custom-call(bf16[12,512,1024]{2,1,0:T(8,128)(2,1)} %get-tuple-elemen, ...), custom_call_target="tpu_custom_call" | custom-call | flops 6442450944 | bytes 20971520 | tf_op jit(solution)/shard_map/attend_backward/pallas_call | solution.py:1199
  225.0 0.7 reshape.60
  225.7 0.0 copy-done
  225.7 0.0 copy-done.1
  225.7 0.6 fusion.refs_9_
  226.3 52.5 %finish.1 = (f32[96,192]{1,0:T(8,128)}, f32[96,192]{1,0:T(8,128)}, f32[96,192]{1,0:T(8,128)}, f32[96,192]{1,0:T(8,128)}, bf16[2,128,768]{2,1,0:T(8,128)(2,1)}, /...) custom-call(bf16[512,768]{1,0:T(8,128)(2,1)} %get-tuple-element.80.refs_3_.refs_0_, ...), custom_call_target="tpu_custom_call" | custom-call | flops 21474836480 | bytes 67108864 | tf_op jit(solution)/shard_map/finish/pallas_call | solution.py:514
  278.8 3.3 %emit.1 = (bf16[2,128,768]{2,1,0:T(8,128)(2,1)}, bf16[2,128,768]{2,1,0:T(8,128)(2,1)}, bf16[2,128,768]{2,1,0:T(8,128)(2,1)}, bf16[2,128,768]{2,1,0:T(8,128)(2,1)...) custom-call(f32[72,128]{1,0:T(8,128)} %get-tuple-element.110.small_r, ...), custom_call_target="tpu_custom_call" | custom-call | tf_op jit(solution)/shard_map/emit/pallas_call | solution.py:557
  (1 shorter events, 0.0 us)
Async XLA Ops:
  170.6 55.1 %copy-start = (f32[8,768]{1,0:T(8,128)S(1)}, f32[8,768]{1,0:T(8,128)}, u32[]{:S(2)}) copy-start(f32[8,768]{1,0:T(8,128)} %get-tuple-element.108) | copy-start | bytes 73732
  170.6 55.1 %copy-start.1 = (f32[1,3072]{1,0:T(1,128)S(1)}, f32[1,3072]{1,0:T(1,128)}, u32[]{:S(2)}) copy-start(f32[1,3072]{1,0:T(1,128)} %get-tuple-element.107) | copy-start | bytes 36868

commit v12 on v11

--- a/solution.py
+++ b/solution.py
@@ -701,7 +701,8 @@
     mat_copy(1).wait_recv()
     mat_copy(3).start()
     for i in range(4):
-        ud_copy(i).start()
+        stream_copy(i, "start")
+
     mat_copy(2).wait_recv()
     mat_copy(3).wait_recv()
     for m in range(5):
@@ -711,13 +712,6 @@
     gather.start(0, 1, 2, 3, 6, 7)
     pltpu.make_async_copy(slab.at[0:4], whole.at[:, own_rows, :], recv.at[6]).start()
     pltpu.make_async_copy(slab.at[4:5], wo.at[:, own_rows, :], recv.at[7]).start()
-
-    settle(columns(down), ud_recv.at[0])
-    ud_copy(4).start()
-    settle(columns(up), ud_recv.at[1])
-    ud_copy(5).start()
-    for i in range(4):
-        stream_copy(i, "start")
 
     settle(spread, recv.at[0])
     for q in range(16):
@@ -735,16 +729,12 @@
                 copy = pltpu.make_async_copy(src, dst, recv.at[5])
             copy.start()
 
+    for i in range(4):
+        ud_copy(i).start()
     gather.middle()
     wo_gather = Gather(place, wo, slab.at[4:5], wo_send, wo_recv)
     ud_gather = Gather(place, ud, None, far_send, far_recv)
     gathers = (ud_gather, wo_gather)
-    settle(columns(z), recv.at[8])
-    ud_copy(4).wait_recv()
-    ud_copy(5).wait_recv()
-    for i in (0, 1, 6, 7):
-        for one in gathers:
-            one.start(i)
     gather.last()
 
     pick_pair = push(
@@ -760,6 +750,11 @@
     def _():
         settle(context.at[first:], recv.at[3])
         lead_copy.start()
+
+    settle(columns(down), ud_recv.at[0])
+    ud_copy(4).start()
+    settle(columns(up), ud_recv.at[1])
+    ud_copy(5).start()
 
     settle(all_ints, recv.at[2])
     seq = 4 * lax.div(d, 2) + z
@@ -782,6 +777,12 @@
     ranks = jnp.transpose(jnp.broadcast_to(rank.astype(F32), (8, seq_len)))
     thr_ref[...] = ranks[:, 0:1].astype(jnp.int32) + jnp.where(core == 0, 1, 0)
 
+    settle(columns(z), recv.at[8])
+    ud_copy(4).wait_recv()
+    ud_copy(5).wait_recv()
+    for i in (0, 1, 6, 7):
+        for one in gathers:
+            one.start(i)
     gather.wait(range(6, 14), ())
     settle(whole.at[:, own_rows, :], recv.at[6])
     keep_whole = pltpu.make_async_copy(whole, whole_out, local.at[1])

time: 283 us -> 293 us (1.035)
  Pallas kernels: 280 us -> 290 us
    pallas_call x1, Pallas kernels: 78.8 us -> 88.2 us  [enter(): pl.pallas_call(enter_kernel, in_specs=[SMEM_SPEC] * 3 + [ANY_SPEC] * 4 +...]
where the time goes in v12:
time: 293 us
  Pallas kernels  290 us (99%)
    pallas_call x1, Pallas kernels, enter(): pl.pallas_call(enter_kernel, in_specs=[SMEM_SPEC] * 3 + [ANY_SPEC] * 4 +...  88.2 us
    pallas_call x1, Pallas kernels, attend_backward(): pl.pallas_call(functools.partial(attend_backward_kernel, block, bool(wire...  54.3 us
    pallas_call x1, Pallas kernels, feed(): pl.pallas_call(functools.partial(feed_kernel, steps, wired), grid=(2 * st...  52.7 us
    pallas_call x1, Pallas kernels, finish(): pl.pallas_call(finish_kernel, in_specs=[ANY_SPEC] * INPUTS + [vmem] * 2,...  52.5 us
    pallas_call x1, Pallas kernels, attend_forward(): pl.pallas_call(functools.partial(attend_forward_kernel, block, bool(wires...  39.3 us

profile of v12, /device:TPU:0, one launch (start us, length us, event | category | flops | bytes accessed | tf_op | source)
XLA Modules:
  0.0 292.5 jit_solution(13959051434480717525)
XLA Ops:
  0.7 88.2 %enter.1 = (bf16[1024,768]{1,0:T(8,128)(2,1)}, bf16[1024,768]{1,0:T(8,128)(2,1)}, bf16[1536,768]{1,0:T(8,128)(2,1)}, bf16[512,768]{1,0:T(8,128)(2,1)}, bf16[512,...) custom-call(s32[16]{0:T(128)} %slot_ref.1, ...), custom_call_target="tpu_custom_call" | custom-call | bytes 67108864 | tf_op jit(solution)/shard_map/enter/pallas_call | solution.py:839
  88.8 39.3 %attend_forward.1 = (bf16[512,768]{1,0:T(8,128)(2,1)}, bf16[12,512,1024]{2,1,0:T(8,128)(2,1)}, bf16[1,768,768]{2,1,0:T(8,128)(2,1)}, bf16[2,768,3072]{2,1,0:T(8,128)(2,1)}, bf16[512,768]{1,0:T(8,128)(2,1)}) custom-call(bf16[512,768]{1,0:T(8,128)(2,1)} %get-tuple-element.81.refs_0_.refs_2_, ...), custom_call_target="tpu_custom_call", output_to_operand_aliasing={{2}: (7, {}), {3}: (8, {})} | custom-call | flops 3221225472 | bytes 16777216 | tf_op jit(solution)/shard_map/attend_forward/pallas_call | solution.py:1027
  128.2 52.7 %feed.1 = (bf16[512,768]{1,0:T(8,128)(2,1)}, f32[512,768]{1,0:T(8,128)}, bf16[512,768]{1,0:T(8,128)(2,1)}, bf16[768,768]{1,0:T(8,128)(2,1)}, bf16[2,4,96,3072]{3...) custom-call(bf16[2,768,3072]{2,1,0:T(8,128)(2,1)} %get-tuple-element.91.refs_0_, ...), custom_call_target="tpu_custom_call" | custom-call | flops 14495514624 | bytes 37748736 | tf_op jit(solution)/shard_map/feed/pallas_call | solution.py:1436
  180.9 0.0 copy-start
  180.9 0.0 copy-start.1
  180.9 54.3 %attend_backward.1 = (bf16[512,768]{1,0:T(8,128)(2,1)}, bf16[768,1024]{1,0:T(8,128)(2,1)}, bf16[768,1024]{1,0:T(8,128)(2,1)}, bf16[768,1536]{1,0:T(8,128)(2,1)},...) custom-call(bf16[12,512,1024]{2,1,0:T(8,128)(2,1)} %get-tuple-elemen, ...), custom_call_target="tpu_custom_call" | custom-call | flops 6442450944 | bytes 20971520 | tf_op jit(solution)/shard_map/attend_backward/pallas_call | solution.py:1200
  235.2 0.7 reshape.60
  235.9 0.0 copy-done
  235.9 0.0 copy-done.1
  235.9 0.6 fusion.refs_9_
  236.6 52.5 %finish.1 = (f32[96,192]{1,0:T(8,128)}, f32[96,192]{1,0:T(8,128)}, f32[96,192]{1,0:T(8,128)}, f32[96,192]{1,0:T(8,128)}, bf16[2,128,768]{2,1,0:T(8,128)(2,1)}, /...) custom-call(bf16[512,768]{1,0:T(8,128)(2,1)} %get-tuple-element.80.refs_3_.refs_0_, ...), custom_call_target="tpu_custom_call" | custom-call | flops 21474836480 | bytes 67108864 | tf_op jit(solution)/shard_map/finish/pallas_call | solution.py:514
  289.1 3.3 %emit.1 = (bf16[2,128,768]{2,1,0:T(8,128)(2,1)}, bf16[2,128,768]{2,1,0:T(8,128)(2,1)}, bf16[2,128,768]{2,1,0:T(8,128)(2,1)}, bf16[2,128,768]{2,1,0:T(8,128)(2,1)...) custom-call(f32[72,128]{1,0:T(8,128)} %get-tuple-element.110.small_r, ...), custom_call_target="tpu_custom_call" | custom-call | tf_op jit(solution)/shard_map/emit/pallas_call | solution.py:557
  (1 shorter events, 0.0 us)
Async XLA Ops:
  180.9 55.0 %copy-start = (f32[8,768]{1,0:T(8,128)S(1)}, f32[8,768]{1,0:T(8,128)}, u32[]{:S(2)}) copy-start(f32[8,768]{1,0:T(8,128)} %get-tuple-element.108) | copy-start | bytes 73732
  180.9 55.0 %copy-start.1 = (f32[1,3072]{1,0:T(1,128)S(1)}, f32[1,3072]{1,0:T(1,128)}, u32[]{:S(2)}) copy-start(f32[1,3072]{1,0:T(1,128)} %get-tuple-element.107) | copy-start | bytes 36868
